TPU v7x, 128 devices: a whole 4x4x4 slice. The times are simulated.
128 devices in a mesh: pipe: 4 (over y), dp: 32 (over z, x, core).
Axes of the slice: x: 4, y: 4, z: 4, core: 2. Of those that a mesh axis runs over, the one named last changes fastest.
Arguments:
- x_in: bfloat16 [4, 1024, 4096], P(None, 'dp'), may hold values from -6 to 6
- cotangent: bfloat16 [4, 1024, 4096], P(None, 'dp'), may hold values from -6 to 6
- weights: bfloat16 [4, 64, 64, 2048], P('pipe', 'dp'), as said below
- live_rows: int32 [4, 64, 32], P('pipe'), may hold values from 0 to 63, as said below
- moment: float32 [4, 64, 64, 2048], P('pipe', 'dp'), may hold values from -0.125 to 0.125
- second: float32 [4, 64, 64, 2048], P('pipe', 'dp'), may hold values from 1.2207031e-05 to 0.00024414062
Outputs:
- weights_out: bfloat16 [4, 64, 64, 2048], P('pipe', 'dp')
- moment_out: float32 [4, 64, 64, 2048], P('pipe', 'dp')
- second_out: float32 [4, 64, 64, 2048], P('pipe', 'dp')
Inputs may be any that keep to these rules, and one draw needn't show every extreme that they name: `live_rows`: for each layer and block column the 32 entries are distinct block rows. `weights`: entry [l, j, b, k * 64 + a] is the weight from input feature live_rows[l, j, k] * 64 + a to output feature j * 64 + b; unstored blocks are zero.
All inputs are finite; a program needn't handle non-finite values.
Results may differ from a plain program's by a relative error of at most 0.009.
Values may be sent and summed in bfloat16 or wider, within the bound.
A program may use at most 256 MiB of HBM per device.

v0:
```python
import math

import jax
import jax.numpy as jnp
from jax import lax
from jax.sharding import PartitionSpec as P

HEAD = 128


column_group = 8


def shifted(value, axis, steps):
    count = lax.axis_size(axis)
    leading, last = (max(0, -steps), min(count, count - steps))
    return lax.ppermute(value, axis, [(source, source + steps) for source in range(leading, last)])


def shrink(magnitude, threshold):
    return jnp.maximum(magnitude - threshold, 0.0) / jnp.maximum(magnitude, threshold)


def column_products(normed, section_weights, live_index):
    tokens, features = normed.shape
    column_count, block_size, wide = section_weights.shape
    live_count = live_index.shape[1]
    group_count = column_count // column_group
    normed_blocks = normed.reshape(tokens, column_count, block_size)

    def column_per_group(members):
        weight_part, index_part = members
        picked = jnp.take(normed_blocks, index_part.reshape(-1), axis=1).reshape(
            tokens, column_group, wide
        )
        return jnp.einsum("tjk,jbk->tjb", picked, weight_part, preferred_element_type=jnp.float32)

    result = lax.map(
        column_per_group,
        (
            section_weights.reshape(group_count, column_group, block_size, wide),
            live_index.reshape(group_count, column_group, live_count),
        ),
    )
    return result.transpose(1, 0, 2, 3).reshape(tokens, features)


def dense_transposed(section_weights, live_index):
    column_count, block_size, wide = section_weights.shape
    live_count = live_index.shape[1]
    group_count = column_count // column_group
    features = column_count * block_size
    targets = jnp.arange(column_count, dtype=jnp.int32)

    def dense_per_group(members):
        weight_part, index_part = members
        chosen = (index_part[:, :, None] == targets[None, None, :]).astype(jnp.bfloat16)
        slab = jnp.einsum(
            "jkr,jbka->jbra",
            chosen,
            weight_part.reshape(column_group, block_size, live_count, block_size),
            preferred_element_type=jnp.float32,
        )
        return slab.astype(jnp.bfloat16).reshape(column_group * block_size, features)

    slabs = lax.map(
        dense_per_group,
        (
            section_weights.reshape(group_count, column_group, block_size, wide),
            live_index.reshape(group_count, column_group, live_count),
        ),
    )
    return slabs.reshape(features, features)


def layer_forward(entering, section_weights, live_index):
    as_float = entering.astype(jnp.float32)
    inverse_rms = lax.rsqrt(jnp.mean(as_float * as_float, axis=-1, keepdims=True) + 1e-05)
    normed = (as_float * inverse_rms).astype(jnp.bfloat16)
    pre_act = column_products(normed, section_weights, live_index)
    return ((as_float + jax.nn.silu(pre_act)).astype(jnp.bfloat16), normed, pre_act)


def layer_backward(arriving, entering, pre_act, dense_weights):
    as_float = entering.astype(jnp.float32)
    inverse_rms = lax.rsqrt(jnp.mean(as_float * as_float, axis=-1, keepdims=True) + 1e-05)
    sigmoid_z = jax.nn.sigmoid(pre_act)
    grad_pre = (
        arriving.astype(jnp.float32) * (sigmoid_z * (1.0 + pre_act * (1.0 - sigmoid_z)))
    ).astype(jnp.bfloat16)
    grad_normed = jnp.dot(grad_pre, dense_weights, preferred_element_type=jnp.float32)
    scaled = as_float * inverse_rms
    leaving = (
        arriving.astype(jnp.float32)
        + inverse_rms
        * (grad_normed - scaled * jnp.mean(grad_normed * scaled, axis=-1, keepdims=True))
    ).astype(jnp.bfloat16)
    return (leaving, grad_pre)


def local(x_in, cotangent, weights, live_rows, moment, second):
    sections = lax.axis_size("pipe")
    section_index = lax.axis_index("pipe")
    micro_count, tokens, features = x_in.shape
    column_count = live_rows.shape[1]
    live_count = live_rows.shape[2]
    own_columns = weights.shape[1]
    block_size = weights.shape[2]
    live_index = live_rows[0]
    section_weights = lax.all_gather(weights[0], "dp", axis=0, tiled=True)
    tick_count = micro_count + sections - 1
    incoming = jnp.zeros((tokens, features), jnp.bfloat16)
    saved_in = jnp.zeros((micro_count, tokens, features), jnp.bfloat16)
    saved_normed = jnp.zeros((micro_count, tokens, features), jnp.bfloat16)
    saved_pre = jnp.zeros((micro_count, tokens, features), jnp.float32)
    for tick_index in range(tick_count):
        slot_raw = tick_index - section_index
        active_now = (slot_raw >= 0) & (slot_raw < micro_count)
        slot_index = jnp.clip(slot_raw, 0, micro_count - 1)
        entering = jnp.where(section_index == 0, x_in[min(tick_index, micro_count - 1)], incoming)

        def forward_work(state, slot_index=slot_index):
            current, store_in, store_normed, store_pre = state
            outgoing, normed, pre_act = layer_forward(current, section_weights, live_index)
            return (
                outgoing,
                store_in.at[slot_index].set(current),
                store_normed.at[slot_index].set(normed),
                store_pre.at[slot_index].set(pre_act),
            )

        def forward_skip(state):
            current, store_in, store_normed, store_pre = state
            return (jnp.zeros_like(current), store_in, store_normed, store_pre)

        outgoing, saved_in, saved_normed, saved_pre = lax.cond(
            active_now, forward_work, forward_skip, (entering, saved_in, saved_normed, saved_pre)
        )
        if tick_index + 1 < tick_count:
            incoming = shifted(outgoing, "pipe", 1)
    dense_weights = dense_transposed(section_weights, live_index)
    incoming_grad = jnp.zeros((tokens, features), jnp.bfloat16)
    saved_grad = jnp.zeros((micro_count, tokens, features), jnp.bfloat16)
    for tick_index in range(tick_count):
        slot_raw = tick_index - (sections - 1 - section_index)
        active_now = (slot_raw >= 0) & (slot_raw < micro_count)
        slot_index = jnp.clip(slot_raw, 0, micro_count - 1)
        arriving = jnp.where(
            section_index == sections - 1,
            cotangent[min(tick_index, micro_count - 1)],
            incoming_grad,
        )

        def backward_work(state, slot_index=slot_index):
            current, store_grad = state
            leaving, grad_pre = layer_backward(
                current, saved_in[slot_index], saved_pre[slot_index], dense_weights
            )
            return (leaving, store_grad.at[slot_index].set(grad_pre))

        def backward_skip(state):
            current, store_grad = state
            return (jnp.zeros_like(current), store_grad)

        leaving, saved_grad = lax.cond(
            active_now, backward_work, backward_skip, (arriving, saved_grad)
        )
        if tick_index + 1 < tick_count:
            incoming_grad = shifted(leaving, "pipe", -1)
    all_rows = micro_count * tokens
    normed_blocks = saved_normed.reshape(all_rows, column_count, block_size)
    grad_blocks = saved_grad.reshape(all_rows, column_count, block_size)
    inverse_tokens = 1.0 / (all_rows * lax.axis_size("dp"))
    cast_type = jnp.bfloat16
    group_size = math.gcd(column_count, column_group)
    group_count = column_count // group_size
    index_part = live_index.reshape(group_count, group_size, live_count)
    grad_part = grad_blocks.reshape(all_rows, group_count, group_size, block_size).transpose(
        1, 0, 2, 3
    )

    def grad_per_group(members):
        index_group, grad_group = members
        picked = jnp.take(normed_blocks, index_group.reshape(-1), axis=1).reshape(
            all_rows, group_size, live_count * block_size
        )
        return (
            jnp.einsum("tjk,tjb->jbk", picked, grad_group, preferred_element_type=jnp.float32)
            * inverse_tokens
        ).astype(cast_type)

    gradient = lax.psum_scatter(
        lax.map(grad_per_group, (index_part, grad_part)).reshape(
            column_count, block_size, live_count * block_size
        ),
        "dp",
        scatter_dimension=0,
        tiled=True,
    ).astype(jnp.float32)
    rate = 0.1 / math.sqrt(live_count * block_size)
    moment_new = 0.9 * moment[0] + 0.1 * gradient
    second_new = 0.95 * second[0] + 0.05 * gradient * gradient
    stepped = weights[0].astype(jnp.float32) - rate * moment_new / (jnp.sqrt(second_new) + 1e-08)
    own_index = lax.dynamic_slice_in_dim(
        live_index, lax.axis_index("dp") * own_columns, own_columns, 0
    )
    blocked = stepped.reshape(own_columns, block_size, live_count, block_size)
    magnitude = jnp.sqrt(jnp.sum(blocked * blocked, axis=(1, 3)))
    leafed = (
        blocked * shrink(magnitude, 0.15 * math.sqrt(block_size / live_count))[:, None, :, None]
    )
    block_squares = jnp.sum(leafed * leafed, axis=(1, 3))
    head_count = features // HEAD
    head_index = own_index // (HEAD // block_size)
    onehot = (
        head_index[:, :, None] == jnp.arange(head_count, dtype=jnp.int32)[None, None, :]
    ).astype(jnp.float32)
    head_squares = lax.psum(jnp.sum(onehot * block_squares[:, :, None], axis=(0, 1)), "dp")
    head_factor = shrink(jnp.sqrt(head_squares), 0.45 * math.sqrt(HEAD))
    headed = leafed * jnp.sum(onehot * head_factor[None, None, :], axis=2)[:, None, :, None]
    layer_squares = lax.psum(jnp.sum(headed * headed), "dp")
    layer_factor = shrink(jnp.sqrt(layer_squares), 0.45 * math.sqrt(features))
    weights_out = (
        (headed * layer_factor)
        .astype(jnp.bfloat16)
        .reshape(own_columns, block_size, live_count * block_size)
    )
    return (weights_out[None], moment_new[None], second_new[None])


def solution(mesh):
    placed = (
        P(None, "dp", None),
        P(None, "dp", None),
        P("pipe", "dp", None, None),
        P("pipe", None, None),
        P("pipe", "dp", None, None),
        P("pipe", "dp", None, None),
    )
    return jax.shard_map(
        local,
        mesh=mesh,
        in_specs=placed,
        out_specs=(
            P("pipe", "dp", None, None),
            P("pipe", "dp", None, None),
            P("pipe", "dp", None, None),
        ),
        check_vma=False,
    )
```

profile of v0, /device:TPU:1, one launch (start us, length us, event | category | flops | bytes accessed | tf_op | source)
XLA Modules:
  0.0 1587.1 jit_solution(2375558503213230283)
XLA Ops:
  8.0 78.6 %all-gather.3.cloned.1.call-done = bf16[1,64,64,2048]{3,2,0,1:T(8,128)(2,1)} async-done(((bf16[1,2,64,2048]{3,2,0,1:T(8,128)(2,1)}), bf16[1,64,64,2048]{3,2,0,1:T(8,128)(2,1)}) %all-gather.3.cloned.1.call-update) | async-done | bytes 16777232 | tf_op jit(solution)/shard_map/all_gather | solution.py:110
  87.3 84.7 %conditional.14 = (bf16[32,4096]{1,0:T(8,128)(2,1)S(1)}, bf16[4,32,4096]{2,1,0:T(8,128)(2,1)}, bf16[4,32,4096]{2,1,0:T(8,128)(2,1)}, f32[4,32,4096]{2,1,0:T(8,128)}) conditional(s32[]{:T(128)} %convert_element_type.242, () %tuple.272, (bf16[4,32,4096]{2,1,0:T(8,128)(2,1)}, pred[32,4096]{1,0:T(8,128)(4,1)S(1)}, bf16[32,4096]{1,0:T(8,128)(2,1)S(1)}, ...), branch_computations={%region_0.1_spmd, %region_1.7_spmd} | conditional | flops 69864752 | bytes 28641040 | solution.py:136
  95.7 69.9 %while.112 = (s32[]{:T(128)}, f32[8,32,8,64]{3,1,2,0:T(8,128)}, bf16[8,8,64,2048]{3,2,1,0:T(8,128)(2,1)}, s32[8,8,32]{2,1,0:T(8,128)S(1)}, bf16[32,64,64]{2,0,1:T(8,128)(2,1)S(1)}, /*index=5*/s32[]{:T(128)}) while((s32[]{:T(128)}, f32[8,32,8,64]{3,1,2,0:T(8,128)}, bf16[8,8,64,2048]{3,2,1,0:T(8,128)(2,1)}, s32[8,8,32]{2,1,0:T(8,128)S(1)}, ...), condition=%wide.region_4.5_spmd, body=%wide.region_3.4_spmd.sunk | while | flops 67636480 | bytes 11680329 | solution.py:38
  180.1 83.5 %conditional.15 = (bf16[32,4096]{1,0:T(8,128)(2,1)}, bf16[4,32,4096]{2,1,0:T(8,128)(2,1)}, bf16[4,32,4096]{2,1,0:T(8,128)(2,1)}, f32[4,32,4096]{2,1,0:T(8,128)}) conditional(s32[]{:T(128)} %convert_element_type.241, (bf16[4,32,4096]{2,1,0:T(8,128)(2,1)}, bf16[4,32,4096]{2,1,0:T(8,128)(2,1)}, f32[4,32,4096]{2,1,0:T(8,128)}) %tuple.274, ...), branch_computations={%region_6.8_spmd, %region_7.13_spmd} | conditional | flops 69864752 | bytes 21301482 | solution.py:136
  187.9 69.8 %while.113 = (s32[]{:T(128)}, f32[8,32,8,64]{3,1,2,0:T(8,128)}, bf16[8,8,64,2048]{3,2,1,0:T(8,128)(2,1)}, s32[8,8,32]{2,1,0:T(8,128)S(1)}, bf16[32,64,64]{2,0,1:T(8,128)(2,1)S(1)}, /*index=5*/s32[]{:T(128)}) while((s32[]{:T(128)}, f32[8,32,8,64]{3,1,2,0:T(8,128)}, bf16[8,8,64,2048]{3,2,1,0:T(8,128)(2,1)}, s32[8,8,32]{2,1,0:T(8,128)S(1)}, ...), condition=%wide.region_10.11_spmd, body=%wide.region_9.10_spmd.sunk | while | flops 67636480 | bytes 11680329 | solution.py:38
  272.8 83.2 %conditional.16 = (bf16[32,4096]{1,0:T(8,128)(2,1)}, bf16[4,32,4096]{2,1,0:T(8,128)(2,1)}, bf16[4,32,4096]{2,1,0:T(8,128)(2,1)}, f32[4,32,4096]{2,1,0:T(8,128)}) conditional(s32[]{:T(128)} %convert_element_type.240, (bf16[4,32,4096]{2,1,0:T(8,128)(2,1)}, bf16[4,32,4096]{2,1,0:T(8,128)(2,1)}, f32[4,32,4096]{2,1,0:T(8,128)}) %tuple.276, ...), branch_computations={%region_12.14_spmd, %region_13.19_spmd} | conditional | flops 69864752 | bytes 21301482 | solution.py:136
  280.3 69.8 %while.114 = (s32[]{:T(128)}, f32[8,32,8,64]{3,1,2,0:T(8,128)}, bf16[8,8,64,2048]{3,2,1,0:T(8,128)(2,1)}, s32[8,8,32]{2,1,0:T(8,128)S(1)}, bf16[32,64,64]{2,0,1:T(8,128)(2,1)S(1)}, /*index=5*/s32[]{:T(128)}) while((s32[]{:T(128)}, f32[8,32,8,64]{3,1,2,0:T(8,128)}, bf16[8,8,64,2048]{3,2,1,0:T(8,128)(2,1)}, s32[8,8,32]{2,1,0:T(8,128)S(1)}, ...), condition=%wide.region_16.17_spmd, body=%wide.region_15.16_spmd.sunk | while | flops 67636480 | bytes 11680329 | solution.py:38
  364.2 83.4 %conditional.17 = (bf16[32,4096]{1,0:T(8,128)(2,1)}, bf16[4,32,4096]{2,1,0:T(8,128)(2,1)}, bf16[4,32,4096]{2,1,0:T(8,128)(2,1)}, f32[4,32,4096]{2,1,0:T(8,128)}) conditional(s32[]{:T(128)} %convert_element_type.239, (bf16[4,32,4096]{2,1,0:T(8,128)(2,1)}, bf16[4,32,4096]{2,1,0:T(8,128)(2,1)}, f32[4,32,4096]{2,1,0:T(8,128)}) %tuple.278, ...), branch_computations={%region_18.20_spmd, %region_19.25_spmd} | conditional | flops 69864752 | bytes 21301482 | solution.py:136
  371.8 69.8 %while.115 = (s32[]{:T(128)}, f32[8,32,8,64]{3,1,2,0:T(8,128)}, bf16[8,8,64,2048]{3,2,1,0:T(8,128)(2,1)}, s32[8,8,32]{2,1,0:T(8,128)S(1)}, bf16[32,64,64]{2,0,1:T(8,128)(2,1)S(1)}, /*index=5*/s32[]{:T(128)}) while((s32[]{:T(128)}, f32[8,32,8,64]{3,1,2,0:T(8,128)}, bf16[8,8,64,2048]{3,2,1,0:T(8,128)(2,1)}, s32[8,8,32]{2,1,0:T(8,128)S(1)}, ...), condition=%wide.region_22.23_spmd, body=%wide.region_21.22_spmd.sunk | while | flops 67636480 | bytes 11680329 | solution.py:38
  456.2 85.9 %collective-permute-start.4 = (bf16[32,4096]{1,0:T(8,128)(2,1)}, bf16[32,4096]{1,0:T(8,128)(2,1)S(1)}, u32[]{:S(2)}, u32[]{:S(2)}) collective-permute-start(bf16[32,4096]{1,0:T(8,128)(2,1)} %get-tuple-element.1129), channel_id=1, source_target_pairs={{0,32},{32,64},{64,96},{1,33},{33,65},{65,97},{2,34},{34,66},{66,9... | collective-permute-start | bytes 786440 | tf_op jit(solution)/shard_map/ppermute | solution.py:17
  555.2 356.7 %while.120 = (s32[]{:T(128)}, bf16[8,512,4096]{2,1,0:T(8,128)(2,1)}, bf16[8,8,64,2048]{3,2,1,0:T(8,128)(2,1)}, s32[8,8,32]{2,1,0:T(8,128)}, s32[]{:T(128)}) while((s32[]{:T(128)}, bf16[8,512,4096]{2,1,0:T(8,128)(2,1)}, bf16[8,8,64,2048]{3,2,1,0:T(8,128)(2,1)}, s32[8,8,32]{2,1,0:T(8,128)}, s32[]{:T(128)}) %tuple.546), condition=%wide.region_43.45_spmd.clone, body=%wide.region_42.44_spmd.clone.sunk | while | flops 136331264 | bytes 39849540 | solution.py:66
  583.1 12.0 broadcast_in_dim.172
  915.5 83.3 %collective-permute-done.6 = bf16[32,4096]{1,0:T(8,128)(2,1)S(1)} collective-permute-done((bf16[32,4096]{1,0:T(8,128)(2,1)S(1)}, bf16[32,4096]{1,0:T(8,128)(2,1)S(1)}, u32[]{:S(2)}, u32[]{:S(2)}) %collective-permute-start.6) | collective-permute-done | bytes 262176 | tf_op jit(solution)/shard_map/ppermute | solution.py:17
  1009.1 140.8 %collective-permute-done.8 = bf16[32,4096]{1,0:T(8,128)(2,1)S(1)} collective-permute-done((bf16[32,4096]{1,0:T(8,128)(2,1)S(1)}, bf16[32,4096]{1,0:T(8,128)(2,1)S(1)}, u32[]{:S(2)}, u32[]{:S(2)}) %collective-permute-start.8) | collective-permute-done | bytes 262176 | tf_op jit(solution)/shard_map/ppermute | solution.py:17
  1149.9 20.3 %conditional.24 = (bf16[32,4096]{1,0:T(8,128)(2,1)S(1)}, bf16[4,32,4096]{2,1,0:T(8,128)(2,1)}) conditional(s32[]{:T(128)} %convert_element_type.232, bf16[4,32,4096]{2,1,0:T(8,128)(2,1)} %get-tuple-element.1141, (pred[32,4096]{1,0:T(8,128)(4,1)S(1)}, bf16[32,4096]{1,0:T(8,128)(2,1)S(1)}, bf16[32,4096]{1,0:T(8,128)(2,1)S(1)}, s32[]{:T(128)}, ...), branch_computations={%region_59.61_spmd, %region_60.65_spmd} | conditional | flops 1077411840 | bytes 38537416 | solution.py:165
  1155.1 13.9 fusion.45
  1177.3 20.3 %conditional.25 = (bf16[32,4096]{1,0:T(8,128)(2,1)S(1)}, bf16[4,32,4096]{2,1,0:T(8,128)(2,1)}) conditional(s32[]{:T(128)} %convert_element_type.231, bf16[4,32,4096]{2,1,0:T(8,128)(2,1)} %get-tuple-element.1143, (pred[32,4096]{1,0:T(8,128)(4,1)S(1)}, bf16[32,4096]{1,0:T(8,128)(2,1)S(1)}, bf16[32,4096]{1,0:T(8,128)(2,1)S(1)}, s32[]{:T(128)}, ...), branch_computations={%region_64.66_spmd, %region_65.70_spmd} | conditional | flops 1077411840 | bytes 38537416 | solution.py:165
  1182.5 13.9 fusion.59
  1204.7 21.0 %conditional.26 = (bf16[32,4096]{1,0:T(8,128)(2,1)}, bf16[4,32,4096]{2,1,0:T(8,128)(2,1)}) conditional(s32[]{:T(128)} %convert_element_type.230, bf16[4,32,4096]{2,1,0:T(8,128)(2,1)} %get-tuple-element.1145, (pred[32,4096]{1,0:T(8,128)(4,1)S(1)}, bf16[32,4096]{1,0:T(8,128)(2,1)S(1)}, bf16[32,4096]{1,0:T(8,128)(2,1)S(1)}, s32[]{:T(128)}, ...), branch_computations={%region_69.71_spmd, %region_70.75_spmd} | conditional | flops 1077411840 | bytes 38537416 | solution.py:165
  1209.9 13.9 fusion.73
  1243.5 80.6 %while.119 = (s32[]{:T(128)}, bf16[8,8,64,2048]{3,2,1,0:T(8,128)(2,1)}, bf16[8,128,8,64]{1,3,2,0:T(8,128)(2,1)}, s32[8,8,32]{2,1,0:T(8,128)}, bf16[128,64,64]{0,2,1:T(8,128)(2,1)S(1)}, /*index=5*/s32[]{:T(128)}) while((s32[]{:T(128)}, bf16[8,8,64,2048]{3,2,1,0:T(8,128)(2,1)}, bf16[8,128,8,64]{1,3,2,0:T(8,128)(2,1)}, ...), condition=%wide.region_78.80_spmd, body=%wide.region_77.79_spmd.sunk | while | flops 272633088 | bytes 14890569 | solution.py:193
  1324.4 120.4 %reduce-scatter.2.cloned.1.call-done = bf16[2,64,2048]{2,1,0:T(8,128)(2,1)} async-done(((bf16[64,64,2048]{2,1,0:T(8,128)(2,1)}), bf16[2,64,2048]{2,1,0:T(8,128)(2,1)}) %reduce-scatter.2.cloned.1.call-update) | async-done | bytes 524304 | tf_op jit(solution)/shard_map/reduce_scatter | solution.py:192
  1449.1 63.9 %psum.14 = f32[32]{0:T(128)S(1)} all-reduce(f32[32]{0:T(128)S(1)} %select_reduce_fusion.1), channel_id=1, replica_groups=mesh['pipe'=4,'dp'=32] {'dp'}, use_global_device_ids=true, to_apply=%region_85.87 | all-reduce | flops 32 | bytes 256 | tf_op jit(solution)/shard_map/psum | solution.py:218
  1514.2 64.2 %psum.15 = f32[]{:T(128)} all-reduce(f32[]{:T(128)} %multiply_reduce_fusion), channel_id=1, replica_groups=mesh['pipe'=4,'dp'=32] {'dp'}, use_global_device_ids=true, to_apply=%region_88.90 | all-reduce | flops 1 | bytes 8 | tf_op jit(solution)/shard_map/psum | solution.py:221
  (611 shorter events, 885.7 us)
Async XLA Ops:
  7.2 79.4 %all-gather.3.cloned.1.call-start = ((), (), s32[]{:S(2)}) async-start(), calls=%async_computation.2 | async-start | bytes 17301504 | tf_op jit(solution)/shard_map/all_gather | solution.py:110
  7.9 1436.9 %reduce-scatter.2.cloned.1.call-start = ((), (), s32[]{:S(2)}) async-start(), calls=%async_computation.1 | async-start | bytes 17301504 | tf_op jit(solution)/shard_map/reduce_scatter | solution.py:192
  86.6 0.7 copy-start.1
  92.1 3.6 copy-start.5
  168.1 2.8 copy-start
  172.7 7.4 collective-permute-start
  181.9 5.9 copy-start.6
  263.6 9.2 collective-permute-start.1
  274.3 5.9 copy-start.7
  355.9 8.3 collective-permute-start.2
  365.7 6.1 copy-start.8
  447.6 7.6 collective-permute-start.3
  455.2 90.5 %copy-start.4 = (s32[1,64,32]{1,2,0:T(8,128)S(1)}, s32[1,64,32]{1,2,0:T(8,128)}, u32[]{:S(2)}) copy-start(s32[1,64,32]{1,2,0:T(8,128)} %param.113) | copy-start | bytes 24580
  456.2 89.5 %collective-permute-start.4 = (bf16[32,4096]{1,0:T(8,128)(2,1)}, bf16[32,4096]{1,0:T(8,128)(2,1)S(1)}, u32[]{:S(2)}, u32[]{:S(2)}) collective-permute-start(bf16[32,4096]{1,0:T(8,128)(2,1)} %get-tuple-element.1129), channel_id=1, source_target_pairs={{0,32},{32,64},{64,96},{1,33},{33,65},{65,97},{2,34},{34,66},{66,9... | collective-permute-start | bytes 786440 | tf_op jit(solution)/shard_map/ppermute | solution.py:17
  546.9 365.0 %collective-permute-start.5 = (bf16[32,4096]{1,0:T(8,128)(2,1)}, bf16[32,4096]{1,0:T(8,128)(2,1)S(1)}, u32[]{:S(2)}, u32[]{:S(2)}) collective-permute-start(bf16[32,4096]{1,0:T(8,128)(2,1)} %get-tuple-element.1133), channel_id=1, source_target_pairs={{0,32},{32,64},{64,96},{1,33},{33,65},{65,97},{2,34},{34,66},{66,9... | collective-permute-start | bytes 786440 | tf_op jit(solution)/shard_map/ppermute | solution.py:17
  911.9 1.0 copy-start.2
  914.1 84.6 %collective-permute-start.6 = (bf16[32,4096]{1,0:T(8,128)(2,1)S(1)}, bf16[32,4096]{1,0:T(8,128)(2,1)S(1)}, u32[]{:S(2)}, u32[]{:S(2)}) collective-permute-start(bf16[32,4096]{1,0:T(8,128)(2,1)S(1)} %get-tuple-element.1138), channel_id=1, source_target_pairs={{32,0},{64,32},{96,64},{33,1},{65,33},{97,65},{34,2},{66,34},{98,6... | collective-permute-start | bytes 786440 | tf_op jit(solution)/shard_map/ppermute | solution.py:17
  998.8 7.5 collective-permute-start.7
  1006.4 143.5 %collective-permute-start.8 = (bf16[32,4096]{1,0:T(8,128)(2,1)S(1)}, bf16[32,4096]{1,0:T(8,128)(2,1)S(1)}, u32[]{:S(2)}, u32[]{:S(2)}) collective-permute-start(bf16[32,4096]{1,0:T(8,128)(2,1)S(1)} %get-tuple-element.1142), channel_id=1, source_target_pairs={{32,0},{64,32},{96,64},{33,1},{65,33},{97,65},{34,2},{66,34},{98,6... | collective-permute-start | bytes 786440 | tf_op jit(solution)/shard_map/ppermute | solution.py:17
  1170.2 7.1 collective-permute-start.9
  1197.6 7.1 collective-permute-start.10
  1225.7 7.4 collective-permute-start.11
  1324.2 120.6 %copy-start.3 = (bf16[1,2,64,2048]{3,2,1,0:T(8,128)(2,1)S(1)}, bf16[1,2,64,2048]{3,2,1,0:T(8,128)(2,1)}, u32[]{:S(2)}) copy-start(bf16[1,2,64,2048]{3,2,1,0:T(8,128)(2,1)} %param.112) | copy-start | bytes 1572868
  1324.2 120.6 %copy-start.10 = (f32[1,2,64,2048]{3,2,1,0:T(8,128)S(1)}, f32[1,2,64,2048]{3,2,1,0:T(8,128)}, u32[]{:S(2)}) copy-start(f32[1,2,64,2048]{3,2,1,0:T(8,128)} %param.115) | copy-start | bytes 3145732
  (1 other events, 0.7 us)
Sparse Core Ops, SparseCore 0:
  10.3 76.2 all-gather.2
  1324.3 120.4 reduce-scatter.1
where the time goes:
time: 1600 us; the launch traced here: 1590 us
  local copies, waits for them, and re-layouts  494 us (31%)
  waiting for transfers between devices  462 us (29%)
  matrix products  265 us (17%)
  blocking collectives  128 us (8%)
  starting transfers between devices  116 us (7%)
  other arithmetic  103 us (6%)
    ppermute x12, waiting for transfers between devices, shifted(): lax.ppermute(value, axis, [(source, source + steps) for source in range(l...  262 us
    reduce_scatter x1, waiting for transfers between devices, local(): lax.psum_scatter(lax.map(grad_per_group, (index_part, grad_part)).reshape...  120 us
    ppermute x12, starting transfers between devices, shifted(): lax.ppermute(value, axis, [(source, source + steps) for source in range(l...  116 us
    dot_general x32, matrix products, column_per_group(): jnp.einsum('tjk,jbk->tjb', picked, weight_part, preferred_element_type=jn...  110 us
    broadcast_in_dim x8, local copies, waits for them, and re-layouts, dense_transposed(): lax.map(dense_per_group, (section_weights.reshape(group_count, column_gro...  96.3 us
    convert_element_type x8, local copies, waits for them, and re-layouts, dense_per_group(): slab.astype(jnp.bfloat16).reshape(column_group * block_size, features)  95.6 us
    all_gather x1, waiting for transfers between devices, local(): section_weights = lax.all_gather(weights[0], 'dp', axis=0, tiled=True)  78.6 us
    reshape x32, local copies, waits for them, and re-layouts, column_per_group(): jnp.take(normed_blocks, index_part.reshape(-1), axis=1)  78 us
  transfers between devices with their start and end apart: 14, of which 13 were waited for; matrix products, arithmetic and copies ran while one was open for 23% of the time, Pallas kernels for 0%

commit v1 on v0

v1 whole, which is shorter than its diff:
```python
import math

import jax
import jax.numpy as jnp
from jax import lax
from jax.experimental import pallas as pl
from jax.experimental.pallas import tpu as pltpu
from jax.sharding import PartitionSpec as P

HEAD = 128


def shifted(value, axis, steps):
    count = lax.axis_size(axis)
    leading, last = (max(0, -steps), min(count, count - steps))
    return lax.ppermute(value, axis, [(source, source + steps) for source in range(leading, last)])


def shrink(magnitude, threshold):
    return jnp.maximum(magnitude - threshold, 0.0) / jnp.maximum(magnitude, threshold)


def pick_half(tile, index, want_odd):
    rolled = pltpu.roll(tile, 64, 1)
    keep = (index % 2) == want_odd
    return jnp.where(keep, tile, rolled)


def expand_kernel(table_ref, w_ref, o_ref):
    j = pl.program_id(0)
    rows = w_ref.shape[1]
    lane = lax.broadcasted_iota(jnp.int32, (rows, 128), 1)
    pairs = o_ref.shape[2] // 128
    for p in range(pairs):
        k0 = table_ref[j * 2 * pairs + 2 * p]
        k1 = table_ref[j * 2 * pairs + 2 * p + 1]
        s0 = pl.multiple_of((jnp.maximum(k0, 0) // 2) * 128, 128)
        s1 = pl.multiple_of((jnp.maximum(k1, 0) // 2) * 128, 128)
        t0 = w_ref[0, :, pl.ds(s0, 128)].astype(jnp.float32)
        t1 = w_ref[0, :, pl.ds(s1, 128)].astype(jnp.float32)
        low = jnp.where(k0 >= 0, pick_half(t0, k0, 0), 0.0)
        high = jnp.where(k1 >= 0, pick_half(t1, k1, 1), 0.0)
        o_ref[0, :, p * 128:(p + 1) * 128] = jnp.where(lane < 64, low, high).astype(o_ref.dtype)


def pack_kernel(table_ref, g_ref, o_ref):
    j = pl.program_id(0)
    rows = g_ref.shape[1]
    lane = lax.broadcasted_iota(jnp.int32, (rows, 128), 1)
    pairs = o_ref.shape[2] // 128
    for q in range(pairs):
        r0 = table_ref[j * 2 * pairs + 2 * q]
        r1 = table_ref[j * 2 * pairs + 2 * q + 1]
        s0 = pl.multiple_of((r0 // 2) * 128, 128)
        s1 = pl.multiple_of((r1 // 2) * 128, 128)
        t0 = g_ref[0, :, pl.ds(s0, 128)].astype(jnp.float32)
        t1 = g_ref[0, :, pl.ds(s1, 128)].astype(jnp.float32)
        low = pick_half(t0, r0, 0)
        high = pick_half(t1, r1, 1)
        o_ref[0, :, q * 128:(q + 1) * 128] = jnp.where(lane < 64, low, high).astype(o_ref.dtype)


def expand_dense(section_weights, live_index):
    column_count, block_size, wide = section_weights.shape
    live_count = live_index.shape[1]
    features = column_count * block_size
    targets = jnp.arange(column_count, dtype=jnp.int32)
    hit = live_index[:, :, None] == targets[None, None, :]
    k_ids = jnp.arange(live_count, dtype=jnp.int32)[None, :, None]
    inverse = jnp.where(
        jnp.any(hit, axis=1), jnp.sum(jnp.where(hit, k_ids, 0), axis=1), -1
    ).astype(jnp.int32)
    out = pl.pallas_call(
        expand_kernel,
        out_shape=jax.ShapeDtypeStruct((column_count, block_size, features), section_weights.dtype),
        grid_spec=pltpu.PrefetchScalarGridSpec(
            num_scalar_prefetch=1,
            grid=(column_count,),
            in_specs=[pl.BlockSpec((1, block_size, wide), lambda j, tbl: (j, 0, 0))],
            out_specs=pl.BlockSpec((1, block_size, features), lambda j, tbl: (j, 0, 0)),
        ),
        cost_estimate=pl.CostEstimate(
            flops=0, transcendentals=0, bytes_accessed=3 * column_count * block_size * wide * 2
        ),
    )(inverse.reshape(-1), section_weights)
    return out.reshape(features, features)


def pack_dense(dense_grad, live_index):
    column_count, live_count = live_index.shape
    features = dense_grad.shape[0]
    block_size = features // column_count
    wide = live_count * block_size
    return pl.pallas_call(
        pack_kernel,
        out_shape=jax.ShapeDtypeStruct((column_count, block_size, wide), dense_grad.dtype),
        grid_spec=pltpu.PrefetchScalarGridSpec(
            num_scalar_prefetch=1,
            grid=(column_count,),
            in_specs=[pl.BlockSpec((1, block_size, features), lambda j, tbl: (j, 0, 0))],
            out_specs=pl.BlockSpec((1, block_size, wide), lambda j, tbl: (j, 0, 0)),
        ),
        cost_estimate=pl.CostEstimate(
            flops=0, transcendentals=0, bytes_accessed=3 * column_count * block_size * wide * 2
        ),
    )(live_index.reshape(-1).astype(jnp.int32), dense_grad.reshape(column_count, block_size, features))


def layer_forward(entering, dense_t):
    as_float = entering.astype(jnp.float32)
    inverse_rms = lax.rsqrt(jnp.mean(as_float * as_float, axis=-1, keepdims=True) + 1e-05)
    normed = (as_float * inverse_rms).astype(jnp.bfloat16)
    pre_act = lax.dot_general(
        normed, dense_t, (((1,), (1,)), ((), ())), preferred_element_type=jnp.float32
    )
    return ((as_float + jax.nn.silu(pre_act)).astype(jnp.bfloat16), normed, pre_act)


def layer_backward(arriving, entering, pre_act, dense_t):
    as_float = entering.astype(jnp.float32)
    inverse_rms = lax.rsqrt(jnp.mean(as_float * as_float, axis=-1, keepdims=True) + 1e-05)
    sigmoid_z = jax.nn.sigmoid(pre_act)
    grad_pre = (
        arriving.astype(jnp.float32) * (sigmoid_z * (1.0 + pre_act * (1.0 - sigmoid_z)))
    ).astype(jnp.bfloat16)
    grad_normed = jnp.dot(grad_pre, dense_t, preferred_element_type=jnp.float32)
    scaled = as_float * inverse_rms
    leaving = (
        arriving.astype(jnp.float32)
        + inverse_rms
        * (grad_normed - scaled * jnp.mean(grad_normed * scaled, axis=-1, keepdims=True))
    ).astype(jnp.bfloat16)
    return (leaving, grad_pre)


def local(x_in, cotangent, weights, live_rows, moment, second):
    sections = lax.axis_size("pipe")
    section_index = lax.axis_index("pipe")
    micro_count, tokens, features = x_in.shape
    column_count = live_rows.shape[1]
    live_count = live_rows.shape[2]
    own_columns = weights.shape[1]
    block_size = weights.shape[2]
    live_index = live_rows[0]
    section_weights = lax.all_gather(weights[0], "dp", axis=0, tiled=True)
    dense_t = expand_dense(section_weights, live_index)
    tick_count = micro_count + sections - 1

    incoming = jnp.zeros((tokens, features), jnp.bfloat16)
    kept_in, kept_normed, kept_pre = [], [], []
    for tick_index in range(tick_count):
        entering = jnp.where(section_index == 0, x_in[min(tick_index, micro_count - 1)], incoming)
        outgoing, normed, pre_act = layer_forward(entering, dense_t)
        kept_in.append(entering)
        kept_normed.append(normed)
        kept_pre.append(pre_act)
        if tick_index + 1 < tick_count:
            incoming = shifted(outgoing, "pipe", 1)
    saved_in = lax.dynamic_slice_in_dim(jnp.stack(kept_in), section_index, micro_count, 0)
    saved_normed = lax.dynamic_slice_in_dim(jnp.stack(kept_normed), section_index, micro_count, 0)
    saved_pre = lax.dynamic_slice_in_dim(jnp.stack(kept_pre), section_index, micro_count, 0)

    incoming_grad = jnp.zeros((tokens, features), jnp.bfloat16)
    kept_grad = []
    for tick_index in range(tick_count):
        slot_index = jnp.clip(tick_index - (sections - 1 - section_index), 0, micro_count - 1)
        arriving = jnp.where(
            section_index == sections - 1,
            cotangent[min(tick_index, micro_count - 1)],
            incoming_grad,
        )
        leaving, grad_pre = layer_backward(
            arriving, saved_in[slot_index], saved_pre[slot_index], dense_t
        )
        kept_grad.append(grad_pre)
        if tick_index + 1 < tick_count:
            incoming_grad = shifted(leaving, "pipe", -1)
    saved_grad = lax.dynamic_slice_in_dim(
        jnp.stack(kept_grad), sections - 1 - section_index, micro_count, 0
    )

    all_rows = micro_count * tokens
    inverse_tokens = 1.0 / (all_rows * lax.axis_size("dp"))
    dense_grad = (
        lax.dot_general(
            saved_grad.reshape(all_rows, features),
            saved_normed.reshape(all_rows, features),
            (((0,), (0,)), ((), ())),
            preferred_element_type=jnp.float32,
        )
        * inverse_tokens
    ).astype(jnp.bfloat16)
    partial = pack_dense(dense_grad, live_index)
    gradient = lax.psum_scatter(partial, "dp", scatter_dimension=0, tiled=True).astype(jnp.float32)

    rate = 0.1 / math.sqrt(live_count * block_size)
    moment_new = 0.9 * moment[0] + 0.1 * gradient
    second_new = 0.95 * second[0] + 0.05 * gradient * gradient
    stepped = weights[0].astype(jnp.float32) - rate * moment_new / (jnp.sqrt(second_new) + 1e-08)
    own_index = lax.dynamic_slice_in_dim(
        live_index, lax.axis_index("dp") * own_columns, own_columns, 0
    )
    blocked = stepped.reshape(own_columns, block_size, live_count, block_size)
    magnitude = jnp.sqrt(jnp.sum(blocked * blocked, axis=(1, 3)))
    leafed = (
        blocked * shrink(magnitude, 0.15 * math.sqrt(block_size / live_count))[:, None, :, None]
    )
    block_squares = jnp.sum(leafed * leafed, axis=(1, 3))
    head_count = features // HEAD
    head_index = own_index // (HEAD // block_size)
    onehot = (
        head_index[:, :, None] == jnp.arange(head_count, dtype=jnp.int32)[None, None, :]
    ).astype(jnp.float32)
    head_squares = lax.psum(jnp.sum(onehot * block_squares[:, :, None], axis=(0, 1)), "dp")
    head_factor = shrink(jnp.sqrt(head_squares), 0.45 * math.sqrt(HEAD))
    headed = leafed * jnp.sum(onehot * head_factor[None, None, :], axis=2)[:, None, :, None]
    layer_squares = jnp.sum(head_factor * head_factor * head_squares)
    layer_factor = shrink(jnp.sqrt(layer_squares), 0.45 * math.sqrt(features))
    weights_out = (
        (headed * layer_factor)
        .astype(jnp.bfloat16)
        .reshape(own_columns, block_size, live_count * block_size)
    )
    return (weights_out[None], moment_new[None], second_new[None])


def solution(mesh):
    placed = (
        P(None, "dp", None),
        P(None, "dp", None),
        P("pipe", "dp", None, None),
        P("pipe", None, None),
        P("pipe", "dp", None, None),
        P("pipe", "dp", None, None),
    )
    return jax.shard_map(
        local,
        mesh=mesh,
        in_specs=placed,
        out_specs=(
            P("pipe", "dp", None, None),
            P("pipe", "dp", None, None),
            P("pipe", "dp", None, None),
        ),
        check_vma=False,
    )
```

time: 1600 us -> 716 us (0.45)
  local copies, waits for them, and re-layouts: 494 us -> 4.57 us
  waiting for transfers between devices: 462 us -> 250 us
  Pallas kernels: 0 us -> 109 us
  starting transfers between devices: 116 us -> 32.1 us
  other arithmetic: 103 us -> 23.6 us
  blocking collectives: 128 us -> 63.9 us
  matrix products: 265 us -> 207 us
    ppermute x12, waiting for transfers between devices: 262 us -> 51.4 us  [shifted(): lax.ppermute(value, axis, [(source, source + steps) for source in range(l...]
    reshape x89 -> x0, local copies, waits for them, and re-layouts: 130 us -> none  [the longest x32 78 us: column_per_group(): jnp.take(normed_blocks, index_part.reshape(-1), axis=1)]
    pallas_call x0 -> x2, Pallas kernels: none -> 109 us  [the longest x1 59.1 us: expand_dense(): pl.pallas_call(expand_kernel, out_shape=jax.ShapeDtypeStruct((column_coun...]
    broadcast_in_dim x25 -> x0, local copies, waits for them, and re-layouts: 99.6 us -> none  [the longest x8 96.3 us: dense_transposed(): lax.map(dense_per_group, (section_weights.reshape(group_count, column_gro...]
    convert_element_type x8 -> x0, local copies, waits for them, and re-layouts: 95.6 us -> none  [dense_per_group(): slab.astype(jnp.bfloat16).reshape(column_group * block_size, features)]
    ppermute x12, starting transfers between devices: 116 us -> 32.1 us  [shifted(): lax.ppermute(value, axis, [(source, source + steps) for source in range(l...]
    psum x1 -> x0, blocking collectives: 64.2 us -> none  [local(): layer_squares = lax.psum(jnp.sum(headed * headed), 'dp')]
    dot_general x51 -> x14, matrix products: 265 us -> 207 us  [the longest x7 108 us: layer_forward(): lax.dot_general(normed, dense_t, (((1,), (1,)), ((), ())), preferred_elem...]
  transfers between devices with their start and end apart: 14 -> 14, of which waited for: 13 -> 14; matrix products, arithmetic and copies ran while one was open for 23% -> 2% of each run, Pallas kernels for 0% -> 0%
where the time goes in v1:
time: 716 us; the launch traced here: 705 us
  waiting for transfers between devices  250 us (35%)
  matrix products  207 us (29%)
  Pallas kernels  109 us (15%)
  blocking collectives  63.9 us (9%)
  starting transfers between devices  32.1 us (4%)
  other arithmetic  23.6 us (3%)
  between operations  15.5 us (2%)
    reduce_scatter x1, waiting for transfers between devices, local(): lax.psum_scatter(partial, 'dp', scatter_dimension=0, tiled=True)  126 us
    dot_general x7, matrix products, layer_forward(): lax.dot_general(normed, dense_t, (((1,), (1,)), ((), ())), preferred_elem...  108 us
    dot_general x6, matrix products, layer_backward(): grad_normed = jnp.dot(grad_pre, dense_t, preferred_element_type=jnp.float32)  82.3 us
    all_gather x1, waiting for transfers between devices, local(): section_weights = lax.all_gather(weights[0], 'dp', axis=0, tiled=True)  72.6 us
    psum x1, blocking collectives, local(): lax.psum(jnp.sum(onehot * block_squares[:, :, None], axis=(0, 1)), 'dp')  63.9 us
    pallas_call x1, Pallas kernels, expand_dense(): pl.pallas_call(expand_kernel, out_shape=jax.ShapeDtypeStruct((column_coun...  59.1 us
    ppermute x12, waiting for transfers between devices, shifted(): lax.ppermute(value, axis, [(source, source + steps) for source in range(l...  51.4 us
    pallas_call x1, Pallas kernels, pack_dense(): pl.pallas_call(pack_kernel, out_shape=jax.ShapeDtypeStruct((column_count,...  49.6 us
  transfers between devices with their start and end apart: 14, of which 14 were waited for; matrix products, arithmetic and copies ran while one was open for 2% of the time, Pallas kernels for 0%

profile of v1, /device:TPU:1, one launch (start us, length us, event | category | flops | bytes accessed | tf_op | source)
XLA Modules:
  0.0 705.3 jit_solution(7863599112746749895)
XLA Ops:
  13.9 72.6 %all-gather.3.cloned.1.call-done = bf16[1,64,64,2048]{3,2,0,1:T(8,128)(2,1)} async-done(((bf16[1,2,64,2048]{3,2,0,1:T(8,128)(2,1)}), bf16[1,64,64,2048]{3,2,0,1:T(8,128)(2,1)}) %all-gather.3.cloned.1.call-update) | async-done | bytes 16777232 | tf_op jit(solution)/shard_map/all_gather | solution.py:145
  86.5 59.1 %shard_map.85 = bf16[64,64,4096]{2,1,0:T(8,128)(2,1)} custom-call(s32[4096]{0:T(1024)} %select_n.126.table_ref, bf16[64,64,2048]{2,1,0:T(8,128)(2,1)} %bitcast.343), custom_call_target="tpu_custom_call" | custom-call | bytes 50331648 | tf_op jit(solution)/shard_map/pallas_call | solution.py:73
  145.6 15.4 %fusion.45 = (bf16[32,4096]{1,0:T(8,128)(2,1)S(1)}, f32[32,4096]{1,0:T(8,128)S(1)}) fusion(bf16[4,32,4096]{2,1,0:T(8,128)(2,1)S(1)} %copy-done.1, pred[]{:T(512)S(6)} %eq.19, bf16[4096,4096]{1,0:T(8,128)(2,1)} %bitcast.329, f32[32]{0:T(128)S(1)} %add_rsqrt_fusion.12), kind=kOutput, calls=%fused_computation.98 | convolution fusion | flops 1075314688 | bytes 34866688 | tf_op jit(solution)/shard_map/dot_general | solution.py:113
  164.3 5.4 collective-permute-done
  169.9 15.4 %fusion.67 = (bf16[32,4096]{1,0:T(8,128)(2,1)S(1)}, f32[32,4096]{1,0:T(8,128)S(1)}) fusion(bf16[32,4096]{1,0:T(8,128)(2,1)S(1)} %get-tuple-element.34, bf16[4096,4096]{1,0:T(8,128)(2,1)} %bitcast.330, f32[32]{0:T(128)S(1)} %add_rsqrt_fusion.11), kind=kOutput, calls=%fused_computation.120 | convolution fusion | flops 1075052544 | bytes 34603136 | tf_op jit(solution)/shard_map/dot_general | solution.py:113
  194.2 15.4 %fusion.70 = (bf16[32,4096]{1,0:T(8,128)(2,1)S(1)}, f32[32,4096]{1,0:T(8,128)S(1)}) fusion(bf16[32,4096]{1,0:T(8,128)(2,1)S(1)} %get-tuple-element.32, bf16[4096,4096]{1,0:T(8,128)(2,1)} %bitcast.331, f32[32]{0:T(128)S(1)} %add_rsqrt_fusion.10), kind=kOutput, calls=%fused_computation.123 | convolution fusion | flops 1075052544 | bytes 34603136 | tf_op jit(solution)/shard_map/dot_general | solution.py:113
  217.7 15.5 %fusion.73 = (bf16[32,4096]{1,0:T(8,128)(2,1)S(1)}, f32[32,4096]{1,0:T(8,128)S(1)}) fusion(bf16[32,4096]{1,0:T(8,128)(2,1)S(1)} %get-tuple-element.30, bf16[4096,4096]{1,0:T(8,128)(2,1)} %bitcast.332, f32[32]{0:T(128)S(1)} %add_rsqrt_fusion.9), kind=kOutput, calls=%fused_computation.126 | convolution fusion | flops 1075052544 | bytes 34603136 | tf_op jit(solution)/shard_map/dot_general | solution.py:113
  240.8 15.5 %fusion.76 = (bf16[32,4096]{1,0:T(8,128)(2,1)S(1)}, f32[32,4096]{1,0:T(8,128)S(1)}) fusion(bf16[32,4096]{1,0:T(8,128)(2,1)S(1)} %get-tuple-element.28, bf16[4096,4096]{1,0:T(8,128)(2,1)} %bitcast.333, f32[32]{0:T(128)S(1)} %add_rsqrt_fusion.8), kind=kOutput, calls=%fused_computation.129 | convolution fusion | flops 1075052544 | bytes 34603136 | tf_op jit(solution)/shard_map/dot_general | solution.py:113
  263.6 15.4 %fusion.79 = (bf16[32,4096]{1,0:T(8,128)(2,1)S(1)}, f32[32,4096]{1,0:T(8,128)S(1)}) fusion(bf16[32,4096]{1,0:T(8,128)(2,1)S(1)} %get-tuple-element.26, bf16[4096,4096]{1,0:T(8,128)(2,1)} %bitcast.334, f32[32]{0:T(128)S(1)} %add_rsqrt_fusion.7), kind=kOutput, calls=%fused_computation.132 | convolution fusion | flops 1075052544 | bytes 34603136 | tf_op jit(solution)/shard_map/dot_general | solution.py:113
  287.3 15.6 %fusion.1 = f32[7,32,4096]{2,1,0:T(8,128)S(1)} fusion(f32[7,32,4096]{2,1,0:T(8,128)S(1)} %bitcast_dynamic-update-slice_fusion, bf16[4096,4096]{1,0:T(8,128)(2,1)} %bitcast.335, bf16[32,4096]{1,0:T(8,128)(2,1)S(1)} %get-tuple-element.24, f32[32]{0:T(128)S(1)} %add_rsqrt_fusion.6), kind=kOutput, calls=%fused_computation.3 | convolution fusion | flops 1074135040 | bytes 34341376 | tf_op jit(solution)/shard_map/dot_general | solution.py:113
  302.9 13.9 %fusion.64 = (f32[32]{0:T(128)S(1)}, f32[32]{0:T(128)S(1)}, f32[32]{0:T(128)S(1)}, f32[32]{0:T(128)S(1)}, f32[32]{0:T(128)S(1)}, /*index=5*/f32[32]{0:T(128)S(1)}, f32[32,4096]{1,0:T(8,128)S(1)}) fusion(bf16[7,32,4096]{2,1,0:T(8,128)(2,1)S(1)} %get-tuple-element.23, s32[]{:T(128)S(6)} %dynamic_slice.94, f32[32]{0:T(128)S(1)} %add_rsqrt_fusion.5, ...), kind=kOutput, calls=%fused_computation.117 | convolution fusion | flops 1077673984 | bytes 36443392 | tf_op jit(solution)/shard_map/dot_general | solution.py:126
  325.5 13.7 %fusion.35 = (f32[32]{0:T(128)S(1)}, f32[32,4096]{1,0:T(8,128)S(1)}) fusion(f32[32]{0:T(128)S(1)} %add_rsqrt_fusion.4, bf16[7,32,4096]{2,1,0:T(8,128)(2,1)S(1)} %get-tuple-element.23, s32[]{:T(128)S(6)} %dynamic_slice.82, bf16[32,4096]{1,0:T(8,128)(2,1)S(1)} %get-tuple-element.22, bf16[4096,4096]{1,0:T(8,128)(2,1)} %bitcast.337), kind=kOutput, calls=%fused_computation.88 | convolution fusion | flops 1074266112 | bytes 34603268 | tf_op jit(solution)/shard_map/dot_general | solution.py:126
  341.6 5.0 collective-permute-done.7
  347.5 13.7 %fusion.32 = (f32[32]{0:T(128)S(1)}, f32[32,4096]{1,0:T(8,128)S(1)}) fusion(f32[32]{0:T(128)S(1)} %add_rsqrt_fusion.3, bf16[7,32,4096]{2,1,0:T(8,128)(2,1)S(1)} %get-tuple-element.23, s32[]{:T(128)S(6)} %dynamic_slice.85, bf16[32,4096]{1,0:T(8,128)(2,1)S(1)} %get-tuple-element.20, bf16[4096,4096]{1,0:T(8,128)(2,1)} %bitcast.338), kind=kOutput, calls=%fused_computation.85 | convolution fusion | flops 1074266112 | bytes 34603268 | tf_op jit(solution)/shard_map/dot_general | solution.py:126
  363.8 4.8 collective-permute-done.8
  369.5 13.7 %fusion.29 = (f32[32]{0:T(128)S(1)}, f32[32,4096]{1,0:T(8,128)S(1)}) fusion(f32[32]{0:T(128)S(1)} %add_rsqrt_fusion.2, bf16[7,32,4096]{2,1,0:T(8,128)(2,1)S(1)} %get-tuple-element.23, s32[]{:T(128)S(6)} %dynamic_slice.88, bf16[32,4096]{1,0:T(8,128)(2,1)S(1)} %get-tuple-element.18, bf16[4096,4096]{1,0:T(8,128)(2,1)} %bitcast.339), kind=kOutput, calls=%fused_computation.82 | convolution fusion | flops 1074266112 | bytes 34603268 | tf_op jit(solution)/shard_map/dot_general | solution.py:126
  385.5 5.0 collective-permute-done.9
  391.4 13.7 %fusion.26 = (f32[32]{0:T(128)S(1)}, f32[32,4096]{1,0:T(8,128)S(1)}) fusion(f32[32]{0:T(128)S(1)} %add_rsqrt_fusion.1, bf16[7,32,4096]{2,1,0:T(8,128)(2,1)S(1)} %get-tuple-element.23, s32[]{:T(128)S(6)} %dynamic_slice.91, bf16[32,4096]{1,0:T(8,128)(2,1)S(1)} %get-tuple-element.16, bf16[4096,4096]{1,0:T(8,128)(2,1)} %bitcast.340), kind=kOutput, calls=%fused_computation.79 | convolution fusion | flops 1074266112 | bytes 34603268 | tf_op jit(solution)/shard_map/dot_general | solution.py:126
  407.5 5.0 collective-permute-done.10
  413.4 13.7 %fusion.23 = (f32[32]{0:T(128)S(1)}, f32[32,4096]{1,0:T(8,128)S(1)}) fusion(f32[32]{0:T(128)S(1)} %add_rsqrt_fusion, bf16[7,32,4096]{2,1,0:T(8,128)(2,1)S(1)} %get-tuple-element.23, s32[]{:T(128)S(6)} %dynamic_slice.94, bf16[32,4096]{1,0:T(8,128)(2,1)S(1)} %get-tuple-element.14, bf16[4096,4096]{1,0:T(8,128)(2,1)} %bitcast.341), kind=kOutput, calls=%fused_computation.76 | convolution fusion | flops 1074266112 | bytes 34603268 | tf_op jit(solution)/shard_map/dot_general | solution.py:126
  435.3 15.9 %fusion = bf16[4096,4096]{1,0:T(8,128)(2,1)} fusion(bf16[7,32,4096]{2,1,0:T(8,128)(2,1)} %bitcast_dynamic-update-slice_fusion.6, s32[]{:T(128)S(6)} %select_n.134, bf16[7,32,4096]{2,1,0:T(8,128)(2,1)} %bitcast_dynamic-update-slice_fusion.12, s32[]{:T(128)S(6)} %select_n.143), kind=kOutput, calls=%fused_computation.1 | convolution fusion | flops 4328521728 | bytes 35651592 | tf_op jit(solution)/shard_map/dot_general | solution.py:185
  451.2 49.6 %shard_map.86 = bf16[64,64,2048]{2,1,0:T(8,128)(2,1)} custom-call(s32[2048]{0:T(1024)} %reshape_squeeze.3.table_ref, bf16[64,64,4096]{2,1,0:T(8,128)(2,1)} %bitcast.342), custom_call_target="tpu_custom_call" | custom-call | bytes 50331648 | tf_op jit(solution)/shard_map/pallas_call | solution.py:94
  501.7 125.6 %reduce-scatter.2.cloned.1.call-done = bf16[2,64,2048]{2,1,0:T(8,128)(2,1)} async-done(((bf16[64,64,2048]{2,1,0:T(8,128)(2,1)}), bf16[2,64,2048]{2,1,0:T(8,128)(2,1)}) %reduce-scatter.2.cloned.1.call-update) | async-done | bytes 524304 | tf_op jit(solution)/shard_map/reduce_scatter | solution.py:194
  631.7 63.9 %psum.7 = f32[32]{0:T(128)S(1)} all-reduce(f32[32]{0:T(128)S(1)} %select_reduce_fusion.2), channel_id=1, replica_groups=mesh['pipe'=4,'dp'=32] {'dp'}, use_global_device_ids=true, to_apply=%region_27.28 | all-reduce | flops 32 | bytes 256 | tf_op jit(solution)/shard_map/psum | solution.py:214
  (132 shorter events, 87.3 us)
Async XLA Ops:
  7.2 79.4 %all-gather.3.cloned.1.call-start = ((), (), s32[]{:S(2)}) async-start(), calls=%async_computation.2 | async-start | bytes 17301504 | tf_op jit(solution)/shard_map/all_gather | solution.py:145
  7.9 619.4 %reduce-scatter.2.cloned.1.call-start = ((), (), s32[]{:S(2)}) async-start(), calls=%async_computation.1 | async-start | bytes 17301504 | tf_op jit(solution)/shard_map/reduce_scatter | solution.py:194
  86.5 59.1 %copy-start.1 = (bf16[4,32,4096]{2,1,0:T(8,128)(2,1)S(1)}, bf16[4,32,4096]{2,1,0:T(8,128)(2,1)}, u32[]{:S(2)}) copy-start(bf16[4,32,4096]{2,1,0:T(8,128)(2,1)} %param.6) | copy-start | bytes 3145732
  161.1 8.6 %collective-permute-start = (bf16[32,4096]{1,0:T(8,128)(2,1)S(1)}, bf16[32,4096]{1,0:T(8,128)(2,1)S(1)}, u32[]{:S(2)}, u32[]{:S(2)}) collective-permute-start(bf16[32,4096]{1,0:T(8,128)(2,1)S(1)} %get-tuple-element.38), channel_id=1, source_target_pairs={{0,32},{32,64},{64,96},{1,33},{33,65},{65,97},{2,34},{34,66},{66,9... | collective-permute-start | bytes 786440 | tf_op jit(solution)/shard_map/ppermute | solution.py:16
  169.7 15.7 %copy-start.8 = (bf16[32,4096]{1,0:T(8,128)(2,1)}, bf16[32,4096]{1,0:T(8,128)(2,1)S(1)}, u32[]{:S(2)}) copy-start(bf16[32,4096]{1,0:T(8,128)(2,1)S(1)} %get-tuple-element.34) | copy-start | bytes 786436
  185.4 8.6 %collective-permute-start.1 = (bf16[32,4096]{1,0:T(8,128)(2,1)S(1)}, bf16[32,4096]{1,0:T(8,128)(2,1)S(1)}, u32[]{:S(2)}, u32[]{:S(2)}) collective-permute-start(bf16[32,4096]{1,0:T(8,128)(2,1)S(1)} %get-tuple-element.40), channel_id=1, source_target_pairs={{0,32},{32,64},{64,96},{1,33},{33,65},{65,97},{2,34},{34,66},{66,9... | collective-permute-start | bytes 786440 | tf_op jit(solution)/shard_map/ppermute | solution.py:16
  194.1 15.6 %copy-start.6 = (bf16[32,4096]{1,0:T(8,128)(2,1)}, bf16[32,4096]{1,0:T(8,128)(2,1)S(1)}, u32[]{:S(2)}) copy-start(bf16[32,4096]{1,0:T(8,128)(2,1)S(1)} %get-tuple-element.32) | copy-start | bytes 786436
  209.7 7.7 %collective-permute-start.2 = (bf16[32,4096]{1,0:T(8,128)(2,1)S(1)}, bf16[32,4096]{1,0:T(8,128)(2,1)S(1)}, u32[]{:S(2)}, u32[]{:S(2)}) collective-permute-start(bf16[32,4096]{1,0:T(8,128)(2,1)S(1)} %get-tuple-element.42), channel_id=1, source_target_pairs={{0,32},{32,64},{64,96},{1,33},{33,65},{65,97},{2,34},{34,66},{66,9... | collective-permute-start | bytes 786440 | tf_op jit(solution)/shard_map/ppermute | solution.py:16
  217.5 15.7 %copy-start.4 = (bf16[32,4096]{1,0:T(8,128)(2,1)}, bf16[32,4096]{1,0:T(8,128)(2,1)S(1)}, u32[]{:S(2)}) copy-start(bf16[32,4096]{1,0:T(8,128)(2,1)S(1)} %get-tuple-element.30) | copy-start | bytes 786436
  233.1 7.4 %collective-permute-start.3 = (bf16[32,4096]{1,0:T(8,128)(2,1)S(1)}, bf16[32,4096]{1,0:T(8,128)(2,1)S(1)}, u32[]{:S(2)}, u32[]{:S(2)}) collective-permute-start(bf16[32,4096]{1,0:T(8,128)(2,1)S(1)} %get-tuple-element.44), channel_id=1, source_target_pairs={{0,32},{32,64},{64,96},{1,33},{33,65},{65,97},{2,34},{34,66},{66,9... | collective-permute-start | bytes 786440 | tf_op jit(solution)/shard_map/ppermute | solution.py:16
  240.6 15.7 %copy-start.2 = (bf16[32,4096]{1,0:T(8,128)(2,1)}, bf16[32,4096]{1,0:T(8,128)(2,1)S(1)}, u32[]{:S(2)}) copy-start(bf16[32,4096]{1,0:T(8,128)(2,1)S(1)} %get-tuple-element.28) | copy-start | bytes 786436
  256.3 7.1 %collective-permute-start.4 = (bf16[32,4096]{1,0:T(8,128)(2,1)S(1)}, bf16[32,4096]{1,0:T(8,128)(2,1)S(1)}, u32[]{:S(2)}, u32[]{:S(2)}) collective-permute-start(bf16[32,4096]{1,0:T(8,128)(2,1)S(1)} %get-tuple-element.46), channel_id=1, source_target_pairs={{0,32},{32,64},{64,96},{1,33},{33,65},{65,97},{2,34},{34,66},{66,9... | collective-permute-start | bytes 786440 | tf_op jit(solution)/shard_map/ppermute | solution.py:16
  279.1 7.1 %collective-permute-start.5 = (bf16[32,4096]{1,0:T(8,128)(2,1)S(1)}, bf16[32,4096]{1,0:T(8,128)(2,1)S(1)}, u32[]{:S(2)}, u32[]{:S(2)}) collective-permute-start(bf16[32,4096]{1,0:T(8,128)(2,1)S(1)} %get-tuple-element.48), channel_id=1, source_target_pairs={{0,32},{32,64},{64,96},{1,33},{33,65},{65,97},{2,34},{34,66},{66,9... | collective-permute-start | bytes 786440 | tf_op jit(solution)/shard_map/ppermute | solution.py:16
  287.3 15.6 %copy-start = (bf16[4,32,4096]{2,1,0:T(8,128)(2,1)S(1)}, bf16[4,32,4096]{2,1,0:T(8,128)(2,1)}, u32[]{:S(2)}) copy-start(bf16[4,32,4096]{2,1,0:T(8,128)(2,1)} %param.7) | copy-start | bytes 3145732
  302.9 15.5 %copy-start.9 = (bf16[32,4096]{1,0:T(8,128)(2,1)S(1)}, bf16[32,4096]{1,0:T(8,128)(2,1)}, u32[]{:S(2)}) copy-start(bf16[32,4096]{1,0:T(8,128)(2,1)} %copy-done.8) | copy-start | bytes 786436
  317.0 7.6 %collective-permute-start.6 = (bf16[32,4096]{1,0:T(8,128)(2,1)S(1)}, bf16[32,4096]{1,0:T(8,128)(2,1)S(1)}, u32[]{:S(2)}, u32[]{:S(2)}) collective-permute-start(bf16[32,4096]{1,0:T(8,128)(2,1)S(1)} %fusion.42), channel_id=1, source_target_pairs={{32,0},{64,32},{96,64},{33,1},{65,33},{97,65},{34,2},{66,34},{98,6... | collective-permute-start | bytes 786440 | tf_op jit(solution)/shard_map/ppermute | solution.py:16
  339.4 7.1 %collective-permute-start.7 = (bf16[32,4096]{1,0:T(8,128)(2,1)S(1)}, bf16[32,4096]{1,0:T(8,128)(2,1)S(1)}, u32[]{:S(2)}, u32[]{:S(2)}) collective-permute-start(bf16[32,4096]{1,0:T(8,128)(2,1)S(1)} %fusion.50), channel_id=1, source_target_pairs={{32,0},{64,32},{96,64},{33,1},{65,33},{97,65},{34,2},{66,34},{98,6... | collective-permute-start | bytes 786440 | tf_op jit(solution)/shard_map/ppermute | solution.py:16
  347.5 15.4 %copy-start.5 = (bf16[32,4096]{1,0:T(8,128)(2,1)S(1)}, bf16[32,4096]{1,0:T(8,128)(2,1)}, u32[]{:S(2)}) copy-start(bf16[32,4096]{1,0:T(8,128)(2,1)} %copy-done.4) | copy-start | bytes 786436
  361.4 7.1 %collective-permute-start.8 = (bf16[32,4096]{1,0:T(8,128)(2,1)S(1)}, bf16[32,4096]{1,0:T(8,128)(2,1)S(1)}, u32[]{:S(2)}, u32[]{:S(2)}) collective-permute-start(bf16[32,4096]{1,0:T(8,128)(2,1)S(1)} %fusion.52), channel_id=1, source_target_pairs={{32,0},{64,32},{96,64},{33,1},{65,33},{97,65},{34,2},{66,34},{98,6... | collective-permute-start | bytes 786440 | tf_op jit(solution)/shard_map/ppermute | solution.py:16
  383.4 7.1 %collective-permute-start.9 = (bf16[32,4096]{1,0:T(8,128)(2,1)S(1)}, bf16[32,4096]{1,0:T(8,128)(2,1)S(1)}, u32[]{:S(2)}, u32[]{:S(2)}) collective-permute-start(bf16[32,4096]{1,0:T(8,128)(2,1)S(1)} %fusion.54), channel_id=1, source_target_pairs={{32,0},{64,32},{96,64},{33,1},{65,33},{97,65},{34,2},{66,34},{98,6... | collective-permute-start | bytes 786440 | tf_op jit(solution)/shard_map/ppermute | solution.py:16
  405.3 7.1 %collective-permute-start.10 = (bf16[32,4096]{1,0:T(8,128)(2,1)S(1)}, bf16[32,4096]{1,0:T(8,128)(2,1)S(1)}, u32[]{:S(2)}, u32[]{:S(2)}) collective-permute-start(bf16[32,4096]{1,0:T(8,128)(2,1)S(1)} %fusion.56), channel_id=1, source_target_pairs={{32,0},{64,32},{96,64},{33,1},{65,33},{97,65},{34,2},{66,34},{98,6... | collective-permute-start | bytes 786440 | tf_op jit(solution)/shard_map/ppermute | solution.py:16
  427.2 7.1 %collective-permute-start.11 = (bf16[32,4096]{1,0:T(8,128)(2,1)S(1)}, bf16[32,4096]{1,0:T(8,128)(2,1)S(1)}, u32[]{:S(2)}, u32[]{:S(2)}) collective-permute-start(bf16[32,4096]{1,0:T(8,128)(2,1)S(1)} %fusion.58), channel_id=1, source_target_pairs={{32,0},{64,32},{96,64},{33,1},{65,33},{97,65},{34,2},{66,34},{98,6... | collective-permute-start | bytes 786440 | tf_op jit(solution)/shard_map/ppermute | solution.py:16
  500.8 126.5 %copy-start.10 = (bf16[1,2,64,2048]{3,2,1,0:T(8,128)(2,1)S(1)}, bf16[1,2,64,2048]{3,2,1,0:T(8,128)(2,1)}, u32[]{:S(2)}) copy-start(bf16[1,2,64,2048]{3,2,1,0:T(8,128)(2,1)} %param.8) | copy-start | bytes 1572868
  500.8 126.5 %copy-start.11 = (f32[1,2,64,2048]{3,2,1,0:T(8,128)S(1)}, f32[1,2,64,2048]{3,2,1,0:T(8,128)}, u32[]{:S(2)}) copy-start(f32[1,2,64,2048]{3,2,1,0:T(8,128)} %param.11) | copy-start | bytes 3145732
  (3 other events, 31.2 us)
Sparse Core Ops, SparseCore 0:
  10.3 76.2 all-gather.2
  501.0 126.3 reduce-scatter.1

commit v2 on v1

--- a/solution.py
+++ b/solution.py
@@ -36,11 +36,12 @@
         k1 = table_ref[j * 2 * pairs + 2 * p + 1]
         s0 = pl.multiple_of((jnp.maximum(k0, 0) // 2) * 128, 128)
         s1 = pl.multiple_of((jnp.maximum(k1, 0) // 2) * 128, 128)
-        t0 = w_ref[0, :, pl.ds(s0, 128)].astype(jnp.float32)
-        t1 = w_ref[0, :, pl.ds(s1, 128)].astype(jnp.float32)
-        low = jnp.where(k0 >= 0, pick_half(t0, k0, 0), 0.0)
-        high = jnp.where(k1 >= 0, pick_half(t1, k1, 1), 0.0)
-        o_ref[0, :, p * 128:(p + 1) * 128] = jnp.where(lane < 64, low, high).astype(o_ref.dtype)
+        t0 = w_ref[0, :, pl.ds(s0, 128)]
+        t1 = w_ref[0, :, pl.ds(s1, 128)]
+        zero = jnp.zeros_like(t0)
+        low = jnp.where(k0 >= 0, pick_half(t0, k0, 0), zero)
+        high = jnp.where(k1 >= 0, pick_half(t1, k1, 1), zero)
+        o_ref[0, :, p * 128:(p + 1) * 128] = jnp.where(lane < 64, low, high)
 
 
 def pack_kernel(table_ref, g_ref, o_ref):
@@ -53,11 +54,11 @@
         r1 = table_ref[j * 2 * pairs + 2 * q + 1]
         s0 = pl.multiple_of((r0 // 2) * 128, 128)
         s1 = pl.multiple_of((r1 // 2) * 128, 128)
-        t0 = g_ref[0, :, pl.ds(s0, 128)].astype(jnp.float32)
-        t1 = g_ref[0, :, pl.ds(s1, 128)].astype(jnp.float32)
+        t0 = g_ref[0, :, pl.ds(s0, 128)]
+        t1 = g_ref[0, :, pl.ds(s1, 128)]
         low = pick_half(t0, r0, 0)
         high = pick_half(t1, r1, 1)
-        o_ref[0, :, q * 128:(q + 1) * 128] = jnp.where(lane < 64, low, high).astype(o_ref.dtype)
+        o_ref[0, :, q * 128:(q + 1) * 128] = jnp.where(lane < 64, low, high)
 
 
 def expand_dense(section_weights, live_index):
@@ -106,6 +107,64 @@
     )(live_index.reshape(-1).astype(jnp.int32), dense_grad.reshape(column_count, block_size, features))
 
 
+def spread_kernel(x_ref, o_ref, recv_ref, send_sem, recv_sem):
+    count = recv_ref.shape[0]
+    me = lax.axis_index("dp")
+    pipe = lax.axis_index("pipe")
+    barrier = pltpu.get_barrier_semaphore()
+    for step in range(1, count):
+        peer = lax.rem(me + step, count)
+        pl.semaphore_signal(barrier, inc=1, device_id=(pipe, peer), device_id_type=pl.DeviceIdType.MESH)
+    pl.semaphore_wait(barrier, count - 1)
+    copies = []
+    for step in range(1, count):
+        peer = lax.rem(me + step, count)
+        copy = pltpu.make_async_remote_copy(
+            src_ref=x_ref,
+            dst_ref=recv_ref.at[me],
+            send_sem=send_sem.at[step],
+            recv_sem=recv_sem.at[me],
+            device_id=(pipe, peer),
+            device_id_type=pl.DeviceIdType.MESH,
+        )
+        copy.start()
+        copies.append(copy)
+    total = x_ref[...]
+    for step in range(1, count):
+        source = lax.rem(me + count - step, count)
+        arrival = pltpu.make_async_remote_copy(
+            src_ref=x_ref,
+            dst_ref=recv_ref.at[source],
+            send_sem=send_sem.at[step],
+            recv_sem=recv_sem.at[source],
+            device_id=(pipe, source),
+            device_id_type=pl.DeviceIdType.MESH,
+        )
+        arrival.wait_recv()
+        total = total + recv_ref[source]
+    for copy in copies:
+        copy.wait_send()
+    o_ref[...] = total
+
+
+def spread_sum(values):
+    count = lax.axis_size("dp")
+    padded = jnp.zeros((8, 128), jnp.float32).at[0, : values.shape[0]].set(values)
+    out = pl.pallas_call(
+        spread_kernel,
+        out_shape=jax.ShapeDtypeStruct((8, 128), jnp.float32),
+        in_specs=[pl.BlockSpec(memory_space=pltpu.VMEM)],
+        out_specs=pl.BlockSpec(memory_space=pltpu.VMEM),
+        scratch_shapes=[
+            pltpu.VMEM((count, 8, 128), jnp.float32),
+            pltpu.SemaphoreType.DMA((count,)),
+            pltpu.SemaphoreType.DMA((count,)),
+        ],
+        compiler_params=pltpu.CompilerParams(collective_id=0, has_side_effects=True),
+    )(padded)
+    return out[0, : values.shape[0]]
+
+
 def layer_forward(entering, dense_t):
     as_float = entering.astype(jnp.float32)
     inverse_rms = lax.rsqrt(jnp.mean(as_float * as_float, axis=-1, keepdims=True) + 1e-05)
@@ -211,7 +270,8 @@
     onehot = (
         head_index[:, :, None] == jnp.arange(head_count, dtype=jnp.int32)[None, None, :]
     ).astype(jnp.float32)
-    head_squares = lax.psum(jnp.sum(onehot * block_squares[:, :, None], axis=(0, 1)), "dp")
+    head_partial = jnp.sum(onehot * block_squares[:, :, None], axis=(0, 1))
+    head_squares = spread_sum(head_partial)
     head_factor = shrink(jnp.sqrt(head_squares), 0.45 * math.sqrt(HEAD))
     headed = leafed * jnp.sum(onehot * head_factor[None, None, :], axis=2)[:, None, :, None]
     layer_squares = jnp.sum(head_factor * head_factor * head_squares)

time: 716 us -> 666 us (0.930)
  blocking collectives: 63.9 us -> 0 us
  Pallas kernels: 109 us -> 122 us
    psum x1 -> x0, blocking collectives: 63.9 us -> none  [local(): lax.psum(jnp.sum(onehot * block_squares[:, :, None], axis=(0, 1)), 'dp')]
    pallas_call x0 -> x1, Pallas kernels: none -> 12.1 us  [spread_sum(): pl.pallas_call(spread_kernel, out_shape=jax.ShapeDtypeStruct((8, 128), jn...]
where the time goes in v2:
time: 666 us; the launch traced here: 656 us
  waiting for transfers between devices  250 us (38%)
  matrix products  207 us (31%)
  Pallas kernels  122 us (18%)
  starting transfers between devices  32.1 us (5%)
  other arithmetic  24.3 us (4%)
  between operations  15.7 us (2%)
    reduce_scatter x1, waiting for transfers between devices, local(): lax.psum_scatter(partial, 'dp', scatter_dimension=0, tiled=True)  126 us
    dot_general x7, matrix products, layer_forward(): lax.dot_general(normed, dense_t, (((1,), (1,)), ((), ())), preferred_elem...  108 us
    dot_general x6, matrix products, layer_backward(): grad_normed = jnp.dot(grad_pre, dense_t, preferred_element_type=jnp.float32)  82.3 us
    all_gather x1, waiting for transfers between devices, local(): section_weights = lax.all_gather(weights[0], 'dp', axis=0, tiled=True)  72.6 us
    pallas_call x1, Pallas kernels, expand_dense(): pl.pallas_call(expand_kernel, out_shape=jax.ShapeDtypeStruct((column_coun...  59.5 us
    ppermute x12, waiting for transfers between devices, shifted(): lax.ppermute(value, axis, [(source, source + steps) for source in range(l...  51.4 us
    pallas_call x1, Pallas kernels, pack_dense(): pl.pallas_call(pack_kernel, out_shape=jax.ShapeDtypeStruct((column_count,...  50 us
    ppermute x12, starting transfers between devices, shifted(): lax.ppermute(value, axis, [(source, source + steps) for source in range(l...  32.1 us
  transfers between devices with their start and end apart: 14, of which 14 were waited for; matrix products, arithmetic and copies ran while one was open for 2% of the time, Pallas kernels for 0%

profile of v2, /device:TPU:1, one launch (start us, length us, event | category | flops | bytes accessed | tf_op | source)
XLA Modules:
  0.0 655.7 jit_solution(8748681171482458947)
XLA Ops:
  13.9 72.6 %all-gather.3.cloned.1.call-done = bf16[1,64,64,2048]{3,2,0,1:T(8,128)(2,1)} async-done(((bf16[1,2,64,2048]{3,2,0,1:T(8,128)(2,1)}), bf16[1,64,64,2048]{3,2,0,1:T(8,128)(2,1)}) %all-gather.3.cloned.1.call-update) | async-done | bytes 16777232 | tf_op jit(solution)/shard_map/all_gather | solution.py:204
  86.5 59.5 %shard_map.85 = bf16[64,64,4096]{2,1,0:T(8,128)(2,1)} custom-call(s32[4096]{0:T(1024)} %select_n.126.table_ref, bf16[64,64,2048]{2,1,0:T(8,128)(2,1)} %bitcast.352), custom_call_target="tpu_custom_call" | custom-call | bytes 50331648 | tf_op jit(solution)/shard_map/pallas_call | solution.py:74
  146.0 15.4 %fusion.45 = (bf16[32,4096]{1,0:T(8,128)(2,1)S(1)}, f32[32,4096]{1,0:T(8,128)S(1)}) fusion(bf16[4,32,4096]{2,1,0:T(8,128)(2,1)S(1)} %copy-done.1, pred[]{:T(512)S(6)} %eq.19, bf16[4096,4096]{1,0:T(8,128)(2,1)} %bitcast.338, f32[32]{0:T(128)S(1)} %add_rsqrt_fusion.12), kind=kOutput, calls=%fused_computation.98 | convolution fusion | flops 1075314688 | bytes 34866688 | tf_op jit(solution)/shard_map/dot_general | solution.py:172
  164.7 5.4 collective-permute-done
  170.3 15.4 %fusion.67 = (bf16[32,4096]{1,0:T(8,128)(2,1)S(1)}, f32[32,4096]{1,0:T(8,128)S(1)}) fusion(bf16[32,4096]{1,0:T(8,128)(2,1)S(1)} %get-tuple-element.46, bf16[4096,4096]{1,0:T(8,128)(2,1)} %bitcast.339, f32[32]{0:T(128)S(1)} %add_rsqrt_fusion.11), kind=kOutput, calls=%fused_computation.120 | convolution fusion | flops 1075052544 | bytes 34603136 | tf_op jit(solution)/shard_map/dot_general | solution.py:172
  194.6 15.4 %fusion.70 = (bf16[32,4096]{1,0:T(8,128)(2,1)S(1)}, f32[32,4096]{1,0:T(8,128)S(1)}) fusion(bf16[32,4096]{1,0:T(8,128)(2,1)S(1)} %get-tuple-element.44, bf16[4096,4096]{1,0:T(8,128)(2,1)} %bitcast.340, f32[32]{0:T(128)S(1)} %add_rsqrt_fusion.10), kind=kOutput, calls=%fused_computation.123 | convolution fusion | flops 1075052544 | bytes 34603136 | tf_op jit(solution)/shard_map/dot_general | solution.py:172
  218.1 15.5 %fusion.73 = (bf16[32,4096]{1,0:T(8,128)(2,1)S(1)}, f32[32,4096]{1,0:T(8,128)S(1)}) fusion(bf16[32,4096]{1,0:T(8,128)(2,1)S(1)} %get-tuple-element.42, bf16[4096,4096]{1,0:T(8,128)(2,1)} %bitcast.341, f32[32]{0:T(128)S(1)} %add_rsqrt_fusion.9), kind=kOutput, calls=%fused_computation.126 | convolution fusion | flops 1075052544 | bytes 34603136 | tf_op jit(solution)/shard_map/dot_general | solution.py:172
  241.2 15.5 %fusion.76 = (bf16[32,4096]{1,0:T(8,128)(2,1)S(1)}, f32[32,4096]{1,0:T(8,128)S(1)}) fusion(bf16[32,4096]{1,0:T(8,128)(2,1)S(1)} %get-tuple-element.40, bf16[4096,4096]{1,0:T(8,128)(2,1)} %bitcast.342, f32[32]{0:T(128)S(1)} %add_rsqrt_fusion.8), kind=kOutput, calls=%fused_computation.129 | convolution fusion | flops 1075052544 | bytes 34603136 | tf_op jit(solution)/shard_map/dot_general | solution.py:172
  264.0 15.4 %fusion.79 = (bf16[32,4096]{1,0:T(8,128)(2,1)S(1)}, f32[32,4096]{1,0:T(8,128)S(1)}) fusion(bf16[32,4096]{1,0:T(8,128)(2,1)S(1)} %get-tuple-element.38, bf16[4096,4096]{1,0:T(8,128)(2,1)} %bitcast.343, f32[32]{0:T(128)S(1)} %add_rsqrt_fusion.7), kind=kOutput, calls=%fused_computation.132 | convolution fusion | flops 1075052544 | bytes 34603136 | tf_op jit(solution)/shard_map/dot_general | solution.py:172
  287.7 15.6 %fusion.1 = f32[7,32,4096]{2,1,0:T(8,128)S(1)} fusion(f32[7,32,4096]{2,1,0:T(8,128)S(1)} %bitcast_dynamic-update-slice_fusion, bf16[4096,4096]{1,0:T(8,128)(2,1)} %bitcast.344, bf16[32,4096]{1,0:T(8,128)(2,1)S(1)} %get-tuple-element.36, f32[32]{0:T(128)S(1)} %add_rsqrt_fusion.6), kind=kOutput, calls=%fused_computation.3 | convolution fusion | flops 1074135040 | bytes 34341376 | tf_op jit(solution)/shard_map/dot_general | solution.py:172
  303.3 14.0 %fusion.64 = (f32[32]{0:T(128)S(1)}, f32[32]{0:T(128)S(1)}, f32[32]{0:T(128)S(1)}, f32[32]{0:T(128)S(1)}, f32[32]{0:T(128)S(1)}, /*index=5*/f32[32]{0:T(128)S(1)}, f32[32,4096]{1,0:T(8,128)S(1)}) fusion(bf16[7,32,4096]{2,1,0:T(8,128)(2,1)S(1)} %get-tuple-element.35, s32[]{:T(128)S(6)} %dynamic_slice.94, f32[32]{0:T(128)S(1)} %add_rsqrt_fusion.5, ...), kind=kOutput, calls=%fused_computation.117 | convolution fusion | flops 1077673984 | bytes 36443392 | tf_op jit(solution)/shard_map/dot_general | solution.py:185
  325.9 13.7 %fusion.35 = (f32[32]{0:T(128)S(1)}, f32[32,4096]{1,0:T(8,128)S(1)}) fusion(f32[32]{0:T(128)S(1)} %add_rsqrt_fusion.4, bf16[7,32,4096]{2,1,0:T(8,128)(2,1)S(1)} %get-tuple-element.35, s32[]{:T(128)S(6)} %dynamic_slice.82, bf16[32,4096]{1,0:T(8,128)(2,1)S(1)} %get-tuple-element.34, bf16[4096,4096]{1,0:T(8,128)(2,1)} %bitcast.346), kind=kOutput, calls=%fused_computation.88 | convolution fusion | flops 1074266112 | bytes 34603268 | tf_op jit(solution)/shard_map/dot_general | solution.py:185
  342.0 5.0 collective-permute-done.7
  347.9 13.7 %fusion.32 = (f32[32]{0:T(128)S(1)}, f32[32,4096]{1,0:T(8,128)S(1)}) fusion(f32[32]{0:T(128)S(1)} %add_rsqrt_fusion.3, bf16[7,32,4096]{2,1,0:T(8,128)(2,1)S(1)} %get-tuple-element.35, s32[]{:T(128)S(6)} %dynamic_slice.85, bf16[32,4096]{1,0:T(8,128)(2,1)S(1)} %get-tuple-element.32, bf16[4096,4096]{1,0:T(8,128)(2,1)} %bitcast.347), kind=kOutput, calls=%fused_computation.85 | convolution fusion | flops 1074266112 | bytes 34603268 | tf_op jit(solution)/shard_map/dot_general | solution.py:185
  364.2 4.8 collective-permute-done.8
  369.9 13.7 %fusion.29 = (f32[32]{0:T(128)S(1)}, f32[32,4096]{1,0:T(8,128)S(1)}) fusion(f32[32]{0:T(128)S(1)} %add_rsqrt_fusion.2, bf16[7,32,4096]{2,1,0:T(8,128)(2,1)S(1)} %get-tuple-element.35, s32[]{:T(128)S(6)} %dynamic_slice.88, bf16[32,4096]{1,0:T(8,128)(2,1)S(1)} %get-tuple-element.30, bf16[4096,4096]{1,0:T(8,128)(2,1)} %bitcast.348), kind=kOutput, calls=%fused_computation.82 | convolution fusion | flops 1074266112 | bytes 34603268 | tf_op jit(solution)/shard_map/dot_general | solution.py:185
  385.9 5.0 collective-permute-done.9
  391.9 13.7 %fusion.26 = (f32[32]{0:T(128)S(1)}, f32[32,4096]{1,0:T(8,128)S(1)}) fusion(f32[32]{0:T(128)S(1)} %add_rsqrt_fusion.1, bf16[7,32,4096]{2,1,0:T(8,128)(2,1)S(1)} %get-tuple-element.35, s32[]{:T(128)S(6)} %dynamic_slice.91, bf16[32,4096]{1,0:T(8,128)(2,1)S(1)} %get-tuple-element.28, bf16[4096,4096]{1,0:T(8,128)(2,1)} %bitcast.349), kind=kOutput, calls=%fused_computation.79 | convolution fusion | flops 1074266112 | bytes 34603268 | tf_op jit(solution)/shard_map/dot_general | solution.py:185
  407.9 5.0 collective-permute-done.10
  413.8 13.7 %fusion.23 = (f32[32]{0:T(128)S(1)}, f32[32,4096]{1,0:T(8,128)S(1)}) fusion(f32[32]{0:T(128)S(1)} %add_rsqrt_fusion, bf16[7,32,4096]{2,1,0:T(8,128)(2,1)S(1)} %get-tuple-element.35, s32[]{:T(128)S(6)} %dynamic_slice.94, bf16[32,4096]{1,0:T(8,128)(2,1)S(1)} %get-tuple-element.26, bf16[4096,4096]{1,0:T(8,128)(2,1)} %bitcast.350), kind=kOutput, calls=%fused_computation.76 | convolution fusion | flops 1074266112 | bytes 34603268 | tf_op jit(solution)/shard_map/dot_general | solution.py:185
  435.7 15.9 %fusion = bf16[4096,4096]{1,0:T(8,128)(2,1)} fusion(bf16[7,32,4096]{2,1,0:T(8,128)(2,1)} %bitcast_dynamic-update-slice_fusion.6, s32[]{:T(128)S(6)} %select_n.134, bf16[7,32,4096]{2,1,0:T(8,128)(2,1)} %bitcast_dynamic-update-slice_fusion.12, s32[]{:T(128)S(6)} %select_n.143), kind=kOutput, calls=%fused_computation.1 | convolution fusion | flops 4328521728 | bytes 35651592 | tf_op jit(solution)/shard_map/dot_general | solution.py:244
  451.6 50.0 %shard_map.86 = bf16[64,64,2048]{2,1,0:T(8,128)(2,1)} custom-call(s32[2048]{0:T(1024)} %reshape_squeeze.3.table_ref, bf16[64,64,4096]{2,1,0:T(8,128)(2,1)} %bitcast.351), custom_call_target="tpu_custom_call" | custom-call | bytes 50331648 | tf_op jit(solution)/shard_map/pallas_call | solution.py:95
  502.5 125.6 %reduce-scatter.2.cloned.1.call-done = bf16[2,64,2048]{2,1,0:T(8,128)(2,1)} async-done(((bf16[64,64,2048]{2,1,0:T(8,128)(2,1)}), bf16[2,64,2048]{2,1,0:T(8,128)(2,1)}) %reduce-scatter.2.cloned.1.call-update) | async-done | bytes 524304 | tf_op jit(solution)/shard_map/reduce_scatter | solution.py:253
  633.0 12.1 %shard_map.87 = f32[8,128]{1,0:T(8,128)} custom-call(f32[8,128]{1,0:T(8,128)} %scatter.4.x_ref), custom_call_target="tpu_custom_call" | custom-call | tf_op jit(solution)/shard_map/pallas_call | solution.py:153
  (133 shorter events, 88.5 us)
Async XLA Ops:
  7.2 79.4 %all-gather.3.cloned.1.call-start = ((), (), s32[]{:S(2)}) async-start(), calls=%async_computation.2 | async-start | bytes 17301504 | tf_op jit(solution)/shard_map/all_gather | solution.py:204
  7.9 620.2 %reduce-scatter.2.cloned.1.call-start = ((), (), s32[]{:S(2)}) async-start(), calls=%async_computation.1 | async-start | bytes 17301504 | tf_op jit(solution)/shard_map/reduce_scatter | solution.py:253
  86.5 59.5 %copy-start.1 = (bf16[4,32,4096]{2,1,0:T(8,128)(2,1)S(1)}, bf16[4,32,4096]{2,1,0:T(8,128)(2,1)}, u32[]{:S(2)}) copy-start(bf16[4,32,4096]{2,1,0:T(8,128)(2,1)} %param.8) | copy-start | bytes 3145732
  161.5 8.6 %collective-permute-start = (bf16[32,4096]{1,0:T(8,128)(2,1)S(1)}, bf16[32,4096]{1,0:T(8,128)(2,1)S(1)}, u32[]{:S(2)}, u32[]{:S(2)}) collective-permute-start(bf16[32,4096]{1,0:T(8,128)(2,1)S(1)} %get-tuple-element.50), channel_id=1, source_target_pairs={{0,32},{32,64},{64,96},{1,33},{33,65},{65,97},{2,34},{34,66},{66,9... | collective-permute-start | bytes 786440 | tf_op jit(solution)/shard_map/ppermute | solution.py:16
  170.1 15.7 %copy-start.8 = (bf16[32,4096]{1,0:T(8,128)(2,1)}, bf16[32,4096]{1,0:T(8,128)(2,1)S(1)}, u32[]{:S(2)}) copy-start(bf16[32,4096]{1,0:T(8,128)(2,1)S(1)} %get-tuple-element.46) | copy-start | bytes 786436
  185.8 8.6 %collective-permute-start.1 = (bf16[32,4096]{1,0:T(8,128)(2,1)S(1)}, bf16[32,4096]{1,0:T(8,128)(2,1)S(1)}, u32[]{:S(2)}, u32[]{:S(2)}) collective-permute-start(bf16[32,4096]{1,0:T(8,128)(2,1)S(1)} %get-tuple-element.52), channel_id=1, source_target_pairs={{0,32},{32,64},{64,96},{1,33},{33,65},{65,97},{2,34},{34,66},{66,9... | collective-permute-start | bytes 786440 | tf_op jit(solution)/shard_map/ppermute | solution.py:16
  194.4 15.6 %copy-start.6 = (bf16[32,4096]{1,0:T(8,128)(2,1)}, bf16[32,4096]{1,0:T(8,128)(2,1)S(1)}, u32[]{:S(2)}) copy-start(bf16[32,4096]{1,0:T(8,128)(2,1)S(1)} %get-tuple-element.44) | copy-start | bytes 786436
  210.1 7.7 %collective-permute-start.2 = (bf16[32,4096]{1,0:T(8,128)(2,1)S(1)}, bf16[32,4096]{1,0:T(8,128)(2,1)S(1)}, u32[]{:S(2)}, u32[]{:S(2)}) collective-permute-start(bf16[32,4096]{1,0:T(8,128)(2,1)S(1)} %get-tuple-element.54), channel_id=1, source_target_pairs={{0,32},{32,64},{64,96},{1,33},{33,65},{65,97},{2,34},{34,66},{66,9... | collective-permute-start | bytes 786440 | tf_op jit(solution)/shard_map/ppermute | solution.py:16
  217.9 15.7 %copy-start.4 = (bf16[32,4096]{1,0:T(8,128)(2,1)}, bf16[32,4096]{1,0:T(8,128)(2,1)S(1)}, u32[]{:S(2)}) copy-start(bf16[32,4096]{1,0:T(8,128)(2,1)S(1)} %get-tuple-element.42) | copy-start | bytes 786436
  233.5 7.4 %collective-permute-start.3 = (bf16[32,4096]{1,0:T(8,128)(2,1)S(1)}, bf16[32,4096]{1,0:T(8,128)(2,1)S(1)}, u32[]{:S(2)}, u32[]{:S(2)}) collective-permute-start(bf16[32,4096]{1,0:T(8,128)(2,1)S(1)} %get-tuple-element.56), channel_id=1, source_target_pairs={{0,32},{32,64},{64,96},{1,33},{33,65},{65,97},{2,34},{34,66},{66,9... | collective-permute-start | bytes 786440 | tf_op jit(solution)/shard_map/ppermute | solution.py:16
  241.0 15.7 %copy-start.2 = (bf16[32,4096]{1,0:T(8,128)(2,1)}, bf16[32,4096]{1,0:T(8,128)(2,1)S(1)}, u32[]{:S(2)}) copy-start(bf16[32,4096]{1,0:T(8,128)(2,1)S(1)} %get-tuple-element.40) | copy-start | bytes 786436
  256.7 7.1 %collective-permute-start.4 = (bf16[32,4096]{1,0:T(8,128)(2,1)S(1)}, bf16[32,4096]{1,0:T(8,128)(2,1)S(1)}, u32[]{:S(2)}, u32[]{:S(2)}) collective-permute-start(bf16[32,4096]{1,0:T(8,128)(2,1)S(1)} %get-tuple-element.58), channel_id=1, source_target_pairs={{0,32},{32,64},{64,96},{1,33},{33,65},{65,97},{2,34},{34,66},{66,9... | collective-permute-start | bytes 786440 | tf_op jit(solution)/shard_map/ppermute | solution.py:16
  279.5 7.1 %collective-permute-start.5 = (bf16[32,4096]{1,0:T(8,128)(2,1)S(1)}, bf16[32,4096]{1,0:T(8,128)(2,1)S(1)}, u32[]{:S(2)}, u32[]{:S(2)}) collective-permute-start(bf16[32,4096]{1,0:T(8,128)(2,1)S(1)} %get-tuple-element.60), channel_id=1, source_target_pairs={{0,32},{32,64},{64,96},{1,33},{33,65},{65,97},{2,34},{34,66},{66,9... | collective-permute-start | bytes 786440 | tf_op jit(solution)/shard_map/ppermute | solution.py:16
  287.7 15.6 %copy-start = (bf16[4,32,4096]{2,1,0:T(8,128)(2,1)S(1)}, bf16[4,32,4096]{2,1,0:T(8,128)(2,1)}, u32[]{:S(2)}) copy-start(bf16[4,32,4096]{2,1,0:T(8,128)(2,1)} %param.9) | copy-start | bytes 3145732
  303.3 15.5 %copy-start.9 = (bf16[32,4096]{1,0:T(8,128)(2,1)S(1)}, bf16[32,4096]{1,0:T(8,128)(2,1)}, u32[]{:S(2)}) copy-start(bf16[32,4096]{1,0:T(8,128)(2,1)} %copy-done.8) | copy-start | bytes 786436
  317.5 7.6 %collective-permute-start.6 = (bf16[32,4096]{1,0:T(8,128)(2,1)S(1)}, bf16[32,4096]{1,0:T(8,128)(2,1)S(1)}, u32[]{:S(2)}, u32[]{:S(2)}) collective-permute-start(bf16[32,4096]{1,0:T(8,128)(2,1)S(1)} %fusion.42), channel_id=1, source_target_pairs={{32,0},{64,32},{96,64},{33,1},{65,33},{97,65},{34,2},{66,34},{98,6... | collective-permute-start | bytes 786440 | tf_op jit(solution)/shard_map/ppermute | solution.py:16
  339.9 7.1 %collective-permute-start.7 = (bf16[32,4096]{1,0:T(8,128)(2,1)S(1)}, bf16[32,4096]{1,0:T(8,128)(2,1)S(1)}, u32[]{:S(2)}, u32[]{:S(2)}) collective-permute-start(bf16[32,4096]{1,0:T(8,128)(2,1)S(1)} %fusion.50), channel_id=1, source_target_pairs={{32,0},{64,32},{96,64},{33,1},{65,33},{97,65},{34,2},{66,34},{98,6... | collective-permute-start | bytes 786440 | tf_op jit(solution)/shard_map/ppermute | solution.py:16
  347.9 15.4 %copy-start.5 = (bf16[32,4096]{1,0:T(8,128)(2,1)S(1)}, bf16[32,4096]{1,0:T(8,128)(2,1)}, u32[]{:S(2)}) copy-start(bf16[32,4096]{1,0:T(8,128)(2,1)} %copy-done.4) | copy-start | bytes 786436
  361.8 7.1 %collective-permute-start.8 = (bf16[32,4096]{1,0:T(8,128)(2,1)S(1)}, bf16[32,4096]{1,0:T(8,128)(2,1)S(1)}, u32[]{:S(2)}, u32[]{:S(2)}) collective-permute-start(bf16[32,4096]{1,0:T(8,128)(2,1)S(1)} %fusion.52), channel_id=1, source_target_pairs={{32,0},{64,32},{96,64},{33,1},{65,33},{97,65},{34,2},{66,34},{98,6... | collective-permute-start | bytes 786440 | tf_op jit(solution)/shard_map/ppermute | solution.py:16
  383.8 7.1 %collective-permute-start.9 = (bf16[32,4096]{1,0:T(8,128)(2,1)S(1)}, bf16[32,4096]{1,0:T(8,128)(2,1)S(1)}, u32[]{:S(2)}, u32[]{:S(2)}) collective-permute-start(bf16[32,4096]{1,0:T(8,128)(2,1)S(1)} %fusion.54), channel_id=1, source_target_pairs={{32,0},{64,32},{96,64},{33,1},{65,33},{97,65},{34,2},{66,34},{98,6... | collective-permute-start | bytes 786440 | tf_op jit(solution)/shard_map/ppermute | solution.py:16
  405.7 7.1 %collective-permute-start.10 = (bf16[32,4096]{1,0:T(8,128)(2,1)S(1)}, bf16[32,4096]{1,0:T(8,128)(2,1)S(1)}, u32[]{:S(2)}, u32[]{:S(2)}) collective-permute-start(bf16[32,4096]{1,0:T(8,128)(2,1)S(1)} %fusion.56), channel_id=1, source_target_pairs={{32,0},{64,32},{96,64},{33,1},{65,33},{97,65},{34,2},{66,34},{98,6... | collective-permute-start | bytes 786440 | tf_op jit(solution)/shard_map/ppermute | solution.py:16
  427.6 7.1 %collective-permute-start.11 = (bf16[32,4096]{1,0:T(8,128)(2,1)S(1)}, bf16[32,4096]{1,0:T(8,128)(2,1)S(1)}, u32[]{:S(2)}, u32[]{:S(2)}) collective-permute-start(bf16[32,4096]{1,0:T(8,128)(2,1)S(1)} %fusion.58), channel_id=1, source_target_pairs={{32,0},{64,32},{96,64},{33,1},{65,33},{97,65},{34,2},{66,34},{98,6... | collective-permute-start | bytes 786440 | tf_op jit(solution)/shard_map/ppermute | solution.py:16
  501.6 126.5 %copy-start.10 = (bf16[1,2,64,2048]{3,2,1,0:T(8,128)(2,1)S(1)}, bf16[1,2,64,2048]{3,2,1,0:T(8,128)(2,1)}, u32[]{:S(2)}) copy-start(bf16[1,2,64,2048]{3,2,1,0:T(8,128)(2,1)} %param.10) | copy-start | bytes 1572868
  501.6 126.5 %copy-start.11 = (f32[1,2,64,2048]{3,2,1,0:T(8,128)S(1)}, f32[1,2,64,2048]{3,2,1,0:T(8,128)}, u32[]{:S(2)}) copy-start(f32[1,2,64,2048]{3,2,1,0:T(8,128)} %param.13) | copy-start | bytes 3145732
  (3 other events, 31.2 us)
Sparse Core Ops, SparseCore 0:
  10.3 76.2 all-gather.2
  501.8 126.3 reduce-scatter.1

commit v3 on v2

--- a/solution.py
+++ b/solution.py
@@ -61,7 +61,13 @@
         o_ref[0, :, q * 128:(q + 1) * 128] = jnp.where(lane < 64, low, high)
 
 
-def expand_dense(section_weights, live_index):
+def gathered_place(j, cores, chips, own):
+    e = j % own
+    device = j // own
+    return ((device % cores) * chips + device // cores) * own + e
+
+
+def expand_dense(section_weights, live_index, cores, chips, own):
     column_count, block_size, wide = section_weights.shape
     live_count = live_index.shape[1]
     features = column_count * block_size
@@ -77,7 +83,12 @@
         grid_spec=pltpu.PrefetchScalarGridSpec(
             num_scalar_prefetch=1,
             grid=(column_count,),
-            in_specs=[pl.BlockSpec((1, block_size, wide), lambda j, tbl: (j, 0, 0))],
+            in_specs=[
+                pl.BlockSpec(
+                    (1, block_size, wide),
+                    lambda j, tbl: (gathered_place(j, cores, chips, own), 0, 0),
+                )
+            ],
             out_specs=pl.BlockSpec((1, block_size, features), lambda j, tbl: (j, 0, 0)),
         ),
         cost_estimate=pl.CostEstimate(
@@ -87,7 +98,7 @@
     return out.reshape(features, features)
 
 
-def pack_dense(dense_grad, live_index):
+def pack_dense(dense_grad, live_index, cores, chips, own):
     column_count, live_count = live_index.shape
     features = dense_grad.shape[0]
     block_size = features // column_count
@@ -99,7 +110,9 @@
             num_scalar_prefetch=1,
             grid=(column_count,),
             in_specs=[pl.BlockSpec((1, block_size, features), lambda j, tbl: (j, 0, 0))],
-            out_specs=pl.BlockSpec((1, block_size, wide), lambda j, tbl: (j, 0, 0)),
+            out_specs=pl.BlockSpec(
+                (1, block_size, wide), lambda j, tbl: (gathered_place(j, cores, chips, own), 0, 0)
+            ),
         ),
         cost_estimate=pl.CostEstimate(
             flops=0, transcendentals=0, bytes_accessed=3 * column_count * block_size * wide * 2
@@ -109,12 +122,13 @@
 
 def spread_kernel(x_ref, o_ref, recv_ref, send_sem, recv_sem):
     count = recv_ref.shape[0]
-    me = lax.axis_index("dp")
+    cores = lax.axis_size("core")
+    me = lax.axis_index("chip") * cores + lax.axis_index("core")
     pipe = lax.axis_index("pipe")
     barrier = pltpu.get_barrier_semaphore()
     for step in range(1, count):
         peer = lax.rem(me + step, count)
-        pl.semaphore_signal(barrier, inc=1, device_id=(pipe, peer), device_id_type=pl.DeviceIdType.MESH)
+        pl.semaphore_signal(barrier, inc=1, device_id=(pipe, peer // cores, peer % cores), device_id_type=pl.DeviceIdType.MESH)
     pl.semaphore_wait(barrier, count - 1)
     copies = []
     for step in range(1, count):
@@ -124,7 +138,7 @@
             dst_ref=recv_ref.at[me],
             send_sem=send_sem.at[step],
             recv_sem=recv_sem.at[me],
-            device_id=(pipe, peer),
+            device_id=(pipe, peer // cores, peer % cores),
             device_id_type=pl.DeviceIdType.MESH,
         )
         copy.start()
@@ -137,7 +151,7 @@
             dst_ref=recv_ref.at[source],
             send_sem=send_sem.at[step],
             recv_sem=recv_sem.at[source],
-            device_id=(pipe, source),
+            device_id=(pipe, source // cores, source % cores),
             device_id_type=pl.DeviceIdType.MESH,
         )
         arrival.wait_recv()
@@ -148,7 +162,7 @@
 
 
 def spread_sum(values):
-    count = lax.axis_size("dp")
+    count = lax.axis_size("chip") * lax.axis_size("core")
     padded = jnp.zeros((8, 128), jnp.float32).at[0, : values.shape[0]].set(values)
     out = pl.pallas_call(
         spread_kernel,
@@ -201,8 +215,14 @@
     own_columns = weights.shape[1]
     block_size = weights.shape[2]
     live_index = live_rows[0]
-    section_weights = lax.all_gather(weights[0], "dp", axis=0, tiled=True)
-    dense_t = expand_dense(section_weights, live_index)
+    cores = lax.axis_size("core")
+    chips = lax.axis_size("chip")
+    dp_size = cores * chips
+    dp_index = lax.axis_index("chip") * cores + lax.axis_index("core")
+    section_weights = lax.all_gather(
+        lax.all_gather(weights[0], "chip", axis=0, tiled=True), "core", axis=0, tiled=True
+    )
+    dense_t = expand_dense(section_weights, live_index, cores, chips, own_columns)
     tick_count = micro_count + sections - 1
 
     incoming = jnp.zeros((tokens, features), jnp.bfloat16)
@@ -239,7 +259,7 @@
     )
 
     all_rows = micro_count * tokens
-    inverse_tokens = 1.0 / (all_rows * lax.axis_size("dp"))
+    inverse_tokens = 1.0 / (all_rows * dp_size)
     dense_grad = (
         lax.dot_general(
             saved_grad.reshape(all_rows, features),
@@ -249,15 +269,20 @@
         )
         * inverse_tokens
     ).astype(jnp.bfloat16)
-    partial = pack_dense(dense_grad, live_index)
-    gradient = lax.psum_scatter(partial, "dp", scatter_dimension=0, tiled=True).astype(jnp.float32)
+    partial = pack_dense(dense_grad, live_index, cores, chips, own_columns)
+    gradient = lax.psum_scatter(
+        lax.psum_scatter(partial, "core", scatter_dimension=0, tiled=True),
+        "chip",
+        scatter_dimension=0,
+        tiled=True,
+    ).astype(jnp.float32)
 
     rate = 0.1 / math.sqrt(live_count * block_size)
     moment_new = 0.9 * moment[0] + 0.1 * gradient
     second_new = 0.95 * second[0] + 0.05 * gradient * gradient
     stepped = weights[0].astype(jnp.float32) - rate * moment_new / (jnp.sqrt(second_new) + 1e-08)
     own_index = lax.dynamic_slice_in_dim(
-        live_index, lax.axis_index("dp") * own_columns, own_columns, 0
+        live_index, dp_index * own_columns, own_columns, 0
     )
     blocked = stepped.reshape(own_columns, block_size, live_count, block_size)
     magnitude = jnp.sqrt(jnp.sum(blocked * blocked, axis=(1, 3)))
@@ -285,22 +310,27 @@
 
 
 def solution(mesh):
+    pipe_size, dp_size = mesh.devices.shape
+    split = jax.sharding.Mesh(
+        mesh.devices.reshape(pipe_size, dp_size // 2, 2), ("pipe", "chip", "core")
+    )
+    dp = ("chip", "core")
     placed = (
-        P(None, "dp", None),
-        P(None, "dp", None),
-        P("pipe", "dp", None, None),
+        P(None, dp, None),
+        P(None, dp, None),
+        P("pipe", dp, None, None),
         P("pipe", None, None),
-        P("pipe", "dp", None, None),
-        P("pipe", "dp", None, None),
+        P("pipe", dp, None, None),
+        P("pipe", dp, None, None),
     )
     return jax.shard_map(
         local,
-        mesh=mesh,
+        mesh=split,
         in_specs=placed,
         out_specs=(
-            P("pipe", "dp", None, None),
-            P("pipe", "dp", None, None),
-            P("pipe", "dp", None, None),
+            P("pipe", dp, None, None),
+            P("pipe", dp, None, None),
+            P("pipe", dp, None, None),
         ),
         check_vma=False,
     )

time: 666 us -> 705 us (1.059)
  waiting for transfers between devices: 250 us -> 291 us
    all_gather x1 -> x2, waiting for transfers between devices: 72.6 us -> 107 us  [the longest x1 76.3 us: local(): lax.all_gather(weights[0], 'chip', axis=0, tiled=True)]
    reduce_scatter x1 -> x2, waiting for transfers between devices: 126 us -> 132 us  [the longest x1 88 us: local(): lax.psum_scatter(lax.psum_scatter(partial, 'core', scatter_dimension=0, t...]
  transfers between devices with their start and end apart: 14 -> 16, of which waited for: 14 -> 16; matrix products, arithmetic and copies ran while one was open for 2% -> 1% of each run, Pallas kernels for 0% -> 0%
where the time goes in v3:
time: 705 us; the launch traced here: 694 us
  waiting for transfers between devices  291 us (41%)
  matrix products  207 us (29%)
  Pallas kernels  122 us (17%)
  starting transfers between devices  32.3 us (5%)
  other arithmetic  22.4 us (3%)
  between operations  15.4 us (2%)
    dot_general x7, matrix products, layer_forward(): lax.dot_general(normed, dense_t, (((1,), (1,)), ((), ())), preferred_elem...  108 us
    reduce_scatter x1, waiting for transfers between devices, local(): lax.psum_scatter(lax.psum_scatter(partial, 'core', scatter_dimension=0, t...  88 us
    dot_general x6, matrix products, layer_backward(): grad_normed = jnp.dot(grad_pre, dense_t, preferred_element_type=jnp.float32)  82.3 us
    all_gather x1, waiting for transfers between devices, local(): lax.all_gather(weights[0], 'chip', axis=0, tiled=True)  76.3 us
    pallas_call x1, Pallas kernels, expand_dense(): pl.pallas_call(expand_kernel, out_shape=jax.ShapeDtypeStruct((column_coun...  59.5 us
    ppermute x12, waiting for transfers between devices, shifted(): lax.ppermute(value, axis, [(source, source + steps) for source in range(l...  51.5 us
    pallas_call x1, Pallas kernels, pack_dense(): pl.pallas_call(pack_kernel, out_shape=jax.ShapeDtypeStruct((column_count,...  50.3 us
    reduce_scatter x1, waiting for transfers between devices, local(): lax.psum_scatter(partial, 'core', scatter_dimension=0, tiled=True)  43.6 us
  transfers between devices with their start and end apart: 16, of which 16 were waited for; matrix products, arithmetic and copies ran while one was open for 1% of the time, Pallas kernels for 0%

profile of v3, /device:TPU:1, one launch (start us, length us, event | category | flops | bytes accessed | tf_op | source)
XLA Modules:
  0.0 694.2 jit_solution(9451835667723200161)
XLA Ops:
  7.9 76.3 %all-gather.5.cloned.1.call-done = bf16[1,32,64,2048]{3,2,0,1:T(8,128)(2,1)} async-done(((bf16[1,2,64,2048]{3,2,0,1:T(8,128)(2,1)}), bf16[1,32,64,2048]{3,2,0,1:T(8,128)(2,1)}) %all-gather.5.cloned.1.call-update) | async-done | bytes 8388624 | tf_op jit(solution)/shard_map/all_gather | solution.py:223
  87.6 31.1 %all-gather.7.cloned.1.call-done = bf16[1,64,64,2048]{3,2,0,1:T(8,128)(2,1)} async-done(((bf16[1,32,64,2048]{3,2,0,1:T(8,128)(2,1)}), bf16[1,64,64,2048]{3,2,0,1:T(8,128)(2,1)}) %all-gather.7.cloned.1.call-update) | async-done | bytes 16777232 | tf_op jit(solution)/shard_map/all_gather | solution.py:222
  118.7 59.5 %shard_map.85 = bf16[64,64,4096]{2,1,0:T(8,128)(2,1)} custom-call(s32[4096]{0:T(1024)} %select_n.126.table_ref, bf16[64,64,2048]{2,1,0:T(8,128)(2,1)} %bitcast.352), custom_call_target="tpu_custom_call" | custom-call | bytes 50331648 | tf_op jit(solution)/shard_map/pallas_call | solution.py:80
  178.3 15.4 %fusion.45 = (bf16[32,4096]{1,0:T(8,128)(2,1)S(1)}, f32[32,4096]{1,0:T(8,128)S(1)}) fusion(bf16[4,32,4096]{2,1,0:T(8,128)(2,1)S(1)} %copy-done.1, pred[]{:T(512)S(6)} %eq.19, bf16[4096,4096]{1,0:T(8,128)(2,1)} %bitcast.338, f32[32]{0:T(128)S(1)} %add_rsqrt_fusion.12), kind=kOutput, calls=%fused_computation.98 | convolution fusion | flops 1075314688 | bytes 34866688 | tf_op jit(solution)/shard_map/dot_general | solution.py:186
  197.0 5.4 collective-permute-done
  202.7 15.4 %fusion.67 = (bf16[32,4096]{1,0:T(8,128)(2,1)S(1)}, f32[32,4096]{1,0:T(8,128)S(1)}) fusion(bf16[32,4096]{1,0:T(8,128)(2,1)S(1)} %get-tuple-element.46, bf16[4096,4096]{1,0:T(8,128)(2,1)} %bitcast.339, f32[32]{0:T(128)S(1)} %add_rsqrt_fusion.11), kind=kOutput, calls=%fused_computation.120 | convolution fusion | flops 1075052544 | bytes 34603136 | tf_op jit(solution)/shard_map/dot_general | solution.py:186
  227.1 15.4 %fusion.70 = (bf16[32,4096]{1,0:T(8,128)(2,1)S(1)}, f32[32,4096]{1,0:T(8,128)S(1)}) fusion(bf16[32,4096]{1,0:T(8,128)(2,1)S(1)} %get-tuple-element.44, bf16[4096,4096]{1,0:T(8,128)(2,1)} %bitcast.340, f32[32]{0:T(128)S(1)} %add_rsqrt_fusion.10), kind=kOutput, calls=%fused_computation.123 | convolution fusion | flops 1075052544 | bytes 34603136 | tf_op jit(solution)/shard_map/dot_general | solution.py:186
  250.5 15.4 %fusion.73 = (bf16[32,4096]{1,0:T(8,128)(2,1)S(1)}, f32[32,4096]{1,0:T(8,128)S(1)}) fusion(bf16[32,4096]{1,0:T(8,128)(2,1)S(1)} %get-tuple-element.42, bf16[4096,4096]{1,0:T(8,128)(2,1)} %bitcast.341, f32[32]{0:T(128)S(1)} %add_rsqrt_fusion.9), kind=kOutput, calls=%fused_computation.126 | convolution fusion | flops 1075052544 | bytes 34603136 | tf_op jit(solution)/shard_map/dot_general | solution.py:186
  273.7 15.5 %fusion.76 = (bf16[32,4096]{1,0:T(8,128)(2,1)S(1)}, f32[32,4096]{1,0:T(8,128)S(1)}) fusion(bf16[32,4096]{1,0:T(8,128)(2,1)S(1)} %get-tuple-element.40, bf16[4096,4096]{1,0:T(8,128)(2,1)} %bitcast.342, f32[32]{0:T(128)S(1)} %add_rsqrt_fusion.8), kind=kOutput, calls=%fused_computation.129 | convolution fusion | flops 1075052544 | bytes 34603136 | tf_op jit(solution)/shard_map/dot_general | solution.py:186
  296.5 15.4 %fusion.79 = (bf16[32,4096]{1,0:T(8,128)(2,1)S(1)}, f32[32,4096]{1,0:T(8,128)S(1)}) fusion(bf16[32,4096]{1,0:T(8,128)(2,1)S(1)} %get-tuple-element.38, bf16[4096,4096]{1,0:T(8,128)(2,1)} %bitcast.343, f32[32]{0:T(128)S(1)} %add_rsqrt_fusion.7), kind=kOutput, calls=%fused_computation.132 | convolution fusion | flops 1075052544 | bytes 34603136 | tf_op jit(solution)/shard_map/dot_general | solution.py:186
  320.1 15.6 %fusion.1 = f32[7,32,4096]{2,1,0:T(8,128)S(1)} fusion(f32[7,32,4096]{2,1,0:T(8,128)S(1)} %bitcast_dynamic-update-slice_fusion, bf16[4096,4096]{1,0:T(8,128)(2,1)} %bitcast.344, bf16[32,4096]{1,0:T(8,128)(2,1)S(1)} %get-tuple-element.36, f32[32]{0:T(128)S(1)} %add_rsqrt_fusion.6), kind=kOutput, calls=%fused_computation.3 | convolution fusion | flops 1074135040 | bytes 34341376 | tf_op jit(solution)/shard_map/dot_general | solution.py:186
  335.7 13.9 %fusion.64 = (f32[32]{0:T(128)S(1)}, f32[32]{0:T(128)S(1)}, f32[32]{0:T(128)S(1)}, f32[32]{0:T(128)S(1)}, f32[32]{0:T(128)S(1)}, /*index=5*/f32[32]{0:T(128)S(1)}, f32[32,4096]{1,0:T(8,128)S(1)}) fusion(bf16[7,32,4096]{2,1,0:T(8,128)(2,1)S(1)} %get-tuple-element.35, s32[]{:T(128)S(6)} %dynamic_slice.94, f32[32]{0:T(128)S(1)} %add_rsqrt_fusion.5, ...), kind=kOutput, calls=%fused_computation.117 | convolution fusion | flops 1077673984 | bytes 36443392 | tf_op jit(solution)/shard_map/dot_general | solution.py:199
  358.4 13.7 %fusion.35 = (f32[32]{0:T(128)S(1)}, f32[32,4096]{1,0:T(8,128)S(1)}) fusion(f32[32]{0:T(128)S(1)} %add_rsqrt_fusion.4, bf16[7,32,4096]{2,1,0:T(8,128)(2,1)S(1)} %get-tuple-element.35, s32[]{:T(128)S(6)} %dynamic_slice.82, bf16[32,4096]{1,0:T(8,128)(2,1)S(1)} %get-tuple-element.34, bf16[4096,4096]{1,0:T(8,128)(2,1)} %bitcast.346), kind=kOutput, calls=%fused_computation.88 | convolution fusion | flops 1074266112 | bytes 34603268 | tf_op jit(solution)/shard_map/dot_general | solution.py:199
  374.4 5.0 collective-permute-done.7
  380.4 13.7 %fusion.32 = (f32[32]{0:T(128)S(1)}, f32[32,4096]{1,0:T(8,128)S(1)}) fusion(f32[32]{0:T(128)S(1)} %add_rsqrt_fusion.3, bf16[7,32,4096]{2,1,0:T(8,128)(2,1)S(1)} %get-tuple-element.35, s32[]{:T(128)S(6)} %dynamic_slice.85, bf16[32,4096]{1,0:T(8,128)(2,1)S(1)} %get-tuple-element.32, bf16[4096,4096]{1,0:T(8,128)(2,1)} %bitcast.347), kind=kOutput, calls=%fused_computation.85 | convolution fusion | flops 1074266112 | bytes 34603268 | tf_op jit(solution)/shard_map/dot_general | solution.py:199
  402.3 13.7 %fusion.29 = (f32[32]{0:T(128)S(1)}, f32[32,4096]{1,0:T(8,128)S(1)}) fusion(f32[32]{0:T(128)S(1)} %add_rsqrt_fusion.2, bf16[7,32,4096]{2,1,0:T(8,128)(2,1)S(1)} %get-tuple-element.35, s32[]{:T(128)S(6)} %dynamic_slice.88, bf16[32,4096]{1,0:T(8,128)(2,1)S(1)} %get-tuple-element.30, bf16[4096,4096]{1,0:T(8,128)(2,1)} %bitcast.348), kind=kOutput, calls=%fused_computation.82 | convolution fusion | flops 1074266112 | bytes 34603268 | tf_op jit(solution)/shard_map/dot_general | solution.py:199
  418.4 5.0 collective-permute-done.9
  424.3 13.7 %fusion.26 = (f32[32]{0:T(128)S(1)}, f32[32,4096]{1,0:T(8,128)S(1)}) fusion(f32[32]{0:T(128)S(1)} %add_rsqrt_fusion.1, bf16[7,32,4096]{2,1,0:T(8,128)(2,1)S(1)} %get-tuple-element.35, s32[]{:T(128)S(6)} %dynamic_slice.91, bf16[32,4096]{1,0:T(8,128)(2,1)S(1)} %get-tuple-element.28, bf16[4096,4096]{1,0:T(8,128)(2,1)} %bitcast.349), kind=kOutput, calls=%fused_computation.79 | convolution fusion | flops 1074266112 | bytes 34603268 | tf_op jit(solution)/shard_map/dot_general | solution.py:199
  446.2 13.7 %fusion.23 = (f32[32]{0:T(128)S(1)}, f32[32,4096]{1,0:T(8,128)S(1)}) fusion(f32[32]{0:T(128)S(1)} %add_rsqrt_fusion, bf16[7,32,4096]{2,1,0:T(8,128)(2,1)S(1)} %get-tuple-element.35, s32[]{:T(128)S(6)} %dynamic_slice.94, bf16[32,4096]{1,0:T(8,128)(2,1)S(1)} %get-tuple-element.26, bf16[4096,4096]{1,0:T(8,128)(2,1)} %bitcast.350), kind=kOutput, calls=%fused_computation.76 | convolution fusion | flops 1074266112 | bytes 34603268 | tf_op jit(solution)/shard_map/dot_general | solution.py:199
  468.1 15.9 %fusion = bf16[4096,4096]{1,0:T(8,128)(2,1)} fusion(bf16[7,32,4096]{2,1,0:T(8,128)(2,1)} %bitcast_dynamic-update-slice_fusion.6, s32[]{:T(128)S(6)} %select_n.134, bf16[7,32,4096]{2,1,0:T(8,128)(2,1)} %bitcast_dynamic-update-slice_fusion.12, s32[]{:T(128)S(6)} %select_n.143), kind=kOutput, calls=%fused_computation.1 | convolution fusion | flops 4328521728 | bytes 35651592 | tf_op jit(solution)/shard_map/dot_general | solution.py:264
  484.1 50.3 %shard_map.86 = bf16[64,64,2048]{2,1,0:T(8,128)(2,1)} custom-call(s32[2048]{0:T(1024)} %reshape_squeeze.3.table_ref, bf16[64,64,4096]{2,1,0:T(8,128)(2,1)} %bitcast.351), custom_call_target="tpu_custom_call" | custom-call | bytes 50331648 | tf_op jit(solution)/shard_map/pallas_call | solution.py:106
  534.4 43.6 %reduce-scatter.3.cloned.1.call-done = bf16[32,64,2048]{2,1,0:T(8,128)(2,1)} async-done(((bf16[64,64,2048]{2,1,0:T(8,128)(2,1)}), bf16[32,64,2048]{2,1,0:T(8,128)(2,1)}) %reduce-scatter.3.cloned.1.call-update) | async-done | bytes 8388624 | tf_op jit(solution)/shard_map/reduce_scatter | solution.py:274
  578.8 88.0 %reduce-scatter.5.cloned.1.call-done = bf16[2,64,2048]{2,1,0:T(8,128)(2,1)} async-done(((bf16[32,64,2048]{2,1,0:T(8,128)(2,1)}), bf16[2,64,2048]{2,1,0:T(8,128)(2,1)}) %reduce-scatter.5.cloned.1.call-update) | async-done | bytes 524304 | tf_op jit(solution)/shard_map/reduce_scatter | solution.py:273
  671.7 12.1 %shard_map.87 = f32[8,128]{1,0:T(8,128)} custom-call(f32[8,128]{1,0:T(8,128)} %scatter.4.x_ref), custom_call_target="tpu_custom_call" | custom-call | tf_op jit(solution)/shard_map/pallas_call | solution.py:167
  (141 shorter events, 95.9 us)
Async XLA Ops:
  7.2 77.1 %all-gather.5.cloned.1.call-start = ((), (), s32[]{:S(2)}) async-start(), calls=%async_computation.4 | async-start | bytes 8912896 | tf_op jit(solution)/shard_map/all_gather | solution.py:223
  7.9 110.8 %all-gather.7.cloned.1.call-start = ((), (), s32[]{:S(2)}) async-start(), calls=%async_computation.5 | async-start | bytes 25165824 | tf_op jit(solution)/shard_map/all_gather | solution.py:222
  84.3 493.7 %reduce-scatter.3.cloned.1.call-start = ((), (), s32[]{:S(2)}) async-start(), calls=%async_computation.2 | async-start | bytes 25165824 | tf_op jit(solution)/shard_map/reduce_scatter | solution.py:274
  193.7 8.7 %collective-permute-start = (bf16[32,4096]{1,0:T(8,128)(2,1)S(1)}, bf16[32,4096]{1,0:T(8,128)(2,1)S(1)}, u32[]{:S(2)}, u32[]{:S(2)}) collective-permute-start(bf16[32,4096]{1,0:T(8,128)(2,1)S(1)} %get-tuple-element.50), channel_id=1, source_target_pairs={{0,32},{32,64},{64,96},{1,33},{33,65},{65,97},{2,34},{34,66},{66,9... | collective-permute-start | bytes 786440 | tf_op jit(solution)/shard_map/ppermute | solution.py:16
  202.5 15.6 %copy-start.8 = (bf16[32,4096]{1,0:T(8,128)(2,1)}, bf16[32,4096]{1,0:T(8,128)(2,1)S(1)}, u32[]{:S(2)}) copy-start(bf16[32,4096]{1,0:T(8,128)(2,1)S(1)} %get-tuple-element.46) | copy-start | bytes 786436
  218.1 8.7 %collective-permute-start.1 = (bf16[32,4096]{1,0:T(8,128)(2,1)S(1)}, bf16[32,4096]{1,0:T(8,128)(2,1)S(1)}, u32[]{:S(2)}, u32[]{:S(2)}) collective-permute-start(bf16[32,4096]{1,0:T(8,128)(2,1)S(1)} %get-tuple-element.52), channel_id=1, source_target_pairs={{0,32},{32,64},{64,96},{1,33},{33,65},{65,97},{2,34},{34,66},{66,9... | collective-permute-start | bytes 786440 | tf_op jit(solution)/shard_map/ppermute | solution.py:16
  226.9 15.7 %copy-start.6 = (bf16[32,4096]{1,0:T(8,128)(2,1)}, bf16[32,4096]{1,0:T(8,128)(2,1)S(1)}, u32[]{:S(2)}) copy-start(bf16[32,4096]{1,0:T(8,128)(2,1)S(1)} %get-tuple-element.44) | copy-start | bytes 786436
  242.5 7.7 %collective-permute-start.2 = (bf16[32,4096]{1,0:T(8,128)(2,1)S(1)}, bf16[32,4096]{1,0:T(8,128)(2,1)S(1)}, u32[]{:S(2)}, u32[]{:S(2)}) collective-permute-start(bf16[32,4096]{1,0:T(8,128)(2,1)S(1)} %get-tuple-element.54), channel_id=1, source_target_pairs={{0,32},{32,64},{64,96},{1,33},{33,65},{65,97},{2,34},{34,66},{66,9... | collective-permute-start | bytes 786440 | tf_op jit(solution)/shard_map/ppermute | solution.py:16
  250.3 15.7 %copy-start.4 = (bf16[32,4096]{1,0:T(8,128)(2,1)}, bf16[32,4096]{1,0:T(8,128)(2,1)S(1)}, u32[]{:S(2)}) copy-start(bf16[32,4096]{1,0:T(8,128)(2,1)S(1)} %get-tuple-element.42) | copy-start | bytes 786436
  266.0 7.4 %collective-permute-start.3 = (bf16[32,4096]{1,0:T(8,128)(2,1)S(1)}, bf16[32,4096]{1,0:T(8,128)(2,1)S(1)}, u32[]{:S(2)}, u32[]{:S(2)}) collective-permute-start(bf16[32,4096]{1,0:T(8,128)(2,1)S(1)} %get-tuple-element.56), channel_id=1, source_target_pairs={{0,32},{32,64},{64,96},{1,33},{33,65},{65,97},{2,34},{34,66},{66,9... | collective-permute-start | bytes 786440 | tf_op jit(solution)/shard_map/ppermute | solution.py:16
  273.5 15.6 %copy-start.2 = (bf16[32,4096]{1,0:T(8,128)(2,1)}, bf16[32,4096]{1,0:T(8,128)(2,1)S(1)}, u32[]{:S(2)}) copy-start(bf16[32,4096]{1,0:T(8,128)(2,1)S(1)} %get-tuple-element.40) | copy-start | bytes 786436
  289.1 7.1 %collective-permute-start.4 = (bf16[32,4096]{1,0:T(8,128)(2,1)S(1)}, bf16[32,4096]{1,0:T(8,128)(2,1)S(1)}, u32[]{:S(2)}, u32[]{:S(2)}) collective-permute-start(bf16[32,4096]{1,0:T(8,128)(2,1)S(1)} %get-tuple-element.58), channel_id=1, source_target_pairs={{0,32},{32,64},{64,96},{1,33},{33,65},{65,97},{2,34},{34,66},{66,9... | collective-permute-start | bytes 786440 | tf_op jit(solution)/shard_map/ppermute | solution.py:16
  312.0 7.1 %collective-permute-start.5 = (bf16[32,4096]{1,0:T(8,128)(2,1)S(1)}, bf16[32,4096]{1,0:T(8,128)(2,1)S(1)}, u32[]{:S(2)}, u32[]{:S(2)}) collective-permute-start(bf16[32,4096]{1,0:T(8,128)(2,1)S(1)} %get-tuple-element.60), channel_id=1, source_target_pairs={{0,32},{32,64},{64,96},{1,33},{33,65},{65,97},{2,34},{34,66},{66,9... | collective-permute-start | bytes 786440 | tf_op jit(solution)/shard_map/ppermute | solution.py:16
  320.1 15.6 %copy-start = (bf16[4,32,4096]{2,1,0:T(8,128)(2,1)S(1)}, bf16[4,32,4096]{2,1,0:T(8,128)(2,1)}, u32[]{:S(2)}) copy-start(bf16[4,32,4096]{2,1,0:T(8,128)(2,1)} %param.9) | copy-start | bytes 3145732
  335.7 15.5 %copy-start.9 = (bf16[32,4096]{1,0:T(8,128)(2,1)S(1)}, bf16[32,4096]{1,0:T(8,128)(2,1)}, u32[]{:S(2)}) copy-start(bf16[32,4096]{1,0:T(8,128)(2,1)} %copy-done.8) | copy-start | bytes 786436
  349.9 7.6 %collective-permute-start.6 = (bf16[32,4096]{1,0:T(8,128)(2,1)S(1)}, bf16[32,4096]{1,0:T(8,128)(2,1)S(1)}, u32[]{:S(2)}, u32[]{:S(2)}) collective-permute-start(bf16[32,4096]{1,0:T(8,128)(2,1)S(1)} %fusion.42), channel_id=1, source_target_pairs={{32,0},{64,32},{96,64},{33,1},{65,33},{97,65},{34,2},{66,34},{98,6... | collective-permute-start | bytes 786440 | tf_op jit(solution)/shard_map/ppermute | solution.py:16
  372.3 7.1 %collective-permute-start.7 = (bf16[32,4096]{1,0:T(8,128)(2,1)S(1)}, bf16[32,4096]{1,0:T(8,128)(2,1)S(1)}, u32[]{:S(2)}, u32[]{:S(2)}) collective-permute-start(bf16[32,4096]{1,0:T(8,128)(2,1)S(1)} %fusion.50), channel_id=1, source_target_pairs={{32,0},{64,32},{96,64},{33,1},{65,33},{97,65},{34,2},{66,34},{98,6... | collective-permute-start | bytes 786440 | tf_op jit(solution)/shard_map/ppermute | solution.py:16
  394.3 7.1 %collective-permute-start.8 = (bf16[32,4096]{1,0:T(8,128)(2,1)S(1)}, bf16[32,4096]{1,0:T(8,128)(2,1)S(1)}, u32[]{:S(2)}, u32[]{:S(2)}) collective-permute-start(bf16[32,4096]{1,0:T(8,128)(2,1)S(1)} %fusion.52), channel_id=1, source_target_pairs={{32,0},{64,32},{96,64},{33,1},{65,33},{97,65},{34,2},{66,34},{98,6... | collective-permute-start | bytes 786440 | tf_op jit(solution)/shard_map/ppermute | solution.py:16
  416.3 7.1 %collective-permute-start.9 = (bf16[32,4096]{1,0:T(8,128)(2,1)S(1)}, bf16[32,4096]{1,0:T(8,128)(2,1)S(1)}, u32[]{:S(2)}, u32[]{:S(2)}) collective-permute-start(bf16[32,4096]{1,0:T(8,128)(2,1)S(1)} %fusion.54), channel_id=1, source_target_pairs={{32,0},{64,32},{96,64},{33,1},{65,33},{97,65},{34,2},{66,34},{98,6... | collective-permute-start | bytes 786440 | tf_op jit(solution)/shard_map/ppermute | solution.py:16
  438.2 7.1 %collective-permute-start.10 = (bf16[32,4096]{1,0:T(8,128)(2,1)S(1)}, bf16[32,4096]{1,0:T(8,128)(2,1)S(1)}, u32[]{:S(2)}, u32[]{:S(2)}) collective-permute-start(bf16[32,4096]{1,0:T(8,128)(2,1)S(1)} %fusion.56), channel_id=1, source_target_pairs={{32,0},{64,32},{96,64},{33,1},{65,33},{97,65},{34,2},{66,34},{98,6... | collective-permute-start | bytes 786440 | tf_op jit(solution)/shard_map/ppermute | solution.py:16
  460.1 7.1 %collective-permute-start.11 = (bf16[32,4096]{1,0:T(8,128)(2,1)S(1)}, bf16[32,4096]{1,0:T(8,128)(2,1)S(1)}, u32[]{:S(2)}, u32[]{:S(2)}) collective-permute-start(bf16[32,4096]{1,0:T(8,128)(2,1)S(1)} %fusion.58), channel_id=1, source_target_pairs={{32,0},{64,32},{96,64},{33,1},{65,33},{97,65},{34,2},{66,34},{98,6... | collective-permute-start | bytes 786440 | tf_op jit(solution)/shard_map/ppermute | solution.py:16
  534.4 132.5 %reduce-scatter.5.cloned.1.call-start = ((), (), s32[]{:S(2)}) async-start(), calls=%async_computation.3 | async-start | bytes 8912896 | tf_op jit(solution)/shard_map/reduce_scatter | solution.py:273
  578.0 88.9 %copy-start.10 = (bf16[1,2,64,2048]{3,2,1,0:T(8,128)(2,1)S(1)}, bf16[1,2,64,2048]{3,2,1,0:T(8,128)(2,1)}, u32[]{:S(2)}) copy-start(bf16[1,2,64,2048]{3,2,1,0:T(8,128)(2,1)} %param.10) | copy-start | bytes 1572868
  578.0 88.9 %copy-start.11 = (f32[1,2,64,2048]{3,2,1,0:T(8,128)S(1)}, f32[1,2,64,2048]{3,2,1,0:T(8,128)}, u32[]{:S(2)}) copy-start(f32[1,2,64,2048]{3,2,1,0:T(8,128)} %param.13) | copy-start | bytes 3145732
  (6 other events, 50.4 us)
Sparse Core Ops, SparseCore 0:
  10.1 74.0 all-gather.4
  85.9 32.7 all-gather.6
  534.5 43.4 reduce-scatter.2
  581.6 85.1 reduce-scatter.4

commit v4 on v2

--- a/solution.py
+++ b/solution.py
@@ -20,50 +20,43 @@
     return jnp.maximum(magnitude - threshold, 0.0) / jnp.maximum(magnitude, threshold)
 
 
-def pick_half(tile, index, want_odd):
-    rolled = pltpu.roll(tile, 64, 1)
-    keep = (index % 2) == want_odd
-    return jnp.where(keep, tile, rolled)
-
-
-def expand_kernel(table_ref, w_ref, o_ref):
-    j = pl.program_id(0)
-    rows = w_ref.shape[1]
-    lane = lax.broadcasted_iota(jnp.int32, (rows, 128), 1)
-    pairs = o_ref.shape[2] // 128
-    for p in range(pairs):
-        k0 = table_ref[j * 2 * pairs + 2 * p]
-        k1 = table_ref[j * 2 * pairs + 2 * p + 1]
-        s0 = pl.multiple_of((jnp.maximum(k0, 0) // 2) * 128, 128)
-        s1 = pl.multiple_of((jnp.maximum(k1, 0) // 2) * 128, 128)
-        t0 = w_ref[0, :, pl.ds(s0, 128)]
-        t1 = w_ref[0, :, pl.ds(s1, 128)]
+def expand_kernel(table_ref, t_ref, o_ref):
+    p = pl.program_id(0)
+    block = 64
+    blocks = o_ref.shape[0] // block
+    lane = lax.broadcasted_iota(jnp.int32, (block, o_ref.shape[1]), 1)
+    for r in range(blocks):
+        k0 = table_ref[(2 * p) * blocks + r]
+        k1 = table_ref[(2 * p + 1) * blocks + r]
+        s0 = pl.multiple_of(jnp.maximum(k0, 0) * block, block)
+        s1 = pl.multiple_of(jnp.maximum(k1, 0) * block, block)
+        t0 = t_ref[pl.ds(s0, block), :]
+        t1 = t_ref[pl.ds(s1, block), :]
         zero = jnp.zeros_like(t0)
-        low = jnp.where(k0 >= 0, pick_half(t0, k0, 0), zero)
-        high = jnp.where(k1 >= 0, pick_half(t1, k1, 1), zero)
-        o_ref[0, :, p * 128:(p + 1) * 128] = jnp.where(lane < 64, low, high)
+        t0 = jnp.where(k0 >= 0, t0, zero)
+        t1 = jnp.where(k1 >= 0, t1, zero)
+        o_ref[r * block:(r + 1) * block, :] = jnp.where(lane < block, t0, t1)
 
 
 def pack_kernel(table_ref, g_ref, o_ref):
-    j = pl.program_id(0)
-    rows = g_ref.shape[1]
-    lane = lax.broadcasted_iota(jnp.int32, (rows, 128), 1)
-    pairs = o_ref.shape[2] // 128
-    for q in range(pairs):
-        r0 = table_ref[j * 2 * pairs + 2 * q]
-        r1 = table_ref[j * 2 * pairs + 2 * q + 1]
-        s0 = pl.multiple_of((r0 // 2) * 128, 128)
-        s1 = pl.multiple_of((r1 // 2) * 128, 128)
-        t0 = g_ref[0, :, pl.ds(s0, 128)]
-        t1 = g_ref[0, :, pl.ds(s1, 128)]
-        low = pick_half(t0, r0, 0)
-        high = pick_half(t1, r1, 1)
-        o_ref[0, :, q * 128:(q + 1) * 128] = jnp.where(lane < 64, low, high)
-
-
-def expand_dense(section_weights, live_index):
-    column_count, block_size, wide = section_weights.shape
-    live_count = live_index.shape[1]
+    p = pl.program_id(0)
+    block = 64
+    live_count = o_ref.shape[1] // block
+    lane = lax.broadcasted_iota(jnp.int32, (block, o_ref.shape[2]), 1)
+    for k in range(live_count):
+        r0 = table_ref[(2 * p) * live_count + k]
+        r1 = table_ref[(2 * p + 1) * live_count + k]
+        s0 = pl.multiple_of(r0 * block, block)
+        s1 = pl.multiple_of(r1 * block, block)
+        t0 = g_ref[pl.ds(s0, block), :]
+        t1 = g_ref[pl.ds(s1, block), :]
+        o_ref[0, k * block:(k + 1) * block, :] = jnp.where(lane < block, t0, t1)
+
+
+def expand_dense(paired_weights, live_index):
+    pair_count, wide, two_blocks = paired_weights.shape
+    column_count, live_count = live_index.shape
+    block_size = two_blocks // 2
     features = column_count * block_size
     targets = jnp.arange(column_count, dtype=jnp.int32)
     hit = live_index[:, :, None] == targets[None, None, :]
@@ -71,20 +64,19 @@
     inverse = jnp.where(
         jnp.any(hit, axis=1), jnp.sum(jnp.where(hit, k_ids, 0), axis=1), -1
     ).astype(jnp.int32)
-    out = pl.pallas_call(
+    return pl.pallas_call(
         expand_kernel,
-        out_shape=jax.ShapeDtypeStruct((column_count, block_size, features), section_weights.dtype),
+        out_shape=jax.ShapeDtypeStruct((features, features), paired_weights.dtype),
         grid_spec=pltpu.PrefetchScalarGridSpec(
             num_scalar_prefetch=1,
-            grid=(column_count,),
-            in_specs=[pl.BlockSpec((1, block_size, wide), lambda j, tbl: (j, 0, 0))],
-            out_specs=pl.BlockSpec((1, block_size, features), lambda j, tbl: (j, 0, 0)),
+            grid=(pair_count,),
+            in_specs=[pl.BlockSpec((None, wide, two_blocks), lambda p, tbl: (p, 0, 0))],
+            out_specs=pl.BlockSpec((features, two_blocks), lambda p, tbl: (0, p)),
         ),
         cost_estimate=pl.CostEstimate(
-            flops=0, transcendentals=0, bytes_accessed=3 * column_count * block_size * wide * 2
-        ),
-    )(inverse.reshape(-1), section_weights)
-    return out.reshape(features, features)
+            flops=0, transcendentals=0, bytes_accessed=3 * pair_count * wide * two_blocks * 2
+        ),
+    )(inverse.reshape(-1), paired_weights)
 
 
 def pack_dense(dense_grad, live_index):
@@ -92,19 +84,20 @@
     features = dense_grad.shape[0]
     block_size = features // column_count
     wide = live_count * block_size
+    pair_count = column_count // 2
     return pl.pallas_call(
         pack_kernel,
-        out_shape=jax.ShapeDtypeStruct((column_count, block_size, wide), dense_grad.dtype),
+        out_shape=jax.ShapeDtypeStruct((pair_count, wide, 2 * block_size), dense_grad.dtype),
         grid_spec=pltpu.PrefetchScalarGridSpec(
             num_scalar_prefetch=1,
-            grid=(column_count,),
-            in_specs=[pl.BlockSpec((1, block_size, features), lambda j, tbl: (j, 0, 0))],
-            out_specs=pl.BlockSpec((1, block_size, wide), lambda j, tbl: (j, 0, 0)),
+            grid=(pair_count,),
+            in_specs=[pl.BlockSpec((features, 2 * block_size), lambda p, tbl: (0, p))],
+            out_specs=pl.BlockSpec((1, wide, 2 * block_size), lambda p, tbl: (p, 0, 0)),
         ),
         cost_estimate=pl.CostEstimate(
-            flops=0, transcendentals=0, bytes_accessed=3 * column_count * block_size * wide * 2
-        ),
-    )(live_index.reshape(-1).astype(jnp.int32), dense_grad.reshape(column_count, block_size, features))
+            flops=0, transcendentals=0, bytes_accessed=3 * pair_count * wide * 2 * block_size * 2
+        ),
+    )(live_index.reshape(-1).astype(jnp.int32), dense_grad)
 
 
 def spread_kernel(x_ref, o_ref, recv_ref, send_sem, recv_sem):
@@ -165,24 +158,24 @@
     return out[0, : values.shape[0]]
 
 
-def layer_forward(entering, dense_t):
+def layer_forward(entering, dense_w):
     as_float = entering.astype(jnp.float32)
     inverse_rms = lax.rsqrt(jnp.mean(as_float * as_float, axis=-1, keepdims=True) + 1e-05)
     normed = (as_float * inverse_rms).astype(jnp.bfloat16)
-    pre_act = lax.dot_general(
-        normed, dense_t, (((1,), (1,)), ((), ())), preferred_element_type=jnp.float32
-    )
+    pre_act = jnp.dot(normed, dense_w, preferred_element_type=jnp.float32)
     return ((as_float + jax.nn.silu(pre_act)).astype(jnp.bfloat16), normed, pre_act)
 
 
-def layer_backward(arriving, entering, pre_act, dense_t):
+def layer_backward(arriving, entering, pre_act, dense_w):
     as_float = entering.astype(jnp.float32)
     inverse_rms = lax.rsqrt(jnp.mean(as_float * as_float, axis=-1, keepdims=True) + 1e-05)
     sigmoid_z = jax.nn.sigmoid(pre_act)
     grad_pre = (
         arriving.astype(jnp.float32) * (sigmoid_z * (1.0 + pre_act * (1.0 - sigmoid_z)))
     ).astype(jnp.bfloat16)
-    grad_normed = jnp.dot(grad_pre, dense_t, preferred_element_type=jnp.float32)
+    grad_normed = lax.dot_general(
+        grad_pre, dense_w, (((1,), (1,)), ((), ())), preferred_element_type=jnp.float32
+    )
     scaled = as_float * inverse_rms
     leaving = (
         arriving.astype(jnp.float32)
@@ -201,15 +194,16 @@
     own_columns = weights.shape[1]
     block_size = weights.shape[2]
     live_index = live_rows[0]
-    section_weights = lax.all_gather(weights[0], "dp", axis=0, tiled=True)
-    dense_t = expand_dense(section_weights, live_index)
+    own_pair = weights[0].transpose(2, 0, 1).reshape(1, live_count * block_size, own_columns * block_size)
+    paired_weights = lax.all_gather(own_pair, "dp", axis=0, tiled=True)
+    dense_w = expand_dense(paired_weights, live_index)
     tick_count = micro_count + sections - 1
 
     incoming = jnp.zeros((tokens, features), jnp.bfloat16)
     kept_in, kept_normed, kept_pre = [], [], []
     for tick_index in range(tick_count):
         entering = jnp.where(section_index == 0, x_in[min(tick_index, micro_count - 1)], incoming)
-        outgoing, normed, pre_act = layer_forward(entering, dense_t)
+        outgoing, normed, pre_act = layer_forward(entering, dense_w)
         kept_in.append(entering)
         kept_normed.append(normed)
         kept_pre.append(pre_act)
@@ -229,7 +223,7 @@
             incoming_grad,
         )
         leaving, grad_pre = layer_backward(
-            arriving, saved_in[slot_index], saved_pre[slot_index], dense_t
+            arriving, saved_in[slot_index], saved_pre[slot_index], dense_w
         )
         kept_grad.append(grad_pre)
         if tick_index + 1 < tick_count:
@@ -242,15 +236,20 @@
     inverse_tokens = 1.0 / (all_rows * lax.axis_size("dp"))
     dense_grad = (
         lax.dot_general(
+            saved_normed.reshape(all_rows, features),
             saved_grad.reshape(all_rows, features),
-            saved_normed.reshape(all_rows, features),
             (((0,), (0,)), ((), ())),
             preferred_element_type=jnp.float32,
         )
         * inverse_tokens
     ).astype(jnp.bfloat16)
     partial = pack_dense(dense_grad, live_index)
-    gradient = lax.psum_scatter(partial, "dp", scatter_dimension=0, tiled=True).astype(jnp.float32)
+    own_grad = lax.psum_scatter(partial, "dp", scatter_dimension=0, tiled=True)
+    gradient = (
+        own_grad.reshape(live_count * block_size, own_columns, block_size)
+        .transpose(1, 2, 0)
+        .astype(jnp.float32)
+    )
 
     rate = 0.1 / math.sqrt(live_count * block_size)
     moment_new = 0.9 * moment[0] + 0.1 * gradient

time: 666 us -> 636 us (0.955)
  Pallas kernels: 122 us -> 78.1 us
  other arithmetic: 24.3 us -> 32.7 us
    pallas_call x2, Pallas kernels: 110 us -> 66 us  [the longest x1 34.6 us: expand_dense(): pl.pallas_call(expand_kernel, out_shape=jax.ShapeDtypeStruct((features, f...]
    unnamed x17, other arithmetic: 11 us -> 18 us
where the time goes in v4:
time: 636 us; the launch traced here: 625 us
  waiting for transfers between devices  251 us (39%)
  matrix products  210 us (33%)
  Pallas kernels  78.1 us (12%)
  other arithmetic  32.7 us (5%)
  starting transfers between devices  32.1 us (5%)
  between operations  15.3 us (2%)
  local copies, waits for them, and re-layouts  6.9 us (1%)
    reduce_scatter x1, waiting for transfers between devices, local(): own_grad = lax.psum_scatter(partial, 'dp', scatter_dimension=0, tiled=True)  126 us
    dot_general x7, matrix products, layer_forward(): pre_act = jnp.dot(normed, dense_w, preferred_element_type=jnp.float32)  101 us
    dot_general x6, matrix products, layer_backward(): lax.dot_general(grad_pre, dense_w, (((1,), (1,)), ((), ())), preferred_el...  93 us
    all_gather x1, waiting for transfers between devices, local(): paired_weights = lax.all_gather(own_pair, 'dp', axis=0, tiled=True)  75.1 us
    ppermute x12, waiting for transfers between devices, shifted(): lax.ppermute(value, axis, [(source, source + steps) for source in range(l...  49.3 us
    pallas_call x1, Pallas kernels, expand_dense(): pl.pallas_call(expand_kernel, out_shape=jax.ShapeDtypeStruct((features, f...  34.6 us
    ppermute x12, starting transfers between devices, shifted(): lax.ppermute(value, axis, [(source, source + steps) for source in range(l...  32 us
    pallas_call x1, Pallas kernels, pack_dense(): pl.pallas_call(pack_kernel, out_shape=jax.ShapeDtypeStruct((pair_count, w...  31.4 us
  transfers between devices with their start and end apart: 14, of which 14 were waited for; matrix products, arithmetic and copies ran while one was open for 2% of the time, Pallas kernels for 0%

profile of v4, /device:TPU:1, one launch (start us, length us, event | category | flops | bytes accessed | tf_op | source)
XLA Modules:
  0.0 625.4 jit_solution(5308581899852892464)
XLA Ops:
  12.0 75.1 %all-gather.2.cloned.1.call-done.t_ref = bf16[32,2048,128]{2,1,0:T(8,128)(2,1)} async-done(((bf16[1,2048,128]{2,1,0:T(8,128)(2,1)}), bf16[32,2048,128]{2,1,0:T(8,128)(2,1)}) %all-gather.2.cloned.1.call-update) | async-done | bytes 16777232 | tf_op jit(solution)/shard_map/all_gather | solution.py:198
  87.1 34.6 %shard_map.85 = bf16[4096,4096]{1,0:T(8,128)(2,1)} custom-call(s32[4096]{0:T(1024)} %select_n.123.table_ref, bf16[32,2048,128]{2,1,0:T(8,128)(2,1)} %all-gather.2.cloned.1.call-done.t_ref), custom_call_target="tpu_custom_call" | custom-call | bytes 50331648 | tf_op jit(solution)/shard_map/pallas_call | solution.py:67
  121.7 14.4 %bitcast_dynamic-update-slice_fusion.5 = (f32[7,32,4096]{2,1,0:T(8,128)}, f32[32,4096]{1,0:T(8,128)S(1)}) fusion(bf16[4096,4096]{1,0:T(8,128)(2,1)} %shard_map.85, f32[32]{0:T(128)S(1)} %add_rsqrt_fusion.12, bf16[4,32,4096]{2,1,0:T(8,128)(2,1)S(1)} %copy-done.1, pred[]{:T(512)S(6)} %eq.18), kind=kOutput, calls=%fused_computation.191 | convolution fusion | flops 1074266112 | bytes 34865664 | tf_op jit(solution)/shard_map/dot_general | solution.py:165
  140.3 4.6 collective-permute-done
  145.2 14.4 %bitcast_dynamic-update-slice_fusion.4 = (f32[7,32,4096]{2,1,0:T(8,128)}, f32[32,4096]{1,0:T(8,128)S(1)}) fusion(f32[7,32,4096]{2,1,0:T(8,128)} %get-tuple-element.51, bf16[4096,4096]{1,0:T(8,128)(2,1)} %shard_map.85, bf16[32,4096]{1,0:T(8,128)(2,1)S(1)} %get-tuple-element.46, f32[32]{0:T(128)S(1)} %add_rsqrt_fusion.11), kind=kOutput, calls=%fused_computation.190 | convolution fusion | flops 1074135040 | bytes 34865280 | tf_op jit(solution)/shard_map/dot_general | solution.py:165
  168.6 14.4 %bitcast_dynamic-update-slice_fusion.3 = (f32[7,32,4096]{2,1,0:T(8,128)}, f32[32,4096]{1,0:T(8,128)S(1)}) fusion(f32[7,32,4096]{2,1,0:T(8,128)} %get-tuple-element.53, bf16[4096,4096]{1,0:T(8,128)(2,1)} %shard_map.85, bf16[32,4096]{1,0:T(8,128)(2,1)S(1)} %get-tuple-element.44, f32[32]{0:T(128)S(1)} %add_rsqrt_fusion.10), kind=kOutput, calls=%fused_computation.189 | convolution fusion | flops 1074135040 | bytes 34865280 | tf_op jit(solution)/shard_map/dot_general | solution.py:165
  191.1 14.4 %bitcast_dynamic-update-slice_fusion.2 = (f32[7,32,4096]{2,1,0:T(8,128)}, f32[32,4096]{1,0:T(8,128)S(1)}) fusion(f32[7,32,4096]{2,1,0:T(8,128)} %get-tuple-element.55, bf16[4096,4096]{1,0:T(8,128)(2,1)} %shard_map.85, bf16[32,4096]{1,0:T(8,128)(2,1)S(1)} %get-tuple-element.42, f32[32]{0:T(128)S(1)} %add_rsqrt_fusion.9), kind=kOutput, calls=%fused_computation.188 | convolution fusion | flops 1074135040 | bytes 34865280 | tf_op jit(solution)/shard_map/dot_general | solution.py:165
  213.2 14.4 %bitcast_dynamic-update-slice_fusion.1 = (f32[7,32,4096]{2,1,0:T(8,128)}, f32[32,4096]{1,0:T(8,128)S(1)}) fusion(f32[7,32,4096]{2,1,0:T(8,128)} %get-tuple-element.57, bf16[4096,4096]{1,0:T(8,128)(2,1)} %shard_map.85, bf16[32,4096]{1,0:T(8,128)(2,1)S(1)} %get-tuple-element.40, f32[32]{0:T(128)S(1)} %add_rsqrt_fusion.8), kind=kOutput, calls=%fused_computation.187 | convolution fusion | flops 1074135040 | bytes 34865280 | tf_op jit(solution)/shard_map/dot_general | solution.py:165
  236.1 14.4 %bitcast_dynamic-update-slice_fusion = (f32[7,32,4096]{2,1,0:T(8,128)}, f32[32,4096]{1,0:T(8,128)S(1)}) fusion(f32[7,32,4096]{2,1,0:T(8,128)} %get-tuple-element.59, bf16[4096,4096]{1,0:T(8,128)(2,1)} %shard_map.85, bf16[32,4096]{1,0:T(8,128)(2,1)S(1)} %get-tuple-element.38, f32[32]{0:T(128)S(1)} %add_rsqrt_fusion.7), kind=kOutput, calls=%fused_computation.186 | convolution fusion | flops 1074135040 | bytes 34865280 | tf_op jit(solution)/shard_map/dot_general | solution.py:165
  259.0 14.4 %fusion.1 = f32[7,32,4096]{2,1,0:T(8,128)} fusion(f32[7,32,4096]{2,1,0:T(8,128)} %get-tuple-element.61, bf16[4096,4096]{1,0:T(8,128)(2,1)} %shard_map.85, bf16[32,4096]{1,0:T(8,128)(2,1)S(1)} %get-tuple-element.36, f32[32]{0:T(128)S(1)} %add_rsqrt_fusion.6), kind=kOutput, calls=%fused_computation.3 | convolution fusion | flops 1074135040 | bytes 34340992 | tf_op jit(solution)/shard_map/dot_general | solution.py:165
  273.4 15.7 %fusion.65 = (f32[32]{0:T(128)S(1)}, f32[32]{0:T(128)S(1)}, f32[32]{0:T(128)S(1)}, f32[32]{0:T(128)S(1)}, f32[32]{0:T(128)S(1)}, /*index=5*/f32[32]{0:T(128)S(1)}, f32[32,4096]{1,0:T(8,128)S(1)}) fusion(bf16[7,32,4096]{2,1,0:T(8,128)(2,1)S(1)} %get-tuple-element.35, s32[]{:T(128)S(6)} %dynamic_slice.95, f32[32]{0:T(128)S(1)} %add_rsqrt_fusion.5, ...), kind=kOutput, calls=%fused_computation.118 | convolution fusion | flops 1077673984 | bytes 36443392 | tf_op jit(solution)/shard_map/dot_general | solution.py:176
  298.9 15.5 %fusion.35 = (f32[32]{0:T(128)S(1)}, f32[32,4096]{1,0:T(8,128)S(1)}) fusion(f32[32]{0:T(128)S(1)} %add_rsqrt_fusion.4, bf16[7,32,4096]{2,1,0:T(8,128)(2,1)S(1)} %get-tuple-element.35, s32[]{:T(128)S(6)} %dynamic_slice.83, bf16[32,4096]{1,0:T(8,128)(2,1)S(1)} %get-tuple-element.34, bf16[4096,4096]{1,0:T(8,128)(2,1)} %shard_map.85), kind=kOutput, calls=%fused_computation.88 | convolution fusion | flops 1074266112 | bytes 34603268 | tf_op jit(solution)/shard_map/dot_general | solution.py:176
  323.7 15.5 %fusion.32 = (f32[32]{0:T(128)S(1)}, f32[32,4096]{1,0:T(8,128)S(1)}) fusion(f32[32]{0:T(128)S(1)} %add_rsqrt_fusion.3, bf16[7,32,4096]{2,1,0:T(8,128)(2,1)S(1)} %get-tuple-element.35, s32[]{:T(128)S(6)} %dynamic_slice.86, bf16[32,4096]{1,0:T(8,128)(2,1)S(1)} %get-tuple-element.32, bf16[4096,4096]{1,0:T(8,128)(2,1)} %shard_map.85), kind=kOutput, calls=%fused_computation.85 | convolution fusion | flops 1074266112 | bytes 34603268 | tf_op jit(solution)/shard_map/dot_general | solution.py:176
  341.5 5.0 collective-permute-done.8
  348.5 15.5 %fusion.29 = (f32[32]{0:T(128)S(1)}, f32[32,4096]{1,0:T(8,128)S(1)}) fusion(f32[32]{0:T(128)S(1)} %add_rsqrt_fusion.2, bf16[7,32,4096]{2,1,0:T(8,128)(2,1)S(1)} %get-tuple-element.35, s32[]{:T(128)S(6)} %dynamic_slice.89, bf16[32,4096]{1,0:T(8,128)(2,1)S(1)} %get-tuple-element.30, bf16[4096,4096]{1,0:T(8,128)(2,1)} %shard_map.85), kind=kOutput, calls=%fused_computation.82 | convolution fusion | flops 1074266112 | bytes 34603268 | tf_op jit(solution)/shard_map/dot_general | solution.py:176
  366.3 5.0 collective-permute-done.9
  373.3 15.5 %fusion.26 = (f32[32]{0:T(128)S(1)}, f32[32,4096]{1,0:T(8,128)S(1)}) fusion(f32[32]{0:T(128)S(1)} %add_rsqrt_fusion.1, bf16[7,32,4096]{2,1,0:T(8,128)(2,1)S(1)} %get-tuple-element.35, s32[]{:T(128)S(6)} %dynamic_slice.92, bf16[32,4096]{1,0:T(8,128)(2,1)S(1)} %get-tuple-element.28, bf16[4096,4096]{1,0:T(8,128)(2,1)} %shard_map.85), kind=kOutput, calls=%fused_computation.79 | convolution fusion | flops 1074266112 | bytes 34603268 | tf_op jit(solution)/shard_map/dot_general | solution.py:176
  391.3 4.8 collective-permute-done.10
  398.1 15.5 %fusion.23 = (f32[32]{0:T(128)S(1)}, f32[32,4096]{1,0:T(8,128)S(1)}) fusion(f32[32]{0:T(128)S(1)} %add_rsqrt_fusion, bf16[7,32,4096]{2,1,0:T(8,128)(2,1)S(1)} %get-tuple-element.35, s32[]{:T(128)S(6)} %dynamic_slice.95, bf16[32,4096]{1,0:T(8,128)(2,1)S(1)} %get-tuple-element.26, bf16[4096,4096]{1,0:T(8,128)(2,1)} %shard_map.85), kind=kOutput, calls=%fused_computation.76 | convolution fusion | flops 1074266112 | bytes 34603268 | tf_op jit(solution)/shard_map/dot_general | solution.py:176
  415.9 5.0 collective-permute-done.11
  422.8 15.9 %fusion.g_ref = bf16[4096,4096]{1,0:T(8,128)(2,1)} fusion(bf16[7,32,4096]{2,1,0:T(8,128)(2,1)} %bitcast_dynamic-update-slice_fusion.6, s32[]{:T(128)S(6)} %select_n.141, bf16[7,32,4096]{2,1,0:T(8,128)(2,1)} %bitcast_dynamic-update-slice_fusion.18, s32[]{:T(128)S(6)} %select_n.130), kind=kOutput, calls=%fused_computation.1 | convolution fusion | flops 4328521728 | bytes 35651592 | tf_op jit(solution)/shard_map/dot_general | solution.py:238
  438.7 31.4 %shard_map.86 = bf16[32,2048,128]{2,1,0:T(8,128)(2,1)} custom-call(s32[2048]{0:T(1024)} %reshape_squeeze.3.table_ref, bf16[4096,4096]{1,0:T(8,128)(2,1)} %fusion.g_ref), custom_call_target="tpu_custom_call" | custom-call | bytes 50331648 | tf_op jit(solution)/shard_map/pallas_call | solution.py:88
  470.3 126.3 %reduce-scatter.2.cloned.1.call-done = bf16[1,2048,128]{2,1,0:T(8,128)(2,1)} async-done(((bf16[32,2048,128]{2,1,0:T(8,128)(2,1)}), bf16[1,2048,128]{2,1,0:T(8,128)(2,1)}) %reduce-scatter.2.cloned.1.call-update) | async-done | bytes 524304 | tf_op jit(solution)/shard_map/reduce_scatter | solution.py:247
  602.9 12.1 %shard_map.87 = f32[8,128]{1,0:T(8,128)} custom-call(f32[8,128]{1,0:T(8,128)} %scatter.4.x_ref), custom_call_target="tpu_custom_call" | custom-call | tf_op jit(solution)/shard_map/pallas_call | solution.py:146
  (119 shorter events, 96.5 us)
Async XLA Ops:
  7.2 4.6 copy-start.1
  7.2 79.9 %all-gather.2.cloned.1.call-start = ((), (), s32[]{:S(2)}) async-start(), calls=%async_computation.1 | async-start | bytes 17301504 | tf_op jit(solution)/shard_map/all_gather | solution.py:198
  9.4 587.3 %reduce-scatter.2.cloned.1.call-start = ((), (), s32[]{:S(2)}) async-start(), calls=%async_computation.2 | async-start | bytes 17301504 | tf_op jit(solution)/shard_map/reduce_scatter | solution.py:247
  136.1 8.8 %copy-start.2 = (bf16[4,32,4096]{2,1,0:T(8,128)(2,1)S(1)}, bf16[4,32,4096]{2,1,0:T(8,128)(2,1)}, u32[]{:S(2)}) copy-start(bf16[4,32,4096]{2,1,0:T(8,128)(2,1)} %param.8) | copy-start | bytes 3145732
  136.2 8.7 %collective-permute-start = (bf16[32,4096]{1,0:T(8,128)(2,1)S(1)}, bf16[32,4096]{1,0:T(8,128)(2,1)S(1)}, u32[]{:S(2)}, u32[]{:S(2)}) collective-permute-start(bf16[32,4096]{1,0:T(8,128)(2,1)S(1)} %fusion.43), channel_id=1, source_target_pairs={{0,32},{32,64},{64,96},{1,33},{33,65},{65,97},{2,34},{34,66},{66,9... | collective-permute-start | bytes 786440 | tf_op jit(solution)/shard_map/ppermute | solution.py:16
  159.7 8.6 %collective-permute-start.1 = (bf16[32,4096]{1,0:T(8,128)(2,1)S(1)}, bf16[32,4096]{1,0:T(8,128)(2,1)S(1)}, u32[]{:S(2)}, u32[]{:S(2)}) collective-permute-start(bf16[32,4096]{1,0:T(8,128)(2,1)S(1)} %fusion.68), channel_id=1, source_target_pairs={{0,32},{32,64},{64,96},{1,33},{33,65},{65,97},{2,34},{34,66},{66,9... | collective-permute-start | bytes 786440 | tf_op jit(solution)/shard_map/ppermute | solution.py:16
  183.1 7.7 %collective-permute-start.2 = (bf16[32,4096]{1,0:T(8,128)(2,1)S(1)}, bf16[32,4096]{1,0:T(8,128)(2,1)S(1)}, u32[]{:S(2)}, u32[]{:S(2)}) collective-permute-start(bf16[32,4096]{1,0:T(8,128)(2,1)S(1)} %fusion.71), channel_id=1, source_target_pairs={{0,32},{32,64},{64,96},{1,33},{33,65},{65,97},{2,34},{34,66},{66,9... | collective-permute-start | bytes 786440 | tf_op jit(solution)/shard_map/ppermute | solution.py:16
  205.6 7.4 %collective-permute-start.3 = (bf16[32,4096]{1,0:T(8,128)(2,1)S(1)}, bf16[32,4096]{1,0:T(8,128)(2,1)S(1)}, u32[]{:S(2)}, u32[]{:S(2)}) collective-permute-start(bf16[32,4096]{1,0:T(8,128)(2,1)S(1)} %fusion.74), channel_id=1, source_target_pairs={{0,32},{32,64},{64,96},{1,33},{33,65},{65,97},{2,34},{34,66},{66,9... | collective-permute-start | bytes 786440 | tf_op jit(solution)/shard_map/ppermute | solution.py:16
  213.2 18.4 %copy-start.4 = (s32[1,64,32]{1,2,0:T(8,128)S(1)}, s32[1,64,32]{1,2,0:T(8,128)}, u32[]{:S(2)}) copy-start(s32[1,64,32]{1,2,0:T(8,128)} %param.11) | copy-start | bytes 24580
  227.8 7.1 %collective-permute-start.4 = (bf16[32,4096]{1,0:T(8,128)(2,1)S(1)}, bf16[32,4096]{1,0:T(8,128)(2,1)S(1)}, u32[]{:S(2)}, u32[]{:S(2)}) collective-permute-start(bf16[32,4096]{1,0:T(8,128)(2,1)S(1)} %fusion.77), channel_id=1, source_target_pairs={{0,32},{32,64},{64,96},{1,33},{33,65},{65,97},{2,34},{34,66},{66,9... | collective-permute-start | bytes 786440 | tf_op jit(solution)/shard_map/ppermute | solution.py:16
  250.6 7.1 %collective-permute-start.5 = (bf16[32,4096]{1,0:T(8,128)(2,1)S(1)}, bf16[32,4096]{1,0:T(8,128)(2,1)S(1)}, u32[]{:S(2)}, u32[]{:S(2)}) collective-permute-start(bf16[32,4096]{1,0:T(8,128)(2,1)S(1)} %fusion.80), channel_id=1, source_target_pairs={{0,32},{32,64},{64,96},{1,33},{33,65},{65,97},{2,34},{34,66},{66,9... | collective-permute-start | bytes 786440 | tf_op jit(solution)/shard_map/ppermute | solution.py:16
  259.0 14.4 %copy-start = (bf16[4,32,4096]{2,1,0:T(8,128)(2,1)S(1)}, bf16[4,32,4096]{2,1,0:T(8,128)(2,1)}, u32[]{:S(2)}) copy-start(bf16[4,32,4096]{2,1,0:T(8,128)(2,1)} %param.9) | copy-start | bytes 3145732
  289.4 7.6 %collective-permute-start.6 = (bf16[32,4096]{1,0:T(8,128)(2,1)S(1)}, bf16[32,4096]{1,0:T(8,128)(2,1)S(1)}, u32[]{:S(2)}, u32[]{:S(2)}) collective-permute-start(bf16[32,4096]{1,0:T(8,128)(2,1)S(1)} %fusion.48), channel_id=1, source_target_pairs={{32,0},{64,32},{96,64},{33,1},{65,33},{97,65},{34,2},{66,34},{98,6... | collective-permute-start | bytes 786440 | tf_op jit(solution)/shard_map/ppermute | solution.py:16
  314.6 7.1 %collective-permute-start.7 = (bf16[32,4096]{1,0:T(8,128)(2,1)S(1)}, bf16[32,4096]{1,0:T(8,128)(2,1)S(1)}, u32[]{:S(2)}, u32[]{:S(2)}) collective-permute-start(bf16[32,4096]{1,0:T(8,128)(2,1)S(1)} %fusion.51), channel_id=1, source_target_pairs={{32,0},{64,32},{96,64},{33,1},{65,33},{97,65},{34,2},{66,34},{98,6... | collective-permute-start | bytes 786440 | tf_op jit(solution)/shard_map/ppermute | solution.py:16
  339.4 7.1 %collective-permute-start.8 = (bf16[32,4096]{1,0:T(8,128)(2,1)S(1)}, bf16[32,4096]{1,0:T(8,128)(2,1)S(1)}, u32[]{:S(2)}, u32[]{:S(2)}) collective-permute-start(bf16[32,4096]{1,0:T(8,128)(2,1)S(1)} %fusion.53), channel_id=1, source_target_pairs={{32,0},{64,32},{96,64},{33,1},{65,33},{97,65},{34,2},{66,34},{98,6... | collective-permute-start | bytes 786440 | tf_op jit(solution)/shard_map/ppermute | solution.py:16
  364.2 7.1 %collective-permute-start.9 = (bf16[32,4096]{1,0:T(8,128)(2,1)S(1)}, bf16[32,4096]{1,0:T(8,128)(2,1)S(1)}, u32[]{:S(2)}, u32[]{:S(2)}) collective-permute-start(bf16[32,4096]{1,0:T(8,128)(2,1)S(1)} %fusion.55), channel_id=1, source_target_pairs={{32,0},{64,32},{96,64},{33,1},{65,33},{97,65},{34,2},{66,34},{98,6... | collective-permute-start | bytes 786440 | tf_op jit(solution)/shard_map/ppermute | solution.py:16
  389.0 7.1 %collective-permute-start.10 = (bf16[32,4096]{1,0:T(8,128)(2,1)S(1)}, bf16[32,4096]{1,0:T(8,128)(2,1)S(1)}, u32[]{:S(2)}, u32[]{:S(2)}) collective-permute-start(bf16[32,4096]{1,0:T(8,128)(2,1)S(1)} %fusion.57), channel_id=1, source_target_pairs={{32,0},{64,32},{96,64},{33,1},{65,33},{97,65},{34,2},{66,34},{98,6... | collective-permute-start | bytes 786440 | tf_op jit(solution)/shard_map/ppermute | solution.py:16
  413.7 7.1 %collective-permute-start.11 = (bf16[32,4096]{1,0:T(8,128)(2,1)S(1)}, bf16[32,4096]{1,0:T(8,128)(2,1)S(1)}, u32[]{:S(2)}, u32[]{:S(2)}) collective-permute-start(bf16[32,4096]{1,0:T(8,128)(2,1)S(1)} %fusion.59), channel_id=1, source_target_pairs={{32,0},{64,32},{96,64},{33,1},{65,33},{97,65},{34,2},{66,34},{98,6... | collective-permute-start | bytes 786440 | tf_op jit(solution)/shard_map/ppermute | solution.py:16
  470.2 127.7 %copy-start.3 = (bf16[1,2,64,2048]{3,2,1,0:T(8,128)(2,1)S(1)}, bf16[1,2,64,2048]{3,2,1,0:T(8,128)(2,1)}, u32[]{:S(2)}) copy-start(bf16[1,2,64,2048]{3,2,1,0:T(8,128)(2,1)} %param.10) | copy-start | bytes 1572868
Sparse Core Ops, SparseCore 0:
  10.8 76.2 all-gather.1
  470.3 126.3 reduce-scatter.1

commit v5 on v4

--- a/solution.py
+++ b/solution.py
@@ -188,7 +188,12 @@
 def local(x_in, cotangent, weights, live_rows, moment, second):
     sections = lax.axis_size("pipe")
     section_index = lax.axis_index("pipe")
-    micro_count, tokens, features = x_in.shape
+    group = 2
+    micro_total, micro_tokens, features = x_in.shape
+    micro_count = micro_total // group
+    tokens = micro_tokens * group
+    x_in = x_in.reshape(micro_count, tokens, features)
+    cotangent = cotangent.reshape(micro_count, tokens, features)
     column_count = live_rows.shape[1]
     live_count = live_rows.shape[2]
     own_columns = weights.shape[1]

time: 636 us -> 578 us (0.909)
  matrix products: 210 us -> 147 us
  starting transfers between devices: 32.1 us -> 21.6 us
  waiting for transfers between devices: 251 us -> 261 us
    dot_general x7 -> x5, matrix products: 101 us -> 68.4 us  [layer_forward(): pre_act = jnp.dot(normed, dense_w, preferred_element_type=jnp.float32)]
    dot_general x6 -> x4, matrix products: 93 us -> 62.9 us  [layer_backward(): lax.dot_general(grad_pre, dense_w, (((1,), (1,)), ((), ())), preferred_el...]
    ppermute x12 -> x8, waiting for transfers between devices: 49.3 us -> 68.4 us  [shifted(): lax.ppermute(value, axis, [(source, source + steps) for source in range(l...]
    ppermute x12 -> x8, starting transfers between devices: 32 us -> 21.6 us  [shifted(): lax.ppermute(value, axis, [(source, source + steps) for source in range(l...]
    unnamed x17 -> x8, other arithmetic: 18 us -> 13.3 us
  transfers between devices with their start and end apart: 14 -> 10, of which waited for: 14 -> 10; matrix products, arithmetic and copies ran while one was open for 2% -> 2% of each run, Pallas kernels for 0% -> 0%
where the time goes in v5:
time: 578 us; the launch traced here: 567 us
  waiting for transfers between devices  261 us (45%)
  matrix products  147 us (25%)
  Pallas kernels  78.1 us (14%)
  other arithmetic  32.2 us (6%)
  starting transfers between devices  21.6 us (4%)
  between operations  15.4 us (3%)
  local copies, waits for them, and re-layouts  11.2 us (2%)
    reduce_scatter x1, waiting for transfers between devices, local(): own_grad = lax.psum_scatter(partial, 'dp', scatter_dimension=0, tiled=True)  120 us
    all_gather x1, waiting for transfers between devices, local(): paired_weights = lax.all_gather(own_pair, 'dp', axis=0, tiled=True)  72.5 us
    dot_general x5, matrix products, layer_forward(): pre_act = jnp.dot(normed, dense_w, preferred_element_type=jnp.float32)  68.4 us
    ppermute x8, waiting for transfers between devices, shifted(): lax.ppermute(value, axis, [(source, source + steps) for source in range(l...  68.4 us
    dot_general x4, matrix products, layer_backward(): lax.dot_general(grad_pre, dense_w, (((1,), (1,)), ((), ())), preferred_el...  62.9 us
    pallas_call x1, Pallas kernels, expand_dense(): pl.pallas_call(expand_kernel, out_shape=jax.ShapeDtypeStruct((features, f...  34.6 us
    pallas_call x1, Pallas kernels, pack_dense(): pl.pallas_call(pack_kernel, out_shape=jax.ShapeDtypeStruct((pair_count, w...  31.4 us
    ppermute x8, starting transfers between devices, shifted(): lax.ppermute(value, axis, [(source, source + steps) for source in range(l...  21.6 us
  transfers between devices with their start and end apart: 10, of which 10 were waited for; matrix products, arithmetic and copies ran while one was open for 2% of the time, Pallas kernels for 0%

profile of v5, /device:TPU:1, one launch (start us, length us, event | category | flops | bytes accessed | tf_op | source)
XLA Modules:
  0.0 567.1 jit_solution(12630987615589375145)
XLA Ops:
  14.6 72.5 %all-gather.2.cloned.1.call-done.t_ref = bf16[32,2048,128]{2,1,0:T(8,128)(2,1)} async-done(((bf16[1,2048,128]{2,1,0:T(8,128)(2,1)}), bf16[32,2048,128]{2,1,0:T(8,128)(2,1)}) %all-gather.2.cloned.1.call-update) | async-done | bytes 16777232 | tf_op jit(solution)/shard_map/all_gather | solution.py:203
  87.1 34.6 %shard_map.85 = bf16[4096,4096]{1,0:T(8,128)(2,1)} custom-call(s32[4096]{0:T(1024)} %select_n.124.table_ref, bf16[32,2048,128]{2,1,0:T(8,128)(2,1)} %all-gather.2.cloned.1.call-done.t_ref), custom_call_target="tpu_custom_call" | custom-call | bytes 50331648 | tf_op jit(solution)/shard_map/pallas_call | solution.py:67
  121.7 13.6 %bitcast_dynamic-update-slice_fusion.3 = (f32[5,64,4096]{2,1,0:T(8,128)S(1)}, f32[64,4096]{1,0:T(8,128)S(1)}) fusion(bf16[64,4096]{1,0:T(8,128)(2,1)S(1)} %fusion.77, bf16[4096,4096]{1,0:T(8,128)(2,1)} %shard_map.85), kind=kOutput, calls=%fused_computation.116 | convolution fusion | flops 2147483648 | bytes 36175872 | tf_op jit(solution)/shard_map/dot_general | solution.py:165
  141.0 8.8 %collective-permute-done = bf16[64,4096]{1,0:T(8,128)(2,1)S(1)} collective-permute-done((bf16[64,4096]{1,0:T(8,128)(2,1)S(1)}, bf16[64,4096]{1,0:T(8,128)(2,1)S(1)}, u32[]{:S(2)}, u32[]{:S(2)}) %collective-permute-start) | collective-permute-done | bytes 524320 | tf_op jit(solution)/shard_map/ppermute | solution.py:16
  150.1 13.7 %bitcast_dynamic-update-slice_fusion.2 = (f32[5,64,4096]{2,1,0:T(8,128)S(1)}, f32[64,4096]{1,0:T(8,128)S(1)}) fusion(f32[5,64,4096]{2,1,0:T(8,128)S(1)} %get-tuple-element.47, bf16[4096,4096]{1,0:T(8,128)(2,1)} %shard_map.85, bf16[64,4096]{1,0:T(8,128)(2,1)S(1)} %get-tuple-element.30, f32[64]{0:T(128)S(1)} %add_rsqrt_fusion.8), kind=kOutput, calls=%fused_computation.115 | convolution fusion | flops 2148270080 | bytes 36176384 | tf_op jit(solution)/shard_map/dot_general | solution.py:165
  169.2 9.2 %collective-permute-done.1 = bf16[64,4096]{1,0:T(8,128)(2,1)S(1)} collective-permute-done((bf16[64,4096]{1,0:T(8,128)(2,1)S(1)}, bf16[64,4096]{1,0:T(8,128)(2,1)S(1)}, u32[]{:S(2)}, u32[]{:S(2)}) %collective-permute-start.1) | collective-permute-done | bytes 524320 | tf_op jit(solution)/shard_map/ppermute | solution.py:16
  178.7 13.7 %bitcast_dynamic-update-slice_fusion.1 = (f32[5,64,4096]{2,1,0:T(8,128)S(1)}, f32[64,4096]{1,0:T(8,128)S(1)}) fusion(f32[5,64,4096]{2,1,0:T(8,128)S(1)} %get-tuple-element.49, bf16[4096,4096]{1,0:T(8,128)(2,1)} %shard_map.85, bf16[64,4096]{1,0:T(8,128)(2,1)S(1)} %get-tuple-element.28, f32[64]{0:T(128)S(1)} %add_rsqrt_fusion.7), kind=kOutput, calls=%fused_computation.114 | convolution fusion | flops 2148270080 | bytes 36176384 | tf_op jit(solution)/shard_map/dot_general | solution.py:165
  192.7 4.6 collective-permute-start.2
  198.3 7.7 %collective-permute-done.2 = bf16[64,4096]{1,0:T(8,128)(2,1)S(1)} collective-permute-done((bf16[64,4096]{1,0:T(8,128)(2,1)S(1)}, bf16[64,4096]{1,0:T(8,128)(2,1)S(1)}, u32[]{:S(2)}, u32[]{:S(2)}) %collective-permute-start.2) | collective-permute-done | bytes 524320 | tf_op jit(solution)/shard_map/ppermute | solution.py:16
  206.3 13.7 %bitcast_dynamic-update-slice_fusion = (f32[5,64,4096]{2,1,0:T(8,128)S(1)}, f32[64,4096]{1,0:T(8,128)S(1)}) fusion(f32[5,64,4096]{2,1,0:T(8,128)S(1)} %get-tuple-element.51, bf16[4096,4096]{1,0:T(8,128)(2,1)} %shard_map.85, bf16[64,4096]{1,0:T(8,128)(2,1)S(1)} %get-tuple-element.26, f32[64]{0:T(128)S(1)} %add_rsqrt_fusion.6), kind=kOutput, calls=%fused_computation.113 | convolution fusion | flops 2148270080 | bytes 36176384 | tf_op jit(solution)/shard_map/dot_general | solution.py:165
  225.5 7.3 %collective-permute-done.3 = bf16[64,4096]{1,0:T(8,128)(2,1)S(1)} collective-permute-done((bf16[64,4096]{1,0:T(8,128)(2,1)S(1)}, bf16[64,4096]{1,0:T(8,128)(2,1)S(1)}, u32[]{:S(2)}, u32[]{:S(2)}) %collective-permute-start.3) | collective-permute-done | bytes 524320 | tf_op jit(solution)/shard_map/ppermute | solution.py:16
  233.1 13.8 %fusion.1 = f32[5,64,4096]{2,1,0:T(8,128)S(1)} fusion(f32[5,64,4096]{2,1,0:T(8,128)S(1)} %get-tuple-element.53, bf16[4096,4096]{1,0:T(8,128)(2,1)} %shard_map.85, bf16[64,4096]{1,0:T(8,128)(2,1)S(1)} %get-tuple-element.24, f32[64]{0:T(128)S(1)} %add_rsqrt_fusion.5), kind=kOutput, calls=%fused_computation.3 | convolution fusion | flops 2148270080 | bytes 35127808 | tf_op jit(solution)/shard_map/dot_general | solution.py:165
  250.0 15.9 %fusion.35 = (f32[64]{0:T(128)S(1)}, f32[64]{0:T(128)S(1)}, f32[64]{0:T(128)S(1)}, f32[64]{0:T(128)S(1)}, f32[64,4096]{1,0:T(8,128)S(1)}) fusion(bf16[5,64,4096]{2,1,0:T(8,128)(2,1)S(1)} %get-tuple-element.38, s32[]{:T(128)S(6)} %dynamic_slice.69, f32[64]{0:T(128)S(1)} %add_rsqrt_fusion.4, s32[]{:T(128)S(6)} %dynamic_slice.60, s32[]{:T(128)S(6)} %dynamic_slice.66, ...), kind=kOutput, calls=%fused_computation.63 | convolution fusion | flops 2150891520 | bytes 37225744 | tf_op jit(solution)/shard_map/dot_general | solution.py:176
  270.5 9.4 %collective-permute-done.4 = bf16[64,4096]{1,0:T(8,128)(2,1)S(1)} collective-permute-done((bf16[64,4096]{1,0:T(8,128)(2,1)S(1)}, bf16[64,4096]{1,0:T(8,128)(2,1)S(1)}, u32[]{:S(2)}, u32[]{:S(2)}) %collective-permute-start.4) | collective-permute-done | bytes 524320 | tf_op jit(solution)/shard_map/ppermute | solution.py:16
  283.1 15.7 %fusion.16 = (f32[64]{0:T(128)S(1)}, f32[64,4096]{1,0:T(8,128)S(1)}) fusion(f32[64]{0:T(128)S(1)} %add_rsqrt_fusion.3, bf16[5,64,4096]{2,1,0:T(8,128)(2,1)S(1)} %get-tuple-element.38, s32[]{:T(128)S(6)} %dynamic_slice.63, bf16[64,4096]{1,0:T(8,128)(2,1)S(1)} %get-tuple-element.57, bf16[4096,4096]{1,0:T(8,128)(2,1)} %shard_map.85), kind=kOutput, calls=%fused_computation.44 | convolution fusion | flops 2148532224 | bytes 35652100 | tf_op jit(solution)/shard_map/dot_general | solution.py:176
  300.5 9.5 %collective-permute-done.5 = bf16[64,4096]{1,0:T(8,128)(2,1)S(1)} collective-permute-done((bf16[64,4096]{1,0:T(8,128)(2,1)S(1)}, bf16[64,4096]{1,0:T(8,128)(2,1)S(1)}, u32[]{:S(2)}, u32[]{:S(2)}) %collective-permute-start.5) | collective-permute-done | bytes 524320 | tf_op jit(solution)/shard_map/ppermute | solution.py:16
  312.4 15.7 %fusion.13 = (f32[64]{0:T(128)S(1)}, f32[64,4096]{1,0:T(8,128)S(1)}) fusion(f32[64]{0:T(128)S(1)} %add_rsqrt_fusion.2, bf16[5,64,4096]{2,1,0:T(8,128)(2,1)S(1)} %get-tuple-element.38, s32[]{:T(128)S(6)} %dynamic_slice.66, bf16[64,4096]{1,0:T(8,128)(2,1)S(1)} %get-tuple-element.61, bf16[4096,4096]{1,0:T(8,128)(2,1)} %shard_map.85), kind=kOutput, calls=%fused_computation.41 | convolution fusion | flops 2148532224 | bytes 35652100 | tf_op jit(solution)/shard_map/dot_general | solution.py:176
  329.8 8.6 %collective-permute-done.6 = bf16[64,4096]{1,0:T(8,128)(2,1)S(1)} collective-permute-done((bf16[64,4096]{1,0:T(8,128)(2,1)S(1)}, bf16[64,4096]{1,0:T(8,128)(2,1)S(1)}, u32[]{:S(2)}, u32[]{:S(2)}) %collective-permute-start.6) | collective-permute-done | bytes 524320 | tf_op jit(solution)/shard_map/ppermute | solution.py:16
  340.9 15.7 %fusion.10 = (f32[64]{0:T(128)S(1)}, f32[64,4096]{1,0:T(8,128)S(1)}) fusion(f32[64]{0:T(128)S(1)} %add_rsqrt_fusion.1, bf16[5,64,4096]{2,1,0:T(8,128)(2,1)S(1)} %get-tuple-element.38, s32[]{:T(128)S(6)} %dynamic_slice.69, bf16[64,4096]{1,0:T(8,128)(2,1)S(1)} %get-tuple-element.65, bf16[4096,4096]{1,0:T(8,128)(2,1)} %shard_map.85), kind=kOutput, calls=%fused_computation.38 | convolution fusion | flops 2148532224 | bytes 35652100 | tf_op jit(solution)/shard_map/dot_general | solution.py:176
  360.0 7.9 %collective-permute-done.7 = bf16[64,4096]{1,0:T(8,128)(2,1)S(1)} collective-permute-done((bf16[64,4096]{1,0:T(8,128)(2,1)}, bf16[64,4096]{1,0:T(8,128)(2,1)S(1)}, u32[]{:S(2)}, u32[]{:S(2)}) %collective-permute-start.7) | collective-permute-done | bytes 524320 | tf_op jit(solution)/shard_map/ppermute | solution.py:16
  370.4 15.9 %fusion.g_ref = bf16[4096,4096]{1,0:T(8,128)(2,1)} fusion(bf16[5,64,4096]{2,1,0:T(8,128)(2,1)} %bitcast_dynamic-update-slice_fusion.4, s32[]{:T(128)S(6)} %select_n.138, bf16[5,64,4096]{2,1,0:T(8,128)(2,1)} %get-tuple-element.37, s32[]{:T(128)S(6)} %select_n.129), kind=kOutput, calls=%fused_computation.1 | convolution fusion | flops 4328521728 | bytes 35651592 | tf_op jit(solution)/shard_map/dot_general | solution.py:243
  386.3 31.4 %shard_map.86 = bf16[32,2048,128]{2,1,0:T(8,128)(2,1)} custom-call(s32[2048]{0:T(1024)} %reshape_squeeze.3.table_ref, bf16[4096,4096]{1,0:T(8,128)(2,1)} %fusion.g_ref), custom_call_target="tpu_custom_call" | custom-call | bytes 50331648 | tf_op jit(solution)/shard_map/pallas_call | solution.py:88
  417.8 120.5 %reduce-scatter.2.cloned.1.call-done = bf16[1,2048,128]{2,1,0:T(8,128)(2,1)} async-done(((bf16[32,2048,128]{2,1,0:T(8,128)(2,1)}), bf16[1,2048,128]{2,1,0:T(8,128)(2,1)}) %reduce-scatter.2.cloned.1.call-update) | async-done | bytes 524304 | tf_op jit(solution)/shard_map/reduce_scatter | solution.py:252
  544.6 12.1 %shard_map.87 = f32[8,128]{1,0:T(8,128)} custom-call(f32[8,128]{1,0:T(8,128)} %scatter.4.x_ref), custom_call_target="tpu_custom_call" | custom-call | tf_op jit(solution)/shard_map/pallas_call | solution.py:146
  (100 shorter events, 60.4 us)
Async XLA Ops:
  7.2 4.2 copy-start.7
  7.2 4.5 copy-start.8
  7.2 6.3 %copy-start.4 = (bf16[4,32,4096]{2,1,0:T(8,128)(2,1)S(1)}, bf16[4,32,4096]{2,1,0:T(8,128)(2,1)}, u32[]{:S(2)}) copy-start(bf16[4,32,4096]{2,1,0:T(8,128)(2,1)} %param.9) | copy-start | bytes 3145732
  7.2 79.9 %all-gather.2.cloned.1.call-start = ((), (), s32[]{:S(2)}) async-start(), calls=%async_computation.1 | async-start | bytes 17301504 | tf_op jit(solution)/shard_map/all_gather | solution.py:203
  9.4 528.9 %reduce-scatter.2.cloned.1.call-start = ((), (), s32[]{:S(2)}) async-start(), calls=%async_computation.2 | async-start | bytes 17301504 | tf_op jit(solution)/shard_map/reduce_scatter | solution.py:252
  11.6 123.7 %copy-start.2 = (bf16[2,32,4096]{2,1,0:T(8,128)(2,1)}, bf16[2,32,4096]{2,1,0:T(8,128)(2,1)S(1)}, u32[]{:S(2)}) copy-start(bf16[2,32,4096]{2,1,0:T(8,128)(2,1)S(1)} %get-tuple-element.32) | copy-start | bytes 1572868
  135.3 14.5 %copy-start = (bf16[2,32,4096]{2,1,0:T(8,128)(2,1)S(1)}, bf16[2,32,4096]{2,1,0:T(8,128)(2,1)}, u32[]{:S(2)}) copy-start(bf16[2,32,4096]{2,1,0:T(8,128)(2,1)} %slice.42) | copy-start | bytes 1572868
  135.6 14.2 %collective-permute-start = (bf16[64,4096]{1,0:T(8,128)(2,1)S(1)}, bf16[64,4096]{1,0:T(8,128)(2,1)S(1)}, u32[]{:S(2)}, u32[]{:S(2)}) collective-permute-start(bf16[64,4096]{1,0:T(8,128)(2,1)S(1)} %fusion.78), channel_id=1, source_target_pairs={{0,32},{32,64},{64,96},{1,33},{33,65},{65,97},{2,34},{34,66},{66,9... | collective-permute-start | bytes 1572872 | tf_op jit(solution)/shard_map/ppermute | solution.py:16
  164.1 14.3 %collective-permute-start.1 = (bf16[64,4096]{1,0:T(8,128)(2,1)S(1)}, bf16[64,4096]{1,0:T(8,128)(2,1)S(1)}, u32[]{:S(2)}, u32[]{:S(2)}) collective-permute-start(bf16[64,4096]{1,0:T(8,128)(2,1)S(1)} %fusion.38), channel_id=1, source_target_pairs={{0,32},{32,64},{64,96},{1,33},{33,65},{65,97},{2,34},{34,66},{66,9... | collective-permute-start | bytes 1572872 | tf_op jit(solution)/shard_map/ppermute | solution.py:16
  192.7 13.3 %collective-permute-start.2 = (bf16[64,4096]{1,0:T(8,128)(2,1)S(1)}, bf16[64,4096]{1,0:T(8,128)(2,1)S(1)}, u32[]{:S(2)}, u32[]{:S(2)}) collective-permute-start(bf16[64,4096]{1,0:T(8,128)(2,1)S(1)} %fusion.41), channel_id=1, source_target_pairs={{0,32},{32,64},{64,96},{1,33},{33,65},{65,97},{2,34},{34,66},{66,9... | collective-permute-start | bytes 1572872 | tf_op jit(solution)/shard_map/ppermute | solution.py:16
  220.3 12.4 %collective-permute-start.3 = (bf16[64,4096]{1,0:T(8,128)(2,1)S(1)}, bf16[64,4096]{1,0:T(8,128)(2,1)S(1)}, u32[]{:S(2)}, u32[]{:S(2)}) collective-permute-start(bf16[64,4096]{1,0:T(8,128)(2,1)S(1)} %fusion.44), channel_id=1, source_target_pairs={{0,32},{32,64},{64,96},{1,33},{33,65},{65,97},{2,34},{34,66},{66,9... | collective-permute-start | bytes 1572872 | tf_op jit(solution)/shard_map/ppermute | solution.py:16
  233.1 16.3 %copy-start.5 = (bf16[4,32,4096]{2,1,0:T(8,128)(2,1)S(1)}, bf16[4,32,4096]{2,1,0:T(8,128)(2,1)}, u32[]{:S(2)}) copy-start(bf16[4,32,4096]{2,1,0:T(8,128)(2,1)} %param.9) | copy-start | bytes 3145732
  246.8 2.5 copy-start.1
  265.9 3.0 copy-start.3
  267.4 12.5 %collective-permute-start.4 = (bf16[64,4096]{1,0:T(8,128)(2,1)S(1)}, bf16[64,4096]{1,0:T(8,128)(2,1)S(1)}, u32[]{:S(2)}, u32[]{:S(2)}) collective-permute-start(bf16[64,4096]{1,0:T(8,128)(2,1)S(1)} %fusion.23), channel_id=1, source_target_pairs={{32,0},{64,32},{96,64},{33,1},{65,33},{97,65},{34,2},{66,34},{98,6... | collective-permute-start | bytes 1572872 | tf_op jit(solution)/shard_map/ppermute | solution.py:16
  281.5 1.5 copy-start.9
  299.1 10.8 %collective-permute-start.5 = (bf16[64,4096]{1,0:T(8,128)(2,1)S(1)}, bf16[64,4096]{1,0:T(8,128)(2,1)S(1)}, u32[]{:S(2)}, u32[]{:S(2)}) collective-permute-start(bf16[64,4096]{1,0:T(8,128)(2,1)S(1)} %fusion.27), channel_id=1, source_target_pairs={{32,0},{64,32},{96,64},{33,1},{65,33},{97,65},{34,2},{66,34},{98,6... | collective-permute-start | bytes 1572872 | tf_op jit(solution)/shard_map/ppermute | solution.py:16
  328.5 9.9 %collective-permute-start.6 = (bf16[64,4096]{1,0:T(8,128)(2,1)S(1)}, bf16[64,4096]{1,0:T(8,128)(2,1)S(1)}, u32[]{:S(2)}, u32[]{:S(2)}) collective-permute-start(bf16[64,4096]{1,0:T(8,128)(2,1)S(1)} %fusion.29), channel_id=1, source_target_pairs={{32,0},{64,32},{96,64},{33,1},{65,33},{97,65},{34,2},{66,34},{98,6... | collective-permute-start | bytes 1572872 | tf_op jit(solution)/shard_map/ppermute | solution.py:16
  357.8 10.1 %collective-permute-start.7 = (bf16[64,4096]{1,0:T(8,128)(2,1)}, bf16[64,4096]{1,0:T(8,128)(2,1)S(1)}, u32[]{:S(2)}, u32[]{:S(2)}) collective-permute-start(bf16[64,4096]{1,0:T(8,128)(2,1)} %fusion.31), channel_id=1, source_target_pairs={{32,0},{64,32},{96,64},{33,1},{65,33},{97,65},{34,2},{66,34},{98,6... | collective-permute-start | bytes 1572872 | tf_op jit(solution)/shard_map/ppermute | solution.py:16
  417.6 121.9 %copy-start.6 = (bf16[1,2,64,2048]{3,2,1,0:T(8,128)(2,1)S(1)}, bf16[1,2,64,2048]{3,2,1,0:T(8,128)(2,1)}, u32[]{:S(2)}) copy-start(bf16[1,2,64,2048]{3,2,1,0:T(8,128)(2,1)} %param.10) | copy-start | bytes 1572868
Sparse Core Ops, SparseCore 0:
  10.9 76.2 all-gather.1
  417.8 120.4 reduce-scatter.1

commit v6 on v5

--- a/solution.py
+++ b/solution.py
@@ -1,3 +1,4 @@
+import functools
 import math
 
 import jax
@@ -25,7 +26,8 @@
     block = 64
     blocks = o_ref.shape[0] // block
     lane = lax.broadcasted_iota(jnp.int32, (block, o_ref.shape[1]), 1)
-    for r in range(blocks):
+
+    def one_block(r, carry):
         k0 = table_ref[(2 * p) * blocks + r]
         k1 = table_ref[(2 * p + 1) * blocks + r]
         s0 = pl.multiple_of(jnp.maximum(k0, 0) * block, block)
@@ -35,22 +37,29 @@
         zero = jnp.zeros_like(t0)
         t0 = jnp.where(k0 >= 0, t0, zero)
         t1 = jnp.where(k1 >= 0, t1, zero)
-        o_ref[r * block:(r + 1) * block, :] = jnp.where(lane < block, t0, t1)
-
-
-def pack_kernel(table_ref, g_ref, o_ref):
+        o_ref[pl.ds(pl.multiple_of(r * block, block), block), :] = jnp.where(lane < block, t0, t1)
+        return carry
+
+    lax.fori_loop(0, blocks, one_block, 0, unroll=4)
+
+
+def pack_kernel(first_k, live_count, table_ref, g_ref, o_ref):
     p = pl.program_id(0)
     block = 64
-    live_count = o_ref.shape[1] // block
+    part_count = o_ref.shape[1] // block
     lane = lax.broadcasted_iota(jnp.int32, (block, o_ref.shape[2]), 1)
-    for k in range(live_count):
-        r0 = table_ref[(2 * p) * live_count + k]
-        r1 = table_ref[(2 * p + 1) * live_count + k]
+
+    def one_block(k, carry):
+        r0 = table_ref[(2 * p) * live_count + first_k + k]
+        r1 = table_ref[(2 * p + 1) * live_count + first_k + k]
         s0 = pl.multiple_of(r0 * block, block)
         s1 = pl.multiple_of(r1 * block, block)
         t0 = g_ref[pl.ds(s0, block), :]
         t1 = g_ref[pl.ds(s1, block), :]
-        o_ref[0, k * block:(k + 1) * block, :] = jnp.where(lane < block, t0, t1)
+        o_ref[0, pl.ds(pl.multiple_of(k * block, block), block), :] = jnp.where(lane < block, t0, t1)
+        return carry
+
+    lax.fori_loop(0, part_count, one_block, 0, unroll=4)
 
 
 def expand_dense(paired_weights, live_index):
@@ -79,14 +88,14 @@
     )(inverse.reshape(-1), paired_weights)
 
 
-def pack_dense(dense_grad, live_index):
+def pack_dense(dense_grad, live_index, first_k, part_count):
     column_count, live_count = live_index.shape
     features = dense_grad.shape[0]
     block_size = features // column_count
-    wide = live_count * block_size
+    wide = part_count * block_size
     pair_count = column_count // 2
     return pl.pallas_call(
-        pack_kernel,
+        functools.partial(pack_kernel, first_k, live_count),
         out_shape=jax.ShapeDtypeStruct((pair_count, wide, 2 * block_size), dense_grad.dtype),
         grid_spec=pltpu.PrefetchScalarGridSpec(
             num_scalar_prefetch=1,
@@ -248,8 +257,16 @@
         )
         * inverse_tokens
     ).astype(jnp.bfloat16)
-    partial = pack_dense(dense_grad, live_index)
-    own_grad = lax.psum_scatter(partial, "dp", scatter_dimension=0, tiled=True)
+    half_k = live_count // 2
+    own_grad = jnp.concatenate(
+        [
+            lax.psum_scatter(
+                pack_dense(dense_grad, live_index, first_k, half_k), "dp", scatter_dimension=0, tiled=True
+            )
+            for first_k in (0, half_k)
+        ],
+        axis=1,
+    )
     gradient = (
         own_grad.reshape(live_count * block_size, own_columns, block_size)
         .transpose(1, 2, 0)

time: 578 us -> 649 us (1.12)
  waiting for transfers between devices: 261 us -> 308 us
  Pallas kernels: 78.1 us -> 103 us
    reduce_scatter x1 -> x2, waiting for transfers between devices: 120 us -> 167 us  [local(): lax.psum_scatter(pack_dense(dense_grad, live_index, first_k, half_k), 'dp...]
    pallas_call x1 -> x2, Pallas kernels: 31.4 us -> 53.2 us  [pack_dense(): pl.pallas_call(functools.partial(pack_kernel, first_k, live_count), out_s...]
  transfers between devices with their start and end apart: 10 -> 11, of which waited for: 10 -> 11; matrix products, arithmetic and copies ran while one was open for 2% -> 2% of each run, Pallas kernels for 0% -> 4%
where the time goes in v6:
time: 649 us; the launch traced here: 638 us
  waiting for transfers between devices  308 us (47%)
  matrix products  147 us (23%)
  Pallas kernels  103 us (16%)
  other arithmetic  33.3 us (5%)
  starting transfers between devices  21.7 us (3%)
  between operations  15.1 us (2%)
  local copies, waits for them, and re-layouts  10.2 us (2%)
    reduce_scatter x2, waiting for transfers between devices, local(): lax.psum_scatter(pack_dense(dense_grad, live_index, first_k, half_k), 'dp...  167 us
    all_gather x1, waiting for transfers between devices, local(): paired_weights = lax.all_gather(own_pair, 'dp', axis=0, tiled=True)  72.5 us
    dot_general x5, matrix products, layer_forward(): pre_act = jnp.dot(normed, dense_w, preferred_element_type=jnp.float32)  68.4 us
    ppermute x8, waiting for transfers between devices, shifted(): lax.ppermute(value, axis, [(source, source + steps) for source in range(l...  68.4 us
    dot_general x4, matrix products, layer_backward(): lax.dot_general(grad_pre, dense_w, (((1,), (1,)), ((), ())), preferred_el...  62.9 us
    pallas_call x2, Pallas kernels, pack_dense(): pl.pallas_call(functools.partial(pack_kernel, first_k, live_count), out_s...  53.2 us
    pallas_call x1, Pallas kernels, expand_dense(): pl.pallas_call(expand_kernel, out_shape=jax.ShapeDtypeStruct((features, f...  37.1 us
    ppermute x8, starting transfers between devices, shifted(): lax.ppermute(value, axis, [(source, source + steps) for source in range(l...  21.6 us
  transfers between devices with their start and end apart: 11, of which 11 were waited for; matrix products, arithmetic and copies ran while one was open for 2% of the time, Pallas kernels for 4%

profile of v6, /device:TPU:1, one launch (start us, length us, event | category | flops | bytes accessed | tf_op | source)
XLA Modules:
  0.0 638.0 jit_solution(17938541862935021936)
XLA Ops:
  14.6 72.5 %all-gather.2.cloned.1.call-done.t_ref = bf16[32,2048,128]{2,1,0:T(8,128)(2,1)} async-done(((bf16[1,2048,128]{2,1,0:T(8,128)(2,1)}), bf16[32,2048,128]{2,1,0:T(8,128)(2,1)}) %all-gather.2.cloned.1.call-update) | async-done | bytes 16777232 | tf_op jit(solution)/shard_map/all_gather | solution.py:212
  87.1 37.1 %shard_map.85 = bf16[4096,4096]{1,0:T(8,128)(2,1)} custom-call(s32[4096]{0:T(1024)} %select_n.124.table_ref, bf16[32,2048,128]{2,1,0:T(8,128)(2,1)} %all-gather.2.cloned.1.call-done.t_ref), custom_call_target="tpu_custom_call" | custom-call | bytes 50331648 | tf_op jit(solution)/shard_map/pallas_call | solution.py:76
  124.2 13.6 %bitcast_dynamic-update-slice_fusion.3 = (f32[5,64,4096]{2,1,0:T(8,128)S(1)}, f32[64,4096]{1,0:T(8,128)S(1)}) fusion(bf16[64,4096]{1,0:T(8,128)(2,1)S(1)} %fusion.77, bf16[4096,4096]{1,0:T(8,128)(2,1)} %shard_map.85), kind=kOutput, calls=%fused_computation.116 | convolution fusion | flops 2147483648 | bytes 36175872 | tf_op jit(solution)/shard_map/dot_general | solution.py:174
  143.5 8.8 %collective-permute-done = bf16[64,4096]{1,0:T(8,128)(2,1)S(1)} collective-permute-done((bf16[64,4096]{1,0:T(8,128)(2,1)S(1)}, bf16[64,4096]{1,0:T(8,128)(2,1)S(1)}, u32[]{:S(2)}, u32[]{:S(2)}) %collective-permute-start) | collective-permute-done | bytes 524320 | tf_op jit(solution)/shard_map/ppermute | solution.py:17
  152.6 13.7 %bitcast_dynamic-update-slice_fusion.2 = (f32[5,64,4096]{2,1,0:T(8,128)S(1)}, f32[64,4096]{1,0:T(8,128)S(1)}) fusion(f32[5,64,4096]{2,1,0:T(8,128)S(1)} %get-tuple-element.47, bf16[4096,4096]{1,0:T(8,128)(2,1)} %shard_map.85, bf16[64,4096]{1,0:T(8,128)(2,1)S(1)} %get-tuple-element.30, f32[64]{0:T(128)S(1)} %add_rsqrt_fusion.8), kind=kOutput, calls=%fused_computation.115 | convolution fusion | flops 2148270080 | bytes 36176384 | tf_op jit(solution)/shard_map/dot_general | solution.py:174
  171.7 9.2 %collective-permute-done.1 = bf16[64,4096]{1,0:T(8,128)(2,1)S(1)} collective-permute-done((bf16[64,4096]{1,0:T(8,128)(2,1)S(1)}, bf16[64,4096]{1,0:T(8,128)(2,1)S(1)}, u32[]{:S(2)}, u32[]{:S(2)}) %collective-permute-start.1) | collective-permute-done | bytes 524320 | tf_op jit(solution)/shard_map/ppermute | solution.py:17
  181.2 13.7 %bitcast_dynamic-update-slice_fusion.1 = (f32[5,64,4096]{2,1,0:T(8,128)S(1)}, f32[64,4096]{1,0:T(8,128)S(1)}) fusion(f32[5,64,4096]{2,1,0:T(8,128)S(1)} %get-tuple-element.49, bf16[4096,4096]{1,0:T(8,128)(2,1)} %shard_map.85, bf16[64,4096]{1,0:T(8,128)(2,1)S(1)} %get-tuple-element.28, f32[64]{0:T(128)S(1)} %add_rsqrt_fusion.7), kind=kOutput, calls=%fused_computation.114 | convolution fusion | flops 2148270080 | bytes 36176384 | tf_op jit(solution)/shard_map/dot_general | solution.py:174
  200.8 7.7 %collective-permute-done.2 = bf16[64,4096]{1,0:T(8,128)(2,1)S(1)} collective-permute-done((bf16[64,4096]{1,0:T(8,128)(2,1)S(1)}, bf16[64,4096]{1,0:T(8,128)(2,1)S(1)}, u32[]{:S(2)}, u32[]{:S(2)}) %collective-permute-start.2) | collective-permute-done | bytes 524320 | tf_op jit(solution)/shard_map/ppermute | solution.py:17
  208.8 13.7 %bitcast_dynamic-update-slice_fusion = (f32[5,64,4096]{2,1,0:T(8,128)S(1)}, f32[64,4096]{1,0:T(8,128)S(1)}) fusion(f32[5,64,4096]{2,1,0:T(8,128)S(1)} %get-tuple-element.51, bf16[4096,4096]{1,0:T(8,128)(2,1)} %shard_map.85, bf16[64,4096]{1,0:T(8,128)(2,1)S(1)} %get-tuple-element.26, f32[64]{0:T(128)S(1)} %add_rsqrt_fusion.6), kind=kOutput, calls=%fused_computation.113 | convolution fusion | flops 2148270080 | bytes 36176384 | tf_op jit(solution)/shard_map/dot_general | solution.py:174
  235.6 13.8 %fusion.1 = f32[5,64,4096]{2,1,0:T(8,128)S(1)} fusion(f32[5,64,4096]{2,1,0:T(8,128)S(1)} %get-tuple-element.53, bf16[4096,4096]{1,0:T(8,128)(2,1)} %shard_map.85, bf16[64,4096]{1,0:T(8,128)(2,1)S(1)} %get-tuple-element.24, f32[64]{0:T(128)S(1)} %add_rsqrt_fusion.5), kind=kOutput, calls=%fused_computation.3 | convolution fusion | flops 2148270080 | bytes 35127808 | tf_op jit(solution)/shard_map/dot_general | solution.py:174
  252.5 15.9 %fusion.35 = (f32[64]{0:T(128)S(1)}, f32[64]{0:T(128)S(1)}, f32[64]{0:T(128)S(1)}, f32[64]{0:T(128)S(1)}, f32[64,4096]{1,0:T(8,128)S(1)}) fusion(bf16[5,64,4096]{2,1,0:T(8,128)(2,1)S(1)} %get-tuple-element.38, s32[]{:T(128)S(6)} %dynamic_slice.69, f32[64]{0:T(128)S(1)} %add_rsqrt_fusion.4, s32[]{:T(128)S(6)} %dynamic_slice.60, s32[]{:T(128)S(6)} %dynamic_slice.66, ...), kind=kOutput, calls=%fused_computation.63 | convolution fusion | flops 2150891520 | bytes 37225744 | tf_op jit(solution)/shard_map/dot_general | solution.py:185
  273.0 9.4 %collective-permute-done.4 = bf16[64,4096]{1,0:T(8,128)(2,1)S(1)} collective-permute-done((bf16[64,4096]{1,0:T(8,128)(2,1)S(1)}, bf16[64,4096]{1,0:T(8,128)(2,1)S(1)}, u32[]{:S(2)}, u32[]{:S(2)}) %collective-permute-start.4) | collective-permute-done | bytes 524320 | tf_op jit(solution)/shard_map/ppermute | solution.py:17
  285.6 15.7 %fusion.16 = (f32[64]{0:T(128)S(1)}, f32[64,4096]{1,0:T(8,128)S(1)}) fusion(f32[64]{0:T(128)S(1)} %add_rsqrt_fusion.3, bf16[5,64,4096]{2,1,0:T(8,128)(2,1)S(1)} %get-tuple-element.38, s32[]{:T(128)S(6)} %dynamic_slice.63, bf16[64,4096]{1,0:T(8,128)(2,1)S(1)} %get-tuple-element.57, bf16[4096,4096]{1,0:T(8,128)(2,1)} %shard_map.85), kind=kOutput, calls=%fused_computation.44 | convolution fusion | flops 2148532224 | bytes 35652100 | tf_op jit(solution)/shard_map/dot_general | solution.py:185
  303.0 9.5 %collective-permute-done.5 = bf16[64,4096]{1,0:T(8,128)(2,1)S(1)} collective-permute-done((bf16[64,4096]{1,0:T(8,128)(2,1)S(1)}, bf16[64,4096]{1,0:T(8,128)(2,1)S(1)}, u32[]{:S(2)}, u32[]{:S(2)}) %collective-permute-start.5) | collective-permute-done | bytes 524320 | tf_op jit(solution)/shard_map/ppermute | solution.py:17
  314.9 15.7 %fusion.13 = (f32[64]{0:T(128)S(1)}, f32[64,4096]{1,0:T(8,128)S(1)}) fusion(f32[64]{0:T(128)S(1)} %add_rsqrt_fusion.2, bf16[5,64,4096]{2,1,0:T(8,128)(2,1)S(1)} %get-tuple-element.38, s32[]{:T(128)S(6)} %dynamic_slice.66, bf16[64,4096]{1,0:T(8,128)(2,1)S(1)} %get-tuple-element.61, bf16[4096,4096]{1,0:T(8,128)(2,1)} %shard_map.85), kind=kOutput, calls=%fused_computation.41 | convolution fusion | flops 2148532224 | bytes 35652100 | tf_op jit(solution)/shard_map/dot_general | solution.py:185
  332.3 8.6 %collective-permute-done.6 = bf16[64,4096]{1,0:T(8,128)(2,1)S(1)} collective-permute-done((bf16[64,4096]{1,0:T(8,128)(2,1)S(1)}, bf16[64,4096]{1,0:T(8,128)(2,1)S(1)}, u32[]{:S(2)}, u32[]{:S(2)}) %collective-permute-start.6) | collective-permute-done | bytes 524320 | tf_op jit(solution)/shard_map/ppermute | solution.py:17
  343.4 15.7 %fusion.10 = (f32[64]{0:T(128)S(1)}, f32[64,4096]{1,0:T(8,128)S(1)}) fusion(f32[64]{0:T(128)S(1)} %add_rsqrt_fusion.1, bf16[5,64,4096]{2,1,0:T(8,128)(2,1)S(1)} %get-tuple-element.38, s32[]{:T(128)S(6)} %dynamic_slice.69, bf16[64,4096]{1,0:T(8,128)(2,1)S(1)} %get-tuple-element.65, bf16[4096,4096]{1,0:T(8,128)(2,1)} %shard_map.85), kind=kOutput, calls=%fused_computation.38 | convolution fusion | flops 2148532224 | bytes 35652100 | tf_op jit(solution)/shard_map/dot_general | solution.py:185
  362.5 7.9 %collective-permute-done.7 = bf16[64,4096]{1,0:T(8,128)(2,1)S(1)} collective-permute-done((bf16[64,4096]{1,0:T(8,128)(2,1)}, bf16[64,4096]{1,0:T(8,128)(2,1)S(1)}, u32[]{:S(2)}, u32[]{:S(2)}) %collective-permute-start.7) | collective-permute-done | bytes 524320 | tf_op jit(solution)/shard_map/ppermute | solution.py:17
  372.9 15.9 %fusion.g_ref = bf16[4096,4096]{1,0:T(8,128)(2,1)} fusion(bf16[5,64,4096]{2,1,0:T(8,128)(2,1)} %bitcast_dynamic-update-slice_fusion.4, s32[]{:T(128)S(6)} %select_n.138, bf16[5,64,4096]{2,1,0:T(8,128)(2,1)} %get-tuple-element.37, s32[]{:T(128)S(6)} %select_n.129), kind=kOutput, calls=%fused_computation.1 | convolution fusion | flops 4328521728 | bytes 35651592 | tf_op jit(solution)/shard_map/dot_general | solution.py:252
  388.8 26.4 %shard_map.86 = bf16[32,1024,128]{2,1,0:T(8,128)(2,1)} custom-call(s32[2048]{0:T(1024)} %reshape_squeeze.4.table_ref, bf16[4096,4096]{1,0:T(8,128)(2,1)} %fusion.g_ref), custom_call_target="tpu_custom_call" | custom-call | bytes 25165824 | tf_op jit(solution)/shard_map/pallas_call | solution.py:97
  415.2 26.9 %shard_map.87 = bf16[32,1024,128]{2,1,0:T(8,128)(2,1)} custom-call(s32[2048]{0:T(1024)} %reshape_squeeze.4.table_ref, bf16[4096,4096]{1,0:T(8,128)(2,1)} %fusion.g_ref), custom_call_target="tpu_custom_call" | custom-call | bytes 25165824 | tf_op jit(solution)/shard_map/pallas_call | solution.py:97
  442.3 70.6 %reduce-scatter.3.cloned.1.call-done = bf16[1,1024,128]{2,1,0:T(8,128)(2,1)} async-done(((bf16[32,1024,128]{2,1,0:T(8,128)(2,1)}), bf16[1,1024,128]{2,1,0:T(8,128)(2,1)}) %reduce-scatter.3.cloned.1.call-update) | async-done | bytes 262160 | tf_op jit(solution)/shard_map/reduce_scatter | solution.py:263
  512.9 96.2 %reduce-scatter.5.cloned.1.call-done = bf16[1,1024,128]{2,1,0:T(8,128)(2,1)} async-done(((bf16[32,1024,128]{2,1,0:T(8,128)(2,1)}), bf16[1,1024,128]{2,1,0:T(8,128)(2,1)}) %reduce-scatter.5.cloned.1.call-update) | async-done | bytes 262160 | tf_op jit(solution)/shard_map/reduce_scatter | solution.py:263
  615.6 12.3 %shard_map.88 = f32[8,128]{1,0:T(8,128)} custom-call(f32[8,128]{1,0:T(8,128)} %scatter.4.x_ref), custom_call_target="tpu_custom_call" | custom-call | tf_op jit(solution)/shard_map/pallas_call | solution.py:155
  (105 shorter events, 72.6 us)
Async XLA Ops:
  7.2 4.2 copy-start.7
  7.2 4.5 copy-start.8
  7.2 6.3 copy-start.4
  7.2 79.9 %all-gather.2.cloned.1.call-start = ((), (), s32[]{:S(2)}) async-start(), calls=%async_computation.2 | async-start | bytes 17301504 | tf_op jit(solution)/shard_map/all_gather | solution.py:212
  9.4 503.4 %reduce-scatter.3.cloned.1.call-start = ((), (), s32[]{:S(2)}) async-start(), calls=%async_computation.3 | async-start | bytes 8650752 | tf_op jit(solution)/shard_map/reduce_scatter | solution.py:263
  11.6 126.2 %copy-start.2 = (bf16[2,32,4096]{2,1,0:T(8,128)(2,1)}, bf16[2,32,4096]{2,1,0:T(8,128)(2,1)S(1)}, u32[]{:S(2)}) copy-start(bf16[2,32,4096]{2,1,0:T(8,128)(2,1)S(1)} %get-tuple-element.32) | copy-start | bytes 1572868
  137.8 14.5 %copy-start = (bf16[2,32,4096]{2,1,0:T(8,128)(2,1)S(1)}, bf16[2,32,4096]{2,1,0:T(8,128)(2,1)}, u32[]{:S(2)}) copy-start(bf16[2,32,4096]{2,1,0:T(8,128)(2,1)} %slice.42) | copy-start | bytes 1572868
  138.1 14.2 %collective-permute-start = (bf16[64,4096]{1,0:T(8,128)(2,1)S(1)}, bf16[64,4096]{1,0:T(8,128)(2,1)S(1)}, u32[]{:S(2)}, u32[]{:S(2)}) collective-permute-start(bf16[64,4096]{1,0:T(8,128)(2,1)S(1)} %fusion.78), channel_id=1, source_target_pairs={{0,32},{32,64},{64,96},{1,33},{33,65},{65,97},{2,34},{34,66},{66,9... | collective-permute-start | bytes 1572872 | tf_op jit(solution)/shard_map/ppermute | solution.py:17
  166.6 14.2 %collective-permute-start.1 = (bf16[64,4096]{1,0:T(8,128)(2,1)S(1)}, bf16[64,4096]{1,0:T(8,128)(2,1)S(1)}, u32[]{:S(2)}, u32[]{:S(2)}) collective-permute-start(bf16[64,4096]{1,0:T(8,128)(2,1)S(1)} %fusion.38), channel_id=1, source_target_pairs={{0,32},{32,64},{64,96},{1,33},{33,65},{65,97},{2,34},{34,66},{66,9... | collective-permute-start | bytes 1572872 | tf_op jit(solution)/shard_map/ppermute | solution.py:17
  195.2 13.3 %collective-permute-start.2 = (bf16[64,4096]{1,0:T(8,128)(2,1)S(1)}, bf16[64,4096]{1,0:T(8,128)(2,1)S(1)}, u32[]{:S(2)}, u32[]{:S(2)}) collective-permute-start(bf16[64,4096]{1,0:T(8,128)(2,1)S(1)} %fusion.41), channel_id=1, source_target_pairs={{0,32},{32,64},{64,96},{1,33},{33,65},{65,97},{2,34},{34,66},{66,9... | collective-permute-start | bytes 1572872 | tf_op jit(solution)/shard_map/ppermute | solution.py:17
  222.8 12.4 %collective-permute-start.3 = (bf16[64,4096]{1,0:T(8,128)(2,1)S(1)}, bf16[64,4096]{1,0:T(8,128)(2,1)S(1)}, u32[]{:S(2)}, u32[]{:S(2)}) collective-permute-start(bf16[64,4096]{1,0:T(8,128)(2,1)S(1)} %fusion.44), channel_id=1, source_target_pairs={{0,32},{32,64},{64,96},{1,33},{33,65},{65,97},{2,34},{34,66},{66,9... | collective-permute-start | bytes 1572872 | tf_op jit(solution)/shard_map/ppermute | solution.py:17
  235.6 16.3 %copy-start.5 = (bf16[4,32,4096]{2,1,0:T(8,128)(2,1)S(1)}, bf16[4,32,4096]{2,1,0:T(8,128)(2,1)}, u32[]{:S(2)}) copy-start(bf16[4,32,4096]{2,1,0:T(8,128)(2,1)} %param.9) | copy-start | bytes 3145732
  249.3 2.5 copy-start.1
  268.4 3.0 copy-start.3
  269.9 12.5 %collective-permute-start.4 = (bf16[64,4096]{1,0:T(8,128)(2,1)S(1)}, bf16[64,4096]{1,0:T(8,128)(2,1)S(1)}, u32[]{:S(2)}, u32[]{:S(2)}) collective-permute-start(bf16[64,4096]{1,0:T(8,128)(2,1)S(1)} %fusion.23), channel_id=1, source_target_pairs={{32,0},{64,32},{96,64},{33,1},{65,33},{97,65},{34,2},{66,34},{98,6... | collective-permute-start | bytes 1572872 | tf_op jit(solution)/shard_map/ppermute | solution.py:17
  284.0 1.5 copy-start.9
  301.6 10.8 %collective-permute-start.5 = (bf16[64,4096]{1,0:T(8,128)(2,1)S(1)}, bf16[64,4096]{1,0:T(8,128)(2,1)S(1)}, u32[]{:S(2)}, u32[]{:S(2)}) collective-permute-start(bf16[64,4096]{1,0:T(8,128)(2,1)S(1)} %fusion.27), channel_id=1, source_target_pairs={{32,0},{64,32},{96,64},{33,1},{65,33},{97,65},{34,2},{66,34},{98,6... | collective-permute-start | bytes 1572872 | tf_op jit(solution)/shard_map/ppermute | solution.py:17
  331.0 9.9 %collective-permute-start.6 = (bf16[64,4096]{1,0:T(8,128)(2,1)S(1)}, bf16[64,4096]{1,0:T(8,128)(2,1)S(1)}, u32[]{:S(2)}, u32[]{:S(2)}) collective-permute-start(bf16[64,4096]{1,0:T(8,128)(2,1)S(1)} %fusion.29), channel_id=1, source_target_pairs={{32,0},{64,32},{96,64},{33,1},{65,33},{97,65},{34,2},{66,34},{98,6... | collective-permute-start | bytes 1572872 | tf_op jit(solution)/shard_map/ppermute | solution.py:17
  360.3 10.1 %collective-permute-start.7 = (bf16[64,4096]{1,0:T(8,128)(2,1)}, bf16[64,4096]{1,0:T(8,128)(2,1)S(1)}, u32[]{:S(2)}, u32[]{:S(2)}) collective-permute-start(bf16[64,4096]{1,0:T(8,128)(2,1)} %fusion.31), channel_id=1, source_target_pairs={{32,0},{64,32},{96,64},{33,1},{65,33},{97,65},{34,2},{66,34},{98,6... | collective-permute-start | bytes 1572872 | tf_op jit(solution)/shard_map/ppermute | solution.py:17
  415.2 193.9 %reduce-scatter.5.cloned.1.call-start = ((), (), s32[]{:S(2)}) async-start(), calls=%async_computation.4 | async-start | bytes 8650752 | tf_op jit(solution)/shard_map/reduce_scatter | solution.py:263
  442.1 168.4 %copy-start.6 = (bf16[1,2,64,2048]{3,2,1,0:T(8,128)(2,1)S(1)}, bf16[1,2,64,2048]{3,2,1,0:T(8,128)(2,1)}, u32[]{:S(2)}) copy-start(bf16[1,2,64,2048]{3,2,1,0:T(8,128)(2,1)} %param.10) | copy-start | bytes 1572868
Sparse Core Ops, SparseCore 0:
  10.9 76.2 all-gather.1
  415.3 97.5 reduce-scatter.2
  517.0 92.0 reduce-scatter.4

commit v7 on v5

--- a/solution.py
+++ b/solution.py
@@ -158,11 +158,67 @@
     return out[0, : values.shape[0]]
 
 
+def forward_mm_kernel(u_ref, w_ref, o_ref):
+    @pl.when(pl.program_id(0) == 0)
+    def _():
+        o_ref[...] = jnp.zeros_like(o_ref)
+
+    o_ref[...] += jnp.dot(u_ref[...], w_ref[...], preferred_element_type=jnp.float32)
+
+
+def backward_mm_kernel(g_ref, w_ref, o_ref):
+    o_ref[...] = lax.dot_general(
+        g_ref[...], w_ref[...], (((1,), (1,)), ((), ())), preferred_element_type=jnp.float32
+    )
+
+
+STRIPE = 512
+
+
+def forward_mm(normed, dense_w):
+    tokens, features = normed.shape
+    return pl.pallas_call(
+        forward_mm_kernel,
+        out_shape=jax.ShapeDtypeStruct((tokens, dense_w.shape[1]), jnp.float32),
+        grid=(features // STRIPE,),
+        in_specs=[
+            pl.BlockSpec((tokens, STRIPE), lambda k: (0, k)),
+            pl.BlockSpec((STRIPE, dense_w.shape[1]), lambda k: (k, 0)),
+        ],
+        out_specs=pl.BlockSpec((tokens, dense_w.shape[1]), lambda k: (0, 0)),
+        cost_estimate=pl.CostEstimate(
+            flops=2 * tokens * features * dense_w.shape[1],
+            transcendentals=0,
+            bytes_accessed=dense_w.size * 2,
+        ),
+    )(normed, dense_w)
+
+
+def backward_mm(grad_pre, dense_w):
+    tokens, columns = grad_pre.shape
+    features = dense_w.shape[0]
+    return pl.pallas_call(
+        backward_mm_kernel,
+        out_shape=jax.ShapeDtypeStruct((tokens, features), jnp.float32),
+        grid=(features // STRIPE,),
+        in_specs=[
+            pl.BlockSpec((tokens, columns), lambda n: (0, 0)),
+            pl.BlockSpec((STRIPE, columns), lambda n: (n, 0)),
+        ],
+        out_specs=pl.BlockSpec((tokens, STRIPE), lambda n: (0, n)),
+        cost_estimate=pl.CostEstimate(
+            flops=2 * tokens * features * columns,
+            transcendentals=0,
+            bytes_accessed=dense_w.size * 2,
+        ),
+    )(grad_pre, dense_w)
+
+
 def layer_forward(entering, dense_w):
     as_float = entering.astype(jnp.float32)
     inverse_rms = lax.rsqrt(jnp.mean(as_float * as_float, axis=-1, keepdims=True) + 1e-05)
     normed = (as_float * inverse_rms).astype(jnp.bfloat16)
-    pre_act = jnp.dot(normed, dense_w, preferred_element_type=jnp.float32)
+    pre_act = forward_mm(normed, dense_w)
     return ((as_float + jax.nn.silu(pre_act)).astype(jnp.bfloat16), normed, pre_act)
 
 
@@ -173,9 +229,7 @@
     grad_pre = (
         arriving.astype(jnp.float32) * (sigmoid_z * (1.0 + pre_act * (1.0 - sigmoid_z)))
     ).astype(jnp.bfloat16)
-    grad_normed = lax.dot_general(
-        grad_pre, dense_w, (((1,), (1,)), ((), ())), preferred_element_type=jnp.float32
-    )
+    grad_normed = backward_mm(grad_pre, dense_w)
     scaled = as_float * inverse_rms
     leaving = (
         arriving.astype(jnp.float32)

time: 578 us -> 607 us (1.050); the launches traced: 567 us -> 603 us
  matrix products: 147 us -> 15.9 us
  Pallas kernels: 78.1 us -> 207 us
  other arithmetic: 32.2 us -> 67.6 us
    dot_general x9 -> x0, matrix products: 131 us -> none  [the longest x5 68.4 us: layer_forward(): pre_act = jnp.dot(normed, dense_w, preferred_element_type=jnp.float32)]
    pallas_call x0 -> x8, Pallas kernels: none -> 129 us  [the longest x4 68.6 us: backward_mm(): pl.pallas_call(backward_mm_kernel, out_shape=jax.ShapeDtypeStruct((tokens...]
    pallas_call x0 -> x1, other arithmetic: none -> 15.2 us  [forward_mm(): pl.pallas_call(forward_mm_kernel, out_shape=jax.ShapeDtypeStruct((tokens,...]
where the time goes in v7:
time: 607 us; the launch traced here: 603 us
  waiting for transfers between devices  260 us (43%)
  Pallas kernels  207 us (34%)
  other arithmetic  67.6 us (11%)
  starting transfers between devices  21.2 us (3%)
  local copies, waits for them, and re-layouts  16.3 us (3%)
  matrix products  15.9 us (3%)
  between operations  15.2 us (3%)
    reduce_scatter x1, waiting for transfers between devices, local(): own_grad = lax.psum_scatter(partial, 'dp', scatter_dimension=0, tiled=True)  120 us
    all_gather x1, waiting for transfers between devices, local(): paired_weights = lax.all_gather(own_pair, 'dp', axis=0, tiled=True)  69.6 us
    ppermute x8, waiting for transfers between devices, shifted(): lax.ppermute(value, axis, [(source, source + steps) for source in range(l...  69.6 us
    pallas_call x4, Pallas kernels, backward_mm(): pl.pallas_call(backward_mm_kernel, out_shape=jax.ShapeDtypeStruct((tokens...  68.6 us
    pallas_call x4, Pallas kernels, forward_mm(): pl.pallas_call(forward_mm_kernel, out_shape=jax.ShapeDtypeStruct((tokens,...  60.8 us
    pallas_call x1, Pallas kernels, expand_dense(): pl.pallas_call(expand_kernel, out_shape=jax.ShapeDtypeStruct((features, f...  34.6 us
    pallas_call x1, Pallas kernels, pack_dense(): pl.pallas_call(pack_kernel, out_shape=jax.ShapeDtypeStruct((pair_count, w...  31.4 us
    ppermute x8, starting transfers between devices, shifted(): lax.ppermute(value, axis, [(source, source + steps) for source in range(l...  21.1 us
  transfers between devices with their start and end apart: 10, of which 10 were waited for; matrix products, arithmetic and copies ran while one was open for 2% of the time, Pallas kernels for 0%

profile of v7, /device:TPU:1, one launch (start us, length us, event | category | flops | bytes accessed | tf_op | source)
XLA Modules:
  0.0 603.4 jit_solution(17701477844659251155)
XLA Ops:
  17.5 69.6 %all-gather.2.cloned.1.call-done.t_ref = bf16[32,2048,128]{2,1,0:T(8,128)(2,1)} async-done(((bf16[1,2048,128]{2,1,0:T(8,128)(2,1)}), bf16[32,2048,128]{2,1,0:T(8,128)(2,1)}) %all-gather.2.cloned.1.call-update) | async-done | bytes 16777232 | tf_op jit(solution)/shard_map/all_gather | solution.py:257
  87.1 34.6 %shard_map.85.w_ref = bf16[4096,4096]{1,0:T(8,128)(2,1)} custom-call(s32[4096]{0:T(1024)} %select_n.124.table_ref, bf16[32,2048,128]{2,1,0:T(8,128)(2,1)} %all-gather.2.cloned.1.call-done.t_ref), custom_call_target="tpu_custom_call" | custom-call | bytes 50331648 | tf_op jit(solution)/shard_map/pallas_call | solution.py:67
  121.7 15.2 %shard_map.86 = f32[64,4096]{1,0:T(8,128)} custom-call(bf16[64,4096]{1,0:T(8,128)(2,1)} %fusion.76.u_ref, bf16[4096,4096]{1,0:T(8,128)(2,1)} %shard_map.85.w_ref), custom_call_target="tpu_custom_call" | custom-call | flops 2147483648 | bytes 33554432 | tf_op jit(solution)/shard_map/pallas_call | solution.py:180
  142.9 10.0 %collective-permute-done = bf16[64,4096]{1,0:T(8,128)(2,1)S(1)} collective-permute-done((bf16[64,4096]{1,0:T(8,128)(2,1)S(1)}, bf16[64,4096]{1,0:T(8,128)(2,1)S(1)}, u32[]{:S(2)}, u32[]{:S(2)}) %collective-permute-start) | collective-permute-done | bytes 524320 | tf_op jit(solution)/shard_map/ppermute | solution.py:16
  154.4 15.2 %shard_map.87 = f32[64,4096]{1,0:T(8,128)} custom-call(bf16[64,4096]{1,0:T(8,128)(2,1)} %get-tuple-element.30.u_ref, bf16[4096,4096]{1,0:T(8,128)(2,1)} %shard_map.85.w_ref), custom_call_target="tpu_custom_call" | custom-call | flops 2147483648 | bytes 33554432 | tf_op jit(solution)/shard_map/pallas_call | solution.py:180
  176.6 9.0 %collective-permute-done.1 = bf16[64,4096]{1,0:T(8,128)(2,1)S(1)} collective-permute-done((bf16[64,4096]{1,0:T(8,128)(2,1)S(1)}, bf16[64,4096]{1,0:T(8,128)(2,1)S(1)}, u32[]{:S(2)}, u32[]{:S(2)}) %collective-permute-start.1) | collective-permute-done | bytes 524320 | tf_op jit(solution)/shard_map/ppermute | solution.py:16
  187.2 15.2 %shard_map.88 = f32[64,4096]{1,0:T(8,128)} custom-call(bf16[64,4096]{1,0:T(8,128)(2,1)} %get-tuple-element.28.u_ref, bf16[4096,4096]{1,0:T(8,128)(2,1)} %shard_map.85.w_ref), custom_call_target="tpu_custom_call" | custom-call | flops 2147483648 | bytes 33554432 | tf_op jit(solution)/shard_map/pallas_call | solution.py:180
  209.4 8.1 %collective-permute-done.2 = bf16[64,4096]{1,0:T(8,128)(2,1)S(1)} collective-permute-done((bf16[64,4096]{1,0:T(8,128)(2,1)S(1)}, bf16[64,4096]{1,0:T(8,128)(2,1)S(1)}, u32[]{:S(2)}, u32[]{:S(2)}) %collective-permute-start.2) | collective-permute-done | bytes 524320 | tf_op jit(solution)/shard_map/ppermute | solution.py:16
  219.0 15.2 %shard_map.89 = f32[64,4096]{1,0:T(8,128)} custom-call(bf16[64,4096]{1,0:T(8,128)(2,1)} %get-tuple-element.26.u_ref, bf16[4096,4096]{1,0:T(8,128)(2,1)} %shard_map.85.w_ref), custom_call_target="tpu_custom_call" | custom-call | flops 2147483648 | bytes 33554432 | tf_op jit(solution)/shard_map/pallas_call | solution.py:180
  236.0 4.3 collective-permute-start.3
  241.4 7.0 %collective-permute-done.3 = bf16[64,4096]{1,0:T(8,128)(2,1)S(1)} collective-permute-done((bf16[64,4096]{1,0:T(8,128)(2,1)S(1)}, bf16[64,4096]{1,0:T(8,128)(2,1)S(1)}, u32[]{:S(2)}, u32[]{:S(2)}) %collective-permute-start.3) | collective-permute-done | bytes 524320 | tf_op jit(solution)/shard_map/ppermute | solution.py:16
  250.0 15.2 %shard_map.96 = f32[5,64,4096]{2,1,0:T(8,128)} fusion(f32[5,64,4096]{2,1,0:T(8,128)} %bitcast_dynamic-update-slice_fusion.1, bf16[64,4096]{1,0:T(8,128)(2,1)} %get-tuple-element.24, bf16[4096,4096]{1,0:T(8,128)(2,1)} %shard_map.85.w_ref), kind=kCustom, calls=%fused_computation.111 | custom fusion | flops 2147483648 | bytes 35127296 | tf_op jit(solution)/shard_map/pallas_call | solution.py:180
  267.9 17.2 %shard_map.90 = f32[64,4096]{1,0:T(8,128)} custom-call(bf16[64,4096]{1,0:T(8,128)(2,1)} %get-tuple-element.58.g_ref, bf16[4096,4096]{1,0:T(8,128)(2,1)} %shard_map.85.w_ref), custom_call_target="tpu_custom_call" | custom-call | flops 2147483648 | bytes 33554432 | tf_op jit(solution)/shard_map/pallas_call | solution.py:200
  290.4 9.5 %collective-permute-done.4 = bf16[64,4096]{1,0:T(8,128)(2,1)S(1)} collective-permute-done((bf16[64,4096]{1,0:T(8,128)(2,1)S(1)}, bf16[64,4096]{1,0:T(8,128)(2,1)S(1)}, u32[]{:S(2)}, u32[]{:S(2)}) %collective-permute-start.4) | collective-permute-done | bytes 524320 | tf_op jit(solution)/shard_map/ppermute | solution.py:16
  304.7 17.1 %shard_map.91 = f32[64,4096]{1,0:T(8,128)} custom-call(bf16[64,4096]{1,0:T(8,128)(2,1)} %get-tuple-element.52.g_ref, bf16[4096,4096]{1,0:T(8,128)(2,1)} %shard_map.85.w_ref), custom_call_target="tpu_custom_call" | custom-call | flops 2147483648 | bytes 33554432 | tf_op jit(solution)/shard_map/pallas_call | solution.py:200
  326.4 9.5 %collective-permute-done.5 = bf16[64,4096]{1,0:T(8,128)(2,1)S(1)} collective-permute-done((bf16[64,4096]{1,0:T(8,128)(2,1)S(1)}, bf16[64,4096]{1,0:T(8,128)(2,1)S(1)}, u32[]{:S(2)}, u32[]{:S(2)}) %collective-permute-start.5) | collective-permute-done | bytes 524320 | tf_op jit(solution)/shard_map/ppermute | solution.py:16
  339.4 17.1 %shard_map.92 = f32[64,4096]{1,0:T(8,128)} custom-call(bf16[64,4096]{1,0:T(8,128)(2,1)} %get-tuple-element.54.g_ref, bf16[4096,4096]{1,0:T(8,128)(2,1)} %shard_map.85.w_ref), custom_call_target="tpu_custom_call" | custom-call | flops 2147483648 | bytes 33554432 | tf_op jit(solution)/shard_map/pallas_call | solution.py:200
  361.1 8.6 %collective-permute-done.6 = bf16[64,4096]{1,0:T(8,128)(2,1)S(1)} collective-permute-done((bf16[64,4096]{1,0:T(8,128)(2,1)S(1)}, bf16[64,4096]{1,0:T(8,128)(2,1)S(1)}, u32[]{:S(2)}, u32[]{:S(2)}) %collective-permute-start.6) | collective-permute-done | bytes 524320 | tf_op jit(solution)/shard_map/ppermute | solution.py:16
  373.1 17.1 %shard_map.93 = f32[64,4096]{1,0:T(8,128)} custom-call(bf16[64,4096]{1,0:T(8,128)(2,1)} %get-tuple-element.56.g_ref, bf16[4096,4096]{1,0:T(8,128)(2,1)} %shard_map.85.w_ref), custom_call_target="tpu_custom_call" | custom-call | flops 2147483648 | bytes 33554432 | tf_op jit(solution)/shard_map/pallas_call | solution.py:200
  396.6 7.9 %collective-permute-done.7 = bf16[64,4096]{1,0:T(8,128)(2,1)S(1)} collective-permute-done((bf16[64,4096]{1,0:T(8,128)(2,1)}, bf16[64,4096]{1,0:T(8,128)(2,1)S(1)}, u32[]{:S(2)}, u32[]{:S(2)}) %collective-permute-start.7) | collective-permute-done | bytes 524320 | tf_op jit(solution)/shard_map/ppermute | solution.py:16
  406.9 15.9 %fusion.g_ref = bf16[4096,4096]{1,0:T(8,128)(2,1)} fusion(bf16[5,64,4096]{2,1,0:T(8,128)(2,1)} %bitcast_dynamic-update-slice_fusion.5, s32[]{:T(128)S(6)} %select_n.138, bf16[5,64,4096]{2,1,0:T(8,128)(2,1)} %get-tuple-element.23, s32[]{:T(128)S(6)} %select_n.129), kind=kOutput, calls=%fused_computation.1 | convolution fusion | flops 4328521728 | bytes 35651592 | tf_op jit(solution)/shard_map/dot_general | solution.py:297
  422.8 31.4 %shard_map.94 = bf16[32,2048,128]{2,1,0:T(8,128)(2,1)} custom-call(s32[2048]{0:T(1024)} %reshape_squeeze.3.table_ref, bf16[4096,4096]{1,0:T(8,128)(2,1)} %fusion.g_ref), custom_call_target="tpu_custom_call" | custom-call | bytes 50331648 | tf_op jit(solution)/shard_map/pallas_call | solution.py:88
  454.4 120.5 %reduce-scatter.2.cloned.1.call-done = bf16[1,2048,128]{2,1,0:T(8,128)(2,1)} async-done(((bf16[32,2048,128]{2,1,0:T(8,128)(2,1)}), bf16[1,2048,128]{2,1,0:T(8,128)(2,1)}) %reduce-scatter.2.cloned.1.call-update) | async-done | bytes 524304 | tf_op jit(solution)/shard_map/reduce_scatter | solution.py:306
  581.1 12.1 %shard_map.95 = f32[8,128]{1,0:T(8,128)} custom-call(f32[8,128]{1,0:T(8,128)} %scatter.4.x_ref), custom_call_target="tpu_custom_call" | custom-call | tf_op jit(solution)/shard_map/pallas_call | solution.py:146
  (132 shorter events, 85.6 us)
Async XLA Ops:
  7.2 4.2 copy-start.19
  7.2 4.5 copy-start.20
  7.2 79.9 %all-gather.2.cloned.1.call-start = ((), (), s32[]{:S(2)}) async-start(), calls=%async_computation.1 | async-start | bytes 17301504 | tf_op jit(solution)/shard_map/all_gather | solution.py:257
  9.4 565.5 %reduce-scatter.2.cloned.1.call-start = ((), (), s32[]{:S(2)}) async-start(), calls=%async_computation.2 | async-start | bytes 17301504 | tf_op jit(solution)/shard_map/reduce_scatter | solution.py:306
  11.6 2.7 copy-start.9
  136.9 5.0 copy-start.7
  136.9 16.0 %copy-start = (bf16[2,32,4096]{2,1,0:T(8,128)(2,1)S(1)}, bf16[2,32,4096]{2,1,0:T(8,128)(2,1)}, u32[]{:S(2)}) copy-start(bf16[2,32,4096]{2,1,0:T(8,128)(2,1)} %slice.42) | copy-start | bytes 1572868
  138.7 14.2 %collective-permute-start = (bf16[64,4096]{1,0:T(8,128)(2,1)S(1)}, bf16[64,4096]{1,0:T(8,128)(2,1)S(1)}, u32[]{:S(2)}, u32[]{:S(2)}) collective-permute-start(bf16[64,4096]{1,0:T(8,128)(2,1)S(1)} %fusion.77), channel_id=1, source_target_pairs={{0,32},{32,64},{64,96},{1,33},{33,65},{65,97},{2,34},{34,66},{66,9... | collective-permute-start | bytes 1572872 | tf_op jit(solution)/shard_map/ppermute | solution.py:16
  169.6 5.9 copy-start.4
  169.6 16.0 %copy-start.1 = (bf16[2,32,4096]{2,1,0:T(8,128)(2,1)S(1)}, bf16[2,32,4096]{2,1,0:T(8,128)(2,1)}, u32[]{:S(2)}) copy-start(bf16[2,32,4096]{2,1,0:T(8,128)(2,1)} %slice.42) | copy-start | bytes 1572868
  171.4 14.2 %collective-permute-start.1 = (bf16[64,4096]{1,0:T(8,128)(2,1)S(1)}, bf16[64,4096]{1,0:T(8,128)(2,1)S(1)}, u32[]{:S(2)}, u32[]{:S(2)}) collective-permute-start(bf16[64,4096]{1,0:T(8,128)(2,1)S(1)} %fusion.37), channel_id=1, source_target_pairs={{0,32},{32,64},{64,96},{1,33},{33,65},{65,97},{2,34},{34,66},{66,9... | collective-permute-start | bytes 1572872 | tf_op jit(solution)/shard_map/ppermute | solution.py:16
  202.4 5.9 copy-start.5
  202.4 15.1 %copy-start.2 = (bf16[2,32,4096]{2,1,0:T(8,128)(2,1)S(1)}, bf16[2,32,4096]{2,1,0:T(8,128)(2,1)}, u32[]{:S(2)}) copy-start(bf16[2,32,4096]{2,1,0:T(8,128)(2,1)} %slice.42) | copy-start | bytes 1572868
  204.2 13.3 %collective-permute-start.2 = (bf16[64,4096]{1,0:T(8,128)(2,1)S(1)}, bf16[64,4096]{1,0:T(8,128)(2,1)S(1)}, u32[]{:S(2)}, u32[]{:S(2)}) collective-permute-start(bf16[64,4096]{1,0:T(8,128)(2,1)S(1)} %fusion.40), channel_id=1, source_target_pairs={{0,32},{32,64},{64,96},{1,33},{33,65},{65,97},{2,34},{34,66},{66,9... | collective-permute-start | bytes 1572872 | tf_op jit(solution)/shard_map/ppermute | solution.py:16
  234.2 6.1 %copy-start.6 = (f32[64,4096]{1,0:T(8,128)S(1)}, f32[64,4096]{1,0:T(8,128)}, u32[]{:S(2)}) copy-start(f32[64,4096]{1,0:T(8,128)} %shard_map.89) | copy-start | bytes 3145732
  234.2 14.2 %copy-start.3 = (bf16[2,32,4096]{2,1,0:T(8,128)(2,1)S(1)}, bf16[2,32,4096]{2,1,0:T(8,128)(2,1)}, u32[]{:S(2)}) copy-start(bf16[2,32,4096]{2,1,0:T(8,128)(2,1)} %slice.42) | copy-start | bytes 1572868
  236.0 12.4 %collective-permute-start.3 = (bf16[64,4096]{1,0:T(8,128)(2,1)S(1)}, bf16[64,4096]{1,0:T(8,128)(2,1)S(1)}, u32[]{:S(2)}, u32[]{:S(2)}) collective-permute-start(bf16[64,4096]{1,0:T(8,128)(2,1)S(1)} %fusion.43), channel_id=1, source_target_pairs={{0,32},{32,64},{64,96},{1,33},{33,65},{65,97},{2,34},{34,66},{66,9... | collective-permute-start | bytes 1572872 | tf_op jit(solution)/shard_map/ppermute | solution.py:16
  285.1 2.0 copy-start.14
  285.1 3.7 copy-start.13
  287.5 12.5 %collective-permute-start.4 = (bf16[64,4096]{1,0:T(8,128)(2,1)S(1)}, bf16[64,4096]{1,0:T(8,128)(2,1)S(1)}, u32[]{:S(2)}, u32[]{:S(2)}) collective-permute-start(bf16[64,4096]{1,0:T(8,128)(2,1)S(1)} %fusion.22), channel_id=1, source_target_pairs={{32,0},{64,32},{96,64},{33,1},{65,33},{97,65},{34,2},{66,34},{98,6... | collective-permute-start | bytes 1572872 | tf_op jit(solution)/shard_map/ppermute | solution.py:16
  325.1 10.8 %collective-permute-start.5 = (bf16[64,4096]{1,0:T(8,128)(2,1)S(1)}, bf16[64,4096]{1,0:T(8,128)(2,1)S(1)}, u32[]{:S(2)}, u32[]{:S(2)}) collective-permute-start(bf16[64,4096]{1,0:T(8,128)(2,1)S(1)} %fusion.26), channel_id=1, source_target_pairs={{32,0},{64,32},{96,64},{33,1},{65,33},{97,65},{34,2},{66,34},{98,6... | collective-permute-start | bytes 1572872 | tf_op jit(solution)/shard_map/ppermute | solution.py:16
  359.8 9.9 %collective-permute-start.6 = (bf16[64,4096]{1,0:T(8,128)(2,1)S(1)}, bf16[64,4096]{1,0:T(8,128)(2,1)S(1)}, u32[]{:S(2)}, u32[]{:S(2)}) collective-permute-start(bf16[64,4096]{1,0:T(8,128)(2,1)S(1)} %fusion.28), channel_id=1, source_target_pairs={{32,0},{64,32},{96,64},{33,1},{65,33},{97,65},{34,2},{66,34},{98,6... | collective-permute-start | bytes 1572872 | tf_op jit(solution)/shard_map/ppermute | solution.py:16
  394.3 10.1 %collective-permute-start.7 = (bf16[64,4096]{1,0:T(8,128)(2,1)}, bf16[64,4096]{1,0:T(8,128)(2,1)S(1)}, u32[]{:S(2)}, u32[]{:S(2)}) collective-permute-start(bf16[64,4096]{1,0:T(8,128)(2,1)} %fusion.30), channel_id=1, source_target_pairs={{32,0},{64,32},{96,64},{33,1},{65,33},{97,65},{34,2},{66,34},{98,6... | collective-permute-start | bytes 1572872 | tf_op jit(solution)/shard_map/ppermute | solution.py:16
  454.2 121.9 %copy-start.18 = (bf16[1,2,64,2048]{3,2,1,0:T(8,128)(2,1)S(1)}, bf16[1,2,64,2048]{3,2,1,0:T(8,128)(2,1)}, u32[]{:S(2)}) copy-start(bf16[1,2,64,2048]{3,2,1,0:T(8,128)(2,1)} %param.10) | copy-start | bytes 1572868
  (8 other events, 9.4 us)
Sparse Core Ops, SparseCore 0:
  10.9 76.2 all-gather.1
  454.3 120.4 reduce-scatter.1

commit v8 on v5

--- a/solution.py
+++ b/solution.py
@@ -21,36 +21,45 @@
 
 
 def expand_kernel(table_ref, t_ref, o_ref):
-    p = pl.program_id(0)
+    per_step = t_ref.shape[0]
     block = 64
     blocks = o_ref.shape[0] // block
-    lane = lax.broadcasted_iota(jnp.int32, (block, o_ref.shape[1]), 1)
-    for r in range(blocks):
-        k0 = table_ref[(2 * p) * blocks + r]
-        k1 = table_ref[(2 * p + 1) * blocks + r]
-        s0 = pl.multiple_of(jnp.maximum(k0, 0) * block, block)
-        s1 = pl.multiple_of(jnp.maximum(k1, 0) * block, block)
-        t0 = t_ref[pl.ds(s0, block), :]
-        t1 = t_ref[pl.ds(s1, block), :]
-        zero = jnp.zeros_like(t0)
-        t0 = jnp.where(k0 >= 0, t0, zero)
-        t1 = jnp.where(k1 >= 0, t1, zero)
-        o_ref[r * block:(r + 1) * block, :] = jnp.where(lane < block, t0, t1)
+    lane = lax.broadcasted_iota(jnp.int32, (block, 2 * block), 1)
+    for pp in range(per_step):
+        p = pl.program_id(0) * per_step + pp
+        for r in range(blocks):
+            k0 = table_ref[(2 * p) * blocks + r]
+            k1 = table_ref[(2 * p + 1) * blocks + r]
+            s0 = pl.multiple_of(jnp.maximum(k0, 0) * block, block)
+            s1 = pl.multiple_of(jnp.maximum(k1, 0) * block, block)
+            t0 = t_ref[pp, pl.ds(s0, block), :]
+            t1 = t_ref[pp, pl.ds(s1, block), :]
+            zero = jnp.zeros_like(t0)
+            t0 = jnp.where(k0 >= 0, t0, zero)
+            t1 = jnp.where(k1 >= 0, t1, zero)
+            o_ref[r * block:(r + 1) * block, pp * 2 * block:(pp + 1) * 2 * block] = jnp.where(
+                lane < block, t0, t1
+            )
 
 
 def pack_kernel(table_ref, g_ref, o_ref):
-    p = pl.program_id(0)
+    per_step = o_ref.shape[0]
     block = 64
     live_count = o_ref.shape[1] // block
-    lane = lax.broadcasted_iota(jnp.int32, (block, o_ref.shape[2]), 1)
-    for k in range(live_count):
-        r0 = table_ref[(2 * p) * live_count + k]
-        r1 = table_ref[(2 * p + 1) * live_count + k]
-        s0 = pl.multiple_of(r0 * block, block)
-        s1 = pl.multiple_of(r1 * block, block)
-        t0 = g_ref[pl.ds(s0, block), :]
-        t1 = g_ref[pl.ds(s1, block), :]
-        o_ref[0, k * block:(k + 1) * block, :] = jnp.where(lane < block, t0, t1)
+    lane = lax.broadcasted_iota(jnp.int32, (block, 2 * block), 1)
+    for pp in range(per_step):
+        p = pl.program_id(0) * per_step + pp
+        for k in range(live_count):
+            r0 = table_ref[(2 * p) * live_count + k]
+            r1 = table_ref[(2 * p + 1) * live_count + k]
+            s0 = pl.multiple_of(r0 * block, block)
+            s1 = pl.multiple_of(r1 * block, block)
+            t0 = g_ref[pl.ds(s0, block), pp * 2 * block:(pp + 1) * 2 * block]
+            t1 = g_ref[pl.ds(s1, block), pp * 2 * block:(pp + 1) * 2 * block]
+            o_ref[pp, k * block:(k + 1) * block, :] = jnp.where(lane < block, t0, t1)
+
+
+PAIRS_PER_STEP = 2
 
 
 def expand_dense(paired_weights, live_index):
@@ -69,9 +78,9 @@
         out_shape=jax.ShapeDtypeStruct((features, features), paired_weights.dtype),
         grid_spec=pltpu.PrefetchScalarGridSpec(
             num_scalar_prefetch=1,
-            grid=(pair_count,),
-            in_specs=[pl.BlockSpec((None, wide, two_blocks), lambda p, tbl: (p, 0, 0))],
-            out_specs=pl.BlockSpec((features, two_blocks), lambda p, tbl: (0, p)),
+            grid=(pair_count // PAIRS_PER_STEP,),
+            in_specs=[pl.BlockSpec((PAIRS_PER_STEP, wide, two_blocks), lambda q, tbl: (q, 0, 0))],
+            out_specs=pl.BlockSpec((features, PAIRS_PER_STEP * two_blocks), lambda q, tbl: (0, q)),
         ),
         cost_estimate=pl.CostEstimate(
             flops=0, transcendentals=0, bytes_accessed=3 * pair_count * wide * two_blocks * 2
@@ -90,9 +99,11 @@
         out_shape=jax.ShapeDtypeStruct((pair_count, wide, 2 * block_size), dense_grad.dtype),
         grid_spec=pltpu.PrefetchScalarGridSpec(
             num_scalar_prefetch=1,
-            grid=(pair_count,),
-            in_specs=[pl.BlockSpec((features, 2 * block_size), lambda p, tbl: (0, p))],
-            out_specs=pl.BlockSpec((1, wide, 2 * block_size), lambda p, tbl: (p, 0, 0)),
+            grid=(pair_count // PAIRS_PER_STEP,),
+            in_specs=[
+                pl.BlockSpec((features, PAIRS_PER_STEP * 2 * block_size), lambda q, tbl: (0, q))
+            ],
+            out_specs=pl.BlockSpec((PAIRS_PER_STEP, wide, 2 * block_size), lambda q, tbl: (q, 0, 0)),
         ),
         cost_estimate=pl.CostEstimate(
             flops=0, transcendentals=0, bytes_accessed=3 * pair_count * wide * 2 * block_size * 2

time: 578 us -> 562 us (0.972)
  Pallas kernels: 78.1 us -> 64.4 us
    pallas_call x1, Pallas kernels: 31.4 us -> 23.9 us  [pack_dense(): pl.pallas_call(pack_kernel, out_shape=jax.ShapeDtypeStruct((pair_count, w...]
    pallas_call x1, Pallas kernels: 34.6 us -> 28.4 us  [expand_dense(): pl.pallas_call(expand_kernel, out_shape=jax.ShapeDtypeStruct((features, f...]
where the time goes in v8:
time: 562 us; the launch traced here: 553 us
  waiting for transfers between devices  261 us (46%)
  matrix products  147 us (26%)
  Pallas kernels  64.4 us (11%)
  other arithmetic  32.2 us (6%)
  starting transfers between devices  22 us (4%)
  between operations  15.4 us (3%)
  local copies, waits for them, and re-layouts  11.2 us (2%)
    reduce_scatter x1, waiting for transfers between devices, local(): own_grad = lax.psum_scatter(partial, 'dp', scatter_dimension=0, tiled=True)  120 us
    all_gather x1, waiting for transfers between devices, local(): paired_weights = lax.all_gather(own_pair, 'dp', axis=0, tiled=True)  72.5 us
    dot_general x5, matrix products, layer_forward(): pre_act = jnp.dot(normed, dense_w, preferred_element_type=jnp.float32)  68.4 us
    ppermute x8, waiting for transfers between devices, shifted(): lax.ppermute(value, axis, [(source, source + steps) for source in range(l...  68 us
    dot_general x4, matrix products, layer_backward(): lax.dot_general(grad_pre, dense_w, (((1,), (1,)), ((), ())), preferred_el...  62.9 us
    pallas_call x1, Pallas kernels, expand_dense(): pl.pallas_call(expand_kernel, out_shape=jax.ShapeDtypeStruct((features, f...  28.4 us
    pallas_call x1, Pallas kernels, pack_dense(): pl.pallas_call(pack_kernel, out_shape=jax.ShapeDtypeStruct((pair_count, w...  23.9 us
    ppermute x8, starting transfers between devices, shifted(): lax.ppermute(value, axis, [(source, source + steps) for source in range(l...  21.9 us
  transfers between devices with their start and end apart: 10, of which 10 were waited for; matrix products, arithmetic and copies ran while one was open for 2% of the time, Pallas kernels for 0%

profile of v8, /device:TPU:1, one launch (start us, length us, event | category | flops | bytes accessed | tf_op | source)
XLA Modules:
  0.0 553.4 jit_solution(16498149342736187256)
XLA Ops:
  14.6 72.5 %all-gather.2.cloned.1.call-done.t_ref = bf16[32,2048,128]{2,1,0:T(8,128)(2,1)} async-done(((bf16[1,2048,128]{2,1,0:T(8,128)(2,1)}), bf16[32,2048,128]{2,1,0:T(8,128)(2,1)}) %all-gather.2.cloned.1.call-update) | async-done | bytes 16777232 | tf_op jit(solution)/shard_map/all_gather | solution.py:214
  87.1 28.4 %shard_map.85 = bf16[4096,4096]{1,0:T(8,128)(2,1)} custom-call(s32[4096]{0:T(1024)} %select_n.124.table_ref, bf16[32,2048,128]{2,1,0:T(8,128)(2,1)} %all-gather.2.cloned.1.call-done.t_ref), custom_call_target="tpu_custom_call" | custom-call | bytes 50331648 | tf_op jit(solution)/shard_map/pallas_call | solution.py:76
  115.5 13.6 %bitcast_dynamic-update-slice_fusion.3 = (f32[5,64,4096]{2,1,0:T(8,128)S(1)}, f32[64,4096]{1,0:T(8,128)S(1)}) fusion(bf16[64,4096]{1,0:T(8,128)(2,1)S(1)} %fusion.77, bf16[4096,4096]{1,0:T(8,128)(2,1)} %shard_map.85), kind=kOutput, calls=%fused_computation.116 | convolution fusion | flops 2147483648 | bytes 36175872 | tf_op jit(solution)/shard_map/dot_general | solution.py:176
  134.8 8.8 %collective-permute-done = bf16[64,4096]{1,0:T(8,128)(2,1)S(1)} collective-permute-done((bf16[64,4096]{1,0:T(8,128)(2,1)S(1)}, bf16[64,4096]{1,0:T(8,128)(2,1)S(1)}, u32[]{:S(2)}, u32[]{:S(2)}) %collective-permute-start) | collective-permute-done | bytes 524320 | tf_op jit(solution)/shard_map/ppermute | solution.py:16
  143.9 13.7 %bitcast_dynamic-update-slice_fusion.2 = (f32[5,64,4096]{2,1,0:T(8,128)S(1)}, f32[64,4096]{1,0:T(8,128)S(1)}) fusion(f32[5,64,4096]{2,1,0:T(8,128)S(1)} %get-tuple-element.47, bf16[4096,4096]{1,0:T(8,128)(2,1)} %shard_map.85, bf16[64,4096]{1,0:T(8,128)(2,1)S(1)} %get-tuple-element.30, f32[64]{0:T(128)S(1)} %add_rsqrt_fusion.8), kind=kOutput, calls=%fused_computation.115 | convolution fusion | flops 2148270080 | bytes 36176384 | tf_op jit(solution)/shard_map/dot_general | solution.py:176
  163.3 8.9 %collective-permute-done.1 = bf16[64,4096]{1,0:T(8,128)(2,1)S(1)} collective-permute-done((bf16[64,4096]{1,0:T(8,128)(2,1)S(1)}, bf16[64,4096]{1,0:T(8,128)(2,1)S(1)}, u32[]{:S(2)}, u32[]{:S(2)}) %collective-permute-start.1) | collective-permute-done | bytes 524320 | tf_op jit(solution)/shard_map/ppermute | solution.py:16
  172.5 13.7 %bitcast_dynamic-update-slice_fusion.1 = (f32[5,64,4096]{2,1,0:T(8,128)S(1)}, f32[64,4096]{1,0:T(8,128)S(1)}) fusion(f32[5,64,4096]{2,1,0:T(8,128)S(1)} %get-tuple-element.49, bf16[4096,4096]{1,0:T(8,128)(2,1)} %shard_map.85, bf16[64,4096]{1,0:T(8,128)(2,1)S(1)} %get-tuple-element.28, f32[64]{0:T(128)S(1)} %add_rsqrt_fusion.7), kind=kOutput, calls=%fused_computation.114 | convolution fusion | flops 2148270080 | bytes 36176384 | tf_op jit(solution)/shard_map/dot_general | solution.py:176
  191.6 8.2 %collective-permute-done.2 = bf16[64,4096]{1,0:T(8,128)(2,1)S(1)} collective-permute-done((bf16[64,4096]{1,0:T(8,128)(2,1)S(1)}, bf16[64,4096]{1,0:T(8,128)(2,1)S(1)}, u32[]{:S(2)}, u32[]{:S(2)}) %collective-permute-start.2) | collective-permute-done | bytes 524320 | tf_op jit(solution)/shard_map/ppermute | solution.py:16
  200.1 13.7 %bitcast_dynamic-update-slice_fusion = (f32[5,64,4096]{2,1,0:T(8,128)S(1)}, f32[64,4096]{1,0:T(8,128)S(1)}) fusion(f32[5,64,4096]{2,1,0:T(8,128)S(1)} %get-tuple-element.51, bf16[4096,4096]{1,0:T(8,128)(2,1)} %shard_map.85, bf16[64,4096]{1,0:T(8,128)(2,1)S(1)} %get-tuple-element.26, f32[64]{0:T(128)S(1)} %add_rsqrt_fusion.6), kind=kOutput, calls=%fused_computation.113 | convolution fusion | flops 2148270080 | bytes 36176384 | tf_op jit(solution)/shard_map/dot_general | solution.py:176
  214.1 4.7 collective-permute-start.3
  219.8 6.8 %collective-permute-done.3 = bf16[64,4096]{1,0:T(8,128)(2,1)S(1)} collective-permute-done((bf16[64,4096]{1,0:T(8,128)(2,1)S(1)}, bf16[64,4096]{1,0:T(8,128)(2,1)S(1)}, u32[]{:S(2)}, u32[]{:S(2)}) %collective-permute-start.3) | collective-permute-done | bytes 524320 | tf_op jit(solution)/shard_map/ppermute | solution.py:16
  226.9 13.8 %fusion.1 = f32[5,64,4096]{2,1,0:T(8,128)S(1)} fusion(f32[5,64,4096]{2,1,0:T(8,128)S(1)} %get-tuple-element.53, bf16[4096,4096]{1,0:T(8,128)(2,1)} %shard_map.85, bf16[64,4096]{1,0:T(8,128)(2,1)S(1)} %get-tuple-element.24, f32[64]{0:T(128)S(1)} %add_rsqrt_fusion.5), kind=kOutput, calls=%fused_computation.3 | convolution fusion | flops 2148270080 | bytes 35127808 | tf_op jit(solution)/shard_map/dot_general | solution.py:176
  243.8 15.9 %fusion.35 = (f32[64]{0:T(128)S(1)}, f32[64]{0:T(128)S(1)}, f32[64]{0:T(128)S(1)}, f32[64]{0:T(128)S(1)}, f32[64,4096]{1,0:T(8,128)S(1)}) fusion(bf16[5,64,4096]{2,1,0:T(8,128)(2,1)S(1)} %get-tuple-element.38, s32[]{:T(128)S(6)} %dynamic_slice.69, f32[64]{0:T(128)S(1)} %add_rsqrt_fusion.4, s32[]{:T(128)S(6)} %dynamic_slice.60, s32[]{:T(128)S(6)} %dynamic_slice.66, ...), kind=kOutput, calls=%fused_computation.63 | convolution fusion | flops 2150891520 | bytes 37225744 | tf_op jit(solution)/shard_map/dot_general | solution.py:187
  264.1 9.6 %collective-permute-done.4 = bf16[64,4096]{1,0:T(8,128)(2,1)S(1)} collective-permute-done((bf16[64,4096]{1,0:T(8,128)(2,1)S(1)}, bf16[64,4096]{1,0:T(8,128)(2,1)S(1)}, u32[]{:S(2)}, u32[]{:S(2)}) %collective-permute-start.4) | collective-permute-done | bytes 524320 | tf_op jit(solution)/shard_map/ppermute | solution.py:16
  276.9 15.7 %fusion.16 = (f32[64]{0:T(128)S(1)}, f32[64,4096]{1,0:T(8,128)S(1)}) fusion(f32[64]{0:T(128)S(1)} %add_rsqrt_fusion.3, bf16[5,64,4096]{2,1,0:T(8,128)(2,1)S(1)} %get-tuple-element.38, s32[]{:T(128)S(6)} %dynamic_slice.63, bf16[64,4096]{1,0:T(8,128)(2,1)S(1)} %get-tuple-element.57, bf16[4096,4096]{1,0:T(8,128)(2,1)} %shard_map.85), kind=kOutput, calls=%fused_computation.44 | convolution fusion | flops 2148532224 | bytes 35652100 | tf_op jit(solution)/shard_map/dot_general | solution.py:187
  294.4 9.3 %collective-permute-done.5 = bf16[64,4096]{1,0:T(8,128)(2,1)S(1)} collective-permute-done((bf16[64,4096]{1,0:T(8,128)(2,1)S(1)}, bf16[64,4096]{1,0:T(8,128)(2,1)S(1)}, u32[]{:S(2)}, u32[]{:S(2)}) %collective-permute-start.5) | collective-permute-done | bytes 524320 | tf_op jit(solution)/shard_map/ppermute | solution.py:16
  306.2 15.7 %fusion.13 = (f32[64]{0:T(128)S(1)}, f32[64,4096]{1,0:T(8,128)S(1)}) fusion(f32[64]{0:T(128)S(1)} %add_rsqrt_fusion.2, bf16[5,64,4096]{2,1,0:T(8,128)(2,1)S(1)} %get-tuple-element.38, s32[]{:T(128)S(6)} %dynamic_slice.66, bf16[64,4096]{1,0:T(8,128)(2,1)S(1)} %get-tuple-element.61, bf16[4096,4096]{1,0:T(8,128)(2,1)} %shard_map.85), kind=kOutput, calls=%fused_computation.41 | convolution fusion | flops 2148532224 | bytes 35652100 | tf_op jit(solution)/shard_map/dot_general | solution.py:187
  323.6 8.6 %collective-permute-done.6 = bf16[64,4096]{1,0:T(8,128)(2,1)S(1)} collective-permute-done((bf16[64,4096]{1,0:T(8,128)(2,1)S(1)}, bf16[64,4096]{1,0:T(8,128)(2,1)S(1)}, u32[]{:S(2)}, u32[]{:S(2)}) %collective-permute-start.6) | collective-permute-done | bytes 524320 | tf_op jit(solution)/shard_map/ppermute | solution.py:16
  334.7 15.7 %fusion.10 = (f32[64]{0:T(128)S(1)}, f32[64,4096]{1,0:T(8,128)S(1)}) fusion(f32[64]{0:T(128)S(1)} %add_rsqrt_fusion.1, bf16[5,64,4096]{2,1,0:T(8,128)(2,1)S(1)} %get-tuple-element.38, s32[]{:T(128)S(6)} %dynamic_slice.69, bf16[64,4096]{1,0:T(8,128)(2,1)S(1)} %get-tuple-element.65, bf16[4096,4096]{1,0:T(8,128)(2,1)} %shard_map.85), kind=kOutput, calls=%fused_computation.38 | convolution fusion | flops 2148532224 | bytes 35652100 | tf_op jit(solution)/shard_map/dot_general | solution.py:187
  353.8 7.9 %collective-permute-done.7 = bf16[64,4096]{1,0:T(8,128)(2,1)S(1)} collective-permute-done((bf16[64,4096]{1,0:T(8,128)(2,1)}, bf16[64,4096]{1,0:T(8,128)(2,1)S(1)}, u32[]{:S(2)}, u32[]{:S(2)}) %collective-permute-start.7) | collective-permute-done | bytes 524320 | tf_op jit(solution)/shard_map/ppermute | solution.py:16
  364.2 15.9 %fusion.g_ref = bf16[4096,4096]{1,0:T(8,128)(2,1)} fusion(bf16[5,64,4096]{2,1,0:T(8,128)(2,1)} %bitcast_dynamic-update-slice_fusion.4, s32[]{:T(128)S(6)} %select_n.138, bf16[5,64,4096]{2,1,0:T(8,128)(2,1)} %get-tuple-element.37, s32[]{:T(128)S(6)} %select_n.129), kind=kOutput, calls=%fused_computation.1 | convolution fusion | flops 4328521728 | bytes 35651592 | tf_op jit(solution)/shard_map/dot_general | solution.py:254
  380.1 23.9 %shard_map.86 = bf16[32,2048,128]{2,1,0:T(8,128)(2,1)} custom-call(s32[2048]{0:T(1024)} %reshape_squeeze.3.table_ref, bf16[4096,4096]{1,0:T(8,128)(2,1)} %fusion.g_ref), custom_call_target="tpu_custom_call" | custom-call | bytes 50331648 | tf_op jit(solution)/shard_map/pallas_call | solution.py:97
  404.1 120.4 %reduce-scatter.2.cloned.1.call-done = bf16[1,2048,128]{2,1,0:T(8,128)(2,1)} async-done(((bf16[32,2048,128]{2,1,0:T(8,128)(2,1)}), bf16[1,2048,128]{2,1,0:T(8,128)(2,1)}) %reduce-scatter.2.cloned.1.call-update) | async-done | bytes 524304 | tf_op jit(solution)/shard_map/reduce_scatter | solution.py:263
  530.8 12.2 %shard_map.87 = f32[8,128]{1,0:T(8,128)} custom-call(f32[8,128]{1,0:T(8,128)} %scatter.4.x_ref), custom_call_target="tpu_custom_call" | custom-call | tf_op jit(solution)/shard_map/pallas_call | solution.py:157
  (100 shorter events, 60.7 us)
Async XLA Ops:
  7.2 4.2 copy-start.7
  7.2 4.5 copy-start.8
  7.2 6.3 %copy-start.4 = (bf16[4,32,4096]{2,1,0:T(8,128)(2,1)S(1)}, bf16[4,32,4096]{2,1,0:T(8,128)(2,1)}, u32[]{:S(2)}) copy-start(bf16[4,32,4096]{2,1,0:T(8,128)(2,1)} %param.9) | copy-start | bytes 3145732
  7.2 79.9 %all-gather.2.cloned.1.call-start = ((), (), s32[]{:S(2)}) async-start(), calls=%async_computation.1 | async-start | bytes 17301504 | tf_op jit(solution)/shard_map/all_gather | solution.py:214
  9.4 515.1 %reduce-scatter.2.cloned.1.call-start = ((), (), s32[]{:S(2)}) async-start(), calls=%async_computation.2 | async-start | bytes 17301504 | tf_op jit(solution)/shard_map/reduce_scatter | solution.py:263
  11.6 117.5 %copy-start.2 = (bf16[2,32,4096]{2,1,0:T(8,128)(2,1)}, bf16[2,32,4096]{2,1,0:T(8,128)(2,1)S(1)}, u32[]{:S(2)}) copy-start(bf16[2,32,4096]{2,1,0:T(8,128)(2,1)S(1)} %get-tuple-element.32) | copy-start | bytes 1572868
  129.1 14.5 %copy-start = (bf16[2,32,4096]{2,1,0:T(8,128)(2,1)S(1)}, bf16[2,32,4096]{2,1,0:T(8,128)(2,1)}, u32[]{:S(2)}) copy-start(bf16[2,32,4096]{2,1,0:T(8,128)(2,1)} %slice.42) | copy-start | bytes 1572868
  129.4 14.2 %collective-permute-start = (bf16[64,4096]{1,0:T(8,128)(2,1)S(1)}, bf16[64,4096]{1,0:T(8,128)(2,1)S(1)}, u32[]{:S(2)}, u32[]{:S(2)}) collective-permute-start(bf16[64,4096]{1,0:T(8,128)(2,1)S(1)} %fusion.78), channel_id=1, source_target_pairs={{0,32},{32,64},{64,96},{1,33},{33,65},{65,97},{2,34},{34,66},{66,9... | collective-permute-start | bytes 1572872 | tf_op jit(solution)/shard_map/ppermute | solution.py:16
  157.9 14.3 %collective-permute-start.1 = (bf16[64,4096]{1,0:T(8,128)(2,1)S(1)}, bf16[64,4096]{1,0:T(8,128)(2,1)S(1)}, u32[]{:S(2)}, u32[]{:S(2)}) collective-permute-start(bf16[64,4096]{1,0:T(8,128)(2,1)S(1)} %fusion.38), channel_id=1, source_target_pairs={{0,32},{32,64},{64,96},{1,33},{33,65},{65,97},{2,34},{34,66},{66,9... | collective-permute-start | bytes 1572872 | tf_op jit(solution)/shard_map/ppermute | solution.py:16
  186.5 13.3 %collective-permute-start.2 = (bf16[64,4096]{1,0:T(8,128)(2,1)S(1)}, bf16[64,4096]{1,0:T(8,128)(2,1)S(1)}, u32[]{:S(2)}, u32[]{:S(2)}) collective-permute-start(bf16[64,4096]{1,0:T(8,128)(2,1)S(1)} %fusion.41), channel_id=1, source_target_pairs={{0,32},{32,64},{64,96},{1,33},{33,65},{65,97},{2,34},{34,66},{66,9... | collective-permute-start | bytes 1572872 | tf_op jit(solution)/shard_map/ppermute | solution.py:16
  214.1 12.4 %collective-permute-start.3 = (bf16[64,4096]{1,0:T(8,128)(2,1)S(1)}, bf16[64,4096]{1,0:T(8,128)(2,1)S(1)}, u32[]{:S(2)}, u32[]{:S(2)}) collective-permute-start(bf16[64,4096]{1,0:T(8,128)(2,1)S(1)} %fusion.44), channel_id=1, source_target_pairs={{0,32},{32,64},{64,96},{1,33},{33,65},{65,97},{2,34},{34,66},{66,9... | collective-permute-start | bytes 1572872 | tf_op jit(solution)/shard_map/ppermute | solution.py:16
  226.9 16.3 %copy-start.5 = (bf16[4,32,4096]{2,1,0:T(8,128)(2,1)S(1)}, bf16[4,32,4096]{2,1,0:T(8,128)(2,1)}, u32[]{:S(2)}) copy-start(bf16[4,32,4096]{2,1,0:T(8,128)(2,1)} %param.9) | copy-start | bytes 3145732
  240.6 2.5 copy-start.1
  259.7 2.8 copy-start.3
  261.2 12.5 %collective-permute-start.4 = (bf16[64,4096]{1,0:T(8,128)(2,1)S(1)}, bf16[64,4096]{1,0:T(8,128)(2,1)S(1)}, u32[]{:S(2)}, u32[]{:S(2)}) collective-permute-start(bf16[64,4096]{1,0:T(8,128)(2,1)S(1)} %fusion.23), channel_id=1, source_target_pairs={{32,0},{64,32},{96,64},{33,1},{65,33},{97,65},{34,2},{66,34},{98,6... | collective-permute-start | bytes 1572872 | tf_op jit(solution)/shard_map/ppermute | solution.py:16
  275.3 1.5 copy-start.9
  292.9 10.8 %collective-permute-start.5 = (bf16[64,4096]{1,0:T(8,128)(2,1)S(1)}, bf16[64,4096]{1,0:T(8,128)(2,1)S(1)}, u32[]{:S(2)}, u32[]{:S(2)}) collective-permute-start(bf16[64,4096]{1,0:T(8,128)(2,1)S(1)} %fusion.27), channel_id=1, source_target_pairs={{32,0},{64,32},{96,64},{33,1},{65,33},{97,65},{34,2},{66,34},{98,6... | collective-permute-start | bytes 1572872 | tf_op jit(solution)/shard_map/ppermute | solution.py:16
  322.3 9.9 %collective-permute-start.6 = (bf16[64,4096]{1,0:T(8,128)(2,1)S(1)}, bf16[64,4096]{1,0:T(8,128)(2,1)S(1)}, u32[]{:S(2)}, u32[]{:S(2)}) collective-permute-start(bf16[64,4096]{1,0:T(8,128)(2,1)S(1)} %fusion.29), channel_id=1, source_target_pairs={{32,0},{64,32},{96,64},{33,1},{65,33},{97,65},{34,2},{66,34},{98,6... | collective-permute-start | bytes 1572872 | tf_op jit(solution)/shard_map/ppermute | solution.py:16
  351.5 10.1 %collective-permute-start.7 = (bf16[64,4096]{1,0:T(8,128)(2,1)}, bf16[64,4096]{1,0:T(8,128)(2,1)S(1)}, u32[]{:S(2)}, u32[]{:S(2)}) collective-permute-start(bf16[64,4096]{1,0:T(8,128)(2,1)} %fusion.31), channel_id=1, source_target_pairs={{32,0},{64,32},{96,64},{33,1},{65,33},{97,65},{34,2},{66,34},{98,6... | collective-permute-start | bytes 1572872 | tf_op jit(solution)/shard_map/ppermute | solution.py:16
  403.9 121.9 %copy-start.6 = (bf16[1,2,64,2048]{3,2,1,0:T(8,128)(2,1)S(1)}, bf16[1,2,64,2048]{3,2,1,0:T(8,128)(2,1)}, u32[]{:S(2)}) copy-start(bf16[1,2,64,2048]{3,2,1,0:T(8,128)(2,1)} %param.10) | copy-start | bytes 1572868
Sparse Core Ops, SparseCore 0:
  10.9 76.2 all-gather.1
  404.1 120.4 reduce-scatter.1

commit v9 on v8

--- a/solution.py
+++ b/solution.py
@@ -59,7 +59,7 @@
             o_ref[pp, k * block:(k + 1) * block, :] = jnp.where(lane < block, t0, t1)
 
 
-PAIRS_PER_STEP = 2
+PAIRS_PER_STEP = 4
 
 
 def expand_dense(paired_weights, live_index):

time: 562 us -> 555 us (0.988)
  Pallas kernels: 64.4 us -> 57.7 us
where the time goes in v9:
time: 555 us; the launch traced here: 547 us
  waiting for transfers between devices  261 us (47%)
  matrix products  147 us (26%)
  Pallas kernels  57.7 us (10%)
  other arithmetic  32.2 us (6%)
  starting transfers between devices  22 us (4%)
  between operations  15.4 us (3%)
  local copies, waits for them, and re-layouts  11.2 us (2%)
    reduce_scatter x1, waiting for transfers between devices, local(): own_grad = lax.psum_scatter(partial, 'dp', scatter_dimension=0, tiled=True)  120 us
    all_gather x1, waiting for transfers between devices, local(): paired_weights = lax.all_gather(own_pair, 'dp', axis=0, tiled=True)  72.5 us
    dot_general x5, matrix products, layer_forward(): pre_act = jnp.dot(normed, dense_w, preferred_element_type=jnp.float32)  68.4 us
    ppermute x8, waiting for transfers between devices, shifted(): lax.ppermute(value, axis, [(source, source + steps) for source in range(l...  68.1 us
    dot_general x4, matrix products, layer_backward(): lax.dot_general(grad_pre, dense_w, (((1,), (1,)), ((), ())), preferred_el...  62.9 us
    pallas_call x1, Pallas kernels, expand_dense(): pl.pallas_call(expand_kernel, out_shape=jax.ShapeDtypeStruct((features, f...  25.8 us
    ppermute x8, starting transfers between devices, shifted(): lax.ppermute(value, axis, [(source, source + steps) for source in range(l...  21.9 us
    pallas_call x1, Pallas kernels, pack_dense(): pl.pallas_call(pack_kernel, out_shape=jax.ShapeDtypeStruct((pair_count, w...  19.7 us
  transfers between devices with their start and end apart: 10, of which 10 were waited for; matrix products, arithmetic and copies ran while one was open for 2% of the time, Pallas kernels for 0%

profile of v9, /device:TPU:1, one launch (start us, length us, event | category | flops | bytes accessed | tf_op | source)
XLA Modules:
  0.0 546.7 jit_solution(7552567184302910224)
XLA Ops:
  14.6 72.5 %all-gather.2.cloned.1.call-done.t_ref = bf16[32,2048,128]{2,1,0:T(8,128)(2,1)} async-done(((bf16[1,2048,128]{2,1,0:T(8,128)(2,1)}), bf16[32,2048,128]{2,1,0:T(8,128)(2,1)}) %all-gather.2.cloned.1.call-update) | async-done | bytes 16777232 | tf_op jit(solution)/shard_map/all_gather | solution.py:214
  87.1 25.8 %shard_map.85 = bf16[4096,4096]{1,0:T(8,128)(2,1)} custom-call(s32[4096]{0:T(1024)} %select_n.124.table_ref, bf16[32,2048,128]{2,1,0:T(8,128)(2,1)} %all-gather.2.cloned.1.call-done.t_ref), custom_call_target="tpu_custom_call" | custom-call | bytes 50331648 | tf_op jit(solution)/shard_map/pallas_call | solution.py:76
  113.0 13.6 %bitcast_dynamic-update-slice_fusion.3 = (f32[5,64,4096]{2,1,0:T(8,128)S(1)}, f32[64,4096]{1,0:T(8,128)S(1)}) fusion(bf16[64,4096]{1,0:T(8,128)(2,1)S(1)} %fusion.77, bf16[4096,4096]{1,0:T(8,128)(2,1)} %shard_map.85), kind=kOutput, calls=%fused_computation.116 | convolution fusion | flops 2147483648 | bytes 36175872 | tf_op jit(solution)/shard_map/dot_general | solution.py:176
  132.2 8.8 %collective-permute-done = bf16[64,4096]{1,0:T(8,128)(2,1)S(1)} collective-permute-done((bf16[64,4096]{1,0:T(8,128)(2,1)S(1)}, bf16[64,4096]{1,0:T(8,128)(2,1)S(1)}, u32[]{:S(2)}, u32[]{:S(2)}) %collective-permute-start) | collective-permute-done | bytes 524320 | tf_op jit(solution)/shard_map/ppermute | solution.py:16
  141.4 13.7 %bitcast_dynamic-update-slice_fusion.2 = (f32[5,64,4096]{2,1,0:T(8,128)S(1)}, f32[64,4096]{1,0:T(8,128)S(1)}) fusion(f32[5,64,4096]{2,1,0:T(8,128)S(1)} %get-tuple-element.47, bf16[4096,4096]{1,0:T(8,128)(2,1)} %shard_map.85, bf16[64,4096]{1,0:T(8,128)(2,1)S(1)} %get-tuple-element.30, f32[64]{0:T(128)S(1)} %add_rsqrt_fusion.8), kind=kOutput, calls=%fused_computation.115 | convolution fusion | flops 2148270080 | bytes 36176384 | tf_op jit(solution)/shard_map/dot_general | solution.py:176
  160.7 8.9 %collective-permute-done.1 = bf16[64,4096]{1,0:T(8,128)(2,1)S(1)} collective-permute-done((bf16[64,4096]{1,0:T(8,128)(2,1)S(1)}, bf16[64,4096]{1,0:T(8,128)(2,1)S(1)}, u32[]{:S(2)}, u32[]{:S(2)}) %collective-permute-start.1) | collective-permute-done | bytes 524320 | tf_op jit(solution)/shard_map/ppermute | solution.py:16
  170.0 13.7 %bitcast_dynamic-update-slice_fusion.1 = (f32[5,64,4096]{2,1,0:T(8,128)S(1)}, f32[64,4096]{1,0:T(8,128)S(1)}) fusion(f32[5,64,4096]{2,1,0:T(8,128)S(1)} %get-tuple-element.49, bf16[4096,4096]{1,0:T(8,128)(2,1)} %shard_map.85, bf16[64,4096]{1,0:T(8,128)(2,1)S(1)} %get-tuple-element.28, f32[64]{0:T(128)S(1)} %add_rsqrt_fusion.7), kind=kOutput, calls=%fused_computation.114 | convolution fusion | flops 2148270080 | bytes 36176384 | tf_op jit(solution)/shard_map/dot_general | solution.py:176
  189.1 8.2 %collective-permute-done.2 = bf16[64,4096]{1,0:T(8,128)(2,1)S(1)} collective-permute-done((bf16[64,4096]{1,0:T(8,128)(2,1)S(1)}, bf16[64,4096]{1,0:T(8,128)(2,1)S(1)}, u32[]{:S(2)}, u32[]{:S(2)}) %collective-permute-start.2) | collective-permute-done | bytes 524320 | tf_op jit(solution)/shard_map/ppermute | solution.py:16
  197.6 13.7 %bitcast_dynamic-update-slice_fusion = (f32[5,64,4096]{2,1,0:T(8,128)S(1)}, f32[64,4096]{1,0:T(8,128)S(1)}) fusion(f32[5,64,4096]{2,1,0:T(8,128)S(1)} %get-tuple-element.51, bf16[4096,4096]{1,0:T(8,128)(2,1)} %shard_map.85, bf16[64,4096]{1,0:T(8,128)(2,1)S(1)} %get-tuple-element.26, f32[64]{0:T(128)S(1)} %add_rsqrt_fusion.6), kind=kOutput, calls=%fused_computation.113 | convolution fusion | flops 2148270080 | bytes 36176384 | tf_op jit(solution)/shard_map/dot_general | solution.py:176
  211.6 4.7 collective-permute-start.3
  217.2 6.8 %collective-permute-done.3 = bf16[64,4096]{1,0:T(8,128)(2,1)S(1)} collective-permute-done((bf16[64,4096]{1,0:T(8,128)(2,1)S(1)}, bf16[64,4096]{1,0:T(8,128)(2,1)S(1)}, u32[]{:S(2)}, u32[]{:S(2)}) %collective-permute-start.3) | collective-permute-done | bytes 524320 | tf_op jit(solution)/shard_map/ppermute | solution.py:16
  224.4 13.8 %fusion.1 = f32[5,64,4096]{2,1,0:T(8,128)S(1)} fusion(f32[5,64,4096]{2,1,0:T(8,128)S(1)} %get-tuple-element.53, bf16[4096,4096]{1,0:T(8,128)(2,1)} %shard_map.85, bf16[64,4096]{1,0:T(8,128)(2,1)S(1)} %get-tuple-element.24, f32[64]{0:T(128)S(1)} %add_rsqrt_fusion.5), kind=kOutput, calls=%fused_computation.3 | convolution fusion | flops 2148270080 | bytes 35127808 | tf_op jit(solution)/shard_map/dot_general | solution.py:176
  241.3 15.9 %fusion.35 = (f32[64]{0:T(128)S(1)}, f32[64]{0:T(128)S(1)}, f32[64]{0:T(128)S(1)}, f32[64]{0:T(128)S(1)}, f32[64,4096]{1,0:T(8,128)S(1)}) fusion(bf16[5,64,4096]{2,1,0:T(8,128)(2,1)S(1)} %get-tuple-element.38, s32[]{:T(128)S(6)} %dynamic_slice.69, f32[64]{0:T(128)S(1)} %add_rsqrt_fusion.4, s32[]{:T(128)S(6)} %dynamic_slice.60, s32[]{:T(128)S(6)} %dynamic_slice.66, ...), kind=kOutput, calls=%fused_computation.63 | convolution fusion | flops 2150891520 | bytes 37225744 | tf_op jit(solution)/shard_map/dot_general | solution.py:187
  261.6 9.6 %collective-permute-done.4 = bf16[64,4096]{1,0:T(8,128)(2,1)S(1)} collective-permute-done((bf16[64,4096]{1,0:T(8,128)(2,1)S(1)}, bf16[64,4096]{1,0:T(8,128)(2,1)S(1)}, u32[]{:S(2)}, u32[]{:S(2)}) %collective-permute-start.4) | collective-permute-done | bytes 524320 | tf_op jit(solution)/shard_map/ppermute | solution.py:16
  274.3 15.7 %fusion.16 = (f32[64]{0:T(128)S(1)}, f32[64,4096]{1,0:T(8,128)S(1)}) fusion(f32[64]{0:T(128)S(1)} %add_rsqrt_fusion.3, bf16[5,64,4096]{2,1,0:T(8,128)(2,1)S(1)} %get-tuple-element.38, s32[]{:T(128)S(6)} %dynamic_slice.63, bf16[64,4096]{1,0:T(8,128)(2,1)S(1)} %get-tuple-element.57, bf16[4096,4096]{1,0:T(8,128)(2,1)} %shard_map.85), kind=kOutput, calls=%fused_computation.44 | convolution fusion | flops 2148532224 | bytes 35652100 | tf_op jit(solution)/shard_map/dot_general | solution.py:187
  291.9 9.4 %collective-permute-done.5 = bf16[64,4096]{1,0:T(8,128)(2,1)S(1)} collective-permute-done((bf16[64,4096]{1,0:T(8,128)(2,1)S(1)}, bf16[64,4096]{1,0:T(8,128)(2,1)S(1)}, u32[]{:S(2)}, u32[]{:S(2)}) %collective-permute-start.5) | collective-permute-done | bytes 524320 | tf_op jit(solution)/shard_map/ppermute | solution.py:16
  303.7 15.7 %fusion.13 = (f32[64]{0:T(128)S(1)}, f32[64,4096]{1,0:T(8,128)S(1)}) fusion(f32[64]{0:T(128)S(1)} %add_rsqrt_fusion.2, bf16[5,64,4096]{2,1,0:T(8,128)(2,1)S(1)} %get-tuple-element.38, s32[]{:T(128)S(6)} %dynamic_slice.66, bf16[64,4096]{1,0:T(8,128)(2,1)S(1)} %get-tuple-element.61, bf16[4096,4096]{1,0:T(8,128)(2,1)} %shard_map.85), kind=kOutput, calls=%fused_computation.41 | convolution fusion | flops 2148532224 | bytes 35652100 | tf_op jit(solution)/shard_map/dot_general | solution.py:187
  321.1 8.6 %collective-permute-done.6 = bf16[64,4096]{1,0:T(8,128)(2,1)S(1)} collective-permute-done((bf16[64,4096]{1,0:T(8,128)(2,1)S(1)}, bf16[64,4096]{1,0:T(8,128)(2,1)S(1)}, u32[]{:S(2)}, u32[]{:S(2)}) %collective-permute-start.6) | collective-permute-done | bytes 524320 | tf_op jit(solution)/shard_map/ppermute | solution.py:16
  332.2 15.7 %fusion.10 = (f32[64]{0:T(128)S(1)}, f32[64,4096]{1,0:T(8,128)S(1)}) fusion(f32[64]{0:T(128)S(1)} %add_rsqrt_fusion.1, bf16[5,64,4096]{2,1,0:T(8,128)(2,1)S(1)} %get-tuple-element.38, s32[]{:T(128)S(6)} %dynamic_slice.69, bf16[64,4096]{1,0:T(8,128)(2,1)S(1)} %get-tuple-element.65, bf16[4096,4096]{1,0:T(8,128)(2,1)} %shard_map.85), kind=kOutput, calls=%fused_computation.38 | convolution fusion | flops 2148532224 | bytes 35652100 | tf_op jit(solution)/shard_map/dot_general | solution.py:187
  351.3 7.9 %collective-permute-done.7 = bf16[64,4096]{1,0:T(8,128)(2,1)S(1)} collective-permute-done((bf16[64,4096]{1,0:T(8,128)(2,1)}, bf16[64,4096]{1,0:T(8,128)(2,1)S(1)}, u32[]{:S(2)}, u32[]{:S(2)}) %collective-permute-start.7) | collective-permute-done | bytes 524320 | tf_op jit(solution)/shard_map/ppermute | solution.py:16
  361.6 15.9 %fusion.g_ref = bf16[4096,4096]{1,0:T(8,128)(2,1)} fusion(bf16[5,64,4096]{2,1,0:T(8,128)(2,1)} %bitcast_dynamic-update-slice_fusion.4, s32[]{:T(128)S(6)} %select_n.138, bf16[5,64,4096]{2,1,0:T(8,128)(2,1)} %get-tuple-element.37, s32[]{:T(128)S(6)} %select_n.129), kind=kOutput, calls=%fused_computation.1 | convolution fusion | flops 4328521728 | bytes 35651592 | tf_op jit(solution)/shard_map/dot_general | solution.py:254
  377.6 19.7 %shard_map.86 = bf16[32,2048,128]{2,1,0:T(8,128)(2,1)} custom-call(s32[2048]{0:T(1024)} %reshape_squeeze.3.table_ref, bf16[4096,4096]{1,0:T(8,128)(2,1)} %fusion.g_ref), custom_call_target="tpu_custom_call" | custom-call | bytes 50331648 | tf_op jit(solution)/shard_map/pallas_call | solution.py:97
  397.5 120.4 %reduce-scatter.2.cloned.1.call-done = bf16[1,2048,128]{2,1,0:T(8,128)(2,1)} async-done(((bf16[32,2048,128]{2,1,0:T(8,128)(2,1)}), bf16[1,2048,128]{2,1,0:T(8,128)(2,1)}) %reduce-scatter.2.cloned.1.call-update) | async-done | bytes 524304 | tf_op jit(solution)/shard_map/reduce_scatter | solution.py:263
  524.2 12.2 %shard_map.87 = f32[8,128]{1,0:T(8,128)} custom-call(f32[8,128]{1,0:T(8,128)} %scatter.4.x_ref), custom_call_target="tpu_custom_call" | custom-call | tf_op jit(solution)/shard_map/pallas_call | solution.py:157
  (100 shorter events, 60.7 us)
Async XLA Ops:
  7.2 4.2 copy-start.7
  7.2 4.5 copy-start.8
  7.2 6.3 %copy-start.4 = (bf16[4,32,4096]{2,1,0:T(8,128)(2,1)S(1)}, bf16[4,32,4096]{2,1,0:T(8,128)(2,1)}, u32[]{:S(2)}) copy-start(bf16[4,32,4096]{2,1,0:T(8,128)(2,1)} %param.9) | copy-start | bytes 3145732
  7.2 79.9 %all-gather.2.cloned.1.call-start = ((), (), s32[]{:S(2)}) async-start(), calls=%async_computation.1 | async-start | bytes 17301504 | tf_op jit(solution)/shard_map/all_gather | solution.py:214
  9.4 508.4 %reduce-scatter.2.cloned.1.call-start = ((), (), s32[]{:S(2)}) async-start(), calls=%async_computation.2 | async-start | bytes 17301504 | tf_op jit(solution)/shard_map/reduce_scatter | solution.py:263
  11.6 114.9 %copy-start.2 = (bf16[2,32,4096]{2,1,0:T(8,128)(2,1)}, bf16[2,32,4096]{2,1,0:T(8,128)(2,1)S(1)}, u32[]{:S(2)}) copy-start(bf16[2,32,4096]{2,1,0:T(8,128)(2,1)S(1)} %get-tuple-element.32) | copy-start | bytes 1572868
  126.6 14.5 %copy-start = (bf16[2,32,4096]{2,1,0:T(8,128)(2,1)S(1)}, bf16[2,32,4096]{2,1,0:T(8,128)(2,1)}, u32[]{:S(2)}) copy-start(bf16[2,32,4096]{2,1,0:T(8,128)(2,1)} %slice.42) | copy-start | bytes 1572868
  126.9 14.2 %collective-permute-start = (bf16[64,4096]{1,0:T(8,128)(2,1)S(1)}, bf16[64,4096]{1,0:T(8,128)(2,1)S(1)}, u32[]{:S(2)}, u32[]{:S(2)}) collective-permute-start(bf16[64,4096]{1,0:T(8,128)(2,1)S(1)} %fusion.78), channel_id=1, source_target_pairs={{0,32},{32,64},{64,96},{1,33},{33,65},{65,97},{2,34},{34,66},{66,9... | collective-permute-start | bytes 1572872 | tf_op jit(solution)/shard_map/ppermute | solution.py:16
  155.4 14.2 %collective-permute-start.1 = (bf16[64,4096]{1,0:T(8,128)(2,1)S(1)}, bf16[64,4096]{1,0:T(8,128)(2,1)S(1)}, u32[]{:S(2)}, u32[]{:S(2)}) collective-permute-start(bf16[64,4096]{1,0:T(8,128)(2,1)S(1)} %fusion.38), channel_id=1, source_target_pairs={{0,32},{32,64},{64,96},{1,33},{33,65},{65,97},{2,34},{34,66},{66,9... | collective-permute-start | bytes 1572872 | tf_op jit(solution)/shard_map/ppermute | solution.py:16
  183.9 13.3 %collective-permute-start.2 = (bf16[64,4096]{1,0:T(8,128)(2,1)S(1)}, bf16[64,4096]{1,0:T(8,128)(2,1)S(1)}, u32[]{:S(2)}, u32[]{:S(2)}) collective-permute-start(bf16[64,4096]{1,0:T(8,128)(2,1)S(1)} %fusion.41), channel_id=1, source_target_pairs={{0,32},{32,64},{64,96},{1,33},{33,65},{65,97},{2,34},{34,66},{66,9... | collective-permute-start | bytes 1572872 | tf_op jit(solution)/shard_map/ppermute | solution.py:16
  211.6 12.4 %collective-permute-start.3 = (bf16[64,4096]{1,0:T(8,128)(2,1)S(1)}, bf16[64,4096]{1,0:T(8,128)(2,1)S(1)}, u32[]{:S(2)}, u32[]{:S(2)}) collective-permute-start(bf16[64,4096]{1,0:T(8,128)(2,1)S(1)} %fusion.44), channel_id=1, source_target_pairs={{0,32},{32,64},{64,96},{1,33},{33,65},{65,97},{2,34},{34,66},{66,9... | collective-permute-start | bytes 1572872 | tf_op jit(solution)/shard_map/ppermute | solution.py:16
  224.3 16.3 %copy-start.5 = (bf16[4,32,4096]{2,1,0:T(8,128)(2,1)S(1)}, bf16[4,32,4096]{2,1,0:T(8,128)(2,1)}, u32[]{:S(2)}) copy-start(bf16[4,32,4096]{2,1,0:T(8,128)(2,1)} %param.9) | copy-start | bytes 3145732
  238.1 2.5 copy-start.1
  257.1 2.8 copy-start.3
  258.6 12.5 %collective-permute-start.4 = (bf16[64,4096]{1,0:T(8,128)(2,1)S(1)}, bf16[64,4096]{1,0:T(8,128)(2,1)S(1)}, u32[]{:S(2)}, u32[]{:S(2)}) collective-permute-start(bf16[64,4096]{1,0:T(8,128)(2,1)S(1)} %fusion.23), channel_id=1, source_target_pairs={{32,0},{64,32},{96,64},{33,1},{65,33},{97,65},{34,2},{66,34},{98,6... | collective-permute-start | bytes 1572872 | tf_op jit(solution)/shard_map/ppermute | solution.py:16
  272.8 1.5 copy-start.9
  290.4 10.8 %collective-permute-start.5 = (bf16[64,4096]{1,0:T(8,128)(2,1)S(1)}, bf16[64,4096]{1,0:T(8,128)(2,1)S(1)}, u32[]{:S(2)}, u32[]{:S(2)}) collective-permute-start(bf16[64,4096]{1,0:T(8,128)(2,1)S(1)} %fusion.27), channel_id=1, source_target_pairs={{32,0},{64,32},{96,64},{33,1},{65,33},{97,65},{34,2},{66,34},{98,6... | collective-permute-start | bytes 1572872 | tf_op jit(solution)/shard_map/ppermute | solution.py:16
  319.8 9.9 %collective-permute-start.6 = (bf16[64,4096]{1,0:T(8,128)(2,1)S(1)}, bf16[64,4096]{1,0:T(8,128)(2,1)S(1)}, u32[]{:S(2)}, u32[]{:S(2)}) collective-permute-start(bf16[64,4096]{1,0:T(8,128)(2,1)S(1)} %fusion.29), channel_id=1, source_target_pairs={{32,0},{64,32},{96,64},{33,1},{65,33},{97,65},{34,2},{66,34},{98,6... | collective-permute-start | bytes 1572872 | tf_op jit(solution)/shard_map/ppermute | solution.py:16
  349.0 10.1 %collective-permute-start.7 = (bf16[64,4096]{1,0:T(8,128)(2,1)}, bf16[64,4096]{1,0:T(8,128)(2,1)S(1)}, u32[]{:S(2)}, u32[]{:S(2)}) collective-permute-start(bf16[64,4096]{1,0:T(8,128)(2,1)} %fusion.31), channel_id=1, source_target_pairs={{32,0},{64,32},{96,64},{33,1},{65,33},{97,65},{34,2},{66,34},{98,6... | collective-permute-start | bytes 1572872 | tf_op jit(solution)/shard_map/ppermute | solution.py:16
  397.3 121.8 %copy-start.6 = (bf16[1,2,64,2048]{3,2,1,0:T(8,128)(2,1)S(1)}, bf16[1,2,64,2048]{3,2,1,0:T(8,128)(2,1)}, u32[]{:S(2)}) copy-start(bf16[1,2,64,2048]{3,2,1,0:T(8,128)(2,1)} %param.10) | copy-start | bytes 1572868
Sparse Core Ops, SparseCore 0:
  10.9 76.2 all-gather.1
  397.4 120.3 reduce-scatter.1

commit v10 on v9

--- a/solution.py
+++ b/solution.py
@@ -59,7 +59,7 @@
             o_ref[pp, k * block:(k + 1) * block, :] = jnp.where(lane < block, t0, t1)
 
 
-PAIRS_PER_STEP = 4
+PAIRS_PER_STEP = 8
 
 
 def expand_dense(paired_weights, live_index):

time: 555 us -> 554 us (level)
  no operation moved by 1% of the time
where the time goes in v10:
time: 554 us; the launch traced here: 546 us
  waiting for transfers between devices  261 us (47%)
  matrix products  147 us (27%)
  Pallas kernels  57 us (10%)
  other arithmetic  32.2 us (6%)
  starting transfers between devices  22 us (4%)
  between operations  15.6 us (3%)
  local copies, waits for them, and re-layouts  11.2 us (2%)
    reduce_scatter x1, waiting for transfers between devices, local(): own_grad = lax.psum_scatter(partial, 'dp', scatter_dimension=0, tiled=True)  120 us
    all_gather x1, waiting for transfers between devices, local(): paired_weights = lax.all_gather(own_pair, 'dp', axis=0, tiled=True)  72.5 us
    dot_general x5, matrix products, layer_forward(): pre_act = jnp.dot(normed, dense_w, preferred_element_type=jnp.float32)  68.4 us
    ppermute x8, waiting for transfers between devices, shifted(): lax.ppermute(value, axis, [(source, source + steps) for source in range(l...  68 us
    dot_general x4, matrix products, layer_backward(): lax.dot_general(grad_pre, dense_w, (((1,), (1,)), ((), ())), preferred_el...  62.9 us
    pallas_call x1, Pallas kernels, expand_dense(): pl.pallas_call(expand_kernel, out_shape=jax.ShapeDtypeStruct((features, f...  25.4 us
    ppermute x8, starting transfers between devices, shifted(): lax.ppermute(value, axis, [(source, source + steps) for source in range(l...  21.9 us
    pallas_call x1, Pallas kernels, pack_dense(): pl.pallas_call(pack_kernel, out_shape=jax.ShapeDtypeStruct((pair_count, w...  19.4 us
  transfers between devices with their start and end apart: 10, of which 10 were waited for; matrix products, arithmetic and copies ran while one was open for 2% of the time, Pallas kernels for 0%

profile of v10, /device:TPU:1, one launch (start us, length us, event | category | flops | bytes accessed | tf_op | source)
XLA Modules:
  0.0 546.2 jit_solution(5177649393133845354)
XLA Ops:
  14.6 72.5 %all-gather.2.cloned.1.call-done.t_ref = bf16[32,2048,128]{2,1,0:T(8,128)(2,1)} async-done(((bf16[1,2048,128]{2,1,0:T(8,128)(2,1)}), bf16[32,2048,128]{2,1,0:T(8,128)(2,1)}) %all-gather.2.cloned.1.call-update) | async-done | bytes 16777232 | tf_op jit(solution)/shard_map/all_gather | solution.py:214
  87.1 25.4 %shard_map.85 = bf16[4096,4096]{1,0:T(8,128)(2,1)} custom-call(s32[4096]{0:T(1024)} %select_n.124.table_ref, bf16[32,2048,128]{2,1,0:T(8,128)(2,1)} %all-gather.2.cloned.1.call-done.t_ref), custom_call_target="tpu_custom_call" | custom-call | bytes 50331648 | tf_op jit(solution)/shard_map/pallas_call | solution.py:76
  112.5 13.6 %bitcast_dynamic-update-slice_fusion.3 = (f32[5,64,4096]{2,1,0:T(8,128)S(1)}, f32[64,4096]{1,0:T(8,128)S(1)}) fusion(bf16[64,4096]{1,0:T(8,128)(2,1)S(1)} %fusion.77, bf16[4096,4096]{1,0:T(8,128)(2,1)} %shard_map.85), kind=kOutput, calls=%fused_computation.116 | convolution fusion | flops 2147483648 | bytes 36175872 | tf_op jit(solution)/shard_map/dot_general | solution.py:176
  132.3 8.3 %collective-permute-done = bf16[64,4096]{1,0:T(8,128)(2,1)S(1)} collective-permute-done((bf16[64,4096]{1,0:T(8,128)(2,1)S(1)}, bf16[64,4096]{1,0:T(8,128)(2,1)S(1)}, u32[]{:S(2)}, u32[]{:S(2)}) %collective-permute-start) | collective-permute-done | bytes 524320 | tf_op jit(solution)/shard_map/ppermute | solution.py:16
  140.9 13.7 %bitcast_dynamic-update-slice_fusion.2 = (f32[5,64,4096]{2,1,0:T(8,128)S(1)}, f32[64,4096]{1,0:T(8,128)S(1)}) fusion(f32[5,64,4096]{2,1,0:T(8,128)S(1)} %get-tuple-element.47, bf16[4096,4096]{1,0:T(8,128)(2,1)} %shard_map.85, bf16[64,4096]{1,0:T(8,128)(2,1)S(1)} %get-tuple-element.30, f32[64]{0:T(128)S(1)} %add_rsqrt_fusion.8), kind=kOutput, calls=%fused_computation.115 | convolution fusion | flops 2148270080 | bytes 36176384 | tf_op jit(solution)/shard_map/dot_general | solution.py:176
  160.0 9.2 %collective-permute-done.1 = bf16[64,4096]{1,0:T(8,128)(2,1)S(1)} collective-permute-done((bf16[64,4096]{1,0:T(8,128)(2,1)S(1)}, bf16[64,4096]{1,0:T(8,128)(2,1)S(1)}, u32[]{:S(2)}, u32[]{:S(2)}) %collective-permute-start.1) | collective-permute-done | bytes 524320 | tf_op jit(solution)/shard_map/ppermute | solution.py:16
  169.5 13.7 %bitcast_dynamic-update-slice_fusion.1 = (f32[5,64,4096]{2,1,0:T(8,128)S(1)}, f32[64,4096]{1,0:T(8,128)S(1)}) fusion(f32[5,64,4096]{2,1,0:T(8,128)S(1)} %get-tuple-element.49, bf16[4096,4096]{1,0:T(8,128)(2,1)} %shard_map.85, bf16[64,4096]{1,0:T(8,128)(2,1)S(1)} %get-tuple-element.28, f32[64]{0:T(128)S(1)} %add_rsqrt_fusion.7), kind=kOutput, calls=%fused_computation.114 | convolution fusion | flops 2148270080 | bytes 36176384 | tf_op jit(solution)/shard_map/dot_general | solution.py:176
  188.6 8.2 %collective-permute-done.2 = bf16[64,4096]{1,0:T(8,128)(2,1)S(1)} collective-permute-done((bf16[64,4096]{1,0:T(8,128)(2,1)S(1)}, bf16[64,4096]{1,0:T(8,128)(2,1)S(1)}, u32[]{:S(2)}, u32[]{:S(2)}) %collective-permute-start.2) | collective-permute-done | bytes 524320 | tf_op jit(solution)/shard_map/ppermute | solution.py:16
  197.2 13.7 %bitcast_dynamic-update-slice_fusion = (f32[5,64,4096]{2,1,0:T(8,128)S(1)}, f32[64,4096]{1,0:T(8,128)S(1)}) fusion(f32[5,64,4096]{2,1,0:T(8,128)S(1)} %get-tuple-element.51, bf16[4096,4096]{1,0:T(8,128)(2,1)} %shard_map.85, bf16[64,4096]{1,0:T(8,128)(2,1)S(1)} %get-tuple-element.26, f32[64]{0:T(128)S(1)} %add_rsqrt_fusion.6), kind=kOutput, calls=%fused_computation.113 | convolution fusion | flops 2148270080 | bytes 36176384 | tf_op jit(solution)/shard_map/dot_general | solution.py:176
  211.1 4.3 collective-permute-start.3
  216.4 7.1 %collective-permute-done.3 = bf16[64,4096]{1,0:T(8,128)(2,1)S(1)} collective-permute-done((bf16[64,4096]{1,0:T(8,128)(2,1)S(1)}, bf16[64,4096]{1,0:T(8,128)(2,1)S(1)}, u32[]{:S(2)}, u32[]{:S(2)}) %collective-permute-start.3) | collective-permute-done | bytes 524320 | tf_op jit(solution)/shard_map/ppermute | solution.py:16
  223.9 13.8 %fusion.1 = f32[5,64,4096]{2,1,0:T(8,128)S(1)} fusion(f32[5,64,4096]{2,1,0:T(8,128)S(1)} %get-tuple-element.53, bf16[4096,4096]{1,0:T(8,128)(2,1)} %shard_map.85, bf16[64,4096]{1,0:T(8,128)(2,1)S(1)} %get-tuple-element.24, f32[64]{0:T(128)S(1)} %add_rsqrt_fusion.5), kind=kOutput, calls=%fused_computation.3 | convolution fusion | flops 2148270080 | bytes 35127808 | tf_op jit(solution)/shard_map/dot_general | solution.py:176
  240.8 15.9 %fusion.35 = (f32[64]{0:T(128)S(1)}, f32[64]{0:T(128)S(1)}, f32[64]{0:T(128)S(1)}, f32[64]{0:T(128)S(1)}, f32[64,4096]{1,0:T(8,128)S(1)}) fusion(bf16[5,64,4096]{2,1,0:T(8,128)(2,1)S(1)} %get-tuple-element.38, s32[]{:T(128)S(6)} %dynamic_slice.69, f32[64]{0:T(128)S(1)} %add_rsqrt_fusion.4, s32[]{:T(128)S(6)} %dynamic_slice.60, s32[]{:T(128)S(6)} %dynamic_slice.66, ...), kind=kOutput, calls=%fused_computation.63 | convolution fusion | flops 2150891520 | bytes 37225744 | tf_op jit(solution)/shard_map/dot_general | solution.py:187
  261.1 9.6 %collective-permute-done.4 = bf16[64,4096]{1,0:T(8,128)(2,1)S(1)} collective-permute-done((bf16[64,4096]{1,0:T(8,128)(2,1)S(1)}, bf16[64,4096]{1,0:T(8,128)(2,1)S(1)}, u32[]{:S(2)}, u32[]{:S(2)}) %collective-permute-start.4) | collective-permute-done | bytes 524320 | tf_op jit(solution)/shard_map/ppermute | solution.py:16
  273.9 15.7 %fusion.16 = (f32[64]{0:T(128)S(1)}, f32[64,4096]{1,0:T(8,128)S(1)}) fusion(f32[64]{0:T(128)S(1)} %add_rsqrt_fusion.3, bf16[5,64,4096]{2,1,0:T(8,128)(2,1)S(1)} %get-tuple-element.38, s32[]{:T(128)S(6)} %dynamic_slice.63, bf16[64,4096]{1,0:T(8,128)(2,1)S(1)} %get-tuple-element.57, bf16[4096,4096]{1,0:T(8,128)(2,1)} %shard_map.85), kind=kOutput, calls=%fused_computation.44 | convolution fusion | flops 2148532224 | bytes 35652100 | tf_op jit(solution)/shard_map/dot_general | solution.py:187
  291.5 9.3 %collective-permute-done.5 = bf16[64,4096]{1,0:T(8,128)(2,1)S(1)} collective-permute-done((bf16[64,4096]{1,0:T(8,128)(2,1)S(1)}, bf16[64,4096]{1,0:T(8,128)(2,1)S(1)}, u32[]{:S(2)}, u32[]{:S(2)}) %collective-permute-start.5) | collective-permute-done | bytes 524320 | tf_op jit(solution)/shard_map/ppermute | solution.py:16
  303.2 15.7 %fusion.13 = (f32[64]{0:T(128)S(1)}, f32[64,4096]{1,0:T(8,128)S(1)}) fusion(f32[64]{0:T(128)S(1)} %add_rsqrt_fusion.2, bf16[5,64,4096]{2,1,0:T(8,128)(2,1)S(1)} %get-tuple-element.38, s32[]{:T(128)S(6)} %dynamic_slice.66, bf16[64,4096]{1,0:T(8,128)(2,1)S(1)} %get-tuple-element.61, bf16[4096,4096]{1,0:T(8,128)(2,1)} %shard_map.85), kind=kOutput, calls=%fused_computation.41 | convolution fusion | flops 2148532224 | bytes 35652100 | tf_op jit(solution)/shard_map/dot_general | solution.py:187
  320.6 8.6 %collective-permute-done.6 = bf16[64,4096]{1,0:T(8,128)(2,1)S(1)} collective-permute-done((bf16[64,4096]{1,0:T(8,128)(2,1)S(1)}, bf16[64,4096]{1,0:T(8,128)(2,1)S(1)}, u32[]{:S(2)}, u32[]{:S(2)}) %collective-permute-start.6) | collective-permute-done | bytes 524320 | tf_op jit(solution)/shard_map/ppermute | solution.py:16
  331.7 15.7 %fusion.10 = (f32[64]{0:T(128)S(1)}, f32[64,4096]{1,0:T(8,128)S(1)}) fusion(f32[64]{0:T(128)S(1)} %add_rsqrt_fusion.1, bf16[5,64,4096]{2,1,0:T(8,128)(2,1)S(1)} %get-tuple-element.38, s32[]{:T(128)S(6)} %dynamic_slice.69, bf16[64,4096]{1,0:T(8,128)(2,1)S(1)} %get-tuple-element.65, bf16[4096,4096]{1,0:T(8,128)(2,1)} %shard_map.85), kind=kOutput, calls=%fused_computation.38 | convolution fusion | flops 2148532224 | bytes 35652100 | tf_op jit(solution)/shard_map/dot_general | solution.py:187
  350.9 7.8 %collective-permute-done.7 = bf16[64,4096]{1,0:T(8,128)(2,1)S(1)} collective-permute-done((bf16[64,4096]{1,0:T(8,128)(2,1)}, bf16[64,4096]{1,0:T(8,128)(2,1)S(1)}, u32[]{:S(2)}, u32[]{:S(2)}) %collective-permute-start.7) | collective-permute-done | bytes 524320 | tf_op jit(solution)/shard_map/ppermute | solution.py:16
  361.2 15.9 %fusion.g_ref = bf16[4096,4096]{1,0:T(8,128)(2,1)} fusion(bf16[5,64,4096]{2,1,0:T(8,128)(2,1)} %bitcast_dynamic-update-slice_fusion.4, s32[]{:T(128)S(6)} %select_n.138, bf16[5,64,4096]{2,1,0:T(8,128)(2,1)} %get-tuple-element.37, s32[]{:T(128)S(6)} %select_n.129), kind=kOutput, calls=%fused_computation.1 | convolution fusion | flops 4328521728 | bytes 35651592 | tf_op jit(solution)/shard_map/dot_general | solution.py:254
  377.1 19.4 %shard_map.86 = bf16[32,2048,128]{2,1,0:T(8,128)(2,1)} custom-call(s32[2048]{0:T(1024)} %reshape_squeeze.3.table_ref, bf16[4096,4096]{1,0:T(8,128)(2,1)} %fusion.g_ref), custom_call_target="tpu_custom_call" | custom-call | bytes 50331648 | tf_op jit(solution)/shard_map/pallas_call | solution.py:97
  396.7 120.5 %reduce-scatter.2.cloned.1.call-done = bf16[1,2048,128]{2,1,0:T(8,128)(2,1)} async-done(((bf16[32,2048,128]{2,1,0:T(8,128)(2,1)}), bf16[1,2048,128]{2,1,0:T(8,128)(2,1)}) %reduce-scatter.2.cloned.1.call-update) | async-done | bytes 524304 | tf_op jit(solution)/shard_map/reduce_scatter | solution.py:263
  523.4 12.2 %shard_map.87 = f32[8,128]{1,0:T(8,128)} custom-call(f32[8,128]{1,0:T(8,128)} %scatter.4.x_ref), custom_call_target="tpu_custom_call" | custom-call | tf_op jit(solution)/shard_map/pallas_call | solution.py:157
  (100 shorter events, 61.0 us)
Async XLA Ops:
  7.2 4.2 copy-start.7
  7.2 4.5 copy-start.8
  7.2 6.3 %copy-start.4 = (bf16[4,32,4096]{2,1,0:T(8,128)(2,1)S(1)}, bf16[4,32,4096]{2,1,0:T(8,128)(2,1)}, u32[]{:S(2)}) copy-start(bf16[4,32,4096]{2,1,0:T(8,128)(2,1)} %param.9) | copy-start | bytes 3145732
  7.2 79.9 %all-gather.2.cloned.1.call-start = ((), (), s32[]{:S(2)}) async-start(), calls=%async_computation.1 | async-start | bytes 17301504 | tf_op jit(solution)/shard_map/all_gather | solution.py:214
  9.4 507.7 %reduce-scatter.2.cloned.1.call-start = ((), (), s32[]{:S(2)}) async-start(), calls=%async_computation.2 | async-start | bytes 17301504 | tf_op jit(solution)/shard_map/reduce_scatter | solution.py:263
  11.6 114.5 %copy-start.2 = (bf16[2,32,4096]{2,1,0:T(8,128)(2,1)}, bf16[2,32,4096]{2,1,0:T(8,128)(2,1)S(1)}, u32[]{:S(2)}) copy-start(bf16[2,32,4096]{2,1,0:T(8,128)(2,1)S(1)} %get-tuple-element.32) | copy-start | bytes 1572868
  126.1 14.5 %copy-start = (bf16[2,32,4096]{2,1,0:T(8,128)(2,1)S(1)}, bf16[2,32,4096]{2,1,0:T(8,128)(2,1)}, u32[]{:S(2)}) copy-start(bf16[2,32,4096]{2,1,0:T(8,128)(2,1)} %slice.42) | copy-start | bytes 1572868
  126.4 14.2 %collective-permute-start = (bf16[64,4096]{1,0:T(8,128)(2,1)S(1)}, bf16[64,4096]{1,0:T(8,128)(2,1)S(1)}, u32[]{:S(2)}, u32[]{:S(2)}) collective-permute-start(bf16[64,4096]{1,0:T(8,128)(2,1)S(1)} %fusion.78), channel_id=1, source_target_pairs={{0,32},{32,64},{64,96},{1,33},{33,65},{65,97},{2,34},{34,66},{66,9... | collective-permute-start | bytes 1572872 | tf_op jit(solution)/shard_map/ppermute | solution.py:16
  154.9 14.2 %collective-permute-start.1 = (bf16[64,4096]{1,0:T(8,128)(2,1)S(1)}, bf16[64,4096]{1,0:T(8,128)(2,1)S(1)}, u32[]{:S(2)}, u32[]{:S(2)}) collective-permute-start(bf16[64,4096]{1,0:T(8,128)(2,1)S(1)} %fusion.38), channel_id=1, source_target_pairs={{0,32},{32,64},{64,96},{1,33},{33,65},{65,97},{2,34},{34,66},{66,9... | collective-permute-start | bytes 1572872 | tf_op jit(solution)/shard_map/ppermute | solution.py:16
  183.5 13.3 %collective-permute-start.2 = (bf16[64,4096]{1,0:T(8,128)(2,1)S(1)}, bf16[64,4096]{1,0:T(8,128)(2,1)S(1)}, u32[]{:S(2)}, u32[]{:S(2)}) collective-permute-start(bf16[64,4096]{1,0:T(8,128)(2,1)S(1)} %fusion.41), channel_id=1, source_target_pairs={{0,32},{32,64},{64,96},{1,33},{33,65},{65,97},{2,34},{34,66},{66,9... | collective-permute-start | bytes 1572872 | tf_op jit(solution)/shard_map/ppermute | solution.py:16
  211.1 12.4 %collective-permute-start.3 = (bf16[64,4096]{1,0:T(8,128)(2,1)S(1)}, bf16[64,4096]{1,0:T(8,128)(2,1)S(1)}, u32[]{:S(2)}, u32[]{:S(2)}) collective-permute-start(bf16[64,4096]{1,0:T(8,128)(2,1)S(1)} %fusion.44), channel_id=1, source_target_pairs={{0,32},{32,64},{64,96},{1,33},{33,65},{65,97},{2,34},{34,66},{66,9... | collective-permute-start | bytes 1572872 | tf_op jit(solution)/shard_map/ppermute | solution.py:16
  223.9 16.3 %copy-start.5 = (bf16[4,32,4096]{2,1,0:T(8,128)(2,1)S(1)}, bf16[4,32,4096]{2,1,0:T(8,128)(2,1)}, u32[]{:S(2)}) copy-start(bf16[4,32,4096]{2,1,0:T(8,128)(2,1)} %param.9) | copy-start | bytes 3145732
  237.6 2.5 copy-start.1
  256.7 2.8 copy-start.3
  258.2 12.5 %collective-permute-start.4 = (bf16[64,4096]{1,0:T(8,128)(2,1)S(1)}, bf16[64,4096]{1,0:T(8,128)(2,1)S(1)}, u32[]{:S(2)}, u32[]{:S(2)}) collective-permute-start(bf16[64,4096]{1,0:T(8,128)(2,1)S(1)} %fusion.23), channel_id=1, source_target_pairs={{32,0},{64,32},{96,64},{33,1},{65,33},{97,65},{34,2},{66,34},{98,6... | collective-permute-start | bytes 1572872 | tf_op jit(solution)/shard_map/ppermute | solution.py:16
  272.3 1.5 copy-start.9
  289.9 10.8 %collective-permute-start.5 = (bf16[64,4096]{1,0:T(8,128)(2,1)S(1)}, bf16[64,4096]{1,0:T(8,128)(2,1)S(1)}, u32[]{:S(2)}, u32[]{:S(2)}) collective-permute-start(bf16[64,4096]{1,0:T(8,128)(2,1)S(1)} %fusion.27), channel_id=1, source_target_pairs={{32,0},{64,32},{96,64},{33,1},{65,33},{97,65},{34,2},{66,34},{98,6... | collective-permute-start | bytes 1572872 | tf_op jit(solution)/shard_map/ppermute | solution.py:16
  319.3 9.9 %collective-permute-start.6 = (bf16[64,4096]{1,0:T(8,128)(2,1)S(1)}, bf16[64,4096]{1,0:T(8,128)(2,1)S(1)}, u32[]{:S(2)}, u32[]{:S(2)}) collective-permute-start(bf16[64,4096]{1,0:T(8,128)(2,1)S(1)} %fusion.29), channel_id=1, source_target_pairs={{32,0},{64,32},{96,64},{33,1},{65,33},{97,65},{34,2},{66,34},{98,6... | collective-permute-start | bytes 1572872 | tf_op jit(solution)/shard_map/ppermute | solution.py:16
  348.6 10.1 %collective-permute-start.7 = (bf16[64,4096]{1,0:T(8,128)(2,1)}, bf16[64,4096]{1,0:T(8,128)(2,1)S(1)}, u32[]{:S(2)}, u32[]{:S(2)}) collective-permute-start(bf16[64,4096]{1,0:T(8,128)(2,1)} %fusion.31), channel_id=1, source_target_pairs={{32,0},{64,32},{96,64},{33,1},{65,33},{97,65},{34,2},{66,34},{98,6... | collective-permute-start | bytes 1572872 | tf_op jit(solution)/shard_map/ppermute | solution.py:16
  396.5 121.9 %copy-start.6 = (bf16[1,2,64,2048]{3,2,1,0:T(8,128)(2,1)S(1)}, bf16[1,2,64,2048]{3,2,1,0:T(8,128)(2,1)}, u32[]{:S(2)}) copy-start(bf16[1,2,64,2048]{3,2,1,0:T(8,128)(2,1)} %param.10) | copy-start | bytes 1572868
Sparse Core Ops, SparseCore 0:
  10.9 76.2 all-gather.1
  396.6 120.4 reduce-scatter.1

commit v11 on v9

--- a/solution.py
+++ b/solution.py
@@ -1,3 +1,4 @@
+import functools
 import math
 
 import jax
@@ -42,10 +43,17 @@
             )
 
 
-def pack_kernel(table_ref, g_ref, o_ref):
+def grad_pack_kernel(scale, table_ref, ut_ref, gz_ref, o_ref, g_ref):
     per_step = o_ref.shape[0]
     block = 64
     live_count = o_ref.shape[1] // block
+    rows = g_ref.shape[0]
+    chunk = 512
+    for c in range(rows // chunk):
+        g_ref[c * chunk:(c + 1) * chunk, :] = (
+            jnp.dot(ut_ref[c * chunk:(c + 1) * chunk, :], gz_ref[...], preferred_element_type=jnp.float32)
+            * scale
+        ).astype(g_ref.dtype)
     lane = lax.broadcasted_iota(jnp.int32, (block, 2 * block), 1)
     for pp in range(per_step):
         p = pl.program_id(0) * per_step + pp
@@ -88,27 +96,32 @@
     )(inverse.reshape(-1), paired_weights)
 
 
-def pack_dense(dense_grad, live_index):
+def grad_pack(normed_rows, grad_rows, live_index, scale):
     column_count, live_count = live_index.shape
-    features = dense_grad.shape[0]
+    all_rows, features = normed_rows.shape
     block_size = features // column_count
     wide = live_count * block_size
     pair_count = column_count // 2
+    stripe = PAIRS_PER_STEP * 2 * block_size
     return pl.pallas_call(
-        pack_kernel,
-        out_shape=jax.ShapeDtypeStruct((pair_count, wide, 2 * block_size), dense_grad.dtype),
+        functools.partial(grad_pack_kernel, scale),
+        out_shape=jax.ShapeDtypeStruct((pair_count, wide, 2 * block_size), jnp.bfloat16),
         grid_spec=pltpu.PrefetchScalarGridSpec(
             num_scalar_prefetch=1,
             grid=(pair_count // PAIRS_PER_STEP,),
             in_specs=[
-                pl.BlockSpec((features, PAIRS_PER_STEP * 2 * block_size), lambda q, tbl: (0, q))
+                pl.BlockSpec((features, all_rows), lambda q, tbl: (0, 0)),
+                pl.BlockSpec((all_rows, stripe), lambda q, tbl: (0, q)),
             ],
             out_specs=pl.BlockSpec((PAIRS_PER_STEP, wide, 2 * block_size), lambda q, tbl: (q, 0, 0)),
+            scratch_shapes=[pltpu.VMEM((features, stripe), jnp.bfloat16)],
         ),
         cost_estimate=pl.CostEstimate(
-            flops=0, transcendentals=0, bytes_accessed=3 * pair_count * wide * 2 * block_size * 2
-        ),
-    )(live_index.reshape(-1).astype(jnp.int32), dense_grad)
+            flops=2 * all_rows * features * features,
+            transcendentals=0,
+            bytes_accessed=2 * all_rows * features * 2 + pair_count * wide * 2 * block_size * 2,
+        ),
+    )(live_index.reshape(-1).astype(jnp.int32), normed_rows.T, grad_rows)
 
 
 def spread_kernel(x_ref, o_ref, recv_ref, send_sem, recv_sem):
@@ -250,16 +263,12 @@
 
     all_rows = micro_count * tokens
     inverse_tokens = 1.0 / (all_rows * lax.axis_size("dp"))
-    dense_grad = (
-        lax.dot_general(
-            saved_normed.reshape(all_rows, features),
-            saved_grad.reshape(all_rows, features),
-            (((0,), (0,)), ((), ())),
-            preferred_element_type=jnp.float32,
-        )
-        * inverse_tokens
-    ).astype(jnp.bfloat16)
-    partial = pack_dense(dense_grad, live_index)
+    partial = grad_pack(
+        saved_normed.reshape(all_rows, features),
+        saved_grad.reshape(all_rows, features),
+        live_index,
+        inverse_tokens,
+    )
     own_grad = lax.psum_scatter(partial, "dp", scatter_dimension=0, tiled=True)
     gradient = (
         own_grad.reshape(live_count * block_size, own_columns, block_size)

time: 555 us -> 544 us (0.980)
  matrix products: 147 us -> 139 us
    dot_general x1 -> x0, matrix products: 15.9 us -> none  [local(): lax.dot_general(saved_normed.reshape(all_rows, features), saved_grad.resh...]
    dot_general x5, matrix products: 68.4 us -> 74.9 us  [layer_forward(): pre_act = jnp.dot(normed, dense_w, preferred_element_type=jnp.float32)]
  transfers between devices with their start and end apart: 10 -> 10, of which waited for: 10 -> 10; matrix products, arithmetic and copies ran while one was open for 2% -> 3% of each run, Pallas kernels for 0% -> 0%
where the time goes in v11:
time: 544 us; the launch traced here: 536 us
  waiting for transfers between devices  258 us (47%)
  matrix products  139 us (26%)
  Pallas kernels  56.9 us (10%)
  other arithmetic  30.5 us (6%)
  starting transfers between devices  21.5 us (4%)
  between operations  15.7 us (3%)
  local copies, waits for them, and re-layouts  14.6 us (3%)
    reduce_scatter x1, waiting for transfers between devices, local(): own_grad = lax.psum_scatter(partial, 'dp', scatter_dimension=0, tiled=True)  120 us
    dot_general x5, matrix products, layer_forward(): pre_act = jnp.dot(normed, dense_w, preferred_element_type=jnp.float32)  74.9 us
    all_gather x1, waiting for transfers between devices, local(): paired_weights = lax.all_gather(own_pair, 'dp', axis=0, tiled=True)  69.1 us
    ppermute x8, waiting for transfers between devices, shifted(): lax.ppermute(value, axis, [(source, source + steps) for source in range(l...  68.3 us
    dot_general x4, matrix products, layer_backward(): lax.dot_general(grad_pre, dense_w, (((1,), (1,)), ((), ())), preferred_el...  63.8 us
    pallas_call x1, Pallas kernels, expand_dense(): pl.pallas_call(expand_kernel, out_shape=jax.ShapeDtypeStruct((features, f...  25.8 us
    ppermute x8, starting transfers between devices, shifted(): lax.ppermute(value, axis, [(source, source + steps) for source in range(l...  21.4 us
    pallas_call x1, Pallas kernels, grad_pack(): pl.pallas_call(functools.partial(grad_pack_kernel, scale), out_shape=jax....  19 us
  transfers between devices with their start and end apart: 10, of which 10 were waited for; matrix products, arithmetic and copies ran while one was open for 3% of the time, Pallas kernels for 0%

profile of v11, /device:TPU:1, one launch (start us, length us, event | category | flops | bytes accessed | tf_op | source)
XLA Modules:
  0.0 535.8 jit_solution(7967770610096113413)
XLA Ops:
  17.5 69.1 %all-gather.2.cloned.1.call-done.t_ref = bf16[32,2048,128]{2,1,0:T(8,128)(2,1)} async-done(((bf16[1,2048,128]{2,1,0:T(8,128)(2,1)}), bf16[32,2048,128]{2,1,0:T(8,128)(2,1)}) %all-gather.2.cloned.1.call-update) | async-done | bytes 16777232 | tf_op jit(solution)/shard_map/all_gather | solution.py:227
  86.6 25.8 %shard_map.85 = bf16[4096,4096]{1,0:T(8,128)(2,1)} custom-call(s32[4096]{0:T(1024)} %select_n.124.table_ref, bf16[32,2048,128]{2,1,0:T(8,128)(2,1)} %all-gather.2.cloned.1.call-done.t_ref), custom_call_target="tpu_custom_call" | custom-call | bytes 50331648 | tf_op jit(solution)/shard_map/pallas_call | solution.py:84
  112.4 16.9 %fusion.77 = (bf16[64,4096]{1,0:T(8,128)(2,1)S(1)}, f32[64,4096]{1,0:T(8,128)S(1)}) fusion(bf16[2,32,4096]{2,1,0:T(8,128)(2,1)} %copy-done.2, bf16[64,4096]{1,0:T(8,128)(2,1)} %fusion.76, bf16[4096,4096]{1,0:T(8,128)(2,1)} %shard_map.85), kind=kOutput, calls=%fused_computation.122 | convolution fusion | flops 2149318656 | bytes 36175872 | tf_op jit(solution)/shard_map/dot_general | solution.py:189
  132.7 10.8 %collective-permute-done = bf16[64,4096]{1,0:T(8,128)(2,1)S(1)} collective-permute-done((bf16[64,4096]{1,0:T(8,128)(2,1)S(1)}, bf16[64,4096]{1,0:T(8,128)(2,1)S(1)}, u32[]{:S(2)}, u32[]{:S(2)}) %collective-permute-start) | collective-permute-done | bytes 524320 | tf_op jit(solution)/shard_map/ppermute | solution.py:17
  143.9 14.8 %fusion.37 = (bf16[64,4096]{1,0:T(8,128)(2,1)}, f32[64,4096]{1,0:T(8,128)S(1)}) fusion(bf16[64,4096]{1,0:T(8,128)(2,1)S(1)} %get-tuple-element.30, bf16[4096,4096]{1,0:T(8,128)(2,1)} %shard_map.85, f32[64]{0:T(128)S(1)} %add_rsqrt_fusion.8), kind=kOutput, calls=%fused_computation.64 | convolution fusion | flops 2150105088 | bytes 35651840 | tf_op jit(solution)/shard_map/dot_general | solution.py:189
  158.6 4.1 collective-permute-start.1
  163.9 9.3 %collective-permute-done.1 = bf16[64,4096]{1,0:T(8,128)(2,1)S(1)} collective-permute-done((bf16[64,4096]{1,0:T(8,128)(2,1)}, bf16[64,4096]{1,0:T(8,128)(2,1)S(1)}, u32[]{:S(2)}, u32[]{:S(2)}) %collective-permute-start.1) | collective-permute-done | bytes 524320 | tf_op jit(solution)/shard_map/ppermute | solution.py:17
  173.5 14.8 %fusion.40 = (bf16[64,4096]{1,0:T(8,128)(2,1)}, f32[64,4096]{1,0:T(8,128)S(1)}) fusion(bf16[64,4096]{1,0:T(8,128)(2,1)S(1)} %get-tuple-element.28, bf16[4096,4096]{1,0:T(8,128)(2,1)} %shard_map.85, f32[64]{0:T(128)S(1)} %add_rsqrt_fusion.7), kind=kOutput, calls=%fused_computation.67 | convolution fusion | flops 2150105088 | bytes 35651840 | tf_op jit(solution)/shard_map/dot_general | solution.py:189
  193.4 8.4 %collective-permute-done.2 = bf16[64,4096]{1,0:T(8,128)(2,1)S(1)} collective-permute-done((bf16[64,4096]{1,0:T(8,128)(2,1)}, bf16[64,4096]{1,0:T(8,128)(2,1)S(1)}, u32[]{:S(2)}, u32[]{:S(2)}) %collective-permute-start.2) | collective-permute-done | bytes 524320 | tf_op jit(solution)/shard_map/ppermute | solution.py:17
  202.1 14.8 %fusion.43 = (bf16[64,4096]{1,0:T(8,128)(2,1)}, f32[64,4096]{1,0:T(8,128)S(1)}) fusion(bf16[64,4096]{1,0:T(8,128)(2,1)S(1)} %get-tuple-element.26, bf16[4096,4096]{1,0:T(8,128)(2,1)} %shard_map.85, f32[64]{0:T(128)S(1)} %add_rsqrt_fusion.6), kind=kOutput, calls=%fused_computation.70 | convolution fusion | flops 2150105088 | bytes 35651840 | tf_op jit(solution)/shard_map/dot_general | solution.py:189
  216.9 4.2 collective-permute-start.3
  222.2 7.3 %collective-permute-done.3 = bf16[64,4096]{1,0:T(8,128)(2,1)S(1)} collective-permute-done((bf16[64,4096]{1,0:T(8,128)(2,1)}, bf16[64,4096]{1,0:T(8,128)(2,1)S(1)}, u32[]{:S(2)}, u32[]{:S(2)}) %collective-permute-start.3) | collective-permute-done | bytes 524320 | tf_op jit(solution)/shard_map/ppermute | solution.py:17
  229.8 13.8 %fusion = f32[5,64,4096]{2,1,0:T(8,128)S(1)} fusion(f32[5,64,4096]{2,1,0:T(8,128)S(1)} %bitcast_dynamic-update-slice_fusion, bf16[4096,4096]{1,0:T(8,128)(2,1)} %shard_map.85, bf16[64,4096]{1,0:T(8,128)(2,1)S(1)} %get-tuple-element.24, f32[64]{0:T(128)S(1)} %add_rsqrt_fusion.5), kind=kOutput, calls=%fused_computation.1 | convolution fusion | flops 2148270080 | bytes 35127808 | tf_op jit(solution)/shard_map/dot_general | solution.py:189
  246.7 15.9 %fusion.34 = (f32[64]{0:T(128)S(1)}, f32[64]{0:T(128)S(1)}, f32[64]{0:T(128)S(1)}, f32[64]{0:T(128)S(1)}, f32[64,4096]{1,0:T(8,128)S(1)}) fusion(bf16[5,64,4096]{2,1,0:T(8,128)(2,1)S(1)} %get-tuple-element.37, s32[]{:T(128)S(6)} %dynamic_slice.69, f32[64]{0:T(128)S(1)} %add_rsqrt_fusion.4, s32[]{:T(128)S(6)} %dynamic_slice.60, s32[]{:T(128)S(6)} %dynamic_slice.66, ...), kind=kOutput, calls=%fused_computation.61 | convolution fusion | flops 2150891520 | bytes 37225744 | tf_op jit(solution)/shard_map/dot_general | solution.py:200
  267.1 9.5 %collective-permute-done.4 = bf16[64,4096]{1,0:T(8,128)(2,1)S(1)} collective-permute-done((bf16[64,4096]{1,0:T(8,128)(2,1)S(1)}, bf16[64,4096]{1,0:T(8,128)(2,1)S(1)}, u32[]{:S(2)}, u32[]{:S(2)}) %collective-permute-start.4) | collective-permute-done | bytes 524320 | tf_op jit(solution)/shard_map/ppermute | solution.py:17
  278.2 15.7 %fusion.15 = (f32[64]{0:T(128)S(1)}, f32[64,4096]{1,0:T(8,128)S(1)}) fusion(f32[64]{0:T(128)S(1)} %add_rsqrt_fusion.3, bf16[5,64,4096]{2,1,0:T(8,128)(2,1)S(1)} %get-tuple-element.37, s32[]{:T(128)S(6)} %dynamic_slice.63, bf16[64,4096]{1,0:T(8,128)(2,1)S(1)} %get-tuple-element.57, bf16[4096,4096]{1,0:T(8,128)(2,1)} %shard_map.85), kind=kOutput, calls=%fused_computation.42 | convolution fusion | flops 2148532224 | bytes 35652100 | tf_op jit(solution)/shard_map/dot_general | solution.py:200
  295.9 9.3 %collective-permute-done.5 = bf16[64,4096]{1,0:T(8,128)(2,1)S(1)} collective-permute-done((bf16[64,4096]{1,0:T(8,128)(2,1)S(1)}, bf16[64,4096]{1,0:T(8,128)(2,1)S(1)}, u32[]{:S(2)}, u32[]{:S(2)}) %collective-permute-start.5) | collective-permute-done | bytes 524320 | tf_op jit(solution)/shard_map/ppermute | solution.py:17
  306.8 15.7 %fusion.12 = (f32[64]{0:T(128)S(1)}, f32[64,4096]{1,0:T(8,128)S(1)}) fusion(f32[64]{0:T(128)S(1)} %add_rsqrt_fusion.2, bf16[5,64,4096]{2,1,0:T(8,128)(2,1)S(1)} %get-tuple-element.37, s32[]{:T(128)S(6)} %dynamic_slice.66, bf16[64,4096]{1,0:T(8,128)(2,1)S(1)} %get-tuple-element.61, bf16[4096,4096]{1,0:T(8,128)(2,1)} %shard_map.85), kind=kOutput, calls=%fused_computation.39 | convolution fusion | flops 2148532224 | bytes 35652100 | tf_op jit(solution)/shard_map/dot_general | solution.py:200
  324.2 8.6 %collective-permute-done.6 = bf16[64,4096]{1,0:T(8,128)(2,1)S(1)} collective-permute-done((bf16[64,4096]{1,0:T(8,128)(2,1)S(1)}, bf16[64,4096]{1,0:T(8,128)(2,1)S(1)}, u32[]{:S(2)}, u32[]{:S(2)}) %collective-permute-start.6) | collective-permute-done | bytes 524320 | tf_op jit(solution)/shard_map/ppermute | solution.py:17
  334.5 16.6 %fusion.9 = (f32[64]{0:T(128)S(1)}, f32[64,4096]{1,0:T(8,128)S(1)}) fusion(f32[64]{0:T(128)S(1)} %add_rsqrt_fusion.1, bf16[5,64,4096]{2,1,0:T(8,128)(2,1)S(1)} %get-tuple-element.37, s32[]{:T(128)S(6)} %dynamic_slice.69, bf16[64,4096]{1,0:T(8,128)(2,1)S(1)} %get-tuple-element.65, bf16[4096,4096]{1,0:T(8,128)(2,1)} %shard_map.85), kind=kOutput, calls=%fused_computation.36 | convolution fusion | flops 2148532224 | bytes 35652100 | tf_op jit(solution)/shard_map/dot_general | solution.py:200
  357.2 5.2 collective-permute-done.7
  367.2 19.0 %shard_map.86 = bf16[32,2048,128]{2,1,0:T(8,128)(2,1)} custom-call(s32[2048]{0:T(1024)} %reshape_squeeze.3.table_ref, bf16[4096,128]{1,0:T(8,128)(2,1)} %bitcast.261, bf16[128,4096]{1,0:T(8,128)(2,1)} %bitcast.260), custom_call_target="tpu_custom_call" | custom-call | flops 4294967296 | bytes 18874368 | tf_op jit(solution)/shard_map/pallas_call | solution.py:106
  386.3 120.4 %reduce-scatter.2.cloned.1.call-done = bf16[1,2048,128]{2,1,0:T(8,128)(2,1)} async-done(((bf16[32,2048,128]{2,1,0:T(8,128)(2,1)}), bf16[1,2048,128]{2,1,0:T(8,128)(2,1)}) %reduce-scatter.2.cloned.1.call-update) | async-done | bytes 524304 | tf_op jit(solution)/shard_map/reduce_scatter | solution.py:272
  513.1 12.1 %shard_map.87 = f32[8,128]{1,0:T(8,128)} custom-call(f32[8,128]{1,0:T(8,128)} %scatter.4.x_ref), custom_call_target="tpu_custom_call" | custom-call | tf_op jit(solution)/shard_map/pallas_call | solution.py:170
  (100 shorter events, 58.3 us)
Async XLA Ops:
  7.2 4.2 copy-start.6
  7.2 4.5 copy-start.8
  7.2 79.4 %all-gather.2.cloned.1.call-start = ((), (), s32[]{:S(2)}) async-start(), calls=%async_computation.1 | async-start | bytes 17301504 | tf_op jit(solution)/shard_map/all_gather | solution.py:227
  9.4 497.4 %reduce-scatter.2.cloned.1.call-start = ((), (), s32[]{:S(2)}) async-start(), calls=%async_computation.2 | async-start | bytes 17301504 | tf_op jit(solution)/shard_map/reduce_scatter | solution.py:272
  11.6 2.7 copy-start.2
  112.4 31.1 %copy-start = (bf16[2,32,4096]{2,1,0:T(8,128)(2,1)S(1)}, bf16[2,32,4096]{2,1,0:T(8,128)(2,1)}, u32[]{:S(2)}) copy-start(bf16[2,32,4096]{2,1,0:T(8,128)(2,1)} %slice.42) | copy-start | bytes 1572868
  129.3 14.2 %collective-permute-start = (bf16[64,4096]{1,0:T(8,128)(2,1)S(1)}, bf16[64,4096]{1,0:T(8,128)(2,1)S(1)}, u32[]{:S(2)}, u32[]{:S(2)}) collective-permute-start(bf16[64,4096]{1,0:T(8,128)(2,1)S(1)} %get-tuple-element.47), channel_id=1, source_target_pairs={{0,32},{32,64},{64,96},{1,33},{33,65},{65,97},{2,34},{34,66},{66,9... | collective-permute-start | bytes 1572872 | tf_op jit(solution)/shard_map/ppermute | solution.py:17
  158.6 14.5 %collective-permute-start.1 = (bf16[64,4096]{1,0:T(8,128)(2,1)}, bf16[64,4096]{1,0:T(8,128)(2,1)S(1)}, u32[]{:S(2)}, u32[]{:S(2)}) collective-permute-start(bf16[64,4096]{1,0:T(8,128)(2,1)} %get-tuple-element.49), channel_id=1, source_target_pairs={{0,32},{32,64},{64,96},{1,33},{33,65},{65,97},{2,34},{34,66},{66,9... | collective-permute-start | bytes 1572872 | tf_op jit(solution)/shard_map/ppermute | solution.py:17
  188.3 13.5 %collective-permute-start.2 = (bf16[64,4096]{1,0:T(8,128)(2,1)}, bf16[64,4096]{1,0:T(8,128)(2,1)S(1)}, u32[]{:S(2)}, u32[]{:S(2)}) collective-permute-start(bf16[64,4096]{1,0:T(8,128)(2,1)} %get-tuple-element.51), channel_id=1, source_target_pairs={{0,32},{32,64},{64,96},{1,33},{33,65},{65,97},{2,34},{34,66},{66,9... | collective-permute-start | bytes 1572872 | tf_op jit(solution)/shard_map/ppermute | solution.py:17
  216.9 12.6 %collective-permute-start.3 = (bf16[64,4096]{1,0:T(8,128)(2,1)}, bf16[64,4096]{1,0:T(8,128)(2,1)S(1)}, u32[]{:S(2)}, u32[]{:S(2)}) collective-permute-start(bf16[64,4096]{1,0:T(8,128)(2,1)} %get-tuple-element.53), channel_id=1, source_target_pairs={{0,32},{32,64},{64,96},{1,33},{33,65},{65,97},{2,34},{34,66},{66,9... | collective-permute-start | bytes 1572872 | tf_op jit(solution)/shard_map/ppermute | solution.py:17
  229.8 16.3 %copy-start.4 = (bf16[4,32,4096]{2,1,0:T(8,128)(2,1)S(1)}, bf16[4,32,4096]{2,1,0:T(8,128)(2,1)}, u32[]{:S(2)}) copy-start(bf16[4,32,4096]{2,1,0:T(8,128)(2,1)} %param.9) | copy-start | bytes 3145732
  243.6 2.6 copy-start.1
  262.6 2.8 copy-start.3
  264.1 12.4 %collective-permute-start.4 = (bf16[64,4096]{1,0:T(8,128)(2,1)S(1)}, bf16[64,4096]{1,0:T(8,128)(2,1)S(1)}, u32[]{:S(2)}, u32[]{:S(2)}) collective-permute-start(bf16[64,4096]{1,0:T(8,128)(2,1)S(1)} %fusion.22), channel_id=1, source_target_pairs={{32,0},{64,32},{96,64},{33,1},{65,33},{97,65},{34,2},{66,34},{98,6... | collective-permute-start | bytes 1572872 | tf_op jit(solution)/shard_map/ppermute | solution.py:17
  294.3 10.8 %collective-permute-start.5 = (bf16[64,4096]{1,0:T(8,128)(2,1)S(1)}, bf16[64,4096]{1,0:T(8,128)(2,1)S(1)}, u32[]{:S(2)}, u32[]{:S(2)}) collective-permute-start(bf16[64,4096]{1,0:T(8,128)(2,1)S(1)} %fusion.26), channel_id=1, source_target_pairs={{32,0},{64,32},{96,64},{33,1},{65,33},{97,65},{34,2},{66,34},{98,6... | collective-permute-start | bytes 1572872 | tf_op jit(solution)/shard_map/ppermute | solution.py:17
  322.9 9.9 %collective-permute-start.6 = (bf16[64,4096]{1,0:T(8,128)(2,1)S(1)}, bf16[64,4096]{1,0:T(8,128)(2,1)S(1)}, u32[]{:S(2)}, u32[]{:S(2)}) collective-permute-start(bf16[64,4096]{1,0:T(8,128)(2,1)S(1)} %fusion.28), channel_id=1, source_target_pairs={{32,0},{64,32},{96,64},{33,1},{65,33},{97,65},{34,2},{66,34},{98,6... | collective-permute-start | bytes 1572872 | tf_op jit(solution)/shard_map/ppermute | solution.py:17
  334.5 16.6 %copy-start.7 = (bf16[5,64,4096]{2,1,0:T(8,128)(2,1)}, bf16[5,64,4096]{2,1,0:T(8,128)(2,1)S(1)}, u32[]{:S(2)}) copy-start(bf16[5,64,4096]{2,1,0:T(8,128)(2,1)S(1)} %get-tuple-element.64) | copy-start | bytes 7864324
  352.3 10.1 %collective-permute-start.7 = (bf16[64,4096]{1,0:T(8,128)(2,1)}, bf16[64,4096]{1,0:T(8,128)(2,1)S(1)}, u32[]{:S(2)}, u32[]{:S(2)}) collective-permute-start(bf16[64,4096]{1,0:T(8,128)(2,1)} %fusion.30), channel_id=1, source_target_pairs={{32,0},{64,32},{96,64},{33,1},{65,33},{97,65},{34,2},{66,34},{98,6... | collective-permute-start | bytes 1572872 | tf_op jit(solution)/shard_map/ppermute | solution.py:17
  386.1 121.9 %copy-start.5 = (bf16[1,2,64,2048]{3,2,1,0:T(8,128)(2,1)S(1)}, bf16[1,2,64,2048]{3,2,1,0:T(8,128)(2,1)}, u32[]{:S(2)}) copy-start(bf16[1,2,64,2048]{3,2,1,0:T(8,128)(2,1)} %param.10) | copy-start | bytes 1572868
Sparse Core Ops, SparseCore 0:
  10.3 76.2 all-gather.1
  386.3 120.4 reduce-scatter.1

commit v12 on v11

--- a/solution.py
+++ b/solution.py
@@ -31,13 +31,10 @@
         for r in range(blocks):
             k0 = table_ref[(2 * p) * blocks + r]
             k1 = table_ref[(2 * p + 1) * blocks + r]
-            s0 = pl.multiple_of(jnp.maximum(k0, 0) * block, block)
-            s1 = pl.multiple_of(jnp.maximum(k1, 0) * block, block)
+            s0 = pl.multiple_of(k0 * block, block)
+            s1 = pl.multiple_of(k1 * block, block)
             t0 = t_ref[pp, pl.ds(s0, block), :]
             t1 = t_ref[pp, pl.ds(s1, block), :]
-            zero = jnp.zeros_like(t0)
-            t0 = jnp.where(k0 >= 0, t0, zero)
-            t1 = jnp.where(k1 >= 0, t1, zero)
             o_ref[r * block:(r + 1) * block, pp * 2 * block:(pp + 1) * 2 * block] = jnp.where(
                 lane < block, t0, t1
             )
@@ -79,7 +76,7 @@
     hit = live_index[:, :, None] == targets[None, None, :]
     k_ids = jnp.arange(live_count, dtype=jnp.int32)[None, :, None]
     inverse = jnp.where(
-        jnp.any(hit, axis=1), jnp.sum(jnp.where(hit, k_ids, 0), axis=1), -1
+        jnp.any(hit, axis=1), jnp.sum(jnp.where(hit, k_ids, 0), axis=1), live_count
     ).astype(jnp.int32)
     return pl.pallas_call(
         expand_kernel,
@@ -224,6 +221,7 @@
     block_size = weights.shape[2]
     live_index = live_rows[0]
     own_pair = weights[0].transpose(2, 0, 1).reshape(1, live_count * block_size, own_columns * block_size)
+    own_pair = jnp.pad(own_pair, ((0, 0), (0, block_size), (0, 0)))
     paired_weights = lax.all_gather(own_pair, "dp", axis=0, tiled=True)
     dense_w = expand_dense(paired_weights, live_index)
     tick_count = micro_count + sections - 1

time: 544 us -> 544 us (level)
  no operation moved by 1% of the time
where the time goes in v12:
time: 544 us; the launch traced here: 534 us
  waiting for transfers between devices  260 us (48%)
  matrix products  139 us (26%)
  Pallas kernels  53.9 us (10%)
  other arithmetic  30.6 us (6%)
  starting transfers between devices  21.7 us (4%)
  between operations  15.5 us (3%)
  local copies, waits for them, and re-layouts  13.6 us (2%)
    reduce_scatter x1, waiting for transfers between devices, local(): own_grad = lax.psum_scatter(partial, 'dp', scatter_dimension=0, tiled=True)  120 us
    dot_general x5, matrix products, layer_forward(): pre_act = jnp.dot(normed, dense_w, preferred_element_type=jnp.float32)  74.8 us
    all_gather x1, waiting for transfers between devices, local(): paired_weights = lax.all_gather(own_pair, 'dp', axis=0, tiled=True)  71.8 us
    ppermute x8, waiting for transfers between devices, shifted(): lax.ppermute(value, axis, [(source, source + steps) for source in range(l...  68 us
    dot_general x4, matrix products, layer_backward(): lax.dot_general(grad_pre, dense_w, (((1,), (1,)), ((), ())), preferred_el...  63.8 us
    pallas_call x1, Pallas kernels, expand_dense(): pl.pallas_call(expand_kernel, out_shape=jax.ShapeDtypeStruct((features, f...  22.8 us
    ppermute x8, starting transfers between devices, shifted(): lax.ppermute(value, axis, [(source, source + steps) for source in range(l...  21.6 us
    pallas_call x1, Pallas kernels, grad_pack(): pl.pallas_call(functools.partial(grad_pack_kernel, scale), out_shape=jax....  19 us
  transfers between devices with their start and end apart: 10, of which 10 were waited for; matrix products, arithmetic and copies ran while one was open for 3% of the time, Pallas kernels for 0%

profile of v12, /device:TPU:1, one launch (start us, length us, event | category | flops | bytes accessed | tf_op | source)
XLA Modules:
  0.0 534.2 jit_solution(16573941030853324154)
XLA Ops:
  16.6 71.8 %all-gather.2.cloned.1.call-done.t_ref = bf16[32,2112,128]{2,1,0:T(8,128)(2,1)} async-done(((bf16[1,2112,128]{2,1,0:T(8,128)(2,1)}), bf16[32,2112,128]{2,1,0:T(8,128)(2,1)}) %all-gather.2.cloned.1.call-update) | async-done | bytes 17301520 | tf_op jit(solution)/shard_map/all_gather | solution.py:225
  88.4 22.8 %shard_map.85 = bf16[4096,4096]{1,0:T(8,128)(2,1)} custom-call(s32[4096]{0:T(1024)} %select_n.124.table_ref, bf16[32,2112,128]{2,1,0:T(8,128)(2,1)} %all-gather.2.cloned.1.call-done.t_ref), custom_call_target="tpu_custom_call" | custom-call | bytes 51904512 | tf_op jit(solution)/shard_map/pallas_call | solution.py:81
  111.1 16.8 %fusion.77 = (bf16[64,4096]{1,0:T(8,128)(2,1)S(1)}, f32[64,4096]{1,0:T(8,128)S(1)}) fusion(bf16[2,32,4096]{2,1,0:T(8,128)(2,1)} %copy-done.2, bf16[64,4096]{1,0:T(8,128)(2,1)} %fusion.76, bf16[4096,4096]{1,0:T(8,128)(2,1)} %shard_map.85), kind=kOutput, calls=%fused_computation.122 | convolution fusion | flops 2149318656 | bytes 36175872 | tf_op jit(solution)/shard_map/dot_general | solution.py:186
  131.2 10.9 %collective-permute-done = bf16[64,4096]{1,0:T(8,128)(2,1)S(1)} collective-permute-done((bf16[64,4096]{1,0:T(8,128)(2,1)S(1)}, bf16[64,4096]{1,0:T(8,128)(2,1)S(1)}, u32[]{:S(2)}, u32[]{:S(2)}) %collective-permute-start) | collective-permute-done | bytes 524320 | tf_op jit(solution)/shard_map/ppermute | solution.py:17
  142.5 14.8 %fusion.37 = (bf16[64,4096]{1,0:T(8,128)(2,1)}, f32[64,4096]{1,0:T(8,128)S(1)}) fusion(bf16[64,4096]{1,0:T(8,128)(2,1)S(1)} %get-tuple-element.30, bf16[4096,4096]{1,0:T(8,128)(2,1)} %shard_map.85, f32[64]{0:T(128)S(1)} %add_rsqrt_fusion.8), kind=kOutput, calls=%fused_computation.64 | convolution fusion | flops 2150105088 | bytes 35651840 | tf_op jit(solution)/shard_map/dot_general | solution.py:186
  157.2 4.6 collective-permute-start.1
  163.0 8.8 %collective-permute-done.1 = bf16[64,4096]{1,0:T(8,128)(2,1)S(1)} collective-permute-done((bf16[64,4096]{1,0:T(8,128)(2,1)}, bf16[64,4096]{1,0:T(8,128)(2,1)S(1)}, u32[]{:S(2)}, u32[]{:S(2)}) %collective-permute-start.1) | collective-permute-done | bytes 524320 | tf_op jit(solution)/shard_map/ppermute | solution.py:17
  172.1 14.8 %fusion.40 = (bf16[64,4096]{1,0:T(8,128)(2,1)}, f32[64,4096]{1,0:T(8,128)S(1)}) fusion(bf16[64,4096]{1,0:T(8,128)(2,1)S(1)} %get-tuple-element.28, bf16[4096,4096]{1,0:T(8,128)(2,1)} %shard_map.85, f32[64]{0:T(128)S(1)} %add_rsqrt_fusion.7), kind=kOutput, calls=%fused_computation.67 | convolution fusion | flops 2150105088 | bytes 35651840 | tf_op jit(solution)/shard_map/dot_general | solution.py:186
  192.0 8.4 %collective-permute-done.2 = bf16[64,4096]{1,0:T(8,128)(2,1)S(1)} collective-permute-done((bf16[64,4096]{1,0:T(8,128)(2,1)}, bf16[64,4096]{1,0:T(8,128)(2,1)S(1)}, u32[]{:S(2)}, u32[]{:S(2)}) %collective-permute-start.2) | collective-permute-done | bytes 524320 | tf_op jit(solution)/shard_map/ppermute | solution.py:17
  200.7 14.8 %fusion.43 = (bf16[64,4096]{1,0:T(8,128)(2,1)}, f32[64,4096]{1,0:T(8,128)S(1)}) fusion(bf16[64,4096]{1,0:T(8,128)(2,1)S(1)} %get-tuple-element.26, bf16[4096,4096]{1,0:T(8,128)(2,1)} %shard_map.85, f32[64]{0:T(128)S(1)} %add_rsqrt_fusion.6), kind=kOutput, calls=%fused_computation.70 | convolution fusion | flops 2150105088 | bytes 35651840 | tf_op jit(solution)/shard_map/dot_general | solution.py:186
  215.5 4.2 collective-permute-start.3
  220.8 7.3 %collective-permute-done.3 = bf16[64,4096]{1,0:T(8,128)(2,1)S(1)} collective-permute-done((bf16[64,4096]{1,0:T(8,128)(2,1)}, bf16[64,4096]{1,0:T(8,128)(2,1)S(1)}, u32[]{:S(2)}, u32[]{:S(2)}) %collective-permute-start.3) | collective-permute-done | bytes 524320 | tf_op jit(solution)/shard_map/ppermute | solution.py:17
  228.4 13.8 %fusion = f32[5,64,4096]{2,1,0:T(8,128)S(1)} fusion(f32[5,64,4096]{2,1,0:T(8,128)S(1)} %bitcast_dynamic-update-slice_fusion, bf16[4096,4096]{1,0:T(8,128)(2,1)} %shard_map.85, bf16[64,4096]{1,0:T(8,128)(2,1)S(1)} %get-tuple-element.24, f32[64]{0:T(128)S(1)} %add_rsqrt_fusion.5), kind=kOutput, calls=%fused_computation.1 | convolution fusion | flops 2148270080 | bytes 35127808 | tf_op jit(solution)/shard_map/dot_general | solution.py:186
  245.4 15.9 %fusion.34 = (f32[64]{0:T(128)S(1)}, f32[64]{0:T(128)S(1)}, f32[64]{0:T(128)S(1)}, f32[64]{0:T(128)S(1)}, f32[64,4096]{1,0:T(8,128)S(1)}) fusion(bf16[5,64,4096]{2,1,0:T(8,128)(2,1)S(1)} %get-tuple-element.37, s32[]{:T(128)S(6)} %dynamic_slice.69, f32[64]{0:T(128)S(1)} %add_rsqrt_fusion.4, s32[]{:T(128)S(6)} %dynamic_slice.60, s32[]{:T(128)S(6)} %dynamic_slice.66, ...), kind=kOutput, calls=%fused_computation.61 | convolution fusion | flops 2150891520 | bytes 37225744 | tf_op jit(solution)/shard_map/dot_general | solution.py:197
  265.7 9.4 %collective-permute-done.4 = bf16[64,4096]{1,0:T(8,128)(2,1)S(1)} collective-permute-done((bf16[64,4096]{1,0:T(8,128)(2,1)S(1)}, bf16[64,4096]{1,0:T(8,128)(2,1)S(1)}, u32[]{:S(2)}, u32[]{:S(2)}) %collective-permute-start.4) | collective-permute-done | bytes 524320 | tf_op jit(solution)/shard_map/ppermute | solution.py:17
  276.8 15.7 %fusion.15 = (f32[64]{0:T(128)S(1)}, f32[64,4096]{1,0:T(8,128)S(1)}) fusion(f32[64]{0:T(128)S(1)} %add_rsqrt_fusion.3, bf16[5,64,4096]{2,1,0:T(8,128)(2,1)S(1)} %get-tuple-element.37, s32[]{:T(128)S(6)} %dynamic_slice.63, bf16[64,4096]{1,0:T(8,128)(2,1)S(1)} %get-tuple-element.57, bf16[4096,4096]{1,0:T(8,128)(2,1)} %shard_map.85), kind=kOutput, calls=%fused_computation.42 | convolution fusion | flops 2148532224 | bytes 35652100 | tf_op jit(solution)/shard_map/dot_general | solution.py:197
  294.4 9.3 %collective-permute-done.5 = bf16[64,4096]{1,0:T(8,128)(2,1)S(1)} collective-permute-done((bf16[64,4096]{1,0:T(8,128)(2,1)S(1)}, bf16[64,4096]{1,0:T(8,128)(2,1)S(1)}, u32[]{:S(2)}, u32[]{:S(2)}) %collective-permute-start.5) | collective-permute-done | bytes 524320 | tf_op jit(solution)/shard_map/ppermute | solution.py:17
  305.4 15.7 %fusion.12 = (f32[64]{0:T(128)S(1)}, f32[64,4096]{1,0:T(8,128)S(1)}) fusion(f32[64]{0:T(128)S(1)} %add_rsqrt_fusion.2, bf16[5,64,4096]{2,1,0:T(8,128)(2,1)S(1)} %get-tuple-element.37, s32[]{:T(128)S(6)} %dynamic_slice.66, bf16[64,4096]{1,0:T(8,128)(2,1)S(1)} %get-tuple-element.61, bf16[4096,4096]{1,0:T(8,128)(2,1)} %shard_map.85), kind=kOutput, calls=%fused_computation.39 | convolution fusion | flops 2148532224 | bytes 35652100 | tf_op jit(solution)/shard_map/dot_general | solution.py:197
  322.8 8.6 %collective-permute-done.6 = bf16[64,4096]{1,0:T(8,128)(2,1)S(1)} collective-permute-done((bf16[64,4096]{1,0:T(8,128)(2,1)S(1)}, bf16[64,4096]{1,0:T(8,128)(2,1)S(1)}, u32[]{:S(2)}, u32[]{:S(2)}) %collective-permute-start.6) | collective-permute-done | bytes 524320 | tf_op jit(solution)/shard_map/ppermute | solution.py:17
  333.1 16.6 %fusion.9 = (f32[64]{0:T(128)S(1)}, f32[64,4096]{1,0:T(8,128)S(1)}) fusion(f32[64]{0:T(128)S(1)} %add_rsqrt_fusion.1, bf16[5,64,4096]{2,1,0:T(8,128)(2,1)S(1)} %get-tuple-element.37, s32[]{:T(128)S(6)} %dynamic_slice.69, bf16[64,4096]{1,0:T(8,128)(2,1)S(1)} %get-tuple-element.65, bf16[4096,4096]{1,0:T(8,128)(2,1)} %shard_map.85), kind=kOutput, calls=%fused_computation.36 | convolution fusion | flops 2148532224 | bytes 35652100 | tf_op jit(solution)/shard_map/dot_general | solution.py:197
  355.8 5.2 collective-permute-done.7
  365.8 19.0 %shard_map.86 = bf16[32,2048,128]{2,1,0:T(8,128)(2,1)} custom-call(s32[2048]{0:T(1024)} %reshape_squeeze.3.table_ref, bf16[4096,128]{1,0:T(8,128)(2,1)} %bitcast.261, bf16[128,4096]{1,0:T(8,128)(2,1)} %bitcast.260), custom_call_target="tpu_custom_call" | custom-call | flops 4294967296 | bytes 18874368 | tf_op jit(solution)/shard_map/pallas_call | solution.py:103
  384.9 120.4 %reduce-scatter.2.cloned.1.call-done = bf16[1,2048,128]{2,1,0:T(8,128)(2,1)} async-done(((bf16[32,2048,128]{2,1,0:T(8,128)(2,1)}), bf16[1,2048,128]{2,1,0:T(8,128)(2,1)}) %reduce-scatter.2.cloned.1.call-update) | async-done | bytes 524304 | tf_op jit(solution)/shard_map/reduce_scatter | solution.py:270
  511.7 12.1 %shard_map.87 = f32[8,128]{1,0:T(8,128)} custom-call(f32[8,128]{1,0:T(8,128)} %scatter.4.x_ref), custom_call_target="tpu_custom_call" | custom-call | tf_op jit(solution)/shard_map/pallas_call | solution.py:167
  (101 shorter events, 57.2 us)
Async XLA Ops:
  7.2 2.4 copy-start.6
  7.2 3.6 copy-start.8
  7.2 81.2 %all-gather.2.cloned.1.call-start = ((), (), s32[]{:S(2)}) async-start(), calls=%async_computation.1 | async-start | bytes 17842176 | tf_op jit(solution)/shard_map/all_gather | solution.py:225
  9.5 495.9 %reduce-scatter.2.cloned.1.call-start = ((), (), s32[]{:S(2)}) async-start(), calls=%async_computation.2 | async-start | bytes 17301504 | tf_op jit(solution)/shard_map/reduce_scatter | solution.py:270
  10.6 2.7 copy-start.2
  111.1 31.0 %copy-start = (bf16[2,32,4096]{2,1,0:T(8,128)(2,1)S(1)}, bf16[2,32,4096]{2,1,0:T(8,128)(2,1)}, u32[]{:S(2)}) copy-start(bf16[2,32,4096]{2,1,0:T(8,128)(2,1)} %slice.42) | copy-start | bytes 1572868
  128.0 14.2 %collective-permute-start = (bf16[64,4096]{1,0:T(8,128)(2,1)S(1)}, bf16[64,4096]{1,0:T(8,128)(2,1)S(1)}, u32[]{:S(2)}, u32[]{:S(2)}) collective-permute-start(bf16[64,4096]{1,0:T(8,128)(2,1)S(1)} %get-tuple-element.47), channel_id=1, source_target_pairs={{0,32},{32,64},{64,96},{1,33},{33,65},{65,97},{2,34},{34,66},{66,9... | collective-permute-start | bytes 1572872 | tf_op jit(solution)/shard_map/ppermute | solution.py:17
  157.2 14.5 %collective-permute-start.1 = (bf16[64,4096]{1,0:T(8,128)(2,1)}, bf16[64,4096]{1,0:T(8,128)(2,1)S(1)}, u32[]{:S(2)}, u32[]{:S(2)}) collective-permute-start(bf16[64,4096]{1,0:T(8,128)(2,1)} %get-tuple-element.49), channel_id=1, source_target_pairs={{0,32},{32,64},{64,96},{1,33},{33,65},{65,97},{2,34},{34,66},{66,9... | collective-permute-start | bytes 1572872 | tf_op jit(solution)/shard_map/ppermute | solution.py:17
  186.9 13.5 %collective-permute-start.2 = (bf16[64,4096]{1,0:T(8,128)(2,1)}, bf16[64,4096]{1,0:T(8,128)(2,1)S(1)}, u32[]{:S(2)}, u32[]{:S(2)}) collective-permute-start(bf16[64,4096]{1,0:T(8,128)(2,1)} %get-tuple-element.51), channel_id=1, source_target_pairs={{0,32},{32,64},{64,96},{1,33},{33,65},{65,97},{2,34},{34,66},{66,9... | collective-permute-start | bytes 1572872 | tf_op jit(solution)/shard_map/ppermute | solution.py:17
  215.5 12.6 %collective-permute-start.3 = (bf16[64,4096]{1,0:T(8,128)(2,1)}, bf16[64,4096]{1,0:T(8,128)(2,1)S(1)}, u32[]{:S(2)}, u32[]{:S(2)}) collective-permute-start(bf16[64,4096]{1,0:T(8,128)(2,1)} %get-tuple-element.53), channel_id=1, source_target_pairs={{0,32},{32,64},{64,96},{1,33},{33,65},{65,97},{2,34},{34,66},{66,9... | collective-permute-start | bytes 1572872 | tf_op jit(solution)/shard_map/ppermute | solution.py:17
  228.4 16.3 %copy-start.4 = (bf16[4,32,4096]{2,1,0:T(8,128)(2,1)S(1)}, bf16[4,32,4096]{2,1,0:T(8,128)(2,1)}, u32[]{:S(2)}) copy-start(bf16[4,32,4096]{2,1,0:T(8,128)(2,1)} %param.9) | copy-start | bytes 3145732
  242.2 2.6 copy-start.1
  261.2 2.8 copy-start.3
  262.8 12.4 %collective-permute-start.4 = (bf16[64,4096]{1,0:T(8,128)(2,1)S(1)}, bf16[64,4096]{1,0:T(8,128)(2,1)S(1)}, u32[]{:S(2)}, u32[]{:S(2)}) collective-permute-start(bf16[64,4096]{1,0:T(8,128)(2,1)S(1)} %fusion.22), channel_id=1, source_target_pairs={{32,0},{64,32},{96,64},{33,1},{65,33},{97,65},{34,2},{66,34},{98,6... | collective-permute-start | bytes 1572872 | tf_op jit(solution)/shard_map/ppermute | solution.py:17
  292.9 10.8 %collective-permute-start.5 = (bf16[64,4096]{1,0:T(8,128)(2,1)S(1)}, bf16[64,4096]{1,0:T(8,128)(2,1)S(1)}, u32[]{:S(2)}, u32[]{:S(2)}) collective-permute-start(bf16[64,4096]{1,0:T(8,128)(2,1)S(1)} %fusion.26), channel_id=1, source_target_pairs={{32,0},{64,32},{96,64},{33,1},{65,33},{97,65},{34,2},{66,34},{98,6... | collective-permute-start | bytes 1572872 | tf_op jit(solution)/shard_map/ppermute | solution.py:17
  321.5 9.9 %collective-permute-start.6 = (bf16[64,4096]{1,0:T(8,128)(2,1)S(1)}, bf16[64,4096]{1,0:T(8,128)(2,1)S(1)}, u32[]{:S(2)}, u32[]{:S(2)}) collective-permute-start(bf16[64,4096]{1,0:T(8,128)(2,1)S(1)} %fusion.28), channel_id=1, source_target_pairs={{32,0},{64,32},{96,64},{33,1},{65,33},{97,65},{34,2},{66,34},{98,6... | collective-permute-start | bytes 1572872 | tf_op jit(solution)/shard_map/ppermute | solution.py:17
  333.1 16.6 %copy-start.7 = (bf16[5,64,4096]{2,1,0:T(8,128)(2,1)}, bf16[5,64,4096]{2,1,0:T(8,128)(2,1)S(1)}, u32[]{:S(2)}) copy-start(bf16[5,64,4096]{2,1,0:T(8,128)(2,1)S(1)} %get-tuple-element.64) | copy-start | bytes 7864324
  350.9 10.1 %collective-permute-start.7 = (bf16[64,4096]{1,0:T(8,128)(2,1)}, bf16[64,4096]{1,0:T(8,128)(2,1)S(1)}, u32[]{:S(2)}, u32[]{:S(2)}) collective-permute-start(bf16[64,4096]{1,0:T(8,128)(2,1)} %fusion.30), channel_id=1, source_target_pairs={{32,0},{64,32},{96,64},{33,1},{65,33},{97,65},{34,2},{66,34},{98,6... | collective-permute-start | bytes 1572872 | tf_op jit(solution)/shard_map/ppermute | solution.py:17
  384.7 121.9 %copy-start.5 = (bf16[1,2,64,2048]{3,2,1,0:T(8,128)(2,1)S(1)}, bf16[1,2,64,2048]{3,2,1,0:T(8,128)(2,1)}, u32[]{:S(2)}) copy-start(bf16[1,2,64,2048]{3,2,1,0:T(8,128)(2,1)} %param.10) | copy-start | bytes 1572868
Sparse Core Ops, SparseCore 0:
  10.8 77.4 all-gather.1
  384.9 120.4 reduce-scatter.1

commit v13 on v11

--- a/solution.py
+++ b/solution.py
@@ -124,37 +124,52 @@
     )(live_index.reshape(-1).astype(jnp.int32), normed_rows.T, grad_rows)
 
 
-def spread_kernel(x_ref, o_ref, recv_ref, send_sem, recv_sem):
-    count = recv_ref.shape[0]
+def spread_kernel(x_ref, o_ref, pair_ref, chip_sum, recv_ref, pair_send, pair_recv, send_sem, recv_sem):
+    chips = recv_ref.shape[0]
     me = lax.axis_index("dp")
     pipe = lax.axis_index("pipe")
+    core = me % 2
+    chip = me // 2
+    partner = chip * 2 + (1 - core)
     barrier = pltpu.get_barrier_semaphore()
-    for step in range(1, count):
-        peer = lax.rem(me + step, count)
-        pl.semaphore_signal(barrier, inc=1, device_id=(pipe, peer), device_id_type=pl.DeviceIdType.MESH)
-    pl.semaphore_wait(barrier, count - 1)
+    pl.semaphore_signal(barrier, inc=1, device_id=(pipe, partner), device_id_type=pl.DeviceIdType.MESH)
+    for step in range(1, chips):
+        other = lax.rem(chip + step, chips) * 2 + core
+        pl.semaphore_signal(barrier, inc=1, device_id=(pipe, other), device_id_type=pl.DeviceIdType.MESH)
+    pl.semaphore_wait(barrier, chips)
+    swap = pltpu.make_async_remote_copy(
+        src_ref=x_ref,
+        dst_ref=pair_ref,
+        send_sem=pair_send,
+        recv_sem=pair_recv,
+        device_id=(pipe, partner),
+        device_id_type=pl.DeviceIdType.MESH,
+    )
+    swap.start()
+    swap.wait()
+    chip_sum[...] = x_ref[...] + pair_ref[...]
     copies = []
-    for step in range(1, count):
-        peer = lax.rem(me + step, count)
+    for step in range(1, chips):
+        other = lax.rem(chip + step, chips) * 2 + core
         copy = pltpu.make_async_remote_copy(
-            src_ref=x_ref,
-            dst_ref=recv_ref.at[me],
+            src_ref=chip_sum,
+            dst_ref=recv_ref.at[chip],
             send_sem=send_sem.at[step],
-            recv_sem=recv_sem.at[me],
-            device_id=(pipe, peer),
+            recv_sem=recv_sem.at[chip],
+            device_id=(pipe, other),
             device_id_type=pl.DeviceIdType.MESH,
         )
         copy.start()
         copies.append(copy)
-    total = x_ref[...]
-    for step in range(1, count):
-        source = lax.rem(me + count - step, count)
+    total = chip_sum[...]
+    for step in range(1, chips):
+        source = lax.rem(chip + chips - step, chips)
         arrival = pltpu.make_async_remote_copy(
-            src_ref=x_ref,
+            src_ref=chip_sum,
             dst_ref=recv_ref.at[source],
             send_sem=send_sem.at[step],
             recv_sem=recv_sem.at[source],
-            device_id=(pipe, source),
+            device_id=(pipe, source * 2 + core),
             device_id_type=pl.DeviceIdType.MESH,
         )
         arrival.wait_recv()
@@ -165,7 +180,7 @@
 
 
 def spread_sum(values):
-    count = lax.axis_size("dp")
+    chips = lax.axis_size("dp") // 2
     padded = jnp.zeros((8, 128), jnp.float32).at[0, : values.shape[0]].set(values)
     out = pl.pallas_call(
         spread_kernel,
@@ -173,9 +188,13 @@
         in_specs=[pl.BlockSpec(memory_space=pltpu.VMEM)],
         out_specs=pl.BlockSpec(memory_space=pltpu.VMEM),
         scratch_shapes=[
-            pltpu.VMEM((count, 8, 128), jnp.float32),
-            pltpu.SemaphoreType.DMA((count,)),
-            pltpu.SemaphoreType.DMA((count,)),
+            pltpu.VMEM((8, 128), jnp.float32),
+            pltpu.VMEM((8, 128), jnp.float32),
+            pltpu.VMEM((chips, 8, 128), jnp.float32),
+            pltpu.SemaphoreType.DMA(()),
+            pltpu.SemaphoreType.DMA(()),
+            pltpu.SemaphoreType.DMA((chips,)),
+            pltpu.SemaphoreType.DMA((chips,)),
         ],
         compiler_params=pltpu.CompilerParams(collective_id=0, has_side_effects=True),
     )(padded)

time: 544 us -> 543 us (level)
  no operation moved by 1% of the time
where the time goes in v13:
time: 543 us; the launch traced here: 535 us
  waiting for transfers between devices  258 us (48%)
  matrix products  139 us (26%)
  Pallas kernels  56.4 us (10%)
  other arithmetic  30.5 us (6%)
  starting transfers between devices  21.5 us (4%)
  between operations  15.7 us (3%)
  local copies, waits for them, and re-layouts  14.6 us (3%)
    reduce_scatter x1, waiting for transfers between devices, local(): own_grad = lax.psum_scatter(partial, 'dp', scatter_dimension=0, tiled=True)  120 us
    dot_general x5, matrix products, layer_forward(): pre_act = jnp.dot(normed, dense_w, preferred_element_type=jnp.float32)  74.9 us
    all_gather x1, waiting for transfers between devices, local(): paired_weights = lax.all_gather(own_pair, 'dp', axis=0, tiled=True)  69.1 us
    ppermute x8, waiting for transfers between devices, shifted(): lax.ppermute(value, axis, [(source, source + steps) for source in range(l...  68.3 us
    dot_general x4, matrix products, layer_backward(): lax.dot_general(grad_pre, dense_w, (((1,), (1,)), ((), ())), preferred_el...  63.8 us
    pallas_call x1, Pallas kernels, expand_dense(): pl.pallas_call(expand_kernel, out_shape=jax.ShapeDtypeStruct((features, f...  25.8 us
    ppermute x8, starting transfers between devices, shifted(): lax.ppermute(value, axis, [(source, source + steps) for source in range(l...  21.4 us
    pallas_call x1, Pallas kernels, grad_pack(): pl.pallas_call(functools.partial(grad_pack_kernel, scale), out_shape=jax....  19 us
  transfers between devices with their start and end apart: 10, of which 10 were waited for; matrix products, arithmetic and copies ran while one was open for 3% of the time, Pallas kernels for 0%

profile of v13, /device:TPU:1, one launch (start us, length us, event | category | flops | bytes accessed | tf_op | source)
XLA Modules:
  0.0 535.3 jit_solution(17908510082408070306)
XLA Ops:
  17.5 69.1 %all-gather.2.cloned.1.call-done.t_ref = bf16[32,2048,128]{2,1,0:T(8,128)(2,1)} async-done(((bf16[1,2048,128]{2,1,0:T(8,128)(2,1)}), bf16[32,2048,128]{2,1,0:T(8,128)(2,1)}) %all-gather.2.cloned.1.call-update) | async-done | bytes 16777232 | tf_op jit(solution)/shard_map/all_gather | solution.py:246
  86.6 25.8 %shard_map.85 = bf16[4096,4096]{1,0:T(8,128)(2,1)} custom-call(s32[4096]{0:T(1024)} %select_n.124.table_ref, bf16[32,2048,128]{2,1,0:T(8,128)(2,1)} %all-gather.2.cloned.1.call-done.t_ref), custom_call_target="tpu_custom_call" | custom-call | bytes 50331648 | tf_op jit(solution)/shard_map/pallas_call | solution.py:84
  112.4 16.9 %fusion.77 = (bf16[64,4096]{1,0:T(8,128)(2,1)S(1)}, f32[64,4096]{1,0:T(8,128)S(1)}) fusion(bf16[2,32,4096]{2,1,0:T(8,128)(2,1)} %copy-done.2, bf16[64,4096]{1,0:T(8,128)(2,1)} %fusion.76, bf16[4096,4096]{1,0:T(8,128)(2,1)} %shard_map.85), kind=kOutput, calls=%fused_computation.122 | convolution fusion | flops 2149318656 | bytes 36175872 | tf_op jit(solution)/shard_map/dot_general | solution.py:208
  132.7 10.8 %collective-permute-done = bf16[64,4096]{1,0:T(8,128)(2,1)S(1)} collective-permute-done((bf16[64,4096]{1,0:T(8,128)(2,1)S(1)}, bf16[64,4096]{1,0:T(8,128)(2,1)S(1)}, u32[]{:S(2)}, u32[]{:S(2)}) %collective-permute-start) | collective-permute-done | bytes 524320 | tf_op jit(solution)/shard_map/ppermute | solution.py:17
  143.9 14.8 %fusion.37 = (bf16[64,4096]{1,0:T(8,128)(2,1)}, f32[64,4096]{1,0:T(8,128)S(1)}) fusion(bf16[64,4096]{1,0:T(8,128)(2,1)S(1)} %get-tuple-element.30, bf16[4096,4096]{1,0:T(8,128)(2,1)} %shard_map.85, f32[64]{0:T(128)S(1)} %add_rsqrt_fusion.8), kind=kOutput, calls=%fused_computation.64 | convolution fusion | flops 2150105088 | bytes 35651840 | tf_op jit(solution)/shard_map/dot_general | solution.py:208
  158.6 4.1 collective-permute-start.1
  163.9 9.3 %collective-permute-done.1 = bf16[64,4096]{1,0:T(8,128)(2,1)S(1)} collective-permute-done((bf16[64,4096]{1,0:T(8,128)(2,1)}, bf16[64,4096]{1,0:T(8,128)(2,1)S(1)}, u32[]{:S(2)}, u32[]{:S(2)}) %collective-permute-start.1) | collective-permute-done | bytes 524320 | tf_op jit(solution)/shard_map/ppermute | solution.py:17
  173.5 14.8 %fusion.40 = (bf16[64,4096]{1,0:T(8,128)(2,1)}, f32[64,4096]{1,0:T(8,128)S(1)}) fusion(bf16[64,4096]{1,0:T(8,128)(2,1)S(1)} %get-tuple-element.28, bf16[4096,4096]{1,0:T(8,128)(2,1)} %shard_map.85, f32[64]{0:T(128)S(1)} %add_rsqrt_fusion.7), kind=kOutput, calls=%fused_computation.67 | convolution fusion | flops 2150105088 | bytes 35651840 | tf_op jit(solution)/shard_map/dot_general | solution.py:208
  193.4 8.4 %collective-permute-done.2 = bf16[64,4096]{1,0:T(8,128)(2,1)S(1)} collective-permute-done((bf16[64,4096]{1,0:T(8,128)(2,1)}, bf16[64,4096]{1,0:T(8,128)(2,1)S(1)}, u32[]{:S(2)}, u32[]{:S(2)}) %collective-permute-start.2) | collective-permute-done | bytes 524320 | tf_op jit(solution)/shard_map/ppermute | solution.py:17
  202.1 14.8 %fusion.43 = (bf16[64,4096]{1,0:T(8,128)(2,1)}, f32[64,4096]{1,0:T(8,128)S(1)}) fusion(bf16[64,4096]{1,0:T(8,128)(2,1)S(1)} %get-tuple-element.26, bf16[4096,4096]{1,0:T(8,128)(2,1)} %shard_map.85, f32[64]{0:T(128)S(1)} %add_rsqrt_fusion.6), kind=kOutput, calls=%fused_computation.70 | convolution fusion | flops 2150105088 | bytes 35651840 | tf_op jit(solution)/shard_map/dot_general | solution.py:208
  216.9 4.2 collective-permute-start.3
  222.2 7.3 %collective-permute-done.3 = bf16[64,4096]{1,0:T(8,128)(2,1)S(1)} collective-permute-done((bf16[64,4096]{1,0:T(8,128)(2,1)}, bf16[64,4096]{1,0:T(8,128)(2,1)S(1)}, u32[]{:S(2)}, u32[]{:S(2)}) %collective-permute-start.3) | collective-permute-done | bytes 524320 | tf_op jit(solution)/shard_map/ppermute | solution.py:17
  229.8 13.8 %fusion = f32[5,64,4096]{2,1,0:T(8,128)S(1)} fusion(f32[5,64,4096]{2,1,0:T(8,128)S(1)} %bitcast_dynamic-update-slice_fusion, bf16[4096,4096]{1,0:T(8,128)(2,1)} %shard_map.85, bf16[64,4096]{1,0:T(8,128)(2,1)S(1)} %get-tuple-element.24, f32[64]{0:T(128)S(1)} %add_rsqrt_fusion.5), kind=kOutput, calls=%fused_computation.1 | convolution fusion | flops 2148270080 | bytes 35127808 | tf_op jit(solution)/shard_map/dot_general | solution.py:208
  246.7 15.9 %fusion.34 = (f32[64]{0:T(128)S(1)}, f32[64]{0:T(128)S(1)}, f32[64]{0:T(128)S(1)}, f32[64]{0:T(128)S(1)}, f32[64,4096]{1,0:T(8,128)S(1)}) fusion(bf16[5,64,4096]{2,1,0:T(8,128)(2,1)S(1)} %get-tuple-element.37, s32[]{:T(128)S(6)} %dynamic_slice.69, f32[64]{0:T(128)S(1)} %add_rsqrt_fusion.4, s32[]{:T(128)S(6)} %dynamic_slice.60, s32[]{:T(128)S(6)} %dynamic_slice.66, ...), kind=kOutput, calls=%fused_computation.61 | convolution fusion | flops 2150891520 | bytes 37225744 | tf_op jit(solution)/shard_map/dot_general | solution.py:219
  267.1 9.5 %collective-permute-done.4 = bf16[64,4096]{1,0:T(8,128)(2,1)S(1)} collective-permute-done((bf16[64,4096]{1,0:T(8,128)(2,1)S(1)}, bf16[64,4096]{1,0:T(8,128)(2,1)S(1)}, u32[]{:S(2)}, u32[]{:S(2)}) %collective-permute-start.4) | collective-permute-done | bytes 524320 | tf_op jit(solution)/shard_map/ppermute | solution.py:17
  278.2 15.7 %fusion.15 = (f32[64]{0:T(128)S(1)}, f32[64,4096]{1,0:T(8,128)S(1)}) fusion(f32[64]{0:T(128)S(1)} %add_rsqrt_fusion.3, bf16[5,64,4096]{2,1,0:T(8,128)(2,1)S(1)} %get-tuple-element.37, s32[]{:T(128)S(6)} %dynamic_slice.63, bf16[64,4096]{1,0:T(8,128)(2,1)S(1)} %get-tuple-element.57, bf16[4096,4096]{1,0:T(8,128)(2,1)} %shard_map.85), kind=kOutput, calls=%fused_computation.42 | convolution fusion | flops 2148532224 | bytes 35652100 | tf_op jit(solution)/shard_map/dot_general | solution.py:219
  295.9 9.3 %collective-permute-done.5 = bf16[64,4096]{1,0:T(8,128)(2,1)S(1)} collective-permute-done((bf16[64,4096]{1,0:T(8,128)(2,1)S(1)}, bf16[64,4096]{1,0:T(8,128)(2,1)S(1)}, u32[]{:S(2)}, u32[]{:S(2)}) %collective-permute-start.5) | collective-permute-done | bytes 524320 | tf_op jit(solution)/shard_map/ppermute | solution.py:17
  306.8 15.7 %fusion.12 = (f32[64]{0:T(128)S(1)}, f32[64,4096]{1,0:T(8,128)S(1)}) fusion(f32[64]{0:T(128)S(1)} %add_rsqrt_fusion.2, bf16[5,64,4096]{2,1,0:T(8,128)(2,1)S(1)} %get-tuple-element.37, s32[]{:T(128)S(6)} %dynamic_slice.66, bf16[64,4096]{1,0:T(8,128)(2,1)S(1)} %get-tuple-element.61, bf16[4096,4096]{1,0:T(8,128)(2,1)} %shard_map.85), kind=kOutput, calls=%fused_computation.39 | convolution fusion | flops 2148532224 | bytes 35652100 | tf_op jit(solution)/shard_map/dot_general | solution.py:219
  324.2 8.6 %collective-permute-done.6 = bf16[64,4096]{1,0:T(8,128)(2,1)S(1)} collective-permute-done((bf16[64,4096]{1,0:T(8,128)(2,1)S(1)}, bf16[64,4096]{1,0:T(8,128)(2,1)S(1)}, u32[]{:S(2)}, u32[]{:S(2)}) %collective-permute-start.6) | collective-permute-done | bytes 524320 | tf_op jit(solution)/shard_map/ppermute | solution.py:17
  334.5 16.6 %fusion.9 = (f32[64]{0:T(128)S(1)}, f32[64,4096]{1,0:T(8,128)S(1)}) fusion(f32[64]{0:T(128)S(1)} %add_rsqrt_fusion.1, bf16[5,64,4096]{2,1,0:T(8,128)(2,1)S(1)} %get-tuple-element.37, s32[]{:T(128)S(6)} %dynamic_slice.69, bf16[64,4096]{1,0:T(8,128)(2,1)S(1)} %get-tuple-element.65, bf16[4096,4096]{1,0:T(8,128)(2,1)} %shard_map.85), kind=kOutput, calls=%fused_computation.36 | convolution fusion | flops 2148532224 | bytes 35652100 | tf_op jit(solution)/shard_map/dot_general | solution.py:219
  357.2 5.2 collective-permute-done.7
  367.2 19.0 %shard_map.86 = bf16[32,2048,128]{2,1,0:T(8,128)(2,1)} custom-call(s32[2048]{0:T(1024)} %reshape_squeeze.3.table_ref, bf16[4096,128]{1,0:T(8,128)(2,1)} %bitcast.261, bf16[128,4096]{1,0:T(8,128)(2,1)} %bitcast.260), custom_call_target="tpu_custom_call" | custom-call | flops 4294967296 | bytes 18874368 | tf_op jit(solution)/shard_map/pallas_call | solution.py:106
  386.3 120.4 %reduce-scatter.2.cloned.1.call-done = bf16[1,2048,128]{2,1,0:T(8,128)(2,1)} async-done(((bf16[32,2048,128]{2,1,0:T(8,128)(2,1)}), bf16[1,2048,128]{2,1,0:T(8,128)(2,1)}) %reduce-scatter.2.cloned.1.call-update) | async-done | bytes 524304 | tf_op jit(solution)/shard_map/reduce_scatter | solution.py:291
  513.1 11.6 %shard_map.87 = f32[8,128]{1,0:T(8,128)} custom-call(f32[8,128]{1,0:T(8,128)} %scatter.4.x_ref), custom_call_target="tpu_custom_call" | custom-call | tf_op jit(solution)/shard_map/pallas_call | solution.py:185
  (100 shorter events, 58.3 us)
Async XLA Ops:
  7.2 4.2 copy-start.6
  7.2 4.5 copy-start.8
  7.2 79.4 %all-gather.2.cloned.1.call-start = ((), (), s32[]{:S(2)}) async-start(), calls=%async_computation.1 | async-start | bytes 17301504 | tf_op jit(solution)/shard_map/all_gather | solution.py:246
  9.4 497.4 %reduce-scatter.2.cloned.1.call-start = ((), (), s32[]{:S(2)}) async-start(), calls=%async_computation.2 | async-start | bytes 17301504 | tf_op jit(solution)/shard_map/reduce_scatter | solution.py:291
  11.6 2.7 copy-start.2
  112.4 31.1 %copy-start = (bf16[2,32,4096]{2,1,0:T(8,128)(2,1)S(1)}, bf16[2,32,4096]{2,1,0:T(8,128)(2,1)}, u32[]{:S(2)}) copy-start(bf16[2,32,4096]{2,1,0:T(8,128)(2,1)} %slice.42) | copy-start | bytes 1572868
  129.3 14.2 %collective-permute-start = (bf16[64,4096]{1,0:T(8,128)(2,1)S(1)}, bf16[64,4096]{1,0:T(8,128)(2,1)S(1)}, u32[]{:S(2)}, u32[]{:S(2)}) collective-permute-start(bf16[64,4096]{1,0:T(8,128)(2,1)S(1)} %get-tuple-element.47), channel_id=1, source_target_pairs={{0,32},{32,64},{64,96},{1,33},{33,65},{65,97},{2,34},{34,66},{66,9... | collective-permute-start | bytes 1572872 | tf_op jit(solution)/shard_map/ppermute | solution.py:17
  158.6 14.5 %collective-permute-start.1 = (bf16[64,4096]{1,0:T(8,128)(2,1)}, bf16[64,4096]{1,0:T(8,128)(2,1)S(1)}, u32[]{:S(2)}, u32[]{:S(2)}) collective-permute-start(bf16[64,4096]{1,0:T(8,128)(2,1)} %get-tuple-element.49), channel_id=1, source_target_pairs={{0,32},{32,64},{64,96},{1,33},{33,65},{65,97},{2,34},{34,66},{66,9... | collective-permute-start | bytes 1572872 | tf_op jit(solution)/shard_map/ppermute | solution.py:17
  188.3 13.5 %collective-permute-start.2 = (bf16[64,4096]{1,0:T(8,128)(2,1)}, bf16[64,4096]{1,0:T(8,128)(2,1)S(1)}, u32[]{:S(2)}, u32[]{:S(2)}) collective-permute-start(bf16[64,4096]{1,0:T(8,128)(2,1)} %get-tuple-element.51), channel_id=1, source_target_pairs={{0,32},{32,64},{64,96},{1,33},{33,65},{65,97},{2,34},{34,66},{66,9... | collective-permute-start | bytes 1572872 | tf_op jit(solution)/shard_map/ppermute | solution.py:17
  216.9 12.6 %collective-permute-start.3 = (bf16[64,4096]{1,0:T(8,128)(2,1)}, bf16[64,4096]{1,0:T(8,128)(2,1)S(1)}, u32[]{:S(2)}, u32[]{:S(2)}) collective-permute-start(bf16[64,4096]{1,0:T(8,128)(2,1)} %get-tuple-element.53), channel_id=1, source_target_pairs={{0,32},{32,64},{64,96},{1,33},{33,65},{65,97},{2,34},{34,66},{66,9... | collective-permute-start | bytes 1572872 | tf_op jit(solution)/shard_map/ppermute | solution.py:17
  229.8 16.3 %copy-start.4 = (bf16[4,32,4096]{2,1,0:T(8,128)(2,1)S(1)}, bf16[4,32,4096]{2,1,0:T(8,128)(2,1)}, u32[]{:S(2)}) copy-start(bf16[4,32,4096]{2,1,0:T(8,128)(2,1)} %param.9) | copy-start | bytes 3145732
  243.6 2.6 copy-start.1
  262.6 2.8 copy-start.3
  264.1 12.4 %collective-permute-start.4 = (bf16[64,4096]{1,0:T(8,128)(2,1)S(1)}, bf16[64,4096]{1,0:T(8,128)(2,1)S(1)}, u32[]{:S(2)}, u32[]{:S(2)}) collective-permute-start(bf16[64,4096]{1,0:T(8,128)(2,1)S(1)} %fusion.22), channel_id=1, source_target_pairs={{32,0},{64,32},{96,64},{33,1},{65,33},{97,65},{34,2},{66,34},{98,6... | collective-permute-start | bytes 1572872 | tf_op jit(solution)/shard_map/ppermute | solution.py:17
  294.3 10.8 %collective-permute-start.5 = (bf16[64,4096]{1,0:T(8,128)(2,1)S(1)}, bf16[64,4096]{1,0:T(8,128)(2,1)S(1)}, u32[]{:S(2)}, u32[]{:S(2)}) collective-permute-start(bf16[64,4096]{1,0:T(8,128)(2,1)S(1)} %fusion.26), channel_id=1, source_target_pairs={{32,0},{64,32},{96,64},{33,1},{65,33},{97,65},{34,2},{66,34},{98,6... | collective-permute-start | bytes 1572872 | tf_op jit(solution)/shard_map/ppermute | solution.py:17
  322.9 9.9 %collective-permute-start.6 = (bf16[64,4096]{1,0:T(8,128)(2,1)S(1)}, bf16[64,4096]{1,0:T(8,128)(2,1)S(1)}, u32[]{:S(2)}, u32[]{:S(2)}) collective-permute-start(bf16[64,4096]{1,0:T(8,128)(2,1)S(1)} %fusion.28), channel_id=1, source_target_pairs={{32,0},{64,32},{96,64},{33,1},{65,33},{97,65},{34,2},{66,34},{98,6... | collective-permute-start | bytes 1572872 | tf_op jit(solution)/shard_map/ppermute | solution.py:17
  334.5 16.6 %copy-start.7 = (bf16[5,64,4096]{2,1,0:T(8,128)(2,1)}, bf16[5,64,4096]{2,1,0:T(8,128)(2,1)S(1)}, u32[]{:S(2)}) copy-start(bf16[5,64,4096]{2,1,0:T(8,128)(2,1)S(1)} %get-tuple-element.64) | copy-start | bytes 7864324
  352.3 10.1 %collective-permute-start.7 = (bf16[64,4096]{1,0:T(8,128)(2,1)}, bf16[64,4096]{1,0:T(8,128)(2,1)S(1)}, u32[]{:S(2)}, u32[]{:S(2)}) collective-permute-start(bf16[64,4096]{1,0:T(8,128)(2,1)} %fusion.30), channel_id=1, source_target_pairs={{32,0},{64,32},{96,64},{33,1},{65,33},{97,65},{34,2},{66,34},{98,6... | collective-permute-start | bytes 1572872 | tf_op jit(solution)/shard_map/ppermute | solution.py:17
  386.1 121.9 %copy-start.5 = (bf16[1,2,64,2048]{3,2,1,0:T(8,128)(2,1)S(1)}, bf16[1,2,64,2048]{3,2,1,0:T(8,128)(2,1)}, u32[]{:S(2)}) copy-start(bf16[1,2,64,2048]{3,2,1,0:T(8,128)(2,1)} %param.10) | copy-start | bytes 1572868
Sparse Core Ops, SparseCore 0:
  10.3 76.2 all-gather.1
  386.3 120.4 reduce-scatter.1

commit v14 on v11

--- a/solution.py
+++ b/solution.py
@@ -68,6 +68,7 @@
 
 
 PAIRS_PER_STEP = 4
+GRAD_PAIRS_PER_STEP = 8
 
 
 def expand_dense(paired_weights, live_index):
@@ -102,18 +103,18 @@
     block_size = features // column_count
     wide = live_count * block_size
     pair_count = column_count // 2
-    stripe = PAIRS_PER_STEP * 2 * block_size
+    stripe = GRAD_PAIRS_PER_STEP * 2 * block_size
     return pl.pallas_call(
         functools.partial(grad_pack_kernel, scale),
         out_shape=jax.ShapeDtypeStruct((pair_count, wide, 2 * block_size), jnp.bfloat16),
         grid_spec=pltpu.PrefetchScalarGridSpec(
             num_scalar_prefetch=1,
-            grid=(pair_count // PAIRS_PER_STEP,),
+            grid=(pair_count // GRAD_PAIRS_PER_STEP,),
             in_specs=[
                 pl.BlockSpec((features, all_rows), lambda q, tbl: (0, 0)),
                 pl.BlockSpec((all_rows, stripe), lambda q, tbl: (0, q)),
             ],
-            out_specs=pl.BlockSpec((PAIRS_PER_STEP, wide, 2 * block_size), lambda q, tbl: (q, 0, 0)),
+            out_specs=pl.BlockSpec((GRAD_PAIRS_PER_STEP, wide, 2 * block_size), lambda q, tbl: (q, 0, 0)),
             scratch_shapes=[pltpu.VMEM((features, stripe), jnp.bfloat16)],
         ),
         cost_estimate=pl.CostEstimate(

time: 544 us -> 546 us (level)
  no operation moved by 1% of the time
where the time goes in v14:
time: 546 us; the launch traced here: 538 us
  waiting for transfers between devices  258 us (47%)
  matrix products  139 us (25%)
  Pallas kernels  59.8 us (11%)
  other arithmetic  30.5 us (6%)
  starting transfers between devices  21.7 us (4%)
  between operations  15.4 us (3%)
  local copies, waits for them, and re-layouts  14.6 us (3%)
    reduce_scatter x1, waiting for transfers between devices, local(): own_grad = lax.psum_scatter(partial, 'dp', scatter_dimension=0, tiled=True)  120 us
    dot_general x5, matrix products, layer_forward(): pre_act = jnp.dot(normed, dense_w, preferred_element_type=jnp.float32)  74.8 us
    all_gather x1, waiting for transfers between devices, local(): paired_weights = lax.all_gather(own_pair, 'dp', axis=0, tiled=True)  69.1 us
    ppermute x8, waiting for transfers between devices, shifted(): lax.ppermute(value, axis, [(source, source + steps) for source in range(l...  68 us
    dot_general x4, matrix products, layer_backward(): lax.dot_general(grad_pre, dense_w, (((1,), (1,)), ((), ())), preferred_el...  63.8 us
    pallas_call x1, Pallas kernels, expand_dense(): pl.pallas_call(expand_kernel, out_shape=jax.ShapeDtypeStruct((features, f...  25.8 us
    pallas_call x1, Pallas kernels, grad_pack(): pl.pallas_call(functools.partial(grad_pack_kernel, scale), out_shape=jax....  21.8 us
    ppermute x8, starting transfers between devices, shifted(): lax.ppermute(value, axis, [(source, source + steps) for source in range(l...  21.6 us
  transfers between devices with their start and end apart: 10, of which 10 were waited for; matrix products, arithmetic and copies ran while one was open for 3% of the time, Pallas kernels for 0%

profile of v14, /device:TPU:1, one launch (start us, length us, event | category | flops | bytes accessed | tf_op | source)
XLA Modules:
  0.0 538.4 jit_solution(16355164420590382298)
XLA Ops:
  17.5 69.1 %all-gather.2.cloned.1.call-done.t_ref = bf16[32,2048,128]{2,1,0:T(8,128)(2,1)} async-done(((bf16[1,2048,128]{2,1,0:T(8,128)(2,1)}), bf16[32,2048,128]{2,1,0:T(8,128)(2,1)}) %all-gather.2.cloned.1.call-update) | async-done | bytes 16777232 | tf_op jit(solution)/shard_map/all_gather | solution.py:228
  86.6 25.8 %shard_map.85 = bf16[4096,4096]{1,0:T(8,128)(2,1)} custom-call(s32[4096]{0:T(1024)} %select_n.124.table_ref, bf16[32,2048,128]{2,1,0:T(8,128)(2,1)} %all-gather.2.cloned.1.call-done.t_ref), custom_call_target="tpu_custom_call" | custom-call | bytes 50331648 | tf_op jit(solution)/shard_map/pallas_call | solution.py:85
  112.4 16.8 %fusion.77 = (bf16[64,4096]{1,0:T(8,128)(2,1)S(1)}, f32[64,4096]{1,0:T(8,128)S(1)}) fusion(bf16[2,32,4096]{2,1,0:T(8,128)(2,1)} %copy-done.2, bf16[64,4096]{1,0:T(8,128)(2,1)} %fusion.76, bf16[4096,4096]{1,0:T(8,128)(2,1)} %shard_map.85), kind=kOutput, calls=%fused_computation.122 | convolution fusion | flops 2149318656 | bytes 36175872 | tf_op jit(solution)/shard_map/dot_general | solution.py:190
  133.0 10.4 %collective-permute-done = bf16[64,4096]{1,0:T(8,128)(2,1)S(1)} collective-permute-done((bf16[64,4096]{1,0:T(8,128)(2,1)S(1)}, bf16[64,4096]{1,0:T(8,128)(2,1)S(1)}, u32[]{:S(2)}, u32[]{:S(2)}) %collective-permute-start) | collective-permute-done | bytes 524320 | tf_op jit(solution)/shard_map/ppermute | solution.py:17
  143.8 14.8 %fusion.37 = (bf16[64,4096]{1,0:T(8,128)(2,1)}, f32[64,4096]{1,0:T(8,128)S(1)}) fusion(bf16[64,4096]{1,0:T(8,128)(2,1)S(1)} %get-tuple-element.30, bf16[4096,4096]{1,0:T(8,128)(2,1)} %shard_map.85, f32[64]{0:T(128)S(1)} %add_rsqrt_fusion.8), kind=kOutput, calls=%fused_computation.64 | convolution fusion | flops 2150105088 | bytes 35651840 | tf_op jit(solution)/shard_map/dot_general | solution.py:190
  158.5 4.1 collective-permute-start.1
  163.8 9.3 %collective-permute-done.1 = bf16[64,4096]{1,0:T(8,128)(2,1)S(1)} collective-permute-done((bf16[64,4096]{1,0:T(8,128)(2,1)}, bf16[64,4096]{1,0:T(8,128)(2,1)S(1)}, u32[]{:S(2)}, u32[]{:S(2)}) %collective-permute-start.1) | collective-permute-done | bytes 524320 | tf_op jit(solution)/shard_map/ppermute | solution.py:17
  173.4 14.8 %fusion.40 = (bf16[64,4096]{1,0:T(8,128)(2,1)}, f32[64,4096]{1,0:T(8,128)S(1)}) fusion(bf16[64,4096]{1,0:T(8,128)(2,1)S(1)} %get-tuple-element.28, bf16[4096,4096]{1,0:T(8,128)(2,1)} %shard_map.85, f32[64]{0:T(128)S(1)} %add_rsqrt_fusion.7), kind=kOutput, calls=%fused_computation.67 | convolution fusion | flops 2150105088 | bytes 35651840 | tf_op jit(solution)/shard_map/dot_general | solution.py:190
  193.3 8.4 %collective-permute-done.2 = bf16[64,4096]{1,0:T(8,128)(2,1)S(1)} collective-permute-done((bf16[64,4096]{1,0:T(8,128)(2,1)}, bf16[64,4096]{1,0:T(8,128)(2,1)S(1)}, u32[]{:S(2)}, u32[]{:S(2)}) %collective-permute-start.2) | collective-permute-done | bytes 524320 | tf_op jit(solution)/shard_map/ppermute | solution.py:17
  202.0 14.8 %fusion.43 = (bf16[64,4096]{1,0:T(8,128)(2,1)}, f32[64,4096]{1,0:T(8,128)S(1)}) fusion(bf16[64,4096]{1,0:T(8,128)(2,1)S(1)} %get-tuple-element.26, bf16[4096,4096]{1,0:T(8,128)(2,1)} %shard_map.85, f32[64]{0:T(128)S(1)} %add_rsqrt_fusion.6), kind=kOutput, calls=%fused_computation.70 | convolution fusion | flops 2150105088 | bytes 35651840 | tf_op jit(solution)/shard_map/dot_general | solution.py:190
  216.8 4.2 collective-permute-start.3
  222.1 7.3 %collective-permute-done.3 = bf16[64,4096]{1,0:T(8,128)(2,1)S(1)} collective-permute-done((bf16[64,4096]{1,0:T(8,128)(2,1)}, bf16[64,4096]{1,0:T(8,128)(2,1)S(1)}, u32[]{:S(2)}, u32[]{:S(2)}) %collective-permute-start.3) | collective-permute-done | bytes 524320 | tf_op jit(solution)/shard_map/ppermute | solution.py:17
  229.7 13.8 %fusion = f32[5,64,4096]{2,1,0:T(8,128)S(1)} fusion(f32[5,64,4096]{2,1,0:T(8,128)S(1)} %bitcast_dynamic-update-slice_fusion, bf16[4096,4096]{1,0:T(8,128)(2,1)} %shard_map.85, bf16[64,4096]{1,0:T(8,128)(2,1)S(1)} %get-tuple-element.24, f32[64]{0:T(128)S(1)} %add_rsqrt_fusion.5), kind=kOutput, calls=%fused_computation.1 | convolution fusion | flops 2148270080 | bytes 35127808 | tf_op jit(solution)/shard_map/dot_general | solution.py:190
  246.7 15.9 %fusion.34 = (f32[64]{0:T(128)S(1)}, f32[64]{0:T(128)S(1)}, f32[64]{0:T(128)S(1)}, f32[64]{0:T(128)S(1)}, f32[64,4096]{1,0:T(8,128)S(1)}) fusion(bf16[5,64,4096]{2,1,0:T(8,128)(2,1)S(1)} %get-tuple-element.37, s32[]{:T(128)S(6)} %dynamic_slice.69, f32[64]{0:T(128)S(1)} %add_rsqrt_fusion.4, s32[]{:T(128)S(6)} %dynamic_slice.60, s32[]{:T(128)S(6)} %dynamic_slice.66, ...), kind=kOutput, calls=%fused_computation.61 | convolution fusion | flops 2150891520 | bytes 37225744 | tf_op jit(solution)/shard_map/dot_general | solution.py:201
  267.0 9.5 %collective-permute-done.4 = bf16[64,4096]{1,0:T(8,128)(2,1)S(1)} collective-permute-done((bf16[64,4096]{1,0:T(8,128)(2,1)S(1)}, bf16[64,4096]{1,0:T(8,128)(2,1)S(1)}, u32[]{:S(2)}, u32[]{:S(2)}) %collective-permute-start.4) | collective-permute-done | bytes 524320 | tf_op jit(solution)/shard_map/ppermute | solution.py:17
  278.1 15.7 %fusion.15 = (f32[64]{0:T(128)S(1)}, f32[64,4096]{1,0:T(8,128)S(1)}) fusion(f32[64]{0:T(128)S(1)} %add_rsqrt_fusion.3, bf16[5,64,4096]{2,1,0:T(8,128)(2,1)S(1)} %get-tuple-element.37, s32[]{:T(128)S(6)} %dynamic_slice.63, bf16[64,4096]{1,0:T(8,128)(2,1)S(1)} %get-tuple-element.57, bf16[4096,4096]{1,0:T(8,128)(2,1)} %shard_map.85), kind=kOutput, calls=%fused_computation.42 | convolution fusion | flops 2148532224 | bytes 35652100 | tf_op jit(solution)/shard_map/dot_general | solution.py:201
  295.7 9.3 %collective-permute-done.5 = bf16[64,4096]{1,0:T(8,128)(2,1)S(1)} collective-permute-done((bf16[64,4096]{1,0:T(8,128)(2,1)S(1)}, bf16[64,4096]{1,0:T(8,128)(2,1)S(1)}, u32[]{:S(2)}, u32[]{:S(2)}) %collective-permute-start.5) | collective-permute-done | bytes 524320 | tf_op jit(solution)/shard_map/ppermute | solution.py:17
  306.7 15.7 %fusion.12 = (f32[64]{0:T(128)S(1)}, f32[64,4096]{1,0:T(8,128)S(1)}) fusion(f32[64]{0:T(128)S(1)} %add_rsqrt_fusion.2, bf16[5,64,4096]{2,1,0:T(8,128)(2,1)S(1)} %get-tuple-element.37, s32[]{:T(128)S(6)} %dynamic_slice.66, bf16[64,4096]{1,0:T(8,128)(2,1)S(1)} %get-tuple-element.61, bf16[4096,4096]{1,0:T(8,128)(2,1)} %shard_map.85), kind=kOutput, calls=%fused_computation.39 | convolution fusion | flops 2148532224 | bytes 35652100 | tf_op jit(solution)/shard_map/dot_general | solution.py:201
  324.1 8.6 %collective-permute-done.6 = bf16[64,4096]{1,0:T(8,128)(2,1)S(1)} collective-permute-done((bf16[64,4096]{1,0:T(8,128)(2,1)S(1)}, bf16[64,4096]{1,0:T(8,128)(2,1)S(1)}, u32[]{:S(2)}, u32[]{:S(2)}) %collective-permute-start.6) | collective-permute-done | bytes 524320 | tf_op jit(solution)/shard_map/ppermute | solution.py:17
  334.4 16.6 %fusion.9 = (f32[64]{0:T(128)S(1)}, f32[64,4096]{1,0:T(8,128)S(1)}) fusion(f32[64]{0:T(128)S(1)} %add_rsqrt_fusion.1, bf16[5,64,4096]{2,1,0:T(8,128)(2,1)S(1)} %get-tuple-element.37, s32[]{:T(128)S(6)} %dynamic_slice.69, bf16[64,4096]{1,0:T(8,128)(2,1)S(1)} %get-tuple-element.65, bf16[4096,4096]{1,0:T(8,128)(2,1)} %shard_map.85), kind=kOutput, calls=%fused_computation.36 | convolution fusion | flops 2148532224 | bytes 35652100 | tf_op jit(solution)/shard_map/dot_general | solution.py:201
  357.1 5.2 collective-permute-done.7
  367.1 21.8 %shard_map.86 = bf16[32,2048,128]{2,1,0:T(8,128)(2,1)} custom-call(s32[2048]{0:T(1024)} %reshape_squeeze.3.table_ref, bf16[4096,128]{1,0:T(8,128)(2,1)} %bitcast.261, bf16[128,4096]{1,0:T(8,128)(2,1)} %bitcast.260), custom_call_target="tpu_custom_call" | custom-call | flops 4294967296 | bytes 18874368 | tf_op jit(solution)/shard_map/pallas_call | solution.py:107
  389.1 120.4 %reduce-scatter.2.cloned.1.call-done = bf16[1,2048,128]{2,1,0:T(8,128)(2,1)} async-done(((bf16[32,2048,128]{2,1,0:T(8,128)(2,1)}), bf16[1,2048,128]{2,1,0:T(8,128)(2,1)}) %reduce-scatter.2.cloned.1.call-update) | async-done | bytes 524304 | tf_op jit(solution)/shard_map/reduce_scatter | solution.py:273
  515.8 12.1 %shard_map.87 = f32[8,128]{1,0:T(8,128)} custom-call(f32[8,128]{1,0:T(8,128)} %scatter.4.x_ref), custom_call_target="tpu_custom_call" | custom-call | tf_op jit(solution)/shard_map/pallas_call | solution.py:171
  (100 shorter events, 58.6 us)
Async XLA Ops:
  7.2 4.2 copy-start.6
  7.2 4.5 copy-start.8
  7.2 79.4 %all-gather.2.cloned.1.call-start = ((), (), s32[]{:S(2)}) async-start(), calls=%async_computation.1 | async-start | bytes 17301504 | tf_op jit(solution)/shard_map/all_gather | solution.py:228
  9.4 500.1 %reduce-scatter.2.cloned.1.call-start = ((), (), s32[]{:S(2)}) async-start(), calls=%async_computation.2 | async-start | bytes 17301504 | tf_op jit(solution)/shard_map/reduce_scatter | solution.py:273
  11.6 2.7 copy-start.2
  112.4 31.0 %copy-start = (bf16[2,32,4096]{2,1,0:T(8,128)(2,1)S(1)}, bf16[2,32,4096]{2,1,0:T(8,128)(2,1)}, u32[]{:S(2)}) copy-start(bf16[2,32,4096]{2,1,0:T(8,128)(2,1)} %slice.42) | copy-start | bytes 1572868
  129.3 14.2 %collective-permute-start = (bf16[64,4096]{1,0:T(8,128)(2,1)S(1)}, bf16[64,4096]{1,0:T(8,128)(2,1)S(1)}, u32[]{:S(2)}, u32[]{:S(2)}) collective-permute-start(bf16[64,4096]{1,0:T(8,128)(2,1)S(1)} %get-tuple-element.47), channel_id=1, source_target_pairs={{0,32},{32,64},{64,96},{1,33},{33,65},{65,97},{2,34},{34,66},{66,9... | collective-permute-start | bytes 1572872 | tf_op jit(solution)/shard_map/ppermute | solution.py:17
  158.5 14.5 %collective-permute-start.1 = (bf16[64,4096]{1,0:T(8,128)(2,1)}, bf16[64,4096]{1,0:T(8,128)(2,1)S(1)}, u32[]{:S(2)}, u32[]{:S(2)}) collective-permute-start(bf16[64,4096]{1,0:T(8,128)(2,1)} %get-tuple-element.49), channel_id=1, source_target_pairs={{0,32},{32,64},{64,96},{1,33},{33,65},{65,97},{2,34},{34,66},{66,9... | collective-permute-start | bytes 1572872 | tf_op jit(solution)/shard_map/ppermute | solution.py:17
  188.2 13.5 %collective-permute-start.2 = (bf16[64,4096]{1,0:T(8,128)(2,1)}, bf16[64,4096]{1,0:T(8,128)(2,1)S(1)}, u32[]{:S(2)}, u32[]{:S(2)}) collective-permute-start(bf16[64,4096]{1,0:T(8,128)(2,1)} %get-tuple-element.51), channel_id=1, source_target_pairs={{0,32},{32,64},{64,96},{1,33},{33,65},{65,97},{2,34},{34,66},{66,9... | collective-permute-start | bytes 1572872 | tf_op jit(solution)/shard_map/ppermute | solution.py:17
  216.8 12.6 %collective-permute-start.3 = (bf16[64,4096]{1,0:T(8,128)(2,1)}, bf16[64,4096]{1,0:T(8,128)(2,1)S(1)}, u32[]{:S(2)}, u32[]{:S(2)}) collective-permute-start(bf16[64,4096]{1,0:T(8,128)(2,1)} %get-tuple-element.53), channel_id=1, source_target_pairs={{0,32},{32,64},{64,96},{1,33},{33,65},{65,97},{2,34},{34,66},{66,9... | collective-permute-start | bytes 1572872 | tf_op jit(solution)/shard_map/ppermute | solution.py:17
  229.7 16.3 %copy-start.4 = (bf16[4,32,4096]{2,1,0:T(8,128)(2,1)S(1)}, bf16[4,32,4096]{2,1,0:T(8,128)(2,1)}, u32[]{:S(2)}) copy-start(bf16[4,32,4096]{2,1,0:T(8,128)(2,1)} %param.9) | copy-start | bytes 3145732
  243.5 2.6 copy-start.1
  262.5 2.8 copy-start.3
  264.0 12.4 %collective-permute-start.4 = (bf16[64,4096]{1,0:T(8,128)(2,1)S(1)}, bf16[64,4096]{1,0:T(8,128)(2,1)S(1)}, u32[]{:S(2)}, u32[]{:S(2)}) collective-permute-start(bf16[64,4096]{1,0:T(8,128)(2,1)S(1)} %fusion.22), channel_id=1, source_target_pairs={{32,0},{64,32},{96,64},{33,1},{65,33},{97,65},{34,2},{66,34},{98,6... | collective-permute-start | bytes 1572872 | tf_op jit(solution)/shard_map/ppermute | solution.py:17
  294.2 10.8 %collective-permute-start.5 = (bf16[64,4096]{1,0:T(8,128)(2,1)S(1)}, bf16[64,4096]{1,0:T(8,128)(2,1)S(1)}, u32[]{:S(2)}, u32[]{:S(2)}) collective-permute-start(bf16[64,4096]{1,0:T(8,128)(2,1)S(1)} %fusion.26), channel_id=1, source_target_pairs={{32,0},{64,32},{96,64},{33,1},{65,33},{97,65},{34,2},{66,34},{98,6... | collective-permute-start | bytes 1572872 | tf_op jit(solution)/shard_map/ppermute | solution.py:17
  322.8 9.9 %collective-permute-start.6 = (bf16[64,4096]{1,0:T(8,128)(2,1)S(1)}, bf16[64,4096]{1,0:T(8,128)(2,1)S(1)}, u32[]{:S(2)}, u32[]{:S(2)}) collective-permute-start(bf16[64,4096]{1,0:T(8,128)(2,1)S(1)} %fusion.28), channel_id=1, source_target_pairs={{32,0},{64,32},{96,64},{33,1},{65,33},{97,65},{34,2},{66,34},{98,6... | collective-permute-start | bytes 1572872 | tf_op jit(solution)/shard_map/ppermute | solution.py:17
  334.4 16.6 %copy-start.7 = (bf16[5,64,4096]{2,1,0:T(8,128)(2,1)}, bf16[5,64,4096]{2,1,0:T(8,128)(2,1)S(1)}, u32[]{:S(2)}) copy-start(bf16[5,64,4096]{2,1,0:T(8,128)(2,1)S(1)} %get-tuple-element.64) | copy-start | bytes 7864324
  352.2 10.1 %collective-permute-start.7 = (bf16[64,4096]{1,0:T(8,128)(2,1)}, bf16[64,4096]{1,0:T(8,128)(2,1)S(1)}, u32[]{:S(2)}, u32[]{:S(2)}) collective-permute-start(bf16[64,4096]{1,0:T(8,128)(2,1)} %fusion.30), channel_id=1, source_target_pairs={{32,0},{64,32},{96,64},{33,1},{65,33},{97,65},{34,2},{66,34},{98,6... | collective-permute-start | bytes 1572872 | tf_op jit(solution)/shard_map/ppermute | solution.py:17
  388.9 121.8 %copy-start.5 = (bf16[1,2,64,2048]{3,2,1,0:T(8,128)(2,1)S(1)}, bf16[1,2,64,2048]{3,2,1,0:T(8,128)(2,1)}, u32[]{:S(2)}) copy-start(bf16[1,2,64,2048]{3,2,1,0:T(8,128)(2,1)} %param.10) | copy-start | bytes 1572868
Sparse Core Ops, SparseCore 0:
  10.3 76.2 all-gather.1
  389.1 120.3 reduce-scatter.1

commit v15 on v14

--- a/solution.py
+++ b/solution.py
@@ -68,7 +68,7 @@
 
 
 PAIRS_PER_STEP = 4
-GRAD_PAIRS_PER_STEP = 8
+GRAD_PAIRS_PER_STEP = 2
 
 
 def expand_dense(paired_weights, live_index):

time: 546 us -> 544 us (level)
  no operation moved by 1% of the time
where the time goes in v15:
time: 544 us; the launch traced here: 537 us
  waiting for transfers between devices  258 us (47%)
  matrix products  139 us (26%)
  Pallas kernels  57.7 us (11%)
  other arithmetic  30.5 us (6%)
  starting transfers between devices  21.2 us (4%)
  between operations  15.6 us (3%)
  local copies, waits for them, and re-layouts  14.6 us (3%)
    reduce_scatter x1, waiting for transfers between devices, local(): own_grad = lax.psum_scatter(partial, 'dp', scatter_dimension=0, tiled=True)  120 us
    dot_general x5, matrix products, layer_forward(): pre_act = jnp.dot(normed, dense_w, preferred_element_type=jnp.float32)  74.9 us
    all_gather x1, waiting for transfers between devices, local(): paired_weights = lax.all_gather(own_pair, 'dp', axis=0, tiled=True)  69.1 us
    ppermute x8, waiting for transfers between devices, shifted(): lax.ppermute(value, axis, [(source, source + steps) for source in range(l...  68.6 us
    dot_general x4, matrix products, layer_backward(): lax.dot_general(grad_pre, dense_w, (((1,), (1,)), ((), ())), preferred_el...  63.8 us
    pallas_call x1, Pallas kernels, expand_dense(): pl.pallas_call(expand_kernel, out_shape=jax.ShapeDtypeStruct((features, f...  25.8 us
    ppermute x8, starting transfers between devices, shifted(): lax.ppermute(value, axis, [(source, source + steps) for source in range(l...  21.1 us
    pallas_call x1, Pallas kernels, grad_pack(): pl.pallas_call(functools.partial(grad_pack_kernel, scale), out_shape=jax....  19.8 us
  transfers between devices with their start and end apart: 10, of which 10 were waited for; matrix products, arithmetic and copies ran while one was open for 3% of the time, Pallas kernels for 0%

profile of v15, /device:TPU:1, one launch (start us, length us, event | category | flops | bytes accessed | tf_op | source)
XLA Modules:
  0.0 536.6 jit_solution(13378690769629355611)
XLA Ops:
  17.5 69.1 %all-gather.2.cloned.1.call-done.t_ref = bf16[32,2048,128]{2,1,0:T(8,128)(2,1)} async-done(((bf16[1,2048,128]{2,1,0:T(8,128)(2,1)}), bf16[32,2048,128]{2,1,0:T(8,128)(2,1)}) %all-gather.2.cloned.1.call-update) | async-done | bytes 16777232 | tf_op jit(solution)/shard_map/all_gather | solution.py:228
  86.6 25.8 %shard_map.85 = bf16[4096,4096]{1,0:T(8,128)(2,1)} custom-call(s32[4096]{0:T(1024)} %select_n.124.table_ref, bf16[32,2048,128]{2,1,0:T(8,128)(2,1)} %all-gather.2.cloned.1.call-done.t_ref), custom_call_target="tpu_custom_call" | custom-call | bytes 50331648 | tf_op jit(solution)/shard_map/pallas_call | solution.py:85
  112.4 16.9 %fusion.77 = (bf16[64,4096]{1,0:T(8,128)(2,1)S(1)}, f32[64,4096]{1,0:T(8,128)S(1)}) fusion(bf16[2,32,4096]{2,1,0:T(8,128)(2,1)} %copy-done.2, bf16[64,4096]{1,0:T(8,128)(2,1)} %fusion.76, bf16[4096,4096]{1,0:T(8,128)(2,1)} %shard_map.85), kind=kOutput, calls=%fused_computation.122 | convolution fusion | flops 2149318656 | bytes 36175872 | tf_op jit(solution)/shard_map/dot_general | solution.py:190
  132.7 10.8 %collective-permute-done = bf16[64,4096]{1,0:T(8,128)(2,1)S(1)} collective-permute-done((bf16[64,4096]{1,0:T(8,128)(2,1)S(1)}, bf16[64,4096]{1,0:T(8,128)(2,1)S(1)}, u32[]{:S(2)}, u32[]{:S(2)}) %collective-permute-start) | collective-permute-done | bytes 524320 | tf_op jit(solution)/shard_map/ppermute | solution.py:17
  143.9 14.8 %fusion.37 = (bf16[64,4096]{1,0:T(8,128)(2,1)}, f32[64,4096]{1,0:T(8,128)S(1)}) fusion(bf16[64,4096]{1,0:T(8,128)(2,1)S(1)} %get-tuple-element.30, bf16[4096,4096]{1,0:T(8,128)(2,1)} %shard_map.85, f32[64]{0:T(128)S(1)} %add_rsqrt_fusion.8), kind=kOutput, calls=%fused_computation.64 | convolution fusion | flops 2150105088 | bytes 35651840 | tf_op jit(solution)/shard_map/dot_general | solution.py:190
  158.6 4.1 collective-permute-start.1
  163.9 9.3 %collective-permute-done.1 = bf16[64,4096]{1,0:T(8,128)(2,1)S(1)} collective-permute-done((bf16[64,4096]{1,0:T(8,128)(2,1)}, bf16[64,4096]{1,0:T(8,128)(2,1)S(1)}, u32[]{:S(2)}, u32[]{:S(2)}) %collective-permute-start.1) | collective-permute-done | bytes 524320 | tf_op jit(solution)/shard_map/ppermute | solution.py:17
  173.5 14.8 %fusion.40 = (bf16[64,4096]{1,0:T(8,128)(2,1)}, f32[64,4096]{1,0:T(8,128)S(1)}) fusion(bf16[64,4096]{1,0:T(8,128)(2,1)S(1)} %get-tuple-element.28, bf16[4096,4096]{1,0:T(8,128)(2,1)} %shard_map.85, f32[64]{0:T(128)S(1)} %add_rsqrt_fusion.7), kind=kOutput, calls=%fused_computation.67 | convolution fusion | flops 2150105088 | bytes 35651840 | tf_op jit(solution)/shard_map/dot_general | solution.py:190
  193.4 8.4 %collective-permute-done.2 = bf16[64,4096]{1,0:T(8,128)(2,1)S(1)} collective-permute-done((bf16[64,4096]{1,0:T(8,128)(2,1)}, bf16[64,4096]{1,0:T(8,128)(2,1)S(1)}, u32[]{:S(2)}, u32[]{:S(2)}) %collective-permute-start.2) | collective-permute-done | bytes 524320 | tf_op jit(solution)/shard_map/ppermute | solution.py:17
  202.1 14.8 %fusion.43 = (bf16[64,4096]{1,0:T(8,128)(2,1)}, f32[64,4096]{1,0:T(8,128)S(1)}) fusion(bf16[64,4096]{1,0:T(8,128)(2,1)S(1)} %get-tuple-element.26, bf16[4096,4096]{1,0:T(8,128)(2,1)} %shard_map.85, f32[64]{0:T(128)S(1)} %add_rsqrt_fusion.6), kind=kOutput, calls=%fused_computation.70 | convolution fusion | flops 2150105088 | bytes 35651840 | tf_op jit(solution)/shard_map/dot_general | solution.py:190
  216.9 4.2 collective-permute-start.3
  222.2 7.3 %collective-permute-done.3 = bf16[64,4096]{1,0:T(8,128)(2,1)S(1)} collective-permute-done((bf16[64,4096]{1,0:T(8,128)(2,1)}, bf16[64,4096]{1,0:T(8,128)(2,1)S(1)}, u32[]{:S(2)}, u32[]{:S(2)}) %collective-permute-start.3) | collective-permute-done | bytes 524320 | tf_op jit(solution)/shard_map/ppermute | solution.py:17
  229.8 13.8 %fusion = f32[5,64,4096]{2,1,0:T(8,128)S(1)} fusion(f32[5,64,4096]{2,1,0:T(8,128)S(1)} %bitcast_dynamic-update-slice_fusion, bf16[4096,4096]{1,0:T(8,128)(2,1)} %shard_map.85, bf16[64,4096]{1,0:T(8,128)(2,1)S(1)} %get-tuple-element.24, f32[64]{0:T(128)S(1)} %add_rsqrt_fusion.5), kind=kOutput, calls=%fused_computation.1 | convolution fusion | flops 2148270080 | bytes 35127808 | tf_op jit(solution)/shard_map/dot_general | solution.py:190
  246.7 15.9 %fusion.34 = (f32[64]{0:T(128)S(1)}, f32[64]{0:T(128)S(1)}, f32[64]{0:T(128)S(1)}, f32[64]{0:T(128)S(1)}, f32[64,4096]{1,0:T(8,128)S(1)}) fusion(bf16[5,64,4096]{2,1,0:T(8,128)(2,1)S(1)} %get-tuple-element.37, s32[]{:T(128)S(6)} %dynamic_slice.69, f32[64]{0:T(128)S(1)} %add_rsqrt_fusion.4, s32[]{:T(128)S(6)} %dynamic_slice.60, s32[]{:T(128)S(6)} %dynamic_slice.66, ...), kind=kOutput, calls=%fused_computation.61 | convolution fusion | flops 2150891520 | bytes 37225744 | tf_op jit(solution)/shard_map/dot_general | solution.py:201
  267.1 9.5 %collective-permute-done.4 = bf16[64,4096]{1,0:T(8,128)(2,1)S(1)} collective-permute-done((bf16[64,4096]{1,0:T(8,128)(2,1)S(1)}, bf16[64,4096]{1,0:T(8,128)(2,1)S(1)}, u32[]{:S(2)}, u32[]{:S(2)}) %collective-permute-start.4) | collective-permute-done | bytes 524320 | tf_op jit(solution)/shard_map/ppermute | solution.py:17
  278.2 15.7 %fusion.15 = (f32[64]{0:T(128)S(1)}, f32[64,4096]{1,0:T(8,128)S(1)}) fusion(f32[64]{0:T(128)S(1)} %add_rsqrt_fusion.3, bf16[5,64,4096]{2,1,0:T(8,128)(2,1)S(1)} %get-tuple-element.37, s32[]{:T(128)S(6)} %dynamic_slice.63, bf16[64,4096]{1,0:T(8,128)(2,1)S(1)} %get-tuple-element.57, bf16[4096,4096]{1,0:T(8,128)(2,1)} %shard_map.85), kind=kOutput, calls=%fused_computation.42 | convolution fusion | flops 2148532224 | bytes 35652100 | tf_op jit(solution)/shard_map/dot_general | solution.py:201
  295.9 9.3 %collective-permute-done.5 = bf16[64,4096]{1,0:T(8,128)(2,1)S(1)} collective-permute-done((bf16[64,4096]{1,0:T(8,128)(2,1)S(1)}, bf16[64,4096]{1,0:T(8,128)(2,1)S(1)}, u32[]{:S(2)}, u32[]{:S(2)}) %collective-permute-start.5) | collective-permute-done | bytes 524320 | tf_op jit(solution)/shard_map/ppermute | solution.py:17
  306.8 15.7 %fusion.12 = (f32[64]{0:T(128)S(1)}, f32[64,4096]{1,0:T(8,128)S(1)}) fusion(f32[64]{0:T(128)S(1)} %add_rsqrt_fusion.2, bf16[5,64,4096]{2,1,0:T(8,128)(2,1)S(1)} %get-tuple-element.37, s32[]{:T(128)S(6)} %dynamic_slice.66, bf16[64,4096]{1,0:T(8,128)(2,1)S(1)} %get-tuple-element.61, bf16[4096,4096]{1,0:T(8,128)(2,1)} %shard_map.85), kind=kOutput, calls=%fused_computation.39 | convolution fusion | flops 2148532224 | bytes 35652100 | tf_op jit(solution)/shard_map/dot_general | solution.py:201
  324.2 8.6 %collective-permute-done.6 = bf16[64,4096]{1,0:T(8,128)(2,1)S(1)} collective-permute-done((bf16[64,4096]{1,0:T(8,128)(2,1)S(1)}, bf16[64,4096]{1,0:T(8,128)(2,1)S(1)}, u32[]{:S(2)}, u32[]{:S(2)}) %collective-permute-start.6) | collective-permute-done | bytes 524320 | tf_op jit(solution)/shard_map/ppermute | solution.py:17
  334.5 16.6 %fusion.9 = (f32[64]{0:T(128)S(1)}, f32[64,4096]{1,0:T(8,128)S(1)}) fusion(f32[64]{0:T(128)S(1)} %add_rsqrt_fusion.1, bf16[5,64,4096]{2,1,0:T(8,128)(2,1)S(1)} %get-tuple-element.37, s32[]{:T(128)S(6)} %dynamic_slice.69, bf16[64,4096]{1,0:T(8,128)(2,1)S(1)} %get-tuple-element.65, bf16[4096,4096]{1,0:T(8,128)(2,1)} %shard_map.85), kind=kOutput, calls=%fused_computation.36 | convolution fusion | flops 2148532224 | bytes 35652100 | tf_op jit(solution)/shard_map/dot_general | solution.py:201
  357.0 5.5 %collective-permute-done.7 = bf16[64,4096]{1,0:T(8,128)(2,1)S(1)} collective-permute-done((bf16[64,4096]{1,0:T(8,128)(2,1)}, bf16[64,4096]{1,0:T(8,128)(2,1)S(1)}, u32[]{:S(2)}, u32[]{:S(2)}) %collective-permute-start.7) | collective-permute-done | bytes 524320 | tf_op jit(solution)/shard_map/ppermute | solution.py:17
  367.2 19.8 %shard_map.86 = bf16[32,2048,128]{2,1,0:T(8,128)(2,1)} custom-call(s32[2048]{0:T(1024)} %reshape_squeeze.3.table_ref, bf16[4096,128]{1,0:T(8,128)(2,1)} %bitcast.261, bf16[128,4096]{1,0:T(8,128)(2,1)} %bitcast.260), custom_call_target="tpu_custom_call" | custom-call | flops 4294967296 | bytes 18874368 | tf_op jit(solution)/shard_map/pallas_call | solution.py:107
  387.2 120.4 %reduce-scatter.2.cloned.1.call-done = bf16[1,2048,128]{2,1,0:T(8,128)(2,1)} async-done(((bf16[32,2048,128]{2,1,0:T(8,128)(2,1)}), bf16[1,2048,128]{2,1,0:T(8,128)(2,1)}) %reduce-scatter.2.cloned.1.call-update) | async-done | bytes 524304 | tf_op jit(solution)/shard_map/reduce_scatter | solution.py:273
  513.9 12.1 %shard_map.87 = f32[8,128]{1,0:T(8,128)} custom-call(f32[8,128]{1,0:T(8,128)} %scatter.4.x_ref), custom_call_target="tpu_custom_call" | custom-call | tf_op jit(solution)/shard_map/pallas_call | solution.py:171
  (100 shorter events, 58.0 us)
Async XLA Ops:
  7.2 4.2 copy-start.6
  7.2 4.5 copy-start.8
  7.2 79.4 %all-gather.2.cloned.1.call-start = ((), (), s32[]{:S(2)}) async-start(), calls=%async_computation.1 | async-start | bytes 17301504 | tf_op jit(solution)/shard_map/all_gather | solution.py:228
  9.4 498.2 %reduce-scatter.2.cloned.1.call-start = ((), (), s32[]{:S(2)}) async-start(), calls=%async_computation.2 | async-start | bytes 17301504 | tf_op jit(solution)/shard_map/reduce_scatter | solution.py:273
  11.6 2.7 copy-start.2
  112.4 31.1 %copy-start = (bf16[2,32,4096]{2,1,0:T(8,128)(2,1)S(1)}, bf16[2,32,4096]{2,1,0:T(8,128)(2,1)}, u32[]{:S(2)}) copy-start(bf16[2,32,4096]{2,1,0:T(8,128)(2,1)} %slice.42) | copy-start | bytes 1572868
  129.3 14.2 %collective-permute-start = (bf16[64,4096]{1,0:T(8,128)(2,1)S(1)}, bf16[64,4096]{1,0:T(8,128)(2,1)S(1)}, u32[]{:S(2)}, u32[]{:S(2)}) collective-permute-start(bf16[64,4096]{1,0:T(8,128)(2,1)S(1)} %get-tuple-element.47), channel_id=1, source_target_pairs={{0,32},{32,64},{64,96},{1,33},{33,65},{65,97},{2,34},{34,66},{66,9... | collective-permute-start | bytes 1572872 | tf_op jit(solution)/shard_map/ppermute | solution.py:17
  158.6 14.5 %collective-permute-start.1 = (bf16[64,4096]{1,0:T(8,128)(2,1)}, bf16[64,4096]{1,0:T(8,128)(2,1)S(1)}, u32[]{:S(2)}, u32[]{:S(2)}) collective-permute-start(bf16[64,4096]{1,0:T(8,128)(2,1)} %get-tuple-element.49), channel_id=1, source_target_pairs={{0,32},{32,64},{64,96},{1,33},{33,65},{65,97},{2,34},{34,66},{66,9... | collective-permute-start | bytes 1572872 | tf_op jit(solution)/shard_map/ppermute | solution.py:17
  188.3 13.5 %collective-permute-start.2 = (bf16[64,4096]{1,0:T(8,128)(2,1)}, bf16[64,4096]{1,0:T(8,128)(2,1)S(1)}, u32[]{:S(2)}, u32[]{:S(2)}) collective-permute-start(bf16[64,4096]{1,0:T(8,128)(2,1)} %get-tuple-element.51), channel_id=1, source_target_pairs={{0,32},{32,64},{64,96},{1,33},{33,65},{65,97},{2,34},{34,66},{66,9... | collective-permute-start | bytes 1572872 | tf_op jit(solution)/shard_map/ppermute | solution.py:17
  216.9 12.6 %collective-permute-start.3 = (bf16[64,4096]{1,0:T(8,128)(2,1)}, bf16[64,4096]{1,0:T(8,128)(2,1)S(1)}, u32[]{:S(2)}, u32[]{:S(2)}) collective-permute-start(bf16[64,4096]{1,0:T(8,128)(2,1)} %get-tuple-element.53), channel_id=1, source_target_pairs={{0,32},{32,64},{64,96},{1,33},{33,65},{65,97},{2,34},{34,66},{66,9... | collective-permute-start | bytes 1572872 | tf_op jit(solution)/shard_map/ppermute | solution.py:17
  229.8 16.3 %copy-start.4 = (bf16[4,32,4096]{2,1,0:T(8,128)(2,1)S(1)}, bf16[4,32,4096]{2,1,0:T(8,128)(2,1)}, u32[]{:S(2)}) copy-start(bf16[4,32,4096]{2,1,0:T(8,128)(2,1)} %param.9) | copy-start | bytes 3145732
  243.6 2.6 copy-start.1
  262.6 2.8 copy-start.3
  264.1 12.4 %collective-permute-start.4 = (bf16[64,4096]{1,0:T(8,128)(2,1)S(1)}, bf16[64,4096]{1,0:T(8,128)(2,1)S(1)}, u32[]{:S(2)}, u32[]{:S(2)}) collective-permute-start(bf16[64,4096]{1,0:T(8,128)(2,1)S(1)} %fusion.22), channel_id=1, source_target_pairs={{32,0},{64,32},{96,64},{33,1},{65,33},{97,65},{34,2},{66,34},{98,6... | collective-permute-start | bytes 1572872 | tf_op jit(solution)/shard_map/ppermute | solution.py:17
  294.3 10.8 %collective-permute-start.5 = (bf16[64,4096]{1,0:T(8,128)(2,1)S(1)}, bf16[64,4096]{1,0:T(8,128)(2,1)S(1)}, u32[]{:S(2)}, u32[]{:S(2)}) collective-permute-start(bf16[64,4096]{1,0:T(8,128)(2,1)S(1)} %fusion.26), channel_id=1, source_target_pairs={{32,0},{64,32},{96,64},{33,1},{65,33},{97,65},{34,2},{66,34},{98,6... | collective-permute-start | bytes 1572872 | tf_op jit(solution)/shard_map/ppermute | solution.py:17
  322.9 9.9 %collective-permute-start.6 = (bf16[64,4096]{1,0:T(8,128)(2,1)S(1)}, bf16[64,4096]{1,0:T(8,128)(2,1)S(1)}, u32[]{:S(2)}, u32[]{:S(2)}) collective-permute-start(bf16[64,4096]{1,0:T(8,128)(2,1)S(1)} %fusion.28), channel_id=1, source_target_pairs={{32,0},{64,32},{96,64},{33,1},{65,33},{97,65},{34,2},{66,34},{98,6... | collective-permute-start | bytes 1572872 | tf_op jit(solution)/shard_map/ppermute | solution.py:17
  334.5 16.6 %copy-start.7 = (bf16[5,64,4096]{2,1,0:T(8,128)(2,1)}, bf16[5,64,4096]{2,1,0:T(8,128)(2,1)S(1)}, u32[]{:S(2)}) copy-start(bf16[5,64,4096]{2,1,0:T(8,128)(2,1)S(1)} %get-tuple-element.64) | copy-start | bytes 7864324
  352.3 10.1 %collective-permute-start.7 = (bf16[64,4096]{1,0:T(8,128)(2,1)}, bf16[64,4096]{1,0:T(8,128)(2,1)S(1)}, u32[]{:S(2)}, u32[]{:S(2)}) collective-permute-start(bf16[64,4096]{1,0:T(8,128)(2,1)} %fusion.30), channel_id=1, source_target_pairs={{32,0},{64,32},{96,64},{33,1},{65,33},{97,65},{34,2},{66,34},{98,6... | collective-permute-start | bytes 1572872 | tf_op jit(solution)/shard_map/ppermute | solution.py:17
  387.0 121.9 %copy-start.5 = (bf16[1,2,64,2048]{3,2,1,0:T(8,128)(2,1)S(1)}, bf16[1,2,64,2048]{3,2,1,0:T(8,128)(2,1)}, u32[]{:S(2)}) copy-start(bf16[1,2,64,2048]{3,2,1,0:T(8,128)(2,1)} %param.10) | copy-start | bytes 1572868
Sparse Core Ops, SparseCore 0:
  10.3 76.2 all-gather.1
  387.1 120.4 reduce-scatter.1
